TPU v7x, 32 devices: a whole 2x2x4 slice. The times are simulated.
32 devices in a mesh: groups: 2 (over y), cache: 4 (over z), fsdp: 2 (over x), head: 2 (over core).
Axes of the slice: x: 2, y: 2, z: 4, core: 2. Of those that a mesh axis runs over, the one named last changes fastest.
Arguments:
- tokens: bfloat16 [1024, 3072], P(('groups', 'cache')), parts along dimension 0, may hold values from -6 to 6
- norm_gain: float32 [3072], replicated, may hold values from 0.1 to 1.9
- w_query: bfloat16 [3072, 4096], P('cache', ('fsdp', 'head')), may hold values from -0.109375 to 0.109375
- w_key: bfloat16 [3072, 4096], P('cache', ('fsdp', 'head')), may hold values from -0.109375 to 0.109375
- w_value: bfloat16 [3072, 4096], P('cache', ('fsdp', 'head')), may hold values from -0.109375 to 0.109375
- w_out: bfloat16 [4096, 3072], P(('fsdp', 'head'), 'cache'), may hold values from -0.09375 to 0.09375
- query_gain: float32 [128], replicated, may hold values from 0.1 to 1.9
- key_gain: float32 [128], replicated, may hold values from 0.1 to 1.9
- cache_keys: bfloat16 [4096, 4096], P(('groups', 'cache'), ('fsdp', 'head')), parts along dimension 0, may hold values from -3 to 3
- cache_values: bfloat16 [4096, 4096], P(('groups', 'cache'), ('fsdp', 'head')), parts along dimension 0, may hold values from -6 to 6
- step_gate: float32 [2, 3072], replicated, may hold values from 2 to 16
- block_list: int32 [8, 4], P('groups'), parts along dimension 0, may hold values from 0 to 7, as said below
- block_home: int32 [16], P('groups'), parts along dimension 0, may hold values from 0 to 7, as said below
- reader_span: int32 [8], P('groups'), parts along dimension 0, may hold values from 0 to 3, as said below
Outputs:
- denoised: bfloat16 [1024, 3072], P(('groups', 'cache'), ('fsdp', 'head')), parts along dimension 0
There are 2 independent parts, one for each index of `groups`. A program takes and returns all parts, laid end to end along the dimension named above; an argument that names none is the same for every part. Nothing has to cross between parts.
Inputs may be any that keep to these rules, and one draw needn't show every extreme that they name: A permutation of the storage slots: block b is held by cache device block_home[b] // 2. `block_list`: each row names 4 different blocks: blocks 0 to 1, then 2 window blocks, the one at position 2 + i being congruent to 2 + i modulo 4; the blocks of one row are held by different cache devices. `reader_span`: every span is named by 1 tiles.
All inputs are finite; a program needn't handle non-finite values.
Results may differ from a plain program's by a relative error of at most 0.023.
Values may be sent and summed in bfloat16 or wider, within the bound.
No kernel may reach another device: no remote copies, remote signals or barrier semaphores. Data moves between devices by JAX's collectives and lax.ppermute only.
A program may use at most 128 MiB of HBM per device.

v0:
```python
import jax
import jax.numpy as jnp
from jax import lax
from jax.sharding import PartitionSpec as P

BLOCK = 256
ITERS = 2


epsilon = 1e-06


def rms_scale(values, gain_row):
    mean_square = jnp.mean(values * values, axis=-1, keepdims=True)
    return values * lax.rsqrt(mean_square + epsilon) * gain_row


def head_norm(projected, gain_row):
    row_count = projected.shape[0]
    split = projected.reshape(row_count, -1, gain_row.shape[0])
    return rms_scale(split, gain_row).astype(jnp.bfloat16).reshape(row_count, -1)


def attend(queries, key_rows, value_rows, head_dim):
    row_count = queries.shape[0]
    head_count = queries.shape[1] // head_dim
    query_heads = queries.reshape(row_count, head_count, head_dim)
    key_heads = key_rows.reshape(-1, head_count, head_dim)
    value_heads = value_rows.reshape(-1, head_count, head_dim)
    scores = jnp.einsum(
        "qhd,khd->hqk", query_heads, key_heads, preferred_element_type=jnp.float32
    ) * head_dim ** (-0.5)
    weights = jnp.exp(scores)
    totals = jnp.sum(weights, axis=2)
    summed = jnp.einsum(
        "hqk,khd->qhd",
        weights.astype(jnp.bfloat16),
        value_heads,
        preferred_element_type=jnp.float32,
    )
    return (
        (summed / jnp.transpose(totals)[:, :, None])
        .astype(jnp.bfloat16)
        .reshape(row_count, head_count * head_dim)
    )


def per_device(
    tokens,
    norm_gain,
    w_query,
    w_key,
    w_value,
    w_out,
    query_gain,
    key_gain,
    cache_keys,
    cache_values,
    step_gate,
    block_list,
    block_home,
    reader_span,
):
    reader_index = lax.axis_index("cache")
    group_index = lax.axis_index(("fsdp", "head"))
    head_dim = query_gain.shape[0]
    panel_width = cache_keys.shape[1]
    held_blocks = cache_keys.shape[0] // BLOCK
    full_query, full_key, full_value = (
        lax.all_gather(w_query, "cache", axis=0, tiled=True),
        lax.all_gather(w_key, "cache", axis=0, tiled=True),
        lax.all_gather(w_value, "cache", axis=0, tiled=True),
    )
    out_panel = lax.all_gather(w_out, "cache", axis=1, tiled=True)
    wanted = jnp.take(block_list, reader_span, axis=0)
    home_slots = jnp.take(block_home, wanted)
    is_mine = home_slots // held_blocks == reader_index
    local_pos = jnp.sum(jnp.where(is_mine, home_slots % held_blocks, 0), axis=1)
    key_blocks = cache_keys.reshape(held_blocks, BLOCK, panel_width)
    value_blocks = cache_values.reshape(held_blocks, BLOCK, panel_width)
    send_keys = jnp.take(key_blocks, local_pos, axis=0)
    send_values = jnp.take(value_blocks, local_pos, axis=0)
    got_keys, got_values = (
        lax.all_to_all(send_keys, "cache", split_axis=0, concat_axis=0, tiled=True),
        lax.all_to_all(send_values, "cache", split_axis=0, concat_axis=0, tiled=True),
    )
    my_span = jnp.take(reader_span, reader_index)
    my_owners = jnp.take(block_home, jnp.take(block_list, my_span, axis=0)) // held_blocks
    fetched_keys = jnp.take(got_keys, my_owners, axis=0).reshape(-1, panel_width)
    fetched_values = jnp.take(got_values, my_owners, axis=0).reshape(-1, panel_width)
    out_columns = lax.all_to_all(
        out_panel, ("fsdp", "head"), split_axis=1, concat_axis=0, tiled=True
    )
    column_count = tokens.shape[1] // lax.axis_size(("fsdp", "head"))
    column_start = group_index * column_count
    current = tokens
    x_share = lax.dynamic_slice_in_dim(tokens, column_start, column_count, 1)
    for step_index in range(ITERS):
        normed = rms_scale(current.astype(jnp.float32), norm_gain).astype(jnp.bfloat16)
        queries = head_norm(
            jnp.dot(normed, full_query, preferred_element_type=jnp.float32), query_gain
        )
        own_keys = head_norm(
            jnp.dot(normed, full_key, preferred_element_type=jnp.float32), key_gain
        )
        own_values = jnp.dot(normed, full_value, preferred_element_type=jnp.float32).astype(
            jnp.bfloat16
        )
        all_keys = jnp.concatenate([fetched_keys, own_keys], axis=0)
        all_values = jnp.concatenate([fetched_values, own_values], axis=0)
        mixed = attend(queries, all_keys, all_values, head_dim)
        step_scale = step_gate[step_index]
        share_scale = lax.dynamic_slice_in_dim(step_scale, column_start, column_count, 0)
        heads_all = lax.all_gather(mixed, ("fsdp", "head"), axis=1, tiled=True)
        update = jnp.dot(heads_all, out_columns, preferred_element_type=jnp.float32)
        x_share = (x_share.astype(jnp.float32) + share_scale * update).astype(jnp.bfloat16)
        if step_index + 1 < ITERS:
            current = lax.all_gather(x_share, ("fsdp", "head"), axis=1, tiled=True)
    return x_share


def solution(mesh):
    in_specs = (
        P(("groups", "cache"), None),
        P(),
        P("cache", ("fsdp", "head")),
        P("cache", ("fsdp", "head")),
        P("cache", ("fsdp", "head")),
        P(("fsdp", "head"), "cache"),
        P(),
        P(),
        P(("groups", "cache"), ("fsdp", "head")),
        P(("groups", "cache"), ("fsdp", "head")),
        P(),
        P("groups", None),
        P("groups"),
        P("groups"),
    )
    out_specs = P(("groups", "cache"), ("fsdp", "head"))
    return jax.shard_map(
        per_device, mesh=mesh, in_specs=in_specs, out_specs=out_specs, check_vma=False
    )
```

profile of v0, /device:TPU:2, one launch (start us, length us, event | category | flops | bytes accessed | tf_op | source)
XLA Modules:
  0.0 649.3 jit_solution(339749050761248842)
XLA Ops:
  6.5 2.7 copy.67
  9.3 0.7 all-gather.7.cloned.1.call-update
  10.1 0.7 all-gather.9.cloned.1.call-update
  10.8 0.5 all-gather.11.cloned.1.call-update
  11.4 0.6 gather_fusion
  12.2 0.7 gather_fusion.1
  12.9 0.2 fusion.52
  13.1 0.7 gather_fusion.5
  13.8 3.3 gather_fusion.3
  17.1 3.7 broadcast_select_fusion.3
  20.8 109.9 %all_to_all.29 = bf16[4,256,1024]{2,1,0:T(8,128)(2,1)} all-to-all(bf16[4,256,1024]{2,1,0:T(8,128)(2,1)S(1)} %get-tuple-element.35), channel_id=1, replica_groups=mesh['groups'=2,'cache'=4,'fsdp'=2,'head'=2] {'cache'}, dimensions={0} | all-to-all | bytes 4194304 | tf_op jit(solution)/shard_map/all_to_all | solution.py:85
  130.7 3.7 all-to-all-start.1
  134.5 0.6 dynamic-slice.7
  135.8 0.6 gather_fusion.2
  136.5 0.2 fusion.14
  136.8 3.6 gather_fusion.4
  140.4 73.7 %all-to-all-done.1 = bf16[4,256,1024]{2,1,0:T(8,128)(2,1)S(1)} async-done(((bf16[4,256,1024]{2,1,0:T(8,128)(2,1)}), bf16[4,256,1024]{2,1,0:T(8,128)(2,1)S(1)}, u32[]{:S(2)}, u32[]{:S(2)}) %all-to-all-start.1) | async-done | bytes 2097184 | tf_op jit(solution)/shard_map/all_to_all | solution.py:84
  214.1 2.1 gather_fusion.6
  216.1 4.0 broadcast_select_fusion.1
  220.1 0.6 copy.81
  220.7 2.9 copy.77
  223.6 2.4 copy.83
  226.1 0.3 copy.64
  226.4 5.8 all-to-all-start.2
  232.2 98.3 %all-gather.7.cloned.1.call-done = bf16[3072,1024]{1,0:T(8,128)(2,1)} async-done(((bf16[768,1024]{1,0:T(8,128)(2,1)}), bf16[3072,1024]{1,0:T(8,128)(2,1)}) %all-gather.7.cloned.1.call-update) | async-done | bytes 6291472 | tf_op jit(solution)/shard_map/all_gather | solution.py:72
  330.5 3.8 convolution_convert_fusion.1
  334.3 0.8 copy.78
  335.1 110.5 %all-gather.9.cloned.1.call-done = bf16[3072,1024]{1,0:T(8,128)(2,1)} async-done(((bf16[768,1024]{1,0:T(8,128)(2,1)}), bf16[3072,1024]{1,0:T(8,128)(2,1)}) %all-gather.9.cloned.1.call-update) | async-done | bytes 6291472 | tf_op jit(solution)/shard_map/all_gather | solution.py:70
  445.7 3.8 convolution_bitcast_fusion.1
  449.6 0.8 copy-done.7
  450.4 0.2 multiply_reduce_fusion.1
  450.7 0.1 copy.61
  450.8 109.9 %all-gather.11.cloned.1.call-done = bf16[3072,1024]{1,0:T(8,128)(2,1)} async-done(((bf16[768,1024]{1,0:T(8,128)(2,1)}), bf16[3072,1024]{1,0:T(8,128)(2,1)}) %all-gather.11.cloned.1.call-update) | async-done | bytes 6291472 | tf_op jit(solution)/shard_map/all_gather | solution.py:71
  560.7 3.8 fusion.63
  564.5 0.8 copy-done.6
  565.4 0.9 copy.84
  566.3 1.2 reduce_sum.84
  567.7 1.2 multiply_convert_fusion.1
  569.0 0.2 mul.174
  569.2 1.2 copy_bitcast_fusion.1
  570.4 1.3 exponential_reduce_fusion.1
  571.6 0.3 copy-done.8
  571.9 1.6 fusion.33
  573.7 8.8 %copy.68 = bf16[4,1024,768]{2,1,0:T(8,128)(2,1)} copy(bf16[4,1024,768]{1,2,0:T(8,128)(2,1)} %bitcast.14) | data formatting | bytes 12582912 | tf_op jit(solution)/shard_map/all_to_all | solution.py:91
  582.5 5.1 all-gather.13.cloned.1.call-done
  587.5 4.3 fusion.29
  591.8 9.0 %all_gather.26 = bf16[128,3072]{1,0:T(8,128)(2,1)S(1)} all-gather(bf16[128,768]{1,0:T(8,128)(2,1)S(1)} %fusion.29), channel_id=1, replica_groups=mesh['groups'=2,'cache'=4,'fsdp'=2,'head'=2] {'fsdp','head'}, dimensions={1}, use_global_device_ids=true | all-gather | bytes 983040 | tf_op jit(solution)/shard_map/all_gather | solution.py:118
  600.8 0.2 fusion.17
  601.1 3.9 convolution_bitcast_fusion
  605.0 0.9 copy.86
  606.0 1.1 convolution_convert_fusion
  607.1 0.8 copy.69
  607.9 1.2 multiply_reduce_fusion
  609.3 1.9 multiply_convert_fusion
  611.3 3.8 fusion.59
  615.1 0.8 copy-done.4
  616.1 0.2 reduce_sum.88
  616.5 0.2 mul.195
  616.7 0.3 copy-done.5
  617.0 0.1 copy_bitcast_fusion
  617.2 2.1 exponential_reduce_fusion
  619.3 1.6 fusion.39
  621.0 16.7 %all-gather.17.cloned.1.call-done = bf16[128,4096]{0,1:T(8,128)(2,1)} async-done(((bf16[128,1024]{0,1:T(8,128)(2,1)}), bf16[128,4096]{0,1:T(8,128)(2,1)}) %all-gather.17.cloned.1.call-update) | async-done | bytes 1048592 | tf_op jit(solution)/shard_map/all_gather | solution.py:114
  637.6 4.9 fusion.28
  (82 shorter events, 1.6 us)
Async XLA Ops:
  6.5 6.6 %copy-start = (bf16[512,1024]{1,0:T(8,128)(2,1)S(1)}, bf16[512,1024]{1,0:T(8,128)(2,1)}, u32[]{:S(2)}) copy-start(bf16[512,1024]{1,0:T(8,128)(2,1)} %param.26) | copy-start | bytes 3145732
  6.5 219.8 %all-gather.15.cloned.1.call-start = ((), (), s32[]{:S(2)}) async-start(), calls=%async_computation.7 | async-start | bytes 7864320 | tf_op jit(solution)/shard_map/all_gather | solution.py:74
  9.3 2.1 copy-start.17
  9.3 2.1 copy-start.13
  9.3 2.9 copy-start.2
  9.3 321.2 %all-gather.7.cloned.1.call-start = ((), (), s32[]{:S(2)}) async-start(), calls=%async_computation.3 | async-start | bytes 7864320 | tf_op jit(solution)/shard_map/all_gather | solution.py:72
  10.0 435.6 %all-gather.9.cloned.1.call-start = ((), (), s32[]{:S(2)}) async-start(), calls=%async_computation.4 | async-start | bytes 7864320 | tf_op jit(solution)/shard_map/all_gather | solution.py:70
  10.8 549.9 %all-gather.11.cloned.1.call-start = ((), (), s32[]{:S(2)}) async-start(), calls=%async_computation.5 | async-start | bytes 7864320 | tf_op jit(solution)/shard_map/all_gather | solution.py:71
  130.7 5.8 copy-start.3
  130.7 6.0 copy-start.16
  130.7 83.3 %all-to-all-start.1 = ((bf16[4,256,1024]{2,1,0:T(8,128)(2,1)}), bf16[4,256,1024]{2,1,0:T(8,128)(2,1)S(1)}, u32[]{:S(2)}, u32[]{:S(2)}) async-start(bf16[4,256,1024]{2,1,0:T(8,128)(2,1)} %get-tuple-element.36), calls=%async_computation.1 | async-start | bytes 4194304 | tf_op jit(solution)/shard_map/all_to_all | solution.py:84
  226.4 104.1 %copy-start.10 = (f32[3072]{0:T(1024)S(1)}, f32[3072]{0:T(1024)}, u32[]{:S(2)}) copy-start(f32[3072]{0:T(1024)} %param.19) | copy-start | bytes 36868
  226.4 347.3 %all-to-all-start.2 = ((bf16[1024,4,768]{0,2,1:T(8,128)(2,1)}), bf16[1024,4,768]{0,2,1:T(8,128)(2,1)}, u32[]{:S(2)}, u32[]{:S(2)}) async-start(bf16[1024,4,768]{0,2,1:T(8,128)(2,1)} %bitcast.111), calls=%async_computation.2 | async-start | bytes 12582912 | tf_op jit(solution)/shard_map/all_to_all | solution.py:91
  232.2 355.4 %all-gather.13.cloned.1.call-start = ((), (), s32[]{:S(2)}) async-start(), calls=%async_computation.6 | async-start | bytes 1310720 | tf_op jit(solution)/shard_map/all_gather | solution.py:114
  449.6 0.8 copy-start.7
  564.5 0.8 copy-start.6
  565.3 2.4 copy-start.15
  570.3 1.6 copy-start.8
  570.4 1.6 copy-start.11
  571.9 1.7 copy-start.14
  573.6 64.1 %all-gather.17.cloned.1.call-start = ((), (), s32[]{:S(2)}) async-start(), calls=%async_computation.8 | async-start | bytes 1310720 | tf_op jit(solution)/shard_map/all_gather | solution.py:114
  587.5 18.4 %slice-start = ((s8[6291456]{0:T(1024)(128)(4,1)}), s8[4194304]{0:T(1024)(128)(4,1)S(1)}, s32[]{:S(2)}) async-start(s8[6291456]{0:T(1024)(128)(4,1)} %bitcast.105), calls=%async_computation.9 | async-start | bytes 8388608
  600.8 5.1 slice-start.1
  615.1 0.8 copy-start.4
  616.0 1.0 copy-start.5
  617.2 2.1 copy-start.9
  617.2 2.1 copy-start.12
  620.9 21.6 %copy-start.1 = (bf16[512,1024]{1,0:T(8,128)(2,1)S(1)}, bf16[512,1024]{1,0:T(8,128)(2,1)}, u32[]{:S(2)}) copy-start(bf16[512,1024]{1,0:T(8,128)(2,1)} %param.26) | copy-start | bytes 3145732
Sparse Core Ops, SparseCore 0:
  9.4 205.9 all-gather.14
  217.0 113.4 all-gather.6
  332.1 113.5 all-gather.8
  447.1 113.5 all-gather.10
  573.7 13.7 all-gather.12
  621.0 16.5 all-gather.16
where the time goes:
time: 653 us; the launch traced here: 649 us
  waiting for transfers between devices  416 us (64%)
  blocking collectives  119 us (18%)
  local copies, waits for them, and re-layouts  37.9 us (6%)
  matrix products  35.9 us (5%)
  other arithmetic  16.1 us (2%)
  between operations  14.6 us (2%)
  starting transfers between devices  9.68 us (1%)
    all_gather x1, waiting for transfers between devices, per_device(): lax.all_gather(w_query, 'cache', axis=0, tiled=True)  111 us
    all_to_all x1, blocking collectives, per_device(): lax.all_to_all(send_values, 'cache', split_axis=0, concat_axis=0, tiled=T...  110 us
    all_gather x1, waiting for transfers between devices, per_device(): lax.all_gather(w_key, 'cache', axis=0, tiled=True)  110 us
    all_gather x1, waiting for transfers between devices, per_device(): lax.all_gather(w_value, 'cache', axis=0, tiled=True)  98.3 us
    all_to_all x1, waiting for transfers between devices, per_device(): lax.all_to_all(send_keys, 'cache', split_axis=0, concat_axis=0, tiled=True)  73.7 us
    all_gather x2, waiting for transfers between devices, per_device(): heads_all = lax.all_gather(mixed, ('fsdp', 'head'), axis=1, tiled=True)  21.7 us
  transfers between devices with their start and end apart: 8, of which 6 were waited for; matrix products, arithmetic and copies ran while one was open for 9% of the time, Pallas kernels for 0%

commit v1 on v0

--- a/solution.py
+++ b/solution.py
@@ -1,6 +1,10 @@
+import functools
+
 import jax
 import jax.numpy as jnp
 from jax import lax
+from jax.experimental import pallas as pl
+from jax.experimental.pallas import tpu as pltpu
 from jax.sharding import PartitionSpec as P
 
 BLOCK = 256
@@ -45,7 +49,7 @@
     )
 
 
-def per_device(
+def gathered_panels(
     tokens,
     norm_gain,
     w_query,
@@ -119,6 +123,213 @@
     return x_share
 
 
+WAYS = 4
+VMEM_LIMIT = 56 * 1024 * 1024
+
+
+def whole_specs(count):
+    return [pl.BlockSpec(memory_space=pltpu.VMEM) for _ in range(count)]
+
+
+def project_kernel(gain_ref, query_gain_ref, key_gain_ref, *refs):
+    pieces, panels = refs[:WAYS], refs[WAYS : 3 * WAYS]
+    q_ref, k_ref, v_ref, normed_ref = refs[3 * WAYS :]
+    tile, width = pieces[0].shape[1:]
+    for r in range(WAYS):
+        rows = [pieces[r ^ k][k].astype(jnp.float32) for k in range(WAYS)]
+        square = sum(jnp.sum(x * x, axis=-1, keepdims=True) for x in rows)
+        scale = lax.rsqrt(square / (WAYS * width) + epsilon)
+        for k in range(WAYS):
+            normed_ref[k, r * tile : (r + 1) * tile, :] = (
+                rows[k] * scale * gain_ref[k : k + 1, :]
+            ).astype(jnp.bfloat16)
+    head_dim = query_gain_ref.shape[1]
+    for h in range(2):
+        total = jnp.dot(normed_ref[0], panels[h][...], preferred_element_type=jnp.float32)
+        for k in range(1, WAYS):
+            total += jnp.dot(
+                normed_ref[k], panels[2 * k + h][...], preferred_element_type=jnp.float32
+            )
+        lanes = slice(h * head_dim, (h + 1) * head_dim)
+        q_ref[:, lanes] = rms_scale(total[:, :head_dim], query_gain_ref[...]).astype(jnp.bfloat16)
+        k_ref[:, lanes] = rms_scale(
+            total[:, head_dim : 2 * head_dim], key_gain_ref[...]
+        ).astype(jnp.bfloat16)
+        v_ref[:, lanes] = total[:, 2 * head_dim :].astype(jnp.bfloat16)
+
+
+def project(pieces, panels, gain_rows, query_gain, key_gain):
+    tile, width = pieces[0].shape[1:]
+    head_dim = query_gain.shape[1]
+    shape = jax.ShapeDtypeStruct((WAYS * tile, 2 * head_dim), jnp.bfloat16)
+    return pl.pallas_call(
+        project_kernel,
+        out_shape=[shape] * 3,
+        in_specs=whole_specs(3 + 3 * WAYS),
+        out_specs=whole_specs(3),
+        scratch_shapes=[pltpu.VMEM((WAYS, WAYS * tile, width), jnp.bfloat16)],
+        compiler_params=pltpu.CompilerParams(vmem_limit_bytes=VMEM_LIMIT),
+    )(gain_rows, query_gain, key_gain, *pieces, *panels)
+
+
+def attend_kernel(pos_ref, q_ref, k_ref, v_ref, *refs):
+    held, mixed_ref = refs[:WAYS], refs[WAYS]
+    head_dim = q_ref.shape[1] // 2
+    tile = q_ref.shape[0] // WAYS
+    across = (((1,), (1,)), ((), ()))
+    for r in range(WAYS):
+        rows = slice(r * tile, (r + 1) * tile)
+        for h in range(2):
+            lanes = slice(h * head_dim, (h + 1) * head_dim)
+            value_lanes = slice((2 + h) * head_dim, (3 + h) * head_dim)
+            query = q_ref[rows, lanes]
+            keys = [k_ref[rows, lanes]]
+            values = [v_ref[rows, lanes]]
+            for k in range(WAYS):
+                start = pl.multiple_of(pos_ref[r * WAYS + k] * BLOCK, BLOCK)
+                keys.append(held[k][pl.ds(start, BLOCK), lanes])
+                values.append(held[k][pl.ds(start, BLOCK), value_lanes])
+            total = jnp.zeros((tile, 1), jnp.float32)
+            summed = jnp.zeros((tile, head_dim), jnp.float32)
+            for key, value in zip(keys, values):
+                scores = lax.dot_general(query, key, across, preferred_element_type=jnp.float32)
+                weights = jnp.exp(scores * head_dim ** (-0.5))
+                total += jnp.sum(weights, axis=-1, keepdims=True)
+                summed += jnp.dot(
+                    weights.astype(jnp.bfloat16), value, preferred_element_type=jnp.float32
+                )
+            mixed_ref[rows, lanes] = (summed / total).astype(jnp.bfloat16)
+
+
+def attend_all(pos, q, k, v, held):
+    return pl.pallas_call(
+        attend_kernel,
+        out_shape=jax.ShapeDtypeStruct(q.shape, jnp.bfloat16),
+        in_specs=[pl.BlockSpec(memory_space=pltpu.SMEM)] + whole_specs(3 + WAYS),
+        out_specs=pl.BlockSpec(memory_space=pltpu.VMEM),
+        compiler_params=pltpu.CompilerParams(vmem_limit_bytes=VMEM_LIMIT),
+    )(pos, q, k, v, *held)
+
+
+def out_kernel(w_ref, *refs):
+    mixed, (keep_ref, send_ref) = refs[:WAYS], refs[WAYS:]
+    depth = mixed[0].shape[1]
+    tile = mixed[0].shape[0] // WAYS
+    for r in range(WAYS):
+        row = jnp.concatenate(
+            [mixed[k][(r ^ k) * tile : ((r ^ k) + 1) * tile, :] for k in range(WAYS)], axis=1
+        )
+        update = jnp.dot(row, w_ref[...], preferred_element_type=jnp.float32)
+        rows = slice((r // 2) * tile, (r // 2 + 1) * tile)
+        if r % 2 == 0:
+            keep_ref[rows, :] = update
+        else:
+            send_ref[rows, :] = update.astype(jnp.bfloat16)
+
+
+def project_out(w_rows, mixed):
+    tile = mixed[0].shape[0] // WAYS
+    width = w_rows.shape[1]
+    return pl.pallas_call(
+        out_kernel,
+        out_shape=[
+            jax.ShapeDtypeStruct((2 * tile, width), jnp.float32),
+            jax.ShapeDtypeStruct((2 * tile, width), jnp.bfloat16),
+        ],
+        in_specs=whole_specs(1 + WAYS),
+        out_specs=whole_specs(2),
+        compiler_params=pltpu.CompilerParams(vmem_limit_bytes=VMEM_LIMIT),
+    )(w_rows, *mixed)
+
+
+SWAP = [(0, 1), (1, 0)]
+
+
+def from_z(value, k):
+    return lax.ppermute(value, "cache", [(i, i ^ k) for i in range(WAYS)])
+
+
+def split_heads(
+    tokens,
+    norm_gain,
+    w_query,
+    w_key,
+    w_value,
+    w_out,
+    query_gain,
+    key_gain,
+    cache_keys,
+    cache_values,
+    step_gate,
+    block_list,
+    block_home,
+    reader_span,
+):
+    z = lax.axis_index("cache")
+    p = lax.axis_index(("fsdp", "head"))
+    y = lax.axis_index("groups")
+    head_dim = query_gain.shape[0]
+    held_blocks = cache_keys.shape[0] // BLOCK
+    width = tokens.shape[1] // WAYS
+    tile = tokens.shape[0]
+    ways = jnp.arange(WAYS, dtype=jnp.int32)
+
+    def head_of(array, k, h):
+        return lax.dynamic_slice_in_dim(array, ((z ^ k) * 2 + (y ^ h)) * head_dim, head_dim, 1)
+
+    def panel_of(k, h):
+        return jnp.concatenate([head_of(w, k, h) for w in (w_query, w_key, w_value)], axis=1)
+
+    def cache_of(k):
+        return jnp.concatenate([head_of(a, k, h) for a in (cache_keys, cache_values) for h in (0, 1)], axis=1)
+
+    piece = lax.dynamic_slice_in_dim(tokens, p * width, width, 1)
+    by_z = jnp.stack([piece] + [from_z(piece, k) for k in range(1, WAYS)])
+    by_x = jnp.stack([by_z, lax.ppermute(by_z, "fsdp", SWAP)])
+    by_core = lax.ppermute(by_x, "head", SWAP)
+    gathered = jnp.stack([by_x, by_core], axis=1).reshape(WAYS * WAYS, tile, width)
+
+    near = [panel_of(0, 0)] + [from_z(panel_of(k, 0), k) for k in range(1, WAYS)]
+    far = [panel_of(0, 1)] + [lax.ppermute(near[k], "groups", SWAP) for k in range(1, WAYS)]
+    panels = [panel for pair in zip(near, far) for panel in pair]
+    held = [cache_of(0)] + [from_z(cache_of(k), k) for k in range(1, WAYS)]
+
+    source = (z ^ p ^ ways)[None, :] * WAYS + (p ^ ways[:, None] ^ ways[None, :])
+    pieces = [jnp.take(gathered, source[j], axis=0) for j in range(WAYS)]
+    x_share = pieces[0][0]
+
+    gain_rows = jnp.take(norm_gain.reshape(WAYS, width), z ^ ways, axis=0)
+    heads = jnp.stack([(z ^ ways) * 2 + y, (z ^ ways) * 2 + 1 - y], axis=1).reshape(-1)
+    w_rows = jnp.take(w_out.reshape(2 * WAYS, head_dim, width), heads, axis=0).reshape(-1, width)
+    gates = lax.dynamic_slice_in_dim(step_gate, z * width, width, 1)
+    slots = jnp.take(block_home, jnp.take(block_list, jnp.take(reader_span, z ^ p ^ ways), axis=0))
+    from_k = slots[:, :, None] // held_blocks == (z ^ ways)[None, None, :]
+    pos = jnp.sum(jnp.where(from_k, (slots % held_blocks)[:, :, None], 0), axis=1).reshape(-1)
+
+    for step in range(ITERS):
+        q, k, v = project(pieces, panels, gain_rows, query_gain[None], key_gain[None])
+        own = attend_all(pos, q, k, v, held)
+        mixed = [own] + [from_z(own, k) for k in range(1, WAYS)]
+        keep, send = project_out(w_rows, mixed)
+        half = keep + lax.ppermute(send, "head", SWAP).astype(jnp.float32)
+        other = lax.ppermute(half[tile:].astype(jnp.bfloat16), "fsdp", SWAP)
+        update = half[:tile] + other.astype(jnp.float32)
+        x_share = (x_share.astype(jnp.float32) + gates[step] * update).astype(jnp.bfloat16)
+        if step + 1 < ITERS:
+            by_z = jnp.stack([x_share] + [from_z(x_share, k) for k in range(1, WAYS)])
+            by_x = lax.ppermute(by_z, "fsdp", SWAP)
+            pieces = [
+                by_z,
+                lax.ppermute(by_z, "head", SWAP),
+                by_x,
+                lax.ppermute(by_x, "head", SWAP),
+            ]
+    moves = [
+        (a * WAYS + b, (a ^ b) * WAYS + a) for a in range(WAYS) for b in range(WAYS)
+    ]
+    return lax.ppermute(x_share, ("cache", "fsdp", "head"), moves)
+
+
 def solution(mesh):
     in_specs = (
         P(("groups", "cache"), None),
@@ -137,6 +348,18 @@
         P("groups"),
     )
     out_specs = P(("groups", "cache"), ("fsdp", "head"))
-    return jax.shard_map(
-        per_device, mesh=mesh, in_specs=in_specs, out_specs=out_specs, check_vma=False
-    )
+    sizes = dict(mesh.shape)
+
+    def program(*args):
+        panel_width, head_dim = args[2].shape[1] // (sizes["fsdp"] * sizes["head"]), args[6].shape[0]
+        fits = (
+            sizes == {"groups": 2, "cache": WAYS, "fsdp": 2, "head": 2}
+            and panel_width == 2 * WAYS * head_dim
+            and args[11].shape[1] == WAYS
+        )
+        plan = split_heads if fits else gathered_panels
+        return jax.shard_map(
+            plan, mesh=mesh, in_specs=in_specs, out_specs=out_specs, check_vma=False
+        )(*args)
+
+    return program

time: 653 us -> 281 us (0.43)
  waiting for transfers between devices: 416 us -> 145 us
  blocking collectives: 119 us -> 0 us
  matrix products: 35.9 us -> 0 us
  Pallas kernels: 0 us -> 35.4 us
  starting transfers between devices: 9.68 us -> 34.9 us
  between operations: 14.6 us -> 0.33 us
  other arithmetic: 16.1 us -> 30.3 us
    all_gather x6 -> x0, waiting for transfers between devices: 341 us -> none  [the longest x1 111 us: per_device(): lax.all_gather(w_query, 'cache', axis=0, tiled=True)]
    ppermute x0 -> x31, waiting for transfers between devices: none -> 145 us  [the longest x18 59.7 us: from_z(): return lax.ppermute(value, 'cache', [(i, i ^ k) for i in range(WAYS)])]
    all_to_all x1 -> x0, blocking collectives: 110 us -> none  [per_device(): lax.all_to_all(send_values, 'cache', split_axis=0, concat_axis=0, tiled=T...]
    all_to_all x2 -> x0, waiting for transfers between devices: 73.7 us -> none  [the longest x1 73.7 us: per_device(): lax.all_to_all(send_keys, 'cache', split_axis=0, concat_axis=0, tiled=True)]
    dot_general x12 -> x0, matrix products: 35.9 us -> none  [the longest x2 9.15 us: per_device(): update = jnp.dot(heads_all, out_columns, preferred_element_type=jnp.float32)]
    pallas_call x0 -> x6, Pallas kernels: none -> 35.4 us  [the longest x2 16.5 us: project(): pl.pallas_call(project_kernel, out_shape=[shape] * 3, in_specs=whole_spec...]
    ppermute x0 -> x31, starting transfers between devices: none -> 34.9 us  [the longest x18 27 us: from_z(): return lax.ppermute(value, 'cache', [(i, i ^ k) for i in range(WAYS)])]
    all_to_all x2 -> x0, starting transfers between devices: 9.52 us -> none  [the longest x1 5.77 us: per_device(): lax.all_to_all(out_panel, ('fsdp', 'head'), split_axis=1, concat_axis=0,...]
  transfers between devices with their start and end apart: 8 -> 31, of which waited for: 6 -> 17; matrix products, arithmetic and copies ran while one was open for 9% -> 19% of each run, Pallas kernels for 0% -> 3%
where the time goes in v1:
time: 281 us; the launch traced here: 280 us
  waiting for transfers between devices  145 us (52%)
  Pallas kernels  35.4 us (13%)
  starting transfers between devices  34.9 us (12%)
  local copies, waits for them, and re-layouts  34.6 us (12%)
  other arithmetic  30.3 us (11%)
    ppermute x18, waiting for transfers between devices, from_z(): return lax.ppermute(value, 'cache', [(i, i ^ k) for i in range(WAYS)])  59.7 us
    ppermute x18, starting transfers between devices, from_z(): return lax.ppermute(value, 'cache', [(i, i ^ k) for i in range(WAYS)])  27 us
    ppermute x3, waiting for transfers between devices, split_heads(): lax.ppermute(near[k], 'groups', SWAP)  21.5 us
    ppermute x1, waiting for transfers between devices, split_heads(): by_x = lax.ppermute(by_z, 'fsdp', SWAP)  18.7 us
    pallas_call x2, Pallas kernels, project(): pl.pallas_call(project_kernel, out_shape=[shape] * 3, in_specs=whole_spec...  16.5 us
    ppermute x1, waiting for transfers between devices, split_heads(): by_x = jnp.stack([by_z, lax.ppermute(by_z, 'fsdp', SWAP)])  16.3 us
    gather x4, local copies, waits for them, and re-layouts, split_heads(): pieces = [jnp.take(gathered, source[j], axis=0) for j in range(WAYS)]  13.9 us
    ppermute x2, waiting for transfers between devices, split_heads(): other = lax.ppermute(half[tile:].astype(jnp.bfloat16), 'fsdp', SWAP)  12 us
  transfers between devices with their start and end apart: 31, of which 17 were waited for; matrix products, arithmetic and copies ran while one was open for 19% of the time, Pallas kernels for 3%

profile of v1, /device:TPU:2, one launch (start us, length us, event | category | flops | bytes accessed | tf_op | source)
XLA Modules:
  0.0 280.3 jit_solution(8671613844007399780)
XLA Ops:
  0.0 1.7 constant_dynamic-slice_fusion.32
  1.7 2.6 collective-permute-start.1
  4.3 1.6 collective-permute-start
  6.1 1.5 constant_dynamic-slice_fusion.19
  8.0 2.5 constant_dynamic-slice_fusion.17
  10.5 0.9 pad_maximum_fusion.7
  11.4 1.7 collective-permute-start.7
  13.1 0.9 pad_maximum_fusion.6
  14.0 2.5 collective-permute-start.5
  17.2 0.9 fusion.17
  21.1 1.7 constant_dynamic-slice_fusion.2
  23.7 0.9 pad_maximum_fusion.8
  25.2 1.2 fusion.16
  27.8 16.3 %collective-permute-done.3 = bf16[4,128,768]{2,1,0:T(8,128)(2,1)S(1)} collective-permute-done((bf16[4,128,768]{2,1,0:T(8,128)(2,1)S(1)}, bf16[4,128,768]{2,1,0:T(8,128)(2,1)S(1)}, u32[]{:S(2)}, u32[]{:S(2)}) %collective-permute-start.3) | collective-permute-done | bytes 786464 | tf_op jit(solution)/shard_map/ppermute | solution.py:288
  44.1 1.9 fusion.15
  47.4 0.9 pad_maximum_fusion.9.refs_0_
  49.9 0.9 pad_maximum_fusion.5.refs_5_
  51.4 9.9 %collective-permute-done.7.refs_8_ = bf16[768,384]{1,0:T(8,128)(2,1)} collective-permute-done((bf16[768,384]{1,0:T(8,128)(2,1)}, bf16[768,384]{1,0:T(8,128)(2,1)}, u32[]{:S(2)}, u32[]{:S(2)}) %collective-permute-start.7) | collective-permute-done | bytes 589856 | tf_op jit(solution)/shard_map/ppermute | solution.py:249
  61.3 1.5 collective-permute-start.8
  64.6 0.9 gather_fusion
  65.5 1.9 pad_maximum_fusion.4.refs_4_
  67.4 1.3 broadcast_select_fusion.4.gain_ref
  68.7 4.2 %collective-permute-start.12 = (bf16[512,512]{1,0:T(8,128)(2,1)}, bf16[512,512]{1,0:T(8,128)(2,1)}, u32[]{:S(2)}, u32[]{:S(2)}) collective-permute-start(bf16[512,512]{1,0:T(8,128)(2,1)} %pad_maximum_fusion.11), channel_id=1, source_target_pairs={{0,8},{4,12},{8,0},{12,4},{1,9},{5,13},{9,1},{13,5},{2,10},{6,14},... | collective-permute-start | bytes 1572872 | tf_op jit(solution)/shard_map/ppermute | solution.py:249
  72.9 3.8 %pad_maximum_fusion = bf16[2,2,4,128,768]{4,3,2,1,0:T(8,128)(2,1)} fusion(bf16[2,1,4,128,768]{4,3,2,1,0:T(8,128)(2,1)} %bitcast.9, bf16[2,1,4,128,768]{4,3,2,1,0:T(8,128)(2,1)} %get-tuple-element.53), kind=kLoop, calls=%fused_computation.9 | loop fusion | flops 1572864 | bytes 6291456 | tf_op jit(solution)/shard_map/stack | solution.py:290
  76.7 3.4 %gather_fusion.8 = bf16[4,128,768]{2,1,0:T(8,128)(2,1)} fusion(bf16[16,128,768]{2,1,0:T(8,128)(2,1)} %bitcast.61, s32[1024]{0:T(1024)S(1)} %pad_clamp_fusion), kind=kCustom, calls=%fused_computation.3.clone | custom fusion | bytes 1572880 | tf_op jit(solution)/shard_map/jit(_take)/gather | solution.py:298
  80.1 3.5 %gather_fusion.7 = bf16[4,128,768]{2,1,0:T(8,128)(2,1)} fusion(bf16[16,128,768]{2,1,0:T(8,128)(2,1)} %bitcast.62, s32[1024]{0:T(1024)} %pad_clamp_fusion.1), kind=kCustom, calls=%fused_computation.2.clone | custom fusion | bytes 1572880 | tf_op jit(solution)/shard_map/jit(_take)/gather | solution.py:298
  83.6 3.5 %gather_fusion.6 = bf16[4,128,768]{2,1,0:T(8,128)(2,1)} fusion(bf16[16,128,768]{2,1,0:T(8,128)(2,1)} %bitcast.63, s32[1024]{0:T(1024)} %pad_clamp_fusion.2), kind=kCustom, calls=%fused_computation.1.clone | custom fusion | bytes 1572880 | tf_op jit(solution)/shard_map/jit(_take)/gather | solution.py:298
  87.1 3.5 %gather_fusion.5 = bf16[4,128,768]{2,1,0:T(8,128)(2,1)} fusion(bf16[16,128,768]{2,1,0:T(8,128)(2,1)} %bitcast.64, s32[1024]{0:T(1024)} %pad_clamp_fusion.8), kind=kCustom, calls=%fused_computation.clone | custom fusion | bytes 1572880 | tf_op jit(solution)/shard_map/jit(_take)/gather | solution.py:298
  91.5 1.5 collective-permute-start.10
  93.1 2.8 %broadcast_select_fusion = (bf16[4,128,768]{2,1,0:T(8,128)(2,1)}, bf16[4,128,768]{2,1,0:T(8,128)(2,1)}) fusion(bf16[4,128,768]{2,1,0:T(8,128)(2,1)} %gather_fusion.8, pred[4]{0:T(512)(128)(4,1)S(1)} %copy-done.29, bf16[4,128,768]{2,1,0:T(8,128)(2,1)} %gather_fusion.7, pred[4]{0:T(512)(128)(4,1)S(1)} %copy-done.30), kind=kLoop, calls=%fused_computation.16 | loop fusion | flops 786432 | bytes 3145736 | tf_op jit(solution)/shard_map/jit(_take)/select_n | solution.py:298
  95.9 1.4 broadcast_select_fusion.2
  97.3 10.2 %collective-permute-done.6.refs_7_ = bf16[768,384]{1,0:T(8,128)(2,1)S(1)} collective-permute-done((bf16[768,384]{1,0:T(8,128)(2,1)}, bf16[768,384]{1,0:T(8,128)(2,1)S(1)}, u32[]{:S(2)}, u32[]{:S(2)}) %collective-permute-start.6) | collective-permute-done | bytes 589856 | tf_op jit(solution)/shard_map/ppermute | solution.py:293
  107.5 11.3 %collective-permute-done.10.refs_11_ = bf16[768,384]{1,0:T(8,128)(2,1)S(1)} collective-permute-done((bf16[768,384]{1,0:T(8,128)(2,1)}, bf16[768,384]{1,0:T(8,128)(2,1)S(1)}, u32[]{:S(2)}, u32[]{:S(2)}) %collective-permute-start.10) | collective-permute-done | bytes 589856 | tf_op jit(solution)/shard_map/ppermute | solution.py:293
  119.6 8.3 %shard_map.136 = (bf16[512,256]{1,0:T(8,128)(2,1)}, bf16[512,256]{1,0:T(8,128)(2,1)}, bf16[512,256]{1,0:T(8,128)(2,1)}) custom-call(f32[4,768]{1,0:T(4,128)} %broadcast_select_fusion.4.gain_ref, f32[1,128]{1,0:T(1,128)} %bitcast.70, f32[1,128]{1,0:T(1,128)} %bitcast.72, bf16[4,128,768]{2,1,0:T(8,128)(2,1)} %get-tuple-element.84.refs_0_, ...), custom_call_target="tpu_custom_call" | custom-call | tf_op jit(solution)/shard_map/pallas_call | solution.py:165
  128.7 5.8 %shard_map.137.refs_0_ = bf16[512,256]{1,0:T(8,128)(2,1)} custom-call(s32[16]{0:T(128)} %reshape.295.pos_ref, bf16[512,256]{1,0:T(8,128)(2,1)} %get-tuple-element.16.q_ref, bf16[512,256]{1,0:T(8,128)(2,1)} %get-tuple-element.17.k_ref, bf16[512,256]{1,0:T(8,128)(2,1)} %get-tuple-element.18.v_ref, bf16[512,512]{1,0:T(8,128)(2,1)} %pad_maximum_fusion.9.refs_0_, ...), custom_call_target="tpu_custom_call" | custom-call | tf_op jit(solution)/shard_map/pallas_call | solution.py:205
  134.4 3.4 %collective-permute-start.16 = (bf16[512,256]{1,0:T(8,128)(2,1)}, bf16[512,256]{1,0:T(8,128)(2,1)S(1)}, u32[]{:S(2)}, u32[]{:S(2)}) collective-permute-start(bf16[512,256]{1,0:T(8,128)(2,1)} %shard_map.137.refs_0_), channel_id=1, source_target_pairs={{0,12},{4,8},{8,4},{12,0},{1,13},{5,9},{9,5},{13,1},{2,14},{6,10},... | collective-permute-start | bytes 786440 | tf_op jit(solution)/shard_map/ppermute | solution.py:249
  137.8 1.0 collective-permute-start.14
  138.8 1.5 bitcast_select_fusion.w_ref
  140.3 5.5 %collective-permute-done.16.refs_3_ = bf16[512,256]{1,0:T(8,128)(2,1)S(1)} collective-permute-done((bf16[512,256]{1,0:T(8,128)(2,1)}, bf16[512,256]{1,0:T(8,128)(2,1)S(1)}, u32[]{:S(2)}, u32[]{:S(2)}) %collective-permute-start.16) | collective-permute-done | bytes 262176 | tf_op jit(solution)/shard_map/ppermute | solution.py:249
  145.8 12.9 %collective-permute-done.15.refs_2_ = bf16[512,256]{1,0:T(8,128)(2,1)S(1)} collective-permute-done((bf16[512,256]{1,0:T(8,128)(2,1)}, bf16[512,256]{1,0:T(8,128)(2,1)S(1)}, u32[]{:S(2)}, u32[]{:S(2)}) %collective-permute-start.15) | collective-permute-done | bytes 262176 | tf_op jit(solution)/shard_map/ppermute | solution.py:249
  160.1 3.7 %shard_map.138 = (f32[256,768]{1,0:T(8,128)}, bf16[256,768]{1,0:T(8,128)(2,1)}) custom-call(bf16[1024,768]{1,0:T(8,128)(2,1)} %bitcast_select_fusion.w_ref, bf16[512,256]{1,0:T(8,128)(2,1)} %shard_map.137.refs_0_, bf16[512,256]{1,0:T(8,128)(2,1)} %copy-done.23, bf16[512,256]{1,0:T(8,128)(2,1)} %copy-done.21, bf16[512,256]{1,0:T(8,128)(2,1)} %copy-done.19), custom_call_target="tpu_custom_call" | custom-call | tf_op jit(solution)/shard_map/pallas_call | solution.py:233
  163.8 1.9 collective-permute-done.17
  165.7 1.2 convert_add_fusion.1
  168.4 5.6 %collective-permute-done.18 = bf16[128,768]{1,0:T(8,128)(2,1)S(1)} collective-permute-done((bf16[128,768]{1,0:T(8,128)(2,1)S(1)}, bf16[128,768]{1,0:T(8,128)(2,1)S(1)}, u32[]{:S(2)}, u32[]{:S(2)}) %collective-permute-start.18) | collective-permute-done | bytes 196640 | tf_op jit(solution)/shard_map/ppermute | solution.py:315
  174.0 1.0 fusion.5
  175.0 1.4 collective-permute-start.21
  176.4 3.0 %collective-permute-start.19 = (bf16[128,768]{1,0:T(8,128)(2,1)S(1)}, bf16[128,768]{1,0:T(8,128)(2,1)S(1)}, u32[]{:S(2)}, u32[]{:S(2)}) collective-permute-start(bf16[128,768]{1,0:T(8,128)(2,1)S(1)} %fusion.5), channel_id=1, source_target_pairs={{0,4},{4,0},{8,12},{12,8},{1,5},{5,1},{9,13},{13,9},{2,6},{6,2},{1... | collective-permute-start | bytes 589832 | tf_op jit(solution)/shard_map/ppermute | solution.py:249
  179.4 5.3 %collective-permute-done.21 = bf16[128,768]{1,0:T(8,128)(2,1)S(1)} collective-permute-done((bf16[128,768]{1,0:T(8,128)(2,1)S(1)}, bf16[128,768]{1,0:T(8,128)(2,1)S(1)}, u32[]{:S(2)}, u32[]{:S(2)}) %collective-permute-start.21) | collective-permute-done | bytes 196640 | tf_op jit(solution)/shard_map/ppermute | solution.py:249
  184.8 7.1 %collective-permute-done.20 = bf16[128,768]{1,0:T(8,128)(2,1)S(1)} collective-permute-done((bf16[128,768]{1,0:T(8,128)(2,1)S(1)}, bf16[128,768]{1,0:T(8,128)(2,1)S(1)}, u32[]{:S(2)}, u32[]{:S(2)}) %collective-permute-start.20) | collective-permute-done | bytes 196640 | tf_op jit(solution)/shard_map/ppermute | solution.py:249
  192.6 18.7 %collective-permute-done.23.refs_2_ = bf16[4,128,768]{2,1,0:T(8,128)(2,1)S(1)} collective-permute-done((bf16[4,128,768]{2,1,0:T(8,128)(2,1)S(1)}, bf16[4,128,768]{2,1,0:T(8,128)(2,1)S(1)}, u32[]{:S(2)}, u32[]{:S(2)}) %collective-permute-start.23) | collective-permute-done | bytes 786464 | tf_op jit(solution)/shard_map/ppermute | solution.py:320
  211.3 2.3 collective-permute-done.24.refs_3_
  213.6 0.9 copy-done.12
  214.5 8.2 %shard_map.139 = (bf16[512,256]{1,0:T(8,128)(2,1)}, bf16[512,256]{1,0:T(8,128)(2,1)}, bf16[512,256]{1,0:T(8,128)(2,1)}) custom-call(f32[4,768]{1,0:T(4,128)} %broadcast_select_fusion.4.gain_ref, f32[1,128]{1,0:T(1,128)} %bitcast.71, f32[1,128]{1,0:T(1,128)} %bitcast.73, bf16[4,128,768]{2,1,0:T(8,128)(2,1)} %copy-done.3, bf16[4,128,768]{2,1,0:T(8,128)(2,1)} %copy-done.11, ...), custom_call_target="tpu_custom_call" | custom-call | tf_op jit(solution)/shard_map/pallas_call | solution.py:165
  222.7 5.8 %shard_map.140.refs_0_ = bf16[512,256]{1,0:T(8,128)(2,1)} custom-call(s32[16]{0:T(128)} %reshape.295.pos_ref, bf16[512,256]{1,0:T(8,128)(2,1)} %get-tuple-element.21.q_ref, bf16[512,256]{1,0:T(8,128)(2,1)} %get-tuple-element.22.k_ref, bf16[512,256]{1,0:T(8,128)(2,1)} %get-tuple-element.23.v_ref, bf16[512,512]{1,0:T(8,128)(2,1)} %pad_maximum_fusion.9.refs_0_, ...), custom_call_target="tpu_custom_call" | custom-call | tf_op jit(solution)/shard_map/pallas_call | solution.py:205
  228.5 1.4 collective-permute-start.27
  229.9 3.0 %collective-permute-start.25 = (bf16[512,256]{1,0:T(8,128)(2,1)}, bf16[512,256]{1,0:T(8,128)(2,1)S(1)}, u32[]{:S(2)}, u32[]{:S(2)}) collective-permute-start(bf16[512,256]{1,0:T(8,128)(2,1)} %shard_map.140.refs_0_), channel_id=1, source_target_pairs={{0,4},{4,0},{8,12},{12,8},{1,5},{5,1},{9,13},{13,9},{2,6},{6,2},{1... | collective-permute-start | bytes 786440 | tf_op jit(solution)/shard_map/ppermute | solution.py:249
  232.9 6.9 %collective-permute-done.27.refs_3_ = bf16[512,256]{1,0:T(8,128)(2,1)S(1)} collective-permute-done((bf16[512,256]{1,0:T(8,128)(2,1)}, bf16[512,256]{1,0:T(8,128)(2,1)S(1)}, u32[]{:S(2)}, u32[]{:S(2)}) %collective-permute-start.27) | collective-permute-done | bytes 262176 | tf_op jit(solution)/shard_map/ppermute | solution.py:249
  239.8 12.1 %collective-permute-done.26.refs_2_ = bf16[512,256]{1,0:T(8,128)(2,1)S(1)} collective-permute-done((bf16[512,256]{1,0:T(8,128)(2,1)}, bf16[512,256]{1,0:T(8,128)(2,1)S(1)}, u32[]{:S(2)}, u32[]{:S(2)}) %collective-permute-start.26) | collective-permute-done | bytes 262176 | tf_op jit(solution)/shard_map/ppermute | solution.py:249
  253.3 3.6 %shard_map.141 = (f32[256,768]{1,0:T(8,128)}, bf16[256,768]{1,0:T(8,128)(2,1)}) custom-call(bf16[1024,768]{1,0:T(8,128)(2,1)} %bitcast_select_fusion.w_ref, bf16[512,256]{1,0:T(8,128)(2,1)} %shard_map.140.refs_0_, bf16[512,256]{1,0:T(8,128)(2,1)} %copy-done.24, bf16[512,256]{1,0:T(8,128)(2,1)} %copy-done.22, bf16[512,256]{1,0:T(8,128)(2,1)} %copy-done.20), custom_call_target="tpu_custom_call" | custom-call | tf_op jit(solution)/shard_map/pallas_call | solution.py:233
  256.9 1.9 collective-permute-done.28
  258.8 1.2 convert_add_fusion
  260.6 6.4 %collective-permute-done.29 = bf16[128,768]{1,0:T(8,128)(2,1)S(1)} collective-permute-done((bf16[128,768]{1,0:T(8,128)(2,1)S(1)}, bf16[128,768]{1,0:T(8,128)(2,1)S(1)}, u32[]{:S(2)}, u32[]{:S(2)}) %collective-permute-start.29) | collective-permute-done | bytes 196640 | tf_op jit(solution)/shard_map/ppermute | solution.py:315
  267.1 1.9 collective-permute-start.30
  269.1 10.6 %collective-permute-done.30 = bf16[128,768]{1,0:T(8,128)(2,1)S(1)} collective-permute-done((bf16[128,768]{1,0:T(8,128)(2,1)S(1)}, bf16[128,768]{1,0:T(8,128)(2,1)S(1)}, u32[]{:S(2)}, u32[]{:S(2)}) %collective-permute-start.30) | collective-permute-done | bytes 196640 | tf_op jit(solution)/shard_map/ppermute | solution.py:330
  (142 shorter events, 21.4 us)
Async XLA Ops:
  0.0 64.6 %copy-start = (bf16[1024,768]{1,0:T(8,128)(2,1)S(1)}, bf16[1024,768]{1,0:T(8,128)(2,1)}, u32[]{:S(2)}) copy-start(bf16[1024,768]{1,0:T(8,128)(2,1)} %param.21) | copy-start | bytes 4718596
  1.7 22.9 %collective-permute-start.1 = (bf16[128,768]{1,0:T(8,128)(2,1)}, bf16[128,768]{1,0:T(8,128)(2,1)}, u32[]{:S(2)}, u32[]{:S(2)}) collective-permute-start(bf16[128,768]{1,0:T(8,128)(2,1)} %constant_dynamic-slice_fusion.32), channel_id=1, source_target_pairs={{0,8},{4,12},{8,0},{12,4},{1,9},{5,13},{9,1},{13,5},{2,10},{6,14},... | collective-permute-start | bytes 589832 | tf_op jit(solution)/shard_map/ppermute | solution.py:249
  4.3 20.5 %collective-permute-start = (bf16[128,768]{1,0:T(8,128)(2,1)}, bf16[128,768]{1,0:T(8,128)(2,1)}, u32[]{:S(2)}, u32[]{:S(2)}) collective-permute-start(bf16[128,768]{1,0:T(8,128)(2,1)} %constant_dynamic-slice_fusion.32), channel_id=1, source_target_pairs={{0,4},{4,0},{8,12},{12,8},{1,5},{5,1},{9,13},{13,9},{2,6},{6,2},{1... | collective-permute-start | bytes 589832 | tf_op jit(solution)/shard_map/ppermute | solution.py:249
  5.9 19.3 %collective-permute-start.2 = (bf16[128,768]{1,0:T(8,128)(2,1)}, bf16[128,768]{1,0:T(8,128)(2,1)}, u32[]{:S(2)}, u32[]{:S(2)}) collective-permute-start(bf16[128,768]{1,0:T(8,128)(2,1)} %constant_dynamic-slice_fusion.32), channel_id=1, source_target_pairs={{0,12},{4,8},{8,4},{12,0},{1,13},{5,9},{9,5},{13,1},{2,14},{6,10},... | collective-permute-start | bytes 589832 | tf_op jit(solution)/shard_map/ppermute | solution.py:249
  6.1 1.8 copy-start.18
  10.5 6.0 %copy-start.2 = (s32[4]{0:T(128)S(1)}, s32[4]{0:T(128)}, u32[]{:S(2)}) copy-start(s32[4]{0:T(128)} %param.29) | copy-start | bytes 52
  10.5 9.2 %copy-start.25 = (s32[4,4]{1,0:T(4,128)S(1)}, s32[4,4]{1,0:T(4,128)}, u32[]{:S(2)}) copy-start(s32[4,4]{1,0:T(4,128)} %param.27) | copy-start | bytes 196
  10.5 9.9 %copy-start.1 = (s32[8]{0:T(128)S(1)}, s32[8]{0:T(128)}, u32[]{:S(2)}) copy-start(s32[8]{0:T(128)} %param.28) | copy-start | bytes 100
  11.4 49.9 %collective-permute-start.7 = (bf16[768,384]{1,0:T(8,128)(2,1)}, bf16[768,384]{1,0:T(8,128)(2,1)}, u32[]{:S(2)}, u32[]{:S(2)}) collective-permute-start(bf16[768,384]{1,0:T(8,128)(2,1)} %pad_maximum_fusion.7), channel_id=1, source_target_pairs={{0,8},{4,12},{8,0},{12,4},{1,9},{5,13},{9,1},{13,5},{2,10},{6,14},... | collective-permute-start | bytes 1769480 | tf_op jit(solution)/shard_map/ppermute | solution.py:249
  14.0 7.1 %copy-start.9 = (bf16[512,1024]{1,0:T(8,128)(2,1)S(1)}, bf16[512,1024]{1,0:T(8,128)(2,1)}, u32[]{:S(2)}) copy-start(bf16[512,1024]{1,0:T(8,128)(2,1)} %param.25) | copy-start | bytes 3145732
  14.0 76.6 %collective-permute-start.5 = (bf16[768,384]{1,0:T(8,128)(2,1)}, bf16[768,384]{1,0:T(8,128)(2,1)}, u32[]{:S(2)}, u32[]{:S(2)}) collective-permute-start(bf16[768,384]{1,0:T(8,128)(2,1)} %pad_maximum_fusion.6), channel_id=1, source_target_pairs={{0,4},{4,0},{8,12},{12,8},{1,5},{5,1},{9,13},{13,9},{2,6},{6,2},{1... | collective-permute-start | bytes 1769480 | tf_op jit(solution)/shard_map/ppermute | solution.py:249
  21.1 2.6 copy-start.16
  21.1 2.6 copy-start.17
  24.6 66.4 %collective-permute-start.9 = (bf16[768,384]{1,0:T(8,128)(2,1)}, bf16[768,384]{1,0:T(8,128)(2,1)}, u32[]{:S(2)}, u32[]{:S(2)}) collective-permute-start(bf16[768,384]{1,0:T(8,128)(2,1)} %pad_maximum_fusion.8), channel_id=1, source_target_pairs={{0,12},{4,8},{8,4},{12,0},{1,13},{5,9},{9,5},{13,1},{2,14},{6,10},... | collective-permute-start | bytes 1769480 | tf_op jit(solution)/shard_map/ppermute | solution.py:249
  24.8 103.0 %collective-permute-start.11 = (bf16[512,512]{1,0:T(8,128)(2,1)}, bf16[512,512]{1,0:T(8,128)(2,1)}, u32[]{:S(2)}, u32[]{:S(2)}) collective-permute-start(bf16[512,512]{1,0:T(8,128)(2,1)} %pad_maximum_fusion.10), channel_id=1, source_target_pairs={{0,4},{4,0},{8,12},{12,8},{1,5},{5,1},{9,13},{13,9},{2,6},{6,2},{1... | collective-permute-start | bytes 1572872 | tf_op jit(solution)/shard_map/ppermute | solution.py:249
  26.4 17.7 %collective-permute-start.3 = (bf16[4,128,768]{2,1,0:T(8,128)(2,1)S(1)}, bf16[4,128,768]{2,1,0:T(8,128)(2,1)S(1)}, u32[]{:S(2)}, u32[]{:S(2)}) collective-permute-start(bf16[4,128,768]{2,1,0:T(8,128)(2,1)S(1)} %get-tuple-element.72), channel_id=1, source_target_pairs={{0,2},{2,0},{1,3},{3,1},{4,6},{6,4},{5,7},{7,5},{8,10},{10,8},{9,1... | collective-permute-start | bytes 2359304 | tf_op jit(solution)/shard_map/ppermute | solution.py:288
  46.0 22.7 %collective-permute-start.4 = (bf16[2,4,128,768]{3,2,1,0:T(8,128)(2,1)}, bf16[2,4,128,768]{3,2,1,0:T(8,128)(2,1)}, u32[]{:S(2)}, u32[]{:S(2)}) collective-permute-start(bf16[2,4,128,768]{3,2,1,0:T(8,128)(2,1)} %get-tuple-element.54), channel_id=1, source_target_pairs={{0,1},{1,0},{2,3},{3,2},{4,5},{5,4},{6,7},{7,6},{8,9},{9,8},{10,11... | collective-permute-start | bytes 4718600 | tf_op jit(solution)/shard_map/ppermute | solution.py:289
  46.6 3.3 %copy-start.14 = (bf16[768,128]{1,0:T(8,128)(2,1)S(1)}, bf16[768,128]{1,0:T(8,128)(2,1)}, u32[]{:S(2)}) copy-start(bf16[768,128]{1,0:T(8,128)(2,1)} %get-tuple-element.50) | copy-start | bytes 589828
  46.6 3.3 %copy-start.15 = (bf16[768,128]{1,0:T(8,128)(2,1)S(1)}, bf16[768,128]{1,0:T(8,128)(2,1)}, u32[]{:S(2)}) copy-start(bf16[768,128]{1,0:T(8,128)(2,1)} %get-tuple-element.95) | copy-start | bytes 589828
  47.4 16.6 %copy-start.26 = (f32[3072]{0:T(1024)S(1)}, f32[3072]{0:T(1024)}, u32[]{:S(2)}) copy-start(f32[3072]{0:T(1024)} %param.17) | copy-start | bytes 36868
  61.3 30.2 %collective-permute-start.8 = (bf16[768,384]{1,0:T(8,128)(2,1)}, bf16[768,384]{1,0:T(8,128)(2,1)}, u32[]{:S(2)}, u32[]{:S(2)}) collective-permute-start(bf16[768,384]{1,0:T(8,128)(2,1)} %collective-permute-done.7.refs_8_), channel_id=1, source_target_pairs={{0,16},{16,0},{1,17},{17,1},{2,18},{18,2},{3,19},{19,3},{4,20},{20... | collective-permute-start | bytes 1769480 | tf_op jit(solution)/shard_map/ppermute | solution.py:293
  64.6 0.9 copy-start.13
  68.7 59.2 %collective-permute-start.12 = (bf16[512,512]{1,0:T(8,128)(2,1)}, bf16[512,512]{1,0:T(8,128)(2,1)}, u32[]{:S(2)}, u32[]{:S(2)}) collective-permute-start(bf16[512,512]{1,0:T(8,128)(2,1)} %pad_maximum_fusion.11), channel_id=1, source_target_pairs={{0,8},{4,12},{8,0},{12,4},{1,9},{5,13},{9,1},{13,5},{2,10},{6,14},... | collective-permute-start | bytes 1572872 | tf_op jit(solution)/shard_map/ppermute | solution.py:249
  83.6 9.5 %copy-start.29 = (pred[4]{0:T(512)(128)(4,1)S(1)}, pred[4]{0:T(512)(128)(4,1)}, u32[]{:S(2)}) copy-start(pred[4]{0:T(512)(128)(4,1)} %get-tuple-element.28) | copy-start | bytes 16
  83.6 9.5 %copy-start.30 = (pred[4]{0:T(512)(128)(4,1)S(1)}, pred[4]{0:T(512)(128)(4,1)}, u32[]{:S(2)}) copy-start(pred[4]{0:T(512)(128)(4,1)} %get-tuple-element.73) | copy-start | bytes 16
  90.6 37.3 %collective-permute-start.13 = (bf16[512,512]{1,0:T(8,128)(2,1)}, bf16[512,512]{1,0:T(8,128)(2,1)S(1)}, u32[]{:S(2)}, u32[]{:S(2)}) collective-permute-start(bf16[512,512]{1,0:T(8,128)(2,1)} %pad_maximum_fusion.12), channel_id=1, source_target_pairs={{0,12},{4,8},{8,4},{12,0},{1,13},{5,9},{9,5},{13,1},{2,14},{6,10},... | collective-permute-start | bytes 1572872 | tf_op jit(solution)/shard_map/ppermute | solution.py:249
  91.0 16.4 %collective-permute-start.6 = (bf16[768,384]{1,0:T(8,128)(2,1)}, bf16[768,384]{1,0:T(8,128)(2,1)S(1)}, u32[]{:S(2)}, u32[]{:S(2)}) collective-permute-start(bf16[768,384]{1,0:T(8,128)(2,1)} %collective-permute-done.5.refs_6_), channel_id=1, source_target_pairs={{0,16},{16,0},{1,17},{17,1},{2,18},{18,2},{3,19},{19,3},{4,20},{20... | collective-permute-start | bytes 1769480 | tf_op jit(solution)/shard_map/ppermute | solution.py:293
  91.5 27.2 %collective-permute-start.10 = (bf16[768,384]{1,0:T(8,128)(2,1)}, bf16[768,384]{1,0:T(8,128)(2,1)S(1)}, u32[]{:S(2)}, u32[]{:S(2)}) collective-permute-start(bf16[768,384]{1,0:T(8,128)(2,1)} %collective-permute-done.9.refs_10_), channel_id=1, source_target_pairs={{0,16},{16,0},{1,17},{17,1},{2,18},{18,2},{3,19},{19,3},{4,20},{20... | collective-permute-start | bytes 1769480 | tf_op jit(solution)/shard_map/ppermute | solution.py:293
  93.0 2.9 %copy-start.4 = (bf16[4,128,768]{2,1,0:T(8,128)(2,1)S(1)}, bf16[4,128,768]{2,1,0:T(8,128)(2,1)}, u32[]{:S(2)}) copy-start(bf16[4,128,768]{2,1,0:T(8,128)(2,1)} %gather_fusion.6) | copy-start | bytes 2359300
  93.1 2.9 %copy-start.5 = (bf16[4,128,768]{2,1,0:T(8,128)(2,1)S(1)}, bf16[4,128,768]{2,1,0:T(8,128)(2,1)}, u32[]{:S(2)}) copy-start(bf16[4,128,768]{2,1,0:T(8,128)(2,1)} %gather_fusion.5) | copy-start | bytes 2359300
  93.1 2.9 %copy-start.27 = (pred[4]{0:T(512)(128)(4,1)S(1)}, pred[4]{0:T(512)(128)(4,1)}, u32[]{:S(2)}) copy-start(pred[4]{0:T(512)(128)(4,1)} %get-tuple-element.75) | copy-start | bytes 16
  93.1 2.9 %copy-start.28 = (pred[4]{0:T(512)(128)(4,1)S(1)}, pred[4]{0:T(512)(128)(4,1)}, u32[]{:S(2)}) copy-start(pred[4]{0:T(512)(128)(4,1)} %get-tuple-element.77) | copy-start | bytes 16
  107.5 11.3 %copy-start.6 = (bf16[768,384]{1,0:T(8,128)(2,1)}, bf16[768,384]{1,0:T(8,128)(2,1)S(1)}, u32[]{:S(2)}) copy-start(bf16[768,384]{1,0:T(8,128)(2,1)S(1)} %collective-permute-done.6.refs_7_) | copy-start | bytes 1769476
  118.8 0.8 copy-start.7
  127.9 0.8 copy-start.8
  128.7 10.2 %copy-start.31 = (pred[1024]{0:T(1024)(128)(4,1)S(1)}, pred[1024]{0:T(1024)(128)(4,1)}, u32[]{:S(2)}) copy-start(pred[1024]{0:T(1024)(128)(4,1)} %broadcast_bitcast_fusion) | copy-start | bytes 3076
  134.4 11.3 %collective-permute-start.16 = (bf16[512,256]{1,0:T(8,128)(2,1)}, bf16[512,256]{1,0:T(8,128)(2,1)S(1)}, u32[]{:S(2)}, u32[]{:S(2)}) collective-permute-start(bf16[512,256]{1,0:T(8,128)(2,1)} %shard_map.137.refs_0_), channel_id=1, source_target_pairs={{0,12},{4,8},{8,4},{12,0},{1,13},{5,9},{9,5},{13,1},{2,14},{6,10},... | collective-permute-start | bytes 786440 | tf_op jit(solution)/shard_map/ppermute | solution.py:249
  137.8 20.8 %collective-permute-start.15 = (bf16[512,256]{1,0:T(8,128)(2,1)}, bf16[512,256]{1,0:T(8,128)(2,1)S(1)}, u32[]{:S(2)}, u32[]{:S(2)}) collective-permute-start(bf16[512,256]{1,0:T(8,128)(2,1)} %shard_map.137.refs_0_), channel_id=1, source_target_pairs={{0,8},{4,12},{8,0},{12,4},{1,9},{5,13},{9,1},{13,5},{2,10},{6,14},... | collective-permute-start | bytes 786440 | tf_op jit(solution)/shard_map/ppermute | solution.py:249
  137.8 20.8 %collective-permute-start.14 = (bf16[512,256]{1,0:T(8,128)(2,1)}, bf16[512,256]{1,0:T(8,128)(2,1)S(1)}, u32[]{:S(2)}, u32[]{:S(2)}) collective-permute-start(bf16[512,256]{1,0:T(8,128)(2,1)} %shard_map.137.refs_0_), channel_id=1, source_target_pairs={{0,4},{4,0},{8,12},{12,8},{1,5},{5,1},{9,13},{13,9},{2,6},{6,2},{1... | collective-permute-start | bytes 786440 | tf_op jit(solution)/shard_map/ppermute | solution.py:249
  145.8 12.9 %copy-start.19 = (bf16[512,256]{1,0:T(8,128)(2,1)}, bf16[512,256]{1,0:T(8,128)(2,1)S(1)}, u32[]{:S(2)}) copy-start(bf16[512,256]{1,0:T(8,128)(2,1)S(1)} %collective-permute-done.16.refs_3_) | copy-start | bytes 786436
  158.7 0.7 copy-start.21
  159.3 0.7 copy-start.23
  163.8 1.9 collective-permute-start.17
  166.9 7.0 %collective-permute-start.18 = (bf16[128,768]{1,0:T(8,128)(2,1)S(1)}, bf16[128,768]{1,0:T(8,128)(2,1)S(1)}, u32[]{:S(2)}, u32[]{:S(2)}) collective-permute-start(bf16[128,768]{1,0:T(8,128)(2,1)S(1)} %slice.93), channel_id=1, source_target_pairs={{0,2},{2,0},{1,3},{3,1},{4,6},{6,4},{5,7},{7,5},{8,10},{10,8},{9,1... | collective-permute-start | bytes 589832 | tf_op jit(solution)/shard_map/ppermute | solution.py:315
  175.0 9.8 %collective-permute-start.21 = (bf16[128,768]{1,0:T(8,128)(2,1)S(1)}, bf16[128,768]{1,0:T(8,128)(2,1)S(1)}, u32[]{:S(2)}, u32[]{:S(2)}) collective-permute-start(bf16[128,768]{1,0:T(8,128)(2,1)S(1)} %fusion.5), channel_id=1, source_target_pairs={{0,12},{4,8},{8,4},{12,0},{1,13},{5,9},{9,5},{13,1},{2,14},{6,10},... | collective-permute-start | bytes 589832 | tf_op jit(solution)/shard_map/ppermute | solution.py:249
  176.4 15.5 %collective-permute-start.20 = (bf16[128,768]{1,0:T(8,128)(2,1)S(1)}, bf16[128,768]{1,0:T(8,128)(2,1)S(1)}, u32[]{:S(2)}, u32[]{:S(2)}) collective-permute-start(bf16[128,768]{1,0:T(8,128)(2,1)S(1)} %fusion.5), channel_id=1, source_target_pairs={{0,8},{4,12},{8,0},{12,4},{1,9},{5,13},{9,1},{13,5},{2,10},{6,14},... | collective-permute-start | bytes 589832 | tf_op jit(solution)/shard_map/ppermute | solution.py:249
  176.4 15.5 %collective-permute-start.19 = (bf16[128,768]{1,0:T(8,128)(2,1)S(1)}, bf16[128,768]{1,0:T(8,128)(2,1)S(1)}, u32[]{:S(2)}, u32[]{:S(2)}) collective-permute-start(bf16[128,768]{1,0:T(8,128)(2,1)S(1)} %fusion.5), channel_id=1, source_target_pairs={{0,4},{4,0},{8,12},{12,8},{1,5},{5,1},{9,13},{13,9},{2,6},{6,2},{1... | collective-permute-start | bytes 589832 | tf_op jit(solution)/shard_map/ppermute | solution.py:249
  192.0 21.6 %copy-start.3 = (bf16[4,128,768]{2,1,0:T(8,128)(2,1)}, bf16[4,128,768]{2,1,0:T(8,128)(2,1)S(1)}, u32[]{:S(2)}) copy-start(bf16[4,128,768]{2,1,0:T(8,128)(2,1)S(1)} %pad_maximum_fusion.3.refs_0_) | copy-start | bytes 2359300
  192.0 19.3 %collective-permute-start.23 = (bf16[4,128,768]{2,1,0:T(8,128)(2,1)S(1)}, bf16[4,128,768]{2,1,0:T(8,128)(2,1)S(1)}, u32[]{:S(2)}, u32[]{:S(2)}) collective-permute-start(bf16[4,128,768]{2,1,0:T(8,128)(2,1)S(1)} %pad_maximum_fusion.3.refs_0_), channel_id=1, source_target_pairs={{0,2},{2,0},{1,3},{3,1},{4,6},{6,4},{5,7},{7,5},{8,10},{10,8},{9,1... | collective-permute-start | bytes 2359304 | tf_op jit(solution)/shard_map/ppermute | solution.py:320
  192.6 18.7 %collective-permute-start.22 = (bf16[4,128,768]{2,1,0:T(8,128)(2,1)S(1)}, bf16[4,128,768]{2,1,0:T(8,128)(2,1)S(1)}, u32[]{:S(2)}, u32[]{:S(2)}) collective-permute-start(bf16[4,128,768]{2,1,0:T(8,128)(2,1)S(1)} %pad_maximum_fusion.3.refs_0_), channel_id=1, source_target_pairs={{0,1},{1,0},{2,3},{3,2},{4,5},{5,4},{6,7},{7,6},{8,9},{9,8},{10,11... | collective-permute-start | bytes 2359304 | tf_op jit(solution)/shard_map/ppermute | solution.py:323
  211.3 2.3 copy-start.10
  211.3 2.3 collective-permute-start.24
  211.3 2.3 copy-start.11
  213.6 0.9 copy-start.12
  228.5 11.3 %collective-permute-start.27 = (bf16[512,256]{1,0:T(8,128)(2,1)}, bf16[512,256]{1,0:T(8,128)(2,1)S(1)}, u32[]{:S(2)}, u32[]{:S(2)}) collective-permute-start(bf16[512,256]{1,0:T(8,128)(2,1)} %shard_map.140.refs_0_), channel_id=1, source_target_pairs={{0,12},{4,8},{8,4},{12,0},{1,13},{5,9},{9,5},{13,1},{2,14},{6,10},... | collective-permute-start | bytes 786440 | tf_op jit(solution)/shard_map/ppermute | solution.py:249
  229.9 22.0 %collective-permute-start.26 = (bf16[512,256]{1,0:T(8,128)(2,1)}, bf16[512,256]{1,0:T(8,128)(2,1)S(1)}, u32[]{:S(2)}, u32[]{:S(2)}) collective-permute-start(bf16[512,256]{1,0:T(8,128)(2,1)} %shard_map.140.refs_0_), channel_id=1, source_target_pairs={{0,8},{4,12},{8,0},{12,4},{1,9},{5,13},{9,1},{13,5},{2,10},{6,14},... | collective-permute-start | bytes 786440 | tf_op jit(solution)/shard_map/ppermute | solution.py:249
  229.9 22.0 %collective-permute-start.25 = (bf16[512,256]{1,0:T(8,128)(2,1)}, bf16[512,256]{1,0:T(8,128)(2,1)S(1)}, u32[]{:S(2)}, u32[]{:S(2)}) collective-permute-start(bf16[512,256]{1,0:T(8,128)(2,1)} %shard_map.140.refs_0_), channel_id=1, source_target_pairs={{0,4},{4,0},{8,12},{12,8},{1,5},{5,1},{9,13},{13,9},{2,6},{6,2},{1... | collective-permute-start | bytes 786440 | tf_op jit(solution)/shard_map/ppermute | solution.py:249
  239.8 12.1 %copy-start.20 = (bf16[512,256]{1,0:T(8,128)(2,1)}, bf16[512,256]{1,0:T(8,128)(2,1)S(1)}, u32[]{:S(2)}) copy-start(bf16[512,256]{1,0:T(8,128)(2,1)S(1)} %collective-permute-done.27.refs_3_) | copy-start | bytes 786436
  251.9 0.7 copy-start.22
  252.6 0.7 copy-start.24
  256.9 1.9 collective-permute-start.28
  260.0 7.0 %collective-permute-start.29 = (bf16[128,768]{1,0:T(8,128)(2,1)S(1)}, bf16[128,768]{1,0:T(8,128)(2,1)S(1)}, u32[]{:S(2)}, u32[]{:S(2)}) collective-permute-start(bf16[128,768]{1,0:T(8,128)(2,1)S(1)} %slice.92), channel_id=1, source_target_pairs={{0,2},{2,0},{1,3},{3,1},{4,6},{6,4},{5,7},{7,5},{8,10},{10,8},{9,1... | collective-permute-start | bytes 589832 | tf_op jit(solution)/shard_map/ppermute | solution.py:315
  267.1 12.5 %collective-permute-start.30 = (bf16[128,768]{1,0:T(8,128)(2,1)S(1)}, bf16[128,768]{1,0:T(8,128)(2,1)S(1)}, u32[]{:S(2)}, u32[]{:S(2)}) collective-permute-start(bf16[128,768]{1,0:T(8,128)(2,1)S(1)} %fusion.2), channel_id=1, source_target_pairs={{0,0},{1,4},{2,8},{3,12},{4,5},{5,1},{6,13},{7,9},{8,10},{9,14},{1... | collective-permute-start | bytes 589832 | tf_op jit(solution)/shard_map/ppermute | solution.py:330

commit v2 on v1

--- a/solution.py
+++ b/solution.py
@@ -124,7 +124,7 @@
 
 
 WAYS = 4
-VMEM_LIMIT = 56 * 1024 * 1024
+MIB = 1024 * 1024
 
 
 def whole_specs(count):
@@ -168,7 +168,7 @@
         in_specs=whole_specs(3 + 3 * WAYS),
         out_specs=whole_specs(3),
         scratch_shapes=[pltpu.VMEM((WAYS, WAYS * tile, width), jnp.bfloat16)],
-        compiler_params=pltpu.CompilerParams(vmem_limit_bytes=VMEM_LIMIT),
+        compiler_params=pltpu.CompilerParams(vmem_limit_bytes=24 * MIB),
     )(gain_rows, query_gain, key_gain, *pieces, *panels)
 
 
@@ -207,7 +207,7 @@
         out_shape=jax.ShapeDtypeStruct(q.shape, jnp.bfloat16),
         in_specs=[pl.BlockSpec(memory_space=pltpu.SMEM)] + whole_specs(3 + WAYS),
         out_specs=pl.BlockSpec(memory_space=pltpu.VMEM),
-        compiler_params=pltpu.CompilerParams(vmem_limit_bytes=VMEM_LIMIT),
+        compiler_params=pltpu.CompilerParams(vmem_limit_bytes=10 * MIB),
     )(pos, q, k, v, *held)
 
 
@@ -238,7 +238,7 @@
         ],
         in_specs=whole_specs(1 + WAYS),
         out_specs=whole_specs(2),
-        compiler_params=pltpu.CompilerParams(vmem_limit_bytes=VMEM_LIMIT),
+        compiler_params=pltpu.CompilerParams(vmem_limit_bytes=10 * MIB),
     )(w_rows, *mixed)
 
 

time: 281 us -> 257 us (0.915)
  other arithmetic: 30.3 us -> 17.8 us
  Pallas kernels: 35.4 us -> 23.1 us
  waiting for transfers between devices: 145 us -> 151 us
  local copies, waits for them, and re-layouts: 34.6 us -> 29.9 us
    ppermute x18, waiting for transfers between devices: 59.7 us -> 66.9 us  [from_z(): return lax.ppermute(value, 'cache', [(i, i ^ k) for i in range(WAYS)])]
    pallas_call x2, Pallas kernels: 7.29 us -> 2.2 us  [project_out(): pl.pallas_call(out_kernel, out_shape=[jax.ShapeDtypeStruct((2 * tile, wid...]
    pallas_call x2, Pallas kernels: 16.5 us -> 11.6 us  [project(): pl.pallas_call(project_kernel, out_shape=[shape] * 3, in_specs=whole_spec...]
    unnamed x65 -> x61, local copies, waits for them, and re-layouts: 6.36 us -> 2.14 us
  transfers between devices with their start and end apart: 31 -> 31, of which waited for: 17 -> 17; matrix products, arithmetic and copies ran while one was open for 19% -> 17% of each run, Pallas kernels for 3% -> 2%
where the time goes in v2:
time: 257 us; the launch traced here: 256 us
  waiting for transfers between devices  151 us (59%)
  starting transfers between devices  33.1 us (13%)
  local copies, waits for them, and re-layouts  29.9 us (12%)
  Pallas kernels  23.1 us (9%)
  other arithmetic  17.8 us (7%)
    ppermute x18, waiting for transfers between devices, from_z(): return lax.ppermute(value, 'cache', [(i, i ^ k) for i in range(WAYS)])  66.9 us
    ppermute x18, starting transfers between devices, from_z(): return lax.ppermute(value, 'cache', [(i, i ^ k) for i in range(WAYS)])  25.1 us
    ppermute x3, waiting for transfers between devices, split_heads(): lax.ppermute(near[k], 'groups', SWAP)  23.3 us
    ppermute x1, waiting for transfers between devices, split_heads(): by_x = lax.ppermute(by_z, 'fsdp', SWAP)  17.5 us
    ppermute x1, waiting for transfers between devices, split_heads(): by_x = jnp.stack([by_z, lax.ppermute(by_z, 'fsdp', SWAP)])  16.9 us
    gather x4, local copies, waits for them, and re-layouts, split_heads(): pieces = [jnp.take(gathered, source[j], axis=0) for j in range(WAYS)]  13.6 us
    ppermute x2, waiting for transfers between devices, split_heads(): other = lax.ppermute(half[tile:].astype(jnp.bfloat16), 'fsdp', SWAP)  12 us
    pallas_call x2, Pallas kernels, project(): pl.pallas_call(project_kernel, out_shape=[shape] * 3, in_specs=whole_spec...  11.6 us
  transfers between devices with their start and end apart: 31, of which 17 were waited for; matrix products, arithmetic and copies ran while one was open for 17% of the time, Pallas kernels for 2%

profile of v2, /device:TPU:2, one launch (start us, length us, event | category | flops | bytes accessed | tf_op | source)
XLA Modules:
  0.0 256.0 jit_solution(17508557764742838773)
XLA Ops:
  0.0 1.7 constant_dynamic-slice_fusion.32
  1.7 2.6 %collective-permute-start.1 = (bf16[128,768]{1,0:T(8,128)(2,1)}, bf16[128,768]{1,0:T(8,128)(2,1)}, u32[]{:S(2)}, u32[]{:S(2)}) collective-permute-start(bf16[128,768]{1,0:T(8,128)(2,1)} %constant_dynamic-slice_fusion.32), channel_id=1, source_target_pairs={{0,8},{4,12},{8,0},{12,4},{1,9},{5,13},{9,1},{13,5},{2,10},{6,14},... | collective-permute-start | bytes 589832 | tf_op jit(solution)/shard_map/ppermute | solution.py:249
  4.3 1.6 collective-permute-start
  6.1 1.5 constant_dynamic-slice_fusion.19
  8.0 2.5 constant_dynamic-slice_fusion.17
  10.5 0.9 pad_maximum_fusion.7
  11.4 1.7 collective-permute-start.7
  13.1 0.9 pad_maximum_fusion.6
  13.9 2.5 collective-permute-start.5
  17.2 0.9 fusion.17
  19.2 0.7 gather_fusion.3
  19.9 1.7 constant_dynamic-slice_fusion.2
  21.7 0.9 pad_maximum_fusion.10
  22.5 0.9 pad_maximum_fusion.8
  24.1 1.2 fusion.16
  26.1 16.9 %collective-permute-done.3 = bf16[4,128,768]{2,1,0:T(8,128)(2,1)S(1)} collective-permute-done((bf16[4,128,768]{2,1,0:T(8,128)(2,1)S(1)}, bf16[4,128,768]{2,1,0:T(8,128)(2,1)S(1)}, u32[]{:S(2)}, u32[]{:S(2)}) %collective-permute-start.3) | collective-permute-done | bytes 786464 | tf_op jit(solution)/shard_map/ppermute | solution.py:288
  43.0 1.9 fusion.15
  44.9 0.9 pad_maximum_fusion.12
  45.8 0.9 pad_maximum_fusion.11
  47.0 14.3 %collective-permute-done.7.refs_8_ = bf16[768,384]{1,0:T(8,128)(2,1)} collective-permute-done((bf16[768,384]{1,0:T(8,128)(2,1)}, bf16[768,384]{1,0:T(8,128)(2,1)}, u32[]{:S(2)}, u32[]{:S(2)}) %collective-permute-start.7) | collective-permute-done | bytes 589856 | tf_op jit(solution)/shard_map/ppermute | solution.py:249
  61.3 1.5 collective-permute-start.8
  63.5 1.8 gather_fusion
  65.4 1.1 pad_maximum_fusion.4.refs_4_
  66.6 1.0 collective-permute-start.12
  67.5 3.8 %pad_maximum_fusion = bf16[2,2,4,128,768]{4,3,2,1,0:T(8,128)(2,1)} fusion(bf16[2,1,4,128,768]{4,3,2,1,0:T(8,128)(2,1)} %bitcast.9, bf16[2,1,4,128,768]{4,3,2,1,0:T(8,128)(2,1)} %get-tuple-element.53), kind=kLoop, calls=%fused_computation.9 | loop fusion | flops 1572864 | bytes 6291456 | tf_op jit(solution)/shard_map/stack | solution.py:290
  71.3 3.4 %gather_fusion.8 = bf16[4,128,768]{2,1,0:T(8,128)(2,1)} fusion(bf16[16,128,768]{2,1,0:T(8,128)(2,1)} %bitcast.65, s32[1024]{0:T(1024)S(1)} %pad_clamp_fusion), kind=kCustom, calls=%fused_computation.3.clone | custom fusion | bytes 1572880 | tf_op jit(solution)/shard_map/jit(_take)/gather | solution.py:298
  74.7 3.4 %gather_fusion.7 = bf16[4,128,768]{2,1,0:T(8,128)(2,1)} fusion(bf16[16,128,768]{2,1,0:T(8,128)(2,1)} %bitcast.66, s32[1024]{0:T(1024)S(1)} %pad_clamp_fusion.1), kind=kCustom, calls=%fused_computation.2.clone | custom fusion | bytes 1572880 | tf_op jit(solution)/shard_map/jit(_take)/gather | solution.py:298
  78.1 3.4 %gather_fusion.6 = bf16[4,128,768]{2,1,0:T(8,128)(2,1)} fusion(bf16[16,128,768]{2,1,0:T(8,128)(2,1)} %bitcast.67, s32[1024]{0:T(1024)S(1)} %pad_clamp_fusion.2), kind=kCustom, calls=%fused_computation.1.clone | custom fusion | bytes 1572880 | tf_op jit(solution)/shard_map/jit(_take)/gather | solution.py:298
  81.5 3.4 %gather_fusion.5 = bf16[4,128,768]{2,1,0:T(8,128)(2,1)} fusion(bf16[16,128,768]{2,1,0:T(8,128)(2,1)} %bitcast.68, s32[1024]{0:T(1024)S(1)} %pad_clamp_fusion.8), kind=kCustom, calls=%fused_computation.clone | custom fusion | bytes 1572880 | tf_op jit(solution)/shard_map/jit(_take)/gather | solution.py:298
  84.9 1.6 collective-permute-start.13
  87.0 1.5 collective-permute-start.10
  88.6 1.7 broadcast_select_fusion
  90.6 12.4 %collective-permute-done.6.refs_7_ = bf16[768,384]{1,0:T(8,128)(2,1)S(1)} collective-permute-done((bf16[768,384]{1,0:T(8,128)(2,1)}, bf16[768,384]{1,0:T(8,128)(2,1)S(1)}, u32[]{:S(2)}, u32[]{:S(2)}) %collective-permute-start.6) | collective-permute-done | bytes 589856 | tf_op jit(solution)/shard_map/ppermute | solution.py:293
  103.0 11.0 %collective-permute-done.10.refs_11_ = bf16[768,384]{1,0:T(8,128)(2,1)S(1)} collective-permute-done((bf16[768,384]{1,0:T(8,128)(2,1)}, bf16[768,384]{1,0:T(8,128)(2,1)S(1)}, u32[]{:S(2)}, u32[]{:S(2)}) %collective-permute-start.10) | collective-permute-done | bytes 589856 | tf_op jit(solution)/shard_map/ppermute | solution.py:293
  114.0 5.9 %shard_map.136 = (bf16[512,256]{1,0:T(8,128)(2,1)S(1)}, bf16[512,256]{1,0:T(8,128)(2,1)S(1)}, bf16[512,256]{1,0:T(8,128)(2,1)S(1)}) custom-call(f32[4,768]{1,0:T(4,128)S(1)} %broadcast_select_fusion.4.gain_ref, f32[1,128]{1,0:T(1,128)S(1)} %bitcast.61, f32[1,128]{1,0:T(1,128)S(1)} %bitcast.63, bf16[4,128,768]{2,1,0:T(8,128)(2,1)S(1)} %get-tuple-element.84.refs_0_, ...), custom_call_target="tpu_custom_call" | custom-call | tf_op jit(solution)/shard_map/pallas_call | solution.py:165
  120.0 4.7 %shard_map.137.refs_0_ = bf16[512,256]{1,0:T(8,128)(2,1)S(1)} custom-call(s32[16]{0:T(128)S(1)} %reshape.295.pos_ref, bf16[512,256]{1,0:T(8,128)(2,1)S(1)} %get-tuple-element.16.q_ref, bf16[512,256]{1,0:T(8,128)(2,1)S(1)} %get-tuple-element.17.k_ref, bf16[512,256]{1,0:T(8,128)(2,1)S(1)} %get-tuple-element.18.v_ref, ...), custom_call_target="tpu_custom_call" | custom-call | tf_op jit(solution)/shard_map/pallas_call | solution.py:205
  124.8 2.6 %collective-permute-start.16 = (bf16[512,256]{1,0:T(8,128)(2,1)S(1)}, bf16[512,256]{1,0:T(8,128)(2,1)S(1)}, u32[]{:S(2)}, u32[]{:S(2)}) collective-permute-start(bf16[512,256]{1,0:T(8,128)(2,1)S(1)} %shard_map.137.refs_0_), channel_id=1, source_target_pairs={{0,12},{4,8},{8,4},{12,0},{1,13},{5,9},{9,5},{13,1},{2,14},{6,10},... | collective-permute-start | bytes 786440 | tf_op jit(solution)/shard_map/ppermute | solution.py:249
  127.4 1.9 collective-permute-start.14
  129.6 6.4 %collective-permute-done.16.refs_3_ = bf16[512,256]{1,0:T(8,128)(2,1)S(1)} collective-permute-done((bf16[512,256]{1,0:T(8,128)(2,1)S(1)}, bf16[512,256]{1,0:T(8,128)(2,1)S(1)}, u32[]{:S(2)}, u32[]{:S(2)}) %collective-permute-start.16) | collective-permute-done | bytes 262176 | tf_op jit(solution)/shard_map/ppermute | solution.py:249
  136.0 12.5 %collective-permute-done.15.refs_2_ = bf16[512,256]{1,0:T(8,128)(2,1)S(1)} collective-permute-done((bf16[512,256]{1,0:T(8,128)(2,1)S(1)}, bf16[512,256]{1,0:T(8,128)(2,1)S(1)}, u32[]{:S(2)}, u32[]{:S(2)}) %collective-permute-start.15) | collective-permute-done | bytes 262176 | tf_op jit(solution)/shard_map/ppermute | solution.py:249
  148.5 1.2 shard_map.138
  149.8 1.7 collective-permute-done.17
  151.5 0.9 copy-done.21
  153.1 1.0 dynamic-slice_reduce_fusion
  154.0 5.5 %collective-permute-done.18 = bf16[128,768]{1,0:T(8,128)(2,1)} collective-permute-done((bf16[128,768]{1,0:T(8,128)(2,1)S(1)}, bf16[128,768]{1,0:T(8,128)(2,1)}, u32[]{:S(2)}, u32[]{:S(2)}) %collective-permute-start.18) | collective-permute-done | bytes 196640 | tf_op jit(solution)/shard_map/ppermute | solution.py:315
  159.6 1.2 fusion.5
  160.8 2.7 %collective-permute-start.21 = (bf16[128,768]{1,0:T(8,128)(2,1)S(1)}, bf16[128,768]{1,0:T(8,128)(2,1)S(1)}, u32[]{:S(2)}, u32[]{:S(2)}) collective-permute-start(bf16[128,768]{1,0:T(8,128)(2,1)S(1)} %fusion.5), channel_id=1, source_target_pairs={{0,12},{4,8},{8,4},{12,0},{1,13},{5,9},{9,5},{13,1},{2,14},{6,10},... | collective-permute-start | bytes 589832 | tf_op jit(solution)/shard_map/ppermute | solution.py:249
  163.5 1.7 collective-permute-start.19
  165.2 5.3 %collective-permute-done.21 = bf16[128,768]{1,0:T(8,128)(2,1)S(1)} collective-permute-done((bf16[128,768]{1,0:T(8,128)(2,1)S(1)}, bf16[128,768]{1,0:T(8,128)(2,1)S(1)}, u32[]{:S(2)}, u32[]{:S(2)}) %collective-permute-start.21) | collective-permute-done | bytes 196640 | tf_op jit(solution)/shard_map/ppermute | solution.py:249
  170.6 8.3 %collective-permute-done.20 = bf16[128,768]{1,0:T(8,128)(2,1)S(1)} collective-permute-done((bf16[128,768]{1,0:T(8,128)(2,1)S(1)}, bf16[128,768]{1,0:T(8,128)(2,1)S(1)}, u32[]{:S(2)}, u32[]{:S(2)}) %collective-permute-start.20) | collective-permute-done | bytes 196640 | tf_op jit(solution)/shard_map/ppermute | solution.py:249
  179.6 17.5 %collective-permute-done.23.refs_2_ = bf16[4,128,768]{2,1,0:T(8,128)(2,1)S(1)} collective-permute-done((bf16[4,128,768]{2,1,0:T(8,128)(2,1)S(1)}, bf16[4,128,768]{2,1,0:T(8,128)(2,1)S(1)}, u32[]{:S(2)}, u32[]{:S(2)}) %collective-permute-start.23) | collective-permute-done | bytes 786464 | tf_op jit(solution)/shard_map/ppermute | solution.py:320
  197.1 2.3 collective-permute-done.24.refs_3_
  199.4 5.7 %shard_map.139 = (bf16[512,256]{1,0:T(8,128)(2,1)S(1)}, bf16[512,256]{1,0:T(8,128)(2,1)S(1)}, bf16[512,256]{1,0:T(8,128)(2,1)S(1)}) custom-call(f32[4,768]{1,0:T(4,128)S(1)} %broadcast_select_fusion.4.gain_ref, f32[1,128]{1,0:T(1,128)S(1)} %bitcast.62, f32[1,128]{1,0:T(1,128)S(1)} %bitcast.64, bf16[4,128,768]{2,1,0:T(8,128)(2,1)S(1)} %pad_maximum_fusion.3.refs_0_, ...), custom_call_target="tpu_custom_call" | custom-call | tf_op jit(solution)/shard_map/pallas_call | solution.py:165
  205.2 4.5 %shard_map.140.refs_0_ = bf16[512,256]{1,0:T(8,128)(2,1)S(1)} custom-call(s32[16]{0:T(128)S(1)} %reshape.295.pos_ref, bf16[512,256]{1,0:T(8,128)(2,1)S(1)} %get-tuple-element.21.q_ref, bf16[512,256]{1,0:T(8,128)(2,1)S(1)} %get-tuple-element.22.k_ref, bf16[512,256]{1,0:T(8,128)(2,1)S(1)} %get-tuple-element.23.v_ref, bf16[512,512]{1,0:T(8,128)(2,1)S(1)} %copy-done.6, ...), custom_call_target="tpu_custom_call" | custom-call | tf_op jit(solution)/shard_map/pallas_call | solution.py:205
  209.7 2.6 %collective-permute-start.27 = (bf16[512,256]{1,0:T(8,128)(2,1)S(1)}, bf16[512,256]{1,0:T(8,128)(2,1)S(1)}, u32[]{:S(2)}, u32[]{:S(2)}) collective-permute-start(bf16[512,256]{1,0:T(8,128)(2,1)S(1)} %shard_map.140.refs_0_), channel_id=1, source_target_pairs={{0,12},{4,8},{8,4},{12,0},{1,13},{5,9},{9,5},{13,1},{2,14},{6,10},... | collective-permute-start | bytes 786440 | tf_op jit(solution)/shard_map/ppermute | solution.py:249
  212.3 1.8 collective-permute-start.25
  214.1 6.7 %collective-permute-done.27.refs_3_ = bf16[512,256]{1,0:T(8,128)(2,1)S(1)} collective-permute-done((bf16[512,256]{1,0:T(8,128)(2,1)S(1)}, bf16[512,256]{1,0:T(8,128)(2,1)S(1)}, u32[]{:S(2)}, u32[]{:S(2)}) %collective-permute-start.27) | collective-permute-done | bytes 262176 | tf_op jit(solution)/shard_map/ppermute | solution.py:249
  220.8 13.3 %collective-permute-done.26.refs_2_ = bf16[512,256]{1,0:T(8,128)(2,1)S(1)} collective-permute-done((bf16[512,256]{1,0:T(8,128)(2,1)S(1)}, bf16[512,256]{1,0:T(8,128)(2,1)S(1)}, u32[]{:S(2)}, u32[]{:S(2)}) %collective-permute-start.26) | collective-permute-done | bytes 262176 | tf_op jit(solution)/shard_map/ppermute | solution.py:249
  234.2 1.0 shard_map.141
  235.2 1.7 collective-permute-done.28
  237.6 6.4 %collective-permute-done.29 = bf16[128,768]{1,0:T(8,128)(2,1)S(1)} collective-permute-done((bf16[128,768]{1,0:T(8,128)(2,1)S(1)}, bf16[128,768]{1,0:T(8,128)(2,1)S(1)}, u32[]{:S(2)}, u32[]{:S(2)}) %collective-permute-start.29) | collective-permute-done | bytes 196640 | tf_op jit(solution)/shard_map/ppermute | solution.py:315
  244.1 1.9 collective-permute-start.30
  246.1 9.2 %collective-permute-done.30 = bf16[128,768]{1,0:T(8,128)(2,1)S(1)} collective-permute-done((bf16[128,768]{1,0:T(8,128)(2,1)S(1)}, bf16[128,768]{1,0:T(8,128)(2,1)S(1)}, u32[]{:S(2)}, u32[]{:S(2)}) %collective-permute-start.30) | collective-permute-done | bytes 196640 | tf_op jit(solution)/shard_map/ppermute | solution.py:330
  255.3 0.7 copy.24
  (138 shorter events, 8.4 us)
Async XLA Ops:
  0.0 63.5 %copy-start = (bf16[1024,768]{1,0:T(8,128)(2,1)S(1)}, bf16[1024,768]{1,0:T(8,128)(2,1)}, u32[]{:S(2)}) copy-start(bf16[1024,768]{1,0:T(8,128)(2,1)} %param.21) | copy-start | bytes 4718596
  1.7 21.7 %collective-permute-start.1 = (bf16[128,768]{1,0:T(8,128)(2,1)}, bf16[128,768]{1,0:T(8,128)(2,1)}, u32[]{:S(2)}, u32[]{:S(2)}) collective-permute-start(bf16[128,768]{1,0:T(8,128)(2,1)} %constant_dynamic-slice_fusion.32), channel_id=1, source_target_pairs={{0,8},{4,12},{8,0},{12,4},{1,9},{5,13},{9,1},{13,5},{2,10},{6,14},... | collective-permute-start | bytes 589832 | tf_op jit(solution)/shard_map/ppermute | solution.py:249
  4.3 19.4 %collective-permute-start = (bf16[128,768]{1,0:T(8,128)(2,1)}, bf16[128,768]{1,0:T(8,128)(2,1)}, u32[]{:S(2)}, u32[]{:S(2)}) collective-permute-start(bf16[128,768]{1,0:T(8,128)(2,1)} %constant_dynamic-slice_fusion.32), channel_id=1, source_target_pairs={{0,4},{4,0},{8,12},{12,8},{1,5},{5,1},{9,13},{13,9},{2,6},{6,2},{1... | collective-permute-start | bytes 589832 | tf_op jit(solution)/shard_map/ppermute | solution.py:249
  5.9 18.1 %collective-permute-start.2 = (bf16[128,768]{1,0:T(8,128)(2,1)}, bf16[128,768]{1,0:T(8,128)(2,1)}, u32[]{:S(2)}, u32[]{:S(2)}) collective-permute-start(bf16[128,768]{1,0:T(8,128)(2,1)} %constant_dynamic-slice_fusion.32), channel_id=1, source_target_pairs={{0,12},{4,8},{8,4},{12,0},{1,13},{5,9},{9,5},{13,1},{2,14},{6,10},... | collective-permute-start | bytes 589832 | tf_op jit(solution)/shard_map/ppermute | solution.py:249
  6.1 1.8 copy-start.27
  10.5 6.0 %copy-start.17 = (s32[4]{0:T(128)S(1)}, s32[4]{0:T(128)}, u32[]{:S(2)}) copy-start(s32[4]{0:T(128)} %param.29) | copy-start | bytes 52
  10.5 8.0 %copy-start.28 = (s32[4,4]{1,0:T(4,128)S(1)}, s32[4,4]{1,0:T(4,128)}, u32[]{:S(2)}) copy-start(s32[4,4]{1,0:T(4,128)} %param.27) | copy-start | bytes 196
  10.5 8.7 %copy-start.16 = (s32[8]{0:T(128)S(1)}, s32[8]{0:T(128)}, u32[]{:S(2)}) copy-start(s32[8]{0:T(128)} %param.28) | copy-start | bytes 100
  11.4 50.0 %collective-permute-start.7 = (bf16[768,384]{1,0:T(8,128)(2,1)}, bf16[768,384]{1,0:T(8,128)(2,1)}, u32[]{:S(2)}, u32[]{:S(2)}) collective-permute-start(bf16[768,384]{1,0:T(8,128)(2,1)} %pad_maximum_fusion.7), channel_id=1, source_target_pairs={{0,8},{4,12},{8,0},{12,4},{1,9},{5,13},{9,1},{13,5},{2,10},{6,14},... | collective-permute-start | bytes 1769480 | tf_op jit(solution)/shard_map/ppermute | solution.py:249
  13.9 6.0 %copy-start.22 = (bf16[512,1024]{1,0:T(8,128)(2,1)S(1)}, bf16[512,1024]{1,0:T(8,128)(2,1)}, u32[]{:S(2)}) copy-start(bf16[512,1024]{1,0:T(8,128)(2,1)} %param.25) | copy-start | bytes 3145732
  13.9 71.0 %collective-permute-start.5 = (bf16[768,384]{1,0:T(8,128)(2,1)}, bf16[768,384]{1,0:T(8,128)(2,1)}, u32[]{:S(2)}, u32[]{:S(2)}) collective-permute-start(bf16[768,384]{1,0:T(8,128)(2,1)} %pad_maximum_fusion.6), channel_id=1, source_target_pairs={{0,4},{4,0},{8,12},{12,8},{1,5},{5,1},{9,13},{13,9},{2,6},{6,2},{1... | collective-permute-start | bytes 1769480 | tf_op jit(solution)/shard_map/ppermute | solution.py:249
  19.9 2.6 %copy-start.25 = (bf16[768,128]{1,0:T(8,128)(2,1)S(1)}, bf16[768,128]{1,0:T(8,128)(2,1)}, u32[]{:S(2)}) copy-start(bf16[768,128]{1,0:T(8,128)(2,1)} %get-tuple-element.48) | copy-start | bytes 589828
  19.9 2.6 %copy-start.26 = (bf16[768,128]{1,0:T(8,128)(2,1)S(1)}, bf16[768,128]{1,0:T(8,128)(2,1)}, u32[]{:S(2)}) copy-start(bf16[768,128]{1,0:T(8,128)(2,1)} %get-tuple-element.97) | copy-start | bytes 589828
  23.5 63.1 %collective-permute-start.9 = (bf16[768,384]{1,0:T(8,128)(2,1)}, bf16[768,384]{1,0:T(8,128)(2,1)}, u32[]{:S(2)}, u32[]{:S(2)}) collective-permute-start(bf16[768,384]{1,0:T(8,128)(2,1)} %pad_maximum_fusion.8), channel_id=1, source_target_pairs={{0,12},{4,8},{8,4},{12,0},{1,13},{5,9},{9,5},{13,1},{2,14},{6,10},... | collective-permute-start | bytes 1769480 | tf_op jit(solution)/shard_map/ppermute | solution.py:249
  23.7 96.3 %collective-permute-start.11 = (bf16[512,512]{1,0:T(8,128)(2,1)}, bf16[512,512]{1,0:T(8,128)(2,1)}, u32[]{:S(2)}, u32[]{:S(2)}) collective-permute-start(bf16[512,512]{1,0:T(8,128)(2,1)} %pad_maximum_fusion.10), channel_id=1, source_target_pairs={{0,4},{4,0},{8,12},{12,8},{1,5},{5,1},{9,13},{13,9},{2,6},{6,2},{1... | collective-permute-start | bytes 1572872 | tf_op jit(solution)/shard_map/ppermute | solution.py:249
  25.3 17.7 %collective-permute-start.3 = (bf16[4,128,768]{2,1,0:T(8,128)(2,1)S(1)}, bf16[4,128,768]{2,1,0:T(8,128)(2,1)S(1)}, u32[]{:S(2)}, u32[]{:S(2)}) collective-permute-start(bf16[4,128,768]{2,1,0:T(8,128)(2,1)S(1)} %get-tuple-element.72), channel_id=1, source_target_pairs={{0,2},{2,0},{1,3},{3,1},{4,6},{6,4},{5,7},{7,5},{8,10},{10,8},{9,1... | collective-permute-start | bytes 2359304 | tf_op jit(solution)/shard_map/ppermute | solution.py:288
  44.8 21.7 %collective-permute-start.4 = (bf16[2,4,128,768]{3,2,1,0:T(8,128)(2,1)}, bf16[2,4,128,768]{3,2,1,0:T(8,128)(2,1)}, u32[]{:S(2)}, u32[]{:S(2)}) collective-permute-start(bf16[2,4,128,768]{3,2,1,0:T(8,128)(2,1)} %get-tuple-element.54), channel_id=1, source_target_pairs={{0,1},{1,0},{2,3},{3,2},{4,5},{5,4},{6,7},{7,6},{8,9},{9,8},{10,11... | collective-permute-start | bytes 4718600 | tf_op jit(solution)/shard_map/ppermute | solution.py:289
  44.8 2.0 copy-start.23
  44.8 2.0 copy-start.24
  45.7 17.2 %copy-start.29 = (f32[3072]{0:T(1024)S(1)}, f32[3072]{0:T(1024)}, u32[]{:S(2)}) copy-start(f32[3072]{0:T(1024)} %param.17) | copy-start | bytes 36868
  45.8 74.2 %copy-start.5 = (bf16[512,512]{1,0:T(8,128)(2,1)}, bf16[512,512]{1,0:T(8,128)(2,1)S(1)}, u32[]{:S(2)}) copy-start(bf16[512,512]{1,0:T(8,128)(2,1)S(1)} %pad_maximum_fusion.9.refs_0_) | copy-start | bytes 1572868
  46.9 67.1 %copy-start.1 = (bf16[768,384]{1,0:T(8,128)(2,1)}, bf16[768,384]{1,0:T(8,128)(2,1)S(1)}, u32[]{:S(2)}) copy-start(bf16[768,384]{1,0:T(8,128)(2,1)S(1)} %pad_maximum_fusion.5.refs_5_) | copy-start | bytes 1769476
  61.3 25.7 %collective-permute-start.8 = (bf16[768,384]{1,0:T(8,128)(2,1)}, bf16[768,384]{1,0:T(8,128)(2,1)}, u32[]{:S(2)}, u32[]{:S(2)}) collective-permute-start(bf16[768,384]{1,0:T(8,128)(2,1)} %collective-permute-done.7.refs_8_), channel_id=1, source_target_pairs={{0,16},{16,0},{1,17},{17,1},{2,18},{18,2},{3,19},{19,3},{4,20},{20... | collective-permute-start | bytes 1769480 | tf_op jit(solution)/shard_map/ppermute | solution.py:293
  66.5 47.5 %copy-start.3 = (bf16[768,384]{1,0:T(8,128)(2,1)}, bf16[768,384]{1,0:T(8,128)(2,1)S(1)}, u32[]{:S(2)}) copy-start(bf16[768,384]{1,0:T(8,128)(2,1)S(1)} %pad_maximum_fusion.4.refs_4_) | copy-start | bytes 1769476
  66.6 53.4 %collective-permute-start.12 = (bf16[512,512]{1,0:T(8,128)(2,1)}, bf16[512,512]{1,0:T(8,128)(2,1)}, u32[]{:S(2)}, u32[]{:S(2)}) collective-permute-start(bf16[512,512]{1,0:T(8,128)(2,1)} %pad_maximum_fusion.11), channel_id=1, source_target_pairs={{0,8},{4,12},{8,0},{12,4},{1,9},{5,13},{9,1},{13,5},{2,10},{6,14},... | collective-permute-start | bytes 1572872 | tf_op jit(solution)/shard_map/ppermute | solution.py:249
  84.9 35.1 %collective-permute-start.13 = (bf16[512,512]{1,0:T(8,128)(2,1)}, bf16[512,512]{1,0:T(8,128)(2,1)S(1)}, u32[]{:S(2)}, u32[]{:S(2)}) collective-permute-start(bf16[512,512]{1,0:T(8,128)(2,1)} %pad_maximum_fusion.12), channel_id=1, source_target_pairs={{0,12},{4,8},{8,4},{12,0},{1,13},{5,9},{9,5},{13,1},{2,14},{6,10},... | collective-permute-start | bytes 1572872 | tf_op jit(solution)/shard_map/ppermute | solution.py:249
  86.5 16.5 %collective-permute-start.6 = (bf16[768,384]{1,0:T(8,128)(2,1)}, bf16[768,384]{1,0:T(8,128)(2,1)S(1)}, u32[]{:S(2)}, u32[]{:S(2)}) collective-permute-start(bf16[768,384]{1,0:T(8,128)(2,1)} %collective-permute-done.5.refs_6_), channel_id=1, source_target_pairs={{0,16},{16,0},{1,17},{17,1},{2,18},{18,2},{3,19},{19,3},{4,20},{20... | collective-permute-start | bytes 1769480 | tf_op jit(solution)/shard_map/ppermute | solution.py:293
  87.0 26.9 %collective-permute-start.10 = (bf16[768,384]{1,0:T(8,128)(2,1)}, bf16[768,384]{1,0:T(8,128)(2,1)S(1)}, u32[]{:S(2)}, u32[]{:S(2)}) collective-permute-start(bf16[768,384]{1,0:T(8,128)(2,1)} %collective-permute-done.9.refs_10_), channel_id=1, source_target_pairs={{0,16},{16,0},{1,17},{17,1},{2,18},{18,2},{3,19},{19,3},{4,20},{20... | collective-permute-start | bytes 1769480 | tf_op jit(solution)/shard_map/ppermute | solution.py:293
  88.6 1.7 copy-start.19
  88.6 1.8 copy-start.20
  90.4 23.6 %copy-start.14 = (f32[128]{0:T(128)S(1)}, f32[128]{0:T(128)}, u32[]{:S(2)}) copy-start(f32[128]{0:T(128)} %param.22) | copy-start | bytes 1540
  90.4 23.6 %copy-start.15 = (f32[128]{0:T(128)S(1)}, f32[128]{0:T(128)}, u32[]{:S(2)}) copy-start(f32[128]{0:T(128)} %param.23) | copy-start | bytes 1540
  90.6 29.3 %copy-start.7 = (bf16[4,128,768]{2,1,0:T(8,128)(2,1)}, bf16[4,128,768]{2,1,0:T(8,128)(2,1)S(1)}, u32[]{:S(2)}) copy-start(bf16[4,128,768]{2,1,0:T(8,128)(2,1)S(1)} %get-tuple-element.84.refs_0_) | copy-start | bytes 2359300
  103.0 16.9 %copy-start.8 = (bf16[768,384]{1,0:T(8,128)(2,1)}, bf16[768,384]{1,0:T(8,128)(2,1)S(1)}, u32[]{:S(2)}) copy-start(bf16[768,384]{1,0:T(8,128)(2,1)S(1)} %collective-permute-done.6.refs_7_) | copy-start | bytes 1769476
  114.0 6.0 %copy-start.10 = (bf16[768,384]{1,0:T(8,128)(2,1)}, bf16[768,384]{1,0:T(8,128)(2,1)S(1)}, u32[]{:S(2)}) copy-start(bf16[768,384]{1,0:T(8,128)(2,1)S(1)} %collective-permute-done.10.refs_11_) | copy-start | bytes 1769476
  120.0 4.8 %copy-start.12 = (bf16[512,512]{1,0:T(8,128)(2,1)}, bf16[512,512]{1,0:T(8,128)(2,1)S(1)}, u32[]{:S(2)}) copy-start(bf16[512,512]{1,0:T(8,128)(2,1)S(1)} %collective-permute-done.13.refs_3_) | copy-start | bytes 1572868
  120.0 9.2 %copy-start.18 = (bf16[8,128,768]{2,1,0:T(8,128)(2,1)S(1)}, bf16[8,128,768]{2,1,0:T(8,128)(2,1)}, u32[]{:S(2)}) copy-start(bf16[8,128,768]{2,1,0:T(8,128)(2,1)} %gather_fusion) | copy-start | bytes 4718596
  124.8 11.2 %collective-permute-start.16 = (bf16[512,256]{1,0:T(8,128)(2,1)S(1)}, bf16[512,256]{1,0:T(8,128)(2,1)S(1)}, u32[]{:S(2)}, u32[]{:S(2)}) collective-permute-start(bf16[512,256]{1,0:T(8,128)(2,1)S(1)} %shard_map.137.refs_0_), channel_id=1, source_target_pairs={{0,12},{4,8},{8,4},{12,0},{1,13},{5,9},{9,5},{13,1},{2,14},{6,10},... | collective-permute-start | bytes 786440 | tf_op jit(solution)/shard_map/ppermute | solution.py:249
  127.4 21.1 %collective-permute-start.15 = (bf16[512,256]{1,0:T(8,128)(2,1)S(1)}, bf16[512,256]{1,0:T(8,128)(2,1)S(1)}, u32[]{:S(2)}, u32[]{:S(2)}) collective-permute-start(bf16[512,256]{1,0:T(8,128)(2,1)S(1)} %shard_map.137.refs_0_), channel_id=1, source_target_pairs={{0,8},{4,12},{8,0},{12,4},{1,9},{5,13},{9,1},{13,5},{2,10},{6,14},... | collective-permute-start | bytes 786440 | tf_op jit(solution)/shard_map/ppermute | solution.py:249
  127.4 21.1 %collective-permute-start.14 = (bf16[512,256]{1,0:T(8,128)(2,1)S(1)}, bf16[512,256]{1,0:T(8,128)(2,1)S(1)}, u32[]{:S(2)}, u32[]{:S(2)}) collective-permute-start(bf16[512,256]{1,0:T(8,128)(2,1)S(1)} %shard_map.137.refs_0_), channel_id=1, source_target_pairs={{0,4},{4,0},{8,12},{12,8},{1,5},{5,1},{9,13},{13,9},{2,6},{6,2},{1... | collective-permute-start | bytes 786440 | tf_op jit(solution)/shard_map/ppermute | solution.py:249
  149.7 1.8 collective-permute-start.17
  151.5 0.9 copy-start.21
  152.4 7.1 %collective-permute-start.18 = (bf16[128,768]{1,0:T(8,128)(2,1)S(1)}, bf16[128,768]{1,0:T(8,128)(2,1)}, u32[]{:S(2)}, u32[]{:S(2)}) collective-permute-start(bf16[128,768]{1,0:T(8,128)(2,1)S(1)} %slice.93), channel_id=1, source_target_pairs={{0,2},{2,0},{1,3},{3,1},{4,6},{6,4},{5,7},{7,5},{8,10},{10,8},{9,1... | collective-permute-start | bytes 589832 | tf_op jit(solution)/shard_map/ppermute | solution.py:315
  153.0 46.3 %copy-start.2 = (bf16[768,384]{1,0:T(8,128)(2,1)S(1)}, bf16[768,384]{1,0:T(8,128)(2,1)}, u32[]{:S(2)}) copy-start(bf16[768,384]{1,0:T(8,128)(2,1)} %copy-done.1) | copy-start | bytes 1769476
  153.0 46.3 %copy-start.4 = (bf16[768,384]{1,0:T(8,128)(2,1)S(1)}, bf16[768,384]{1,0:T(8,128)(2,1)}, u32[]{:S(2)}) copy-start(bf16[768,384]{1,0:T(8,128)(2,1)} %copy-done.3) | copy-start | bytes 1769476
  153.0 46.4 %copy-start.9 = (bf16[768,384]{1,0:T(8,128)(2,1)S(1)}, bf16[768,384]{1,0:T(8,128)(2,1)}, u32[]{:S(2)}) copy-start(bf16[768,384]{1,0:T(8,128)(2,1)} %copy-done.8) | copy-start | bytes 1769476
  153.0 46.4 %copy-start.11 = (bf16[768,384]{1,0:T(8,128)(2,1)S(1)}, bf16[768,384]{1,0:T(8,128)(2,1)}, u32[]{:S(2)}) copy-start(bf16[768,384]{1,0:T(8,128)(2,1)} %copy-done.10) | copy-start | bytes 1769476
  160.8 9.8 %collective-permute-start.21 = (bf16[128,768]{1,0:T(8,128)(2,1)S(1)}, bf16[128,768]{1,0:T(8,128)(2,1)S(1)}, u32[]{:S(2)}, u32[]{:S(2)}) collective-permute-start(bf16[128,768]{1,0:T(8,128)(2,1)S(1)} %fusion.5), channel_id=1, source_target_pairs={{0,12},{4,8},{8,4},{12,0},{1,13},{5,9},{9,5},{13,1},{2,14},{6,10},... | collective-permute-start | bytes 589832 | tf_op jit(solution)/shard_map/ppermute | solution.py:249
  163.5 15.4 %collective-permute-start.20 = (bf16[128,768]{1,0:T(8,128)(2,1)S(1)}, bf16[128,768]{1,0:T(8,128)(2,1)S(1)}, u32[]{:S(2)}, u32[]{:S(2)}) collective-permute-start(bf16[128,768]{1,0:T(8,128)(2,1)S(1)} %fusion.5), channel_id=1, source_target_pairs={{0,8},{4,12},{8,0},{12,4},{1,9},{5,13},{9,1},{13,5},{2,10},{6,14},... | collective-permute-start | bytes 589832 | tf_op jit(solution)/shard_map/ppermute | solution.py:249
  163.5 15.4 %collective-permute-start.19 = (bf16[128,768]{1,0:T(8,128)(2,1)S(1)}, bf16[128,768]{1,0:T(8,128)(2,1)S(1)}, u32[]{:S(2)}, u32[]{:S(2)}) collective-permute-start(bf16[128,768]{1,0:T(8,128)(2,1)S(1)} %fusion.5), channel_id=1, source_target_pairs={{0,4},{4,0},{8,12},{12,8},{1,5},{5,1},{9,13},{13,9},{2,6},{6,2},{1... | collective-permute-start | bytes 589832 | tf_op jit(solution)/shard_map/ppermute | solution.py:249
  179.0 26.2 %copy-start.6 = (bf16[512,512]{1,0:T(8,128)(2,1)S(1)}, bf16[512,512]{1,0:T(8,128)(2,1)}, u32[]{:S(2)}) copy-start(bf16[512,512]{1,0:T(8,128)(2,1)} %copy-done.5) | copy-start | bytes 1572868
  179.0 26.2 %copy-start.13 = (bf16[512,512]{1,0:T(8,128)(2,1)S(1)}, bf16[512,512]{1,0:T(8,128)(2,1)}, u32[]{:S(2)}) copy-start(bf16[512,512]{1,0:T(8,128)(2,1)} %copy-done.12) | copy-start | bytes 1572868
  179.0 18.1 %collective-permute-start.23 = (bf16[4,128,768]{2,1,0:T(8,128)(2,1)S(1)}, bf16[4,128,768]{2,1,0:T(8,128)(2,1)S(1)}, u32[]{:S(2)}, u32[]{:S(2)}) collective-permute-start(bf16[4,128,768]{2,1,0:T(8,128)(2,1)S(1)} %pad_maximum_fusion.3.refs_0_), channel_id=1, source_target_pairs={{0,2},{2,0},{1,3},{3,1},{4,6},{6,4},{5,7},{7,5},{8,10},{10,8},{9,1... | collective-permute-start | bytes 2359304 | tf_op jit(solution)/shard_map/ppermute | solution.py:320
  179.6 17.5 %collective-permute-start.22 = (bf16[4,128,768]{2,1,0:T(8,128)(2,1)S(1)}, bf16[4,128,768]{2,1,0:T(8,128)(2,1)S(1)}, u32[]{:S(2)}, u32[]{:S(2)}) collective-permute-start(bf16[4,128,768]{2,1,0:T(8,128)(2,1)S(1)} %pad_maximum_fusion.3.refs_0_), channel_id=1, source_target_pairs={{0,1},{1,0},{2,3},{3,2},{4,5},{5,4},{6,7},{7,6},{8,9},{9,8},{10,11... | collective-permute-start | bytes 2359304 | tf_op jit(solution)/shard_map/ppermute | solution.py:323
  197.1 2.3 collective-permute-start.24
  209.7 11.2 %collective-permute-start.27 = (bf16[512,256]{1,0:T(8,128)(2,1)S(1)}, bf16[512,256]{1,0:T(8,128)(2,1)S(1)}, u32[]{:S(2)}, u32[]{:S(2)}) collective-permute-start(bf16[512,256]{1,0:T(8,128)(2,1)S(1)} %shard_map.140.refs_0_), channel_id=1, source_target_pairs={{0,12},{4,8},{8,4},{12,0},{1,13},{5,9},{9,5},{13,1},{2,14},{6,10},... | collective-permute-start | bytes 786440 | tf_op jit(solution)/shard_map/ppermute | solution.py:249
  212.3 21.8 %collective-permute-start.26 = (bf16[512,256]{1,0:T(8,128)(2,1)S(1)}, bf16[512,256]{1,0:T(8,128)(2,1)S(1)}, u32[]{:S(2)}, u32[]{:S(2)}) collective-permute-start(bf16[512,256]{1,0:T(8,128)(2,1)S(1)} %shard_map.140.refs_0_), channel_id=1, source_target_pairs={{0,8},{4,12},{8,0},{12,4},{1,9},{5,13},{9,1},{13,5},{2,10},{6,14},... | collective-permute-start | bytes 786440 | tf_op jit(solution)/shard_map/ppermute | solution.py:249
  212.3 21.8 %collective-permute-start.25 = (bf16[512,256]{1,0:T(8,128)(2,1)S(1)}, bf16[512,256]{1,0:T(8,128)(2,1)S(1)}, u32[]{:S(2)}, u32[]{:S(2)}) collective-permute-start(bf16[512,256]{1,0:T(8,128)(2,1)S(1)} %shard_map.140.refs_0_), channel_id=1, source_target_pairs={{0,4},{4,0},{8,12},{12,8},{1,5},{5,1},{9,13},{13,9},{2,6},{6,2},{1... | collective-permute-start | bytes 786440 | tf_op jit(solution)/shard_map/ppermute | solution.py:249
  235.2 1.8 collective-permute-start.28
  237.0 7.0 %collective-permute-start.29 = (bf16[128,768]{1,0:T(8,128)(2,1)S(1)}, bf16[128,768]{1,0:T(8,128)(2,1)S(1)}, u32[]{:S(2)}, u32[]{:S(2)}) collective-permute-start(bf16[128,768]{1,0:T(8,128)(2,1)S(1)} %slice.92), channel_id=1, source_target_pairs={{0,2},{2,0},{1,3},{3,1},{4,6},{6,4},{5,7},{7,5},{8,10},{10,8},{9,1... | collective-permute-start | bytes 589832 | tf_op jit(solution)/shard_map/ppermute | solution.py:315
  244.1 11.2 %collective-permute-start.30 = (bf16[128,768]{1,0:T(8,128)(2,1)S(1)}, bf16[128,768]{1,0:T(8,128)(2,1)S(1)}, u32[]{:S(2)}, u32[]{:S(2)}) collective-permute-start(bf16[128,768]{1,0:T(8,128)(2,1)S(1)} %fusion.2), channel_id=1, source_target_pairs={{0,0},{1,4},{2,8},{3,12},{4,5},{5,1},{6,13},{7,9},{8,10},{9,14},{1... | collective-permute-start | bytes 589832 | tf_op jit(solution)/shard_map/ppermute | solution.py:330

commit v3 on v2

--- a/solution.py
+++ b/solution.py
@@ -127,29 +127,112 @@
 MIB = 1024 * 1024
 
 
+def in_hbm(value):
+    return pltpu.with_memory_space_constraint(value, pltpu.HBM)
+
+
+HBM_SPEC = pl.BlockSpec(memory_space=pltpu.HBM)
+
+
 def whole_specs(count):
     return [pl.BlockSpec(memory_space=pltpu.VMEM) for _ in range(count)]
 
 
-def project_kernel(gain_ref, query_gain_ref, key_gain_ref, *refs):
-    pieces, panels = refs[:WAYS], refs[WAYS : 3 * WAYS]
-    q_ref, k_ref, v_ref, normed_ref = refs[3 * WAYS :]
-    tile, width = pieces[0].shape[1:]
-    for r in range(WAYS):
-        rows = [pieces[r ^ k][k].astype(jnp.float32) for k in range(WAYS)]
-        square = sum(jnp.sum(x * x, axis=-1, keepdims=True) for x in rows)
-        scale = lax.rsqrt(square / (WAYS * width) + epsilon)
-        for k in range(WAYS):
-            normed_ref[k, r * tile : (r + 1) * tile, :] = (
-                rows[k] * scale * gain_ref[k : k + 1, :]
-            ).astype(jnp.bfloat16)
+def head_lanes(k, h, head_dim):
+    z, y = lax.axis_index("cache"), lax.axis_index("groups")
+    return pl.ds(pl.multiple_of(((z ^ k) * 2 + (y ^ h)) * head_dim, head_dim), head_dim)
+
+
+def pack_panels_kernel(slots, gain_ref, *refs):
+    weights, panels, (end_ref, held_ref, sems) = refs[:3], refs[3:-3], refs[-3:]
+    end_ref[...] = jnp.zeros_like(end_ref)
+    head_dim = gain_ref.shape[1]
+    copies = []
+    for i, (k, h) in enumerate(slots):
+        for m, weight in enumerate(weights):
+            copies.append(
+                pltpu.make_async_copy(
+                    weight.at[:, head_lanes(k, h, head_dim)],
+                    held_ref.at[i, :, m * head_dim : (m + 1) * head_dim],
+                    sems.at[i * 3 + m],
+                )
+            )
+            copies[-1].start()
+    for i, panel in enumerate(panels):
+        for m in range(3):
+            copies[i * 3 + m].wait()
+            lanes = slice(m * head_dim, (m + 1) * head_dim)
+            panel[:, lanes] = (held_ref[i, :, lanes].astype(jnp.float32) * gain_ref[...]).astype(
+                jnp.bfloat16
+            )
+
+
+def pack_panels(slots, gain_lanes, weights):
+    depth, head_dim = gain_lanes.shape
+    shape = jax.ShapeDtypeStruct((depth, 3 * head_dim), jnp.bfloat16)
+    return pl.pallas_call(
+        functools.partial(pack_panels_kernel, slots),
+        out_shape=[shape] * len(slots) + [jax.ShapeDtypeStruct((8, head_dim), jnp.float32)],
+        in_specs=whole_specs(1) + [HBM_SPEC] * 3,
+        out_specs=whole_specs(len(slots) + 1),
+        scratch_shapes=[
+            pltpu.VMEM((len(slots), depth, 3 * head_dim), jnp.bfloat16),
+            pltpu.SemaphoreType.DMA((3 * len(slots),)),
+        ],
+        compiler_params=pltpu.CompilerParams(vmem_limit_bytes=10 * MIB),
+    )(gain_lanes, *[in_hbm(w) for w in weights])
+
+
+def pack_cache_kernel(ks, keys_ref, values_ref, *refs):
+    packs, sems = refs[:-1], refs[-1]
+    head_dim = packs[0].shape[1] // 4
+    copies = []
+    for i, (k, pack) in enumerate(zip(ks, packs)):
+        for m in range(4):
+            source = (keys_ref, values_ref)[m // 2]
+            copies.append(
+                pltpu.make_async_copy(
+                    source.at[:, head_lanes(k, m % 2, head_dim)],
+                    pack.at[:, m * head_dim : (m + 1) * head_dim],
+                    sems.at[i * 4 + m],
+                )
+            )
+            copies[-1].start()
+    for copy in copies:
+        copy.wait()
+
+
+def pack_cache(ks, keys, values, head_dim):
+    shape = jax.ShapeDtypeStruct((keys.shape[0], 4 * head_dim), jnp.bfloat16)
+    return pl.pallas_call(
+        functools.partial(pack_cache_kernel, ks),
+        out_shape=[shape] * len(ks),
+        in_specs=[HBM_SPEC] * 2,
+        out_specs=whole_specs(len(ks)),
+        scratch_shapes=[pltpu.SemaphoreType.DMA((4 * len(ks),))],
+        compiler_params=pltpu.CompilerParams(vmem_limit_bytes=6 * MIB),
+    )(*map(in_hbm, (keys, values)))
+
+
+def project_rows(part, panel, query_gain_ref, key_gain_ref, outs):
+    q_ref, k_ref, v_ref = outs
     head_dim = query_gain_ref.shape[1]
+    totals = [None, None]
+    squares = [0.0] * WAYS
+    columns = 0
+    for k in range(WAYS):
+        blocks = [part(r, k) for r in range(WAYS)]
+        rows = jnp.concatenate(blocks, axis=0)
+        columns += rows.shape[1]
+        for h in range(2):
+            product = jnp.dot(rows, panel(k, h), preferred_element_type=jnp.float32)
+            totals[h] = product if k == 0 else totals[h] + product
+        for r in range(WAYS):
+            wide = blocks[r].astype(jnp.float32)
+            squares[r] += jnp.sum(wide * wide, axis=-1, keepdims=True)
+    scale = lax.rsqrt(jnp.concatenate(squares, axis=0) / columns + epsilon)
     for h in range(2):
-        total = jnp.dot(normed_ref[0], panels[h][...], preferred_element_type=jnp.float32)
-        for k in range(1, WAYS):
-            total += jnp.dot(
-                normed_ref[k], panels[2 * k + h][...], preferred_element_type=jnp.float32
-            )
+        total = totals[h] * scale
         lanes = slice(h * head_dim, (h + 1) * head_dim)
         q_ref[:, lanes] = rms_scale(total[:, :head_dim], query_gain_ref[...]).astype(jnp.bfloat16)
         k_ref[:, lanes] = rms_scale(
@@ -158,37 +241,22 @@
         v_ref[:, lanes] = total[:, 2 * head_dim :].astype(jnp.bfloat16)
 
 
-def project(pieces, panels, gain_rows, query_gain, key_gain):
-    tile, width = pieces[0].shape[1:]
-    head_dim = query_gain.shape[1]
-    shape = jax.ShapeDtypeStruct((WAYS * tile, 2 * head_dim), jnp.bfloat16)
-    return pl.pallas_call(
-        project_kernel,
-        out_shape=[shape] * 3,
-        in_specs=whole_specs(3 + 3 * WAYS),
-        out_specs=whole_specs(3),
-        scratch_shapes=[pltpu.VMEM((WAYS, WAYS * tile, width), jnp.bfloat16)],
-        compiler_params=pltpu.CompilerParams(vmem_limit_bytes=24 * MIB),
-    )(gain_rows, query_gain, key_gain, *pieces, *panels)
-
-
-def attend_kernel(pos_ref, q_ref, k_ref, v_ref, *refs):
-    held, mixed_ref = refs[:WAYS], refs[WAYS]
+def attend_rows(pos_ref, q_ref, k_ref, v_ref, held, mixed_ref):
     head_dim = q_ref.shape[1] // 2
     tile = q_ref.shape[0] // WAYS
     across = (((1,), (1,)), ((), ()))
-    for r in range(WAYS):
-        rows = slice(r * tile, (r + 1) * tile)
-        for h in range(2):
+    for h in range(2):
+        for r in range(WAYS):
+            rows = slice(r * tile, (r + 1) * tile)
             lanes = slice(h * head_dim, (h + 1) * head_dim)
             value_lanes = slice((2 + h) * head_dim, (3 + h) * head_dim)
             query = q_ref[rows, lanes]
             keys = [k_ref[rows, lanes]]
             values = [v_ref[rows, lanes]]
             for k in range(WAYS):
-                start = pl.multiple_of(pos_ref[r * WAYS + k] * BLOCK, BLOCK)
-                keys.append(held[k][pl.ds(start, BLOCK), lanes])
-                values.append(held[k][pl.ds(start, BLOCK), value_lanes])
+                block = pl.ds(pl.multiple_of(pos_ref[r * WAYS + k] * BLOCK, BLOCK), BLOCK)
+                keys.append(held[k][block, lanes])
+                values.append(held[k][block, value_lanes])
             total = jnp.zeros((tile, 1), jnp.float32)
             summed = jnp.zeros((tile, head_dim), jnp.float32)
             for key, value in zip(keys, values):
@@ -201,14 +269,87 @@
             mixed_ref[rows, lanes] = (summed / total).astype(jnp.bfloat16)
 
 
-def attend_all(pos, q, k, v, held):
+def project_kernel(source_ref, query_gain_ref, key_gain_ref, gathered_ref, *refs):
+    panels, outs = refs[: 2 * WAYS], refs[2 * WAYS :]
+
+    def part(j, k):
+        return gathered_ref[source_ref[j * WAYS + k]]
+
+    def panel(k, h):
+        return panels[2 * k + h][...]
+
+    project_rows(part, panel, query_gain_ref, key_gain_ref, outs)
+
+
+def attend_kernel(pos_ref, q_ref, k_ref, v_ref, *refs):
+    attend_rows(pos_ref, q_ref, k_ref, v_ref, refs[:WAYS], refs[WAYS])
+
+
+def both_kernel(pos_ref, query_gain_ref, key_gain_ref, *refs):
+    pairs, panels, caches = refs[: 2 * WAYS], refs[2 * WAYS : 4 * WAYS], refs[4 * WAYS : 5 * WAYS]
+    mixed_ref, panel_ref, held_ref, *outs, panel_sems, held_sems = refs[5 * WAYS :]
+    copies = [
+        pltpu.make_async_copy(source, panel_ref.at[i], panel_sems.at[i])
+        for i, source in enumerate(panels)
+    ]
+    late = [
+        pltpu.make_async_copy(source, held_ref.at[i], held_sems.at[i])
+        for i, source in enumerate(caches)
+    ]
+    for copy in copies + late:
+        copy.start()
+
+    def part(j, k):
+        return pairs[2 * j + k // 2][k % 2]
+
+    def panel(k, h):
+        copies[2 * k + h].wait()
+        return panel_ref[2 * k + h]
+
+    project_rows(part, panel, query_gain_ref, key_gain_ref, outs)
+    for copy in late:
+        copy.wait()
+    attend_rows(pos_ref, *outs, [held_ref.at[k] for k in range(WAYS)], mixed_ref)
+
+
+def mix_first(source, pos, gains, gathered, panels, held):
+    tile, head_dim = gathered.shape[1], gains[0].shape[1]
+    shape = jax.ShapeDtypeStruct((WAYS * tile, 2 * head_dim), jnp.bfloat16)
+    qkv = pl.pallas_call(
+        project_kernel,
+        out_shape=[shape] * 3,
+        in_specs=[pl.BlockSpec(memory_space=pltpu.SMEM)] + whole_specs(3 + len(panels)),
+        out_specs=whole_specs(3),
+        compiler_params=pltpu.CompilerParams(vmem_limit_bytes=14 * MIB),
+    )(source, *gains, gathered, *panels)
     return pl.pallas_call(
         attend_kernel,
-        out_shape=jax.ShapeDtypeStruct(q.shape, jnp.bfloat16),
-        in_specs=[pl.BlockSpec(memory_space=pltpu.SMEM)] + whole_specs(3 + WAYS),
-        out_specs=pl.BlockSpec(memory_space=pltpu.VMEM),
+        out_shape=shape,
+        in_specs=[pl.BlockSpec(memory_space=pltpu.SMEM)] + whole_specs(3 + len(held)),
+        out_specs=whole_specs(1)[0],
         compiler_params=pltpu.CompilerParams(vmem_limit_bytes=10 * MIB),
-    )(pos, q, k, v, *held)
+    )(pos, *qkv, *held)
+
+
+def mix_again(pos, gains, parts, panels, held):
+    tile, head_dim = parts[0].shape[1], gains[0].shape[1]
+    shape = (WAYS * tile, 2 * head_dim)
+    return pl.pallas_call(
+        both_kernel,
+        out_shape=jax.ShapeDtypeStruct(shape, jnp.bfloat16),
+        in_specs=[pl.BlockSpec(memory_space=pltpu.SMEM)]
+        + whole_specs(2 + len(parts))
+        + [HBM_SPEC] * (len(panels) + len(held)),
+        out_specs=whole_specs(1)[0],
+        scratch_shapes=[
+            pltpu.VMEM((len(panels), *panels[0].shape), jnp.bfloat16),
+            pltpu.VMEM((len(held), *held[0].shape), jnp.bfloat16),
+            *[pltpu.VMEM(shape, jnp.bfloat16)] * 3,
+            pltpu.SemaphoreType.DMA((len(panels),)),
+            pltpu.SemaphoreType.DMA((len(held),)),
+        ],
+        compiler_params=pltpu.CompilerParams(vmem_limit_bytes=20 * MIB),
+    )(pos, *gains, *parts, *map(in_hbm, panels), *map(in_hbm, held))
 
 
 def out_kernel(w_ref, *refs):
@@ -217,7 +358,7 @@
     tile = mixed[0].shape[0] // WAYS
     for r in range(WAYS):
         row = jnp.concatenate(
-            [mixed[k][(r ^ k) * tile : ((r ^ k) + 1) * tile, :] for k in range(WAYS)], axis=1
+            [mixed[k][r * tile : (r + 1) * tile, :] for k in range(WAYS)], axis=1
         )
         update = jnp.dot(row, w_ref[...], preferred_element_type=jnp.float32)
         rows = slice((r // 2) * tile, (r // 2 + 1) * tile)
@@ -274,60 +415,74 @@
     tile = tokens.shape[0]
     ways = jnp.arange(WAYS, dtype=jnp.int32)
 
-    def head_of(array, k, h):
-        return lax.dynamic_slice_in_dim(array, ((z ^ k) * 2 + (y ^ h)) * head_dim, head_dim, 1)
-
-    def panel_of(k, h):
-        return jnp.concatenate([head_of(w, k, h) for w in (w_query, w_key, w_value)], axis=1)
-
-    def cache_of(k):
-        return jnp.concatenate([head_of(a, k, h) for a in (cache_keys, cache_values) for h in (0, 1)], axis=1)
-
+    def gather_pairs(by_z):
+        low = jnp.stack(by_z[:2])
+        low_x = lax.ppermute(low, "fsdp", SWAP)
+        high = jnp.stack(by_z[2:])
+        high_x = lax.ppermute(high, "fsdp", SWAP)
+        mine = [low, high, low_x, high_x]
+        low_c, high_c, low_xc, high_xc = [lax.ppermute(pair, "head", SWAP) for pair in mine]
+        return [low, high, low_c, high_c, low_x, high_x, low_xc, high_xc]
+
+    weights = (w_query, w_key, w_value)
+    gain_lanes = jnp.broadcast_to(
+        lax.dynamic_slice_in_dim(norm_gain, z * width, width, 0)[:, None], (width, head_dim)
+    )
+    order = (2, 3, 1)
+    *sends, end = pack_panels([(k, 0) for k in order], gain_lanes, weights)
+    sends = dict(zip(order, sends))
+    near = {k: from_z(sends[k], k) for k in order}
+    tokens, _ = lax.optimization_barrier((tokens, end))
     piece = lax.dynamic_slice_in_dim(tokens, p * width, width, 1)
-    by_z = jnp.stack([piece] + [from_z(piece, k) for k in range(1, WAYS)])
-    by_x = jnp.stack([by_z, lax.ppermute(by_z, "fsdp", SWAP)])
-    by_core = lax.ppermute(by_x, "head", SWAP)
-    gathered = jnp.stack([by_x, by_core], axis=1).reshape(WAYS * WAYS, tile, width)
-
-    near = [panel_of(0, 0)] + [from_z(panel_of(k, 0), k) for k in range(1, WAYS)]
-    far = [panel_of(0, 1)] + [lax.ppermute(near[k], "groups", SWAP) for k in range(1, WAYS)]
-    panels = [panel for pair in zip(near, far) for panel in pair]
-    held = [cache_of(0)] + [from_z(cache_of(k), k) for k in range(1, WAYS)]
-
-    source = (z ^ p ^ ways)[None, :] * WAYS + (p ^ ways[:, None] ^ ways[None, :])
-    pieces = [jnp.take(gathered, source[j], axis=0) for j in range(WAYS)]
-    x_share = pieces[0][0]
-
-    gain_rows = jnp.take(norm_gain.reshape(WAYS, width), z ^ ways, axis=0)
+    far_piece = from_z(piece, 2)
+    parts = gather_pairs([piece, from_z(piece, 1), far_piece, from_z(far_piece, 1)])
+    far = {k: lax.ppermute(near[k], "groups", SWAP) for k in order}
+    packs = dict(zip((2, 3, 1, 0), pack_cache((2, 3, 1, 0), cache_keys, cache_values, head_dim)))
+    held = [packs[0]]
+    for k in range(1, WAYS):
+        pack, _ = lax.optimization_barrier((packs[k], near[k]))
+        held.append(from_z(pack, k))
+    near[0], far[0], _ = pack_panels([(0, 0), (0, 1)], gain_lanes, weights)
+    panels = [side[k] for k in range(WAYS) for side in (near, far)]
+    gathered = jnp.concatenate(parts, axis=0)
+    source = (z ^ p ^ ways)[None, :] * WAYS + (z ^ p ^ ways)[:, None]
+    source = source.reshape(-1)
+    x_share = lax.dynamic_index_in_dim(gathered, source[0], 0, keepdims=False)
+    gains = (query_gain[None], key_gain[None])
+
     heads = jnp.stack([(z ^ ways) * 2 + y, (z ^ ways) * 2 + 1 - y], axis=1).reshape(-1)
     w_rows = jnp.take(w_out.reshape(2 * WAYS, head_dim, width), heads, axis=0).reshape(-1, width)
     gates = lax.dynamic_slice_in_dim(step_gate, z * width, width, 1)
-    slots = jnp.take(block_home, jnp.take(block_list, jnp.take(reader_span, z ^ p ^ ways), axis=0))
+    slots = jnp.take(block_home, jnp.take(block_list, jnp.take(reader_span, p ^ ways), axis=0))
     from_k = slots[:, :, None] // held_blocks == (z ^ ways)[None, None, :]
     pos = jnp.sum(jnp.where(from_k, (slots % held_blocks)[:, :, None], 0), axis=1).reshape(-1)
 
     for step in range(ITERS):
-        q, k, v = project(pieces, panels, gain_rows, query_gain[None], key_gain[None])
-        own = attend_all(pos, q, k, v, held)
+        if step == 0:
+            own = mix_first(source, pos, gains, gathered, panels, held)
+        else:
+            own = mix_again(pos, gains, parts, panels, held)
         mixed = [own] + [from_z(own, k) for k in range(1, WAYS)]
         keep, send = project_out(w_rows, mixed)
         half = keep + lax.ppermute(send, "head", SWAP).astype(jnp.float32)
-        other = lax.ppermute(half[tile:].astype(jnp.bfloat16), "fsdp", SWAP)
-        update = half[:tile] + other.astype(jnp.float32)
-        x_share = (x_share.astype(jnp.float32) + gates[step] * update).astype(jnp.bfloat16)
+        base, other = x_share.astype(jnp.float32), half[tile:]
         if step + 1 < ITERS:
-            by_z = jnp.stack([x_share] + [from_z(x_share, k) for k in range(1, WAYS)])
-            by_x = lax.ppermute(by_z, "fsdp", SWAP)
-            pieces = [
-                by_z,
-                lax.ppermute(by_z, "head", SWAP),
-                by_x,
-                lax.ppermute(by_x, "head", SWAP),
-            ]
-    moves = [
-        (a * WAYS + b, (a ^ b) * WAYS + a) for a in range(WAYS) for b in range(WAYS)
+            other = lax.ppermute(other.astype(jnp.bfloat16), "fsdp", SWAP)
+            update = half[:tile] + other.astype(jnp.float32)
+            x_share = (base + gates[step] * update).astype(jnp.bfloat16)
+            far = from_z(x_share, 2)
+            parts = gather_pairs([x_share, from_z(x_share, 1), far, from_z(far, 1)])
+    base = (base + gates[step] * half[:tile]).astype(jnp.bfloat16)
+    other = (gates[step] * other).astype(jnp.bfloat16)
+    ends = [
+        lax.ppermute(
+            value,
+            ("cache", "fsdp", "head"),
+            [(a * WAYS + b, (b ^ flip) * WAYS + a) for a in range(WAYS) for b in range(WAYS)],
+        )
+        for value, flip in ((base, 0), (other, 2))
     ]
-    return lax.ppermute(x_share, ("cache", "fsdp", "head"), moves)
+    return (ends[0].astype(jnp.float32) + ends[1].astype(jnp.float32)).astype(jnp.bfloat16)
 
 
 def solution(mesh):

time: 257 us -> 244 us (0.949)
  starting transfers between devices: 33.1 us -> 53.7 us
  local copies, waits for them, and re-layouts: 29.9 us -> 12.4 us
  waiting for transfers between devices: 151 us -> 141 us
  other arithmetic: 17.8 us -> 8.63 us
  Pallas kernels: 23.1 us -> 27.5 us
    ppermute x11 -> x18, waiting for transfers between devices: 81.2 us -> 60.3 us  [the longest x3 25.3 us: split_heads(): far = {k: lax.ppermute(near[k], 'groups', SWAP) for k in order}]
    gather x9 -> x4, local copies, waits for them, and re-layouts: 16.1 us -> 2.47 us  [the longest x1 1.17 us: split_heads(): jnp.take(reader_span, p ^ ways)]
    ppermute x18, starting transfers between devices: 25.1 us -> 37.6 us  [from_z(): return lax.ppermute(value, 'cache', [(i, i ^ k) for i in range(WAYS)])]
    ppermute x18, waiting for transfers between devices: 66.9 us -> 76.9 us  [from_z(): return lax.ppermute(value, 'cache', [(i, i ^ k) for i in range(WAYS)])]
    ppermute x11 -> x18, starting transfers between devices: 7.88 us -> 16 us  [the longest x2 7.99 us: split_heads(): lax.ppermute(value, ('cache', 'fsdp', 'head'), [(a * WAYS + b, (b ^ flip)...]
    dynamic_slice x4 -> x1, local copies, waits for them, and re-layouts: 7.41 us -> 0.77 us  [split_heads(): lax.dynamic_slice_in_dim(norm_gain, z * width, width, 0)[:, None]]
    concatenate x9 -> x0, other arithmetic: 6.62 us -> none  [the longest x5 3.89 us: panel_of(): jnp.concatenate([head_of(w, k, h) for w in (w_query, w_key, w_value)], ax...]
    another operation x4, other arithmetic: 7 us -> 1.27 us  [the longest x2 1.19 us: gather_pairs(): low = jnp.stack(by_z[:2])]
  transfers between devices with their start and end apart: 31 -> 38, of which waited for: 17 -> 21; matrix products, arithmetic and copies ran while one was open for 17% -> 6% of each run, Pallas kernels for 2% -> 5%
where the time goes in v3:
time: 244 us; the launch traced here: 243 us
  waiting for transfers between devices  141 us (58%)
  starting transfers between devices  53.7 us (22%)
  Pallas kernels  27.5 us (11%)
  local copies, waits for them, and re-layouts  12.4 us (5%)
  other arithmetic  8.63 us (4%)
    ppermute x18, waiting for transfers between devices, from_z(): return lax.ppermute(value, 'cache', [(i, i ^ k) for i in range(WAYS)])  76.9 us
    ppermute x18, starting transfers between devices, from_z(): return lax.ppermute(value, 'cache', [(i, i ^ k) for i in range(WAYS)])  37.6 us
    ppermute x3, waiting for transfers between devices, split_heads(): far = {k: lax.ppermute(near[k], 'groups', SWAP) for k in order}  25.3 us
    ppermute x2, waiting for transfers between devices, gather_pairs(): high_x = lax.ppermute(high, 'fsdp', SWAP)  13.2 us
    pallas_call x1, Pallas kernels, mix_again(): pl.pallas_call(both_kernel, out_shape=jax.ShapeDtypeStruct(shape, jnp.bfl...  9.68 us
    ppermute x2, waiting for transfers between devices, split_heads(): lax.ppermute(value, ('cache', 'fsdp', 'head'), [(a * WAYS + b, (b ^ flip)...  9.12 us
    ppermute x2, starting transfers between devices, split_heads(): lax.ppermute(value, ('cache', 'fsdp', 'head'), [(a * WAYS + b, (b ^ flip)...  7.99 us
    ppermute x2, waiting for transfers between devices, gather_pairs(): low_x = lax.ppermute(low, 'fsdp', SWAP)  5.52 us
  transfers between devices with their start and end apart: 38, of which 21 were waited for; matrix products, arithmetic and copies ran while one was open for 6% of the time, Pallas kernels for 5%

profile of v3, /device:TPU:2, one launch (start us, length us, event | category | flops | bytes accessed | tf_op | source)
XLA Modules:
  0.0 243.5 jit_solution(8732524286974095855)
XLA Ops:
  0.0 1.8 constant_dynamic-update-slice_fusion.9
  1.8 1.6 collective-permute-start
  3.4 2.6 %collective-permute-start.1 = (bf16[128,768]{1,0:T(8,128)(2,1)}, bf16[128,768]{1,0:T(8,128)(2,1)S(1)}, u32[]{:S(2)}, u32[]{:S(2)}) collective-permute-start(bf16[128,768]{1,0:T(8,128)(2,1)} %get-tuple-element.46), channel_id=1, source_target_pairs={{0,8},{4,12},{8,0},{12,4},{1,9},{5,13},{9,1},{13,5},{2,10},{6,14},... | collective-permute-start | bytes 589832 | tf_op jit(solution)/shard_map/ppermute | solution.py:390
  6.0 0.8 dynamic_slice.16
  6.9 2.9 %shard_map.137 = (bf16[768,384]{1,0:T(8,128)(2,1)}, bf16[768,384]{1,0:T(8,128)(2,1)}, bf16[768,384]{1,0:T(8,128)(2,1)}, f32[8,128]{1,0:T(8,128)}) custom-call(f32[768,128]{1,0:T(8,128)S(1)} %broadcast_in_dim.65.gain_ref, bf16[768,1024]{1,0:T(8,128)(2,1)} %refs_0_.3, bf16[768,1024]{1,0:T(8,128)(2,1)} %refs_1_.3, bf16[768,1024]{1,0:T(8,128)(2,1)} %refs_2_.3), custom_call_target="tpu_custom_call" | custom-call | tf_op jit(solution)/shard_map/pallas_call | solution.py:173
  10.7 3.6 %collective-permute-start.13 = (bf16[768,384]{1,0:T(8,128)(2,1)}, bf16[768,384]{1,0:T(8,128)(2,1)}, u32[]{:S(2)}, u32[]{:S(2)}) collective-permute-start(bf16[768,384]{1,0:T(8,128)(2,1)} %get-tuple-element.28), channel_id=1, source_target_pairs={{0,12},{4,8},{8,4},{12,0},{1,13},{5,9},{9,5},{13,1},{2,14},{6,10},... | collective-permute-start | bytes 1769480 | tf_op jit(solution)/shard_map/ppermute | solution.py:390
  15.6 1.2 gather_fusion.1
  16.8 1.2 fusion.9
  18.0 1.2 compare_and_fusion
  19.2 2.0 shard_map.136
  21.2 0.8 copy-done.5
  22.0 0.8 copy-done.7
  23.5 0.7 compare_select_fusion
  24.3 0.7 gather_fusion.3
  25.0 0.7 add_select_fusion.1
  26.1 1.8 gather_fusion
  28.0 1.9 shard_map.139
  29.9 1.2 pad_maximum_fusion
  31.1 0.6 collective-permute-start.5
  31.7 23.3 %collective-permute-done.2 = bf16[128,768]{1,0:T(8,128)(2,1)S(1)} collective-permute-done((bf16[128,768]{1,0:T(8,128)(2,1)S(1)}, bf16[128,768]{1,0:T(8,128)(2,1)S(1)}, u32[]{:S(2)}, u32[]{:S(2)}) %collective-permute-start.2) | collective-permute-done | bytes 196640 | tf_op jit(solution)/shard_map/ppermute | solution.py:390
  56.3 1.7 collective-permute-start.10
  58.0 7.2 %collective-permute-done.6 = bf16[2,128,768]{2,1,0:T(8,128)(2,1)S(1)} collective-permute-done((bf16[2,128,768]{2,1,0:T(8,128)(2,1)S(1)}, bf16[2,128,768]{2,1,0:T(8,128)(2,1)S(1)}, u32[]{:S(2)}, u32[]{:S(2)}) %collective-permute-start.6) | collective-permute-done | bytes 393248 | tf_op jit(solution)/shard_map/ppermute | solution.py:422
  65.3 2.8 %collective-permute-start.15 = (bf16[512,512]{1,0:T(8,128)(2,1)S(1)}, bf16[512,512]{1,0:T(8,128)(2,1)S(1)}, u32[]{:S(2)}, u32[]{:S(2)}) collective-permute-start(bf16[512,512]{1,0:T(8,128)(2,1)S(1)} %get-tuple-element.34), channel_id=1, source_target_pairs={{0,4},{4,0},{8,12},{12,8},{1,5},{5,1},{9,13},{13,9},{2,6},{6,2},{1... | collective-permute-start | bytes 1572872 | tf_op jit(solution)/shard_map/ppermute | solution.py:390
  68.2 1.4 collective-permute-start.16
  69.6 1.2 collective-permute-start.17
  70.8 0.6 collective-permute-start.12
  71.4 0.6 collective-permute-done.10.refs_3_.refs_11_
  72.0 1.7 collective-permute-start.14
  73.9 13.1 %collective-permute-done.12.refs_5_.refs_13_ = bf16[768,384]{1,0:T(8,128)(2,1)S(1)} collective-permute-done((bf16[768,384]{1,0:T(8,128)(2,1)S(1)}, bf16[768,384]{1,0:T(8,128)(2,1)S(1)}, u32[]{:S(2)}, u32[]{:S(2)}) %collective-permute-start.12) | collective-permute-done | bytes 589856 | tf_op jit(solution)/shard_map/ppermute | solution.py:439
  87.0 11.6 %collective-permute-done.14.refs_7_.refs_15_ = bf16[768,384]{1,0:T(8,128)(2,1)S(1)} collective-permute-done((bf16[768,384]{1,0:T(8,128)(2,1)}, bf16[768,384]{1,0:T(8,128)(2,1)S(1)}, u32[]{:S(2)}, u32[]{:S(2)}) %collective-permute-start.14) | collective-permute-done | bytes 589856 | tf_op jit(solution)/shard_map/ppermute | solution.py:439
  98.6 5.1 %shard_map.138 = (bf16[512,256]{1,0:T(8,128)(2,1)S(1)}, bf16[512,256]{1,0:T(8,128)(2,1)S(1)}, bf16[512,256]{1,0:T(8,128)(2,1)S(1)}) custom-call(s32[16]{0:T(128)S(1)} %add.165.source_ref, f32[1,128]{1,0:T(1,128)S(1)} %bitcast.44, f32[1,128]{1,0:T(1,128)S(1)} %bitcast.46, bf16[16,128,768]{2,1,0:T(8,128)(2,1)S(1)} %constant_dynamic-update-slice_fusion.gathered_ref, ...), custom_call_target="tpu_custom_call" | custom-call | tf_op jit(solution)/shard_map/pallas_call | solution.py:318
  103.8 2.6 %collective-permute-done.16.refs_2_.refs_18_ = bf16[512,512]{1,0:T(8,128)(2,1)S(1)} collective-permute-done((bf16[512,512]{1,0:T(8,128)(2,1)S(1)}, bf16[512,512]{1,0:T(8,128)(2,1)S(1)}, u32[]{:S(2)}, u32[]{:S(2)}) %collective-permute-start.16) | collective-permute-done | bytes 524320 | tf_op jit(solution)/shard_map/ppermute | solution.py:390
  106.4 3.9 %shard_map.140.refs_0_ = bf16[512,256]{1,0:T(8,128)(2,1)S(1)} custom-call(s32[16]{0:T(128)S(1)} %reshape.272.pos_ref, bf16[512,256]{1,0:T(8,128)(2,1)S(1)} %get-tuple-element.29.q_ref, bf16[512,256]{1,0:T(8,128)(2,1)S(1)} %get-tuple-element.30.k_ref, bf16[512,256]{1,0:T(8,128)(2,1)S(1)} %get-tuple-element.31.v_ref, ...), custom_call_target="tpu_custom_call" | custom-call | tf_op jit(solution)/shard_map/pallas_call | solution.py:325
  110.3 11.2 %collective-permute-start.18 = (bf16[512,256]{1,0:T(8,128)(2,1)S(1)}, bf16[512,256]{1,0:T(8,128)(2,1)S(1)}, u32[]{:S(2)}, u32[]{:S(2)}) collective-permute-start(bf16[512,256]{1,0:T(8,128)(2,1)S(1)} %shard_map.140.refs_0_), channel_id=1, source_target_pairs={{0,4},{4,0},{8,12},{12,8},{1,5},{5,1},{9,13},{13,9},{2,6},{6,2},{1... | collective-permute-start | bytes 786440 | tf_op jit(solution)/shard_map/ppermute | solution.py:390
  121.4 1.1 collective-permute-start.19
  122.5 1.5 collective-permute-start.20
  124.3 7.6 %collective-permute-done.18.refs_1_ = bf16[512,256]{1,0:T(8,128)(2,1)S(1)} collective-permute-done((bf16[512,256]{1,0:T(8,128)(2,1)S(1)}, bf16[512,256]{1,0:T(8,128)(2,1)S(1)}, u32[]{:S(2)}, u32[]{:S(2)}) %collective-permute-start.18) | collective-permute-done | bytes 262176 | tf_op jit(solution)/shard_map/ppermute | solution.py:390
  131.9 10.9 %collective-permute-done.19.refs_2_ = bf16[512,256]{1,0:T(8,128)(2,1)S(1)} collective-permute-done((bf16[512,256]{1,0:T(8,128)(2,1)S(1)}, bf16[512,256]{1,0:T(8,128)(2,1)S(1)}, u32[]{:S(2)}, u32[]{:S(2)}) %collective-permute-start.19) | collective-permute-done | bytes 262176 | tf_op jit(solution)/shard_map/ppermute | solution.py:390
  142.8 1.0 shard_map.141
  143.9 1.7 collective-permute-done.21
  145.6 1.0 convert_add_fusion.1
  146.6 1.0 slice.58
  147.6 0.6 collective-permute-start.22
  148.3 0.9 dynamic-slice_reduce_fusion
  149.2 5.4 %collective-permute-done.22 = bf16[128,768]{1,0:T(8,128)(2,1)S(1)} collective-permute-done((bf16[128,768]{1,0:T(8,128)(2,1)S(1)}, bf16[128,768]{1,0:T(8,128)(2,1)S(1)}, u32[]{:S(2)}, u32[]{:S(2)}) %collective-permute-start.22) | collective-permute-done | bytes 196640 | tf_op jit(solution)/shard_map/ppermute | solution.py:470
  154.6 1.1 fusion.5
  155.7 5.4 %collective-permute-start.24 = (bf16[128,768]{1,0:T(8,128)(2,1)S(1)}, bf16[128,768]{1,0:T(8,128)(2,1)S(1)}, u32[]{:S(2)}, u32[]{:S(2)}) collective-permute-start(bf16[128,768]{1,0:T(8,128)(2,1)S(1)} %fusion.5), channel_id=1, source_target_pairs={{0,8},{4,12},{8,0},{12,4},{1,9},{5,13},{9,1},{13,5},{2,10},{6,14},... | collective-permute-start | bytes 589832 | tf_op jit(solution)/shard_map/ppermute | solution.py:390
  161.1 8.7 %collective-permute-done.24 = bf16[128,768]{1,0:T(8,128)(2,1)S(1)} collective-permute-done((bf16[128,768]{1,0:T(8,128)(2,1)S(1)}, bf16[128,768]{1,0:T(8,128)(2,1)S(1)}, u32[]{:S(2)}, u32[]{:S(2)}) %collective-permute-start.24) | collective-permute-done | bytes 196640 | tf_op jit(solution)/shard_map/ppermute | solution.py:390
  170.6 4.9 %collective-permute-done.25 = bf16[128,768]{1,0:T(8,128)(2,1)S(1)} collective-permute-done((bf16[128,768]{1,0:T(8,128)(2,1)S(1)}, bf16[128,768]{1,0:T(8,128)(2,1)S(1)}, u32[]{:S(2)}, u32[]{:S(2)}) %collective-permute-start.25) | collective-permute-done | bytes 196640 | tf_op jit(solution)/shard_map/ppermute | solution.py:390
  175.5 0.6 collective-permute-start.29
  176.6 5.5 %collective-permute-done.28.refs_4_ = bf16[2,128,768]{2,1,0:T(8,128)(2,1)S(1)} collective-permute-done((bf16[2,128,768]{2,1,0:T(8,128)(2,1)S(1)}, bf16[2,128,768]{2,1,0:T(8,128)(2,1)S(1)}, u32[]{:S(2)}, u32[]{:S(2)}) %collective-permute-start.28) | collective-permute-done | bytes 393248 | tf_op jit(solution)/shard_map/ppermute | solution.py:420
  182.1 6.0 %collective-permute-done.29.refs_5_ = bf16[2,128,768]{2,1,0:T(8,128)(2,1)S(1)} collective-permute-done((bf16[2,128,768]{2,1,0:T(8,128)(2,1)S(1)}, bf16[2,128,768]{2,1,0:T(8,128)(2,1)S(1)}, u32[]{:S(2)}, u32[]{:S(2)}) %collective-permute-start.29) | collective-permute-done | bytes 393248 | tf_op jit(solution)/shard_map/ppermute | solution.py:422
  188.2 1.7 collective-permute-done.31.refs_7_
  189.9 9.7 %shard_map.142.refs_0_ = bf16[512,256]{1,0:T(8,128)(2,1)S(1)} custom-call(s32[16]{0:T(128)S(1)} %reshape.272.pos_ref, f32[1,128]{1,0:T(1,128)S(1)} %bitcast.45, f32[1,128]{1,0:T(1,128)S(1)} %bitcast.47, bf16[2,128,768]{2,1,0:T(8,128)(2,1)S(1)} %pad_maximum_fusion.2.refs_0_, bf16[2,128,768]{2,1,0:T(8,128)(2,1)S(1)} %pad_maximum_fusion.3.refs_1_, ...), custom_call_target="tpu_custom_call" | custom-call | tf_op jit(solution)/shard_map/pallas_call | solution.py:337
  199.6 1.8 collective-permute-start.32
  201.4 2.6 %collective-permute-start.34 = (bf16[512,256]{1,0:T(8,128)(2,1)S(1)}, bf16[512,256]{1,0:T(8,128)(2,1)S(1)}, u32[]{:S(2)}, u32[]{:S(2)}) collective-permute-start(bf16[512,256]{1,0:T(8,128)(2,1)S(1)} %shard_map.142.refs_0_), channel_id=1, source_target_pairs={{0,12},{4,8},{8,4},{12,0},{1,13},{5,9},{9,5},{13,1},{2,14},{6,10},... | collective-permute-start | bytes 786440 | tf_op jit(solution)/shard_map/ppermute | solution.py:390
  204.0 7.9 %collective-permute-done.32.refs_1_ = bf16[512,256]{1,0:T(8,128)(2,1)S(1)} collective-permute-done((bf16[512,256]{1,0:T(8,128)(2,1)S(1)}, bf16[512,256]{1,0:T(8,128)(2,1)S(1)}, u32[]{:S(2)}, u32[]{:S(2)}) %collective-permute-start.32) | collective-permute-done | bytes 262176 | tf_op jit(solution)/shard_map/ppermute | solution.py:390
  211.9 10.7 %collective-permute-done.33.refs_2_ = bf16[512,256]{1,0:T(8,128)(2,1)S(1)} collective-permute-done((bf16[512,256]{1,0:T(8,128)(2,1)S(1)}, bf16[512,256]{1,0:T(8,128)(2,1)S(1)}, u32[]{:S(2)}, u32[]{:S(2)}) %collective-permute-start.33) | collective-permute-done | bytes 262176 | tf_op jit(solution)/shard_map/ppermute | solution.py:390
  222.7 1.0 shard_map.143
  223.8 1.7 collective-permute-done.35
  226.2 7.4 %collective-permute-start.36 = (bf16[128,768]{1,0:T(8,128)(2,1)S(1)}, bf16[128,768]{1,0:T(8,128)(2,1)S(1)}, u32[]{:S(2)}, u32[]{:S(2)}) collective-permute-start(bf16[128,768]{1,0:T(8,128)(2,1)S(1)} %get-tuple-element.49), channel_id=1, source_target_pairs={{0,0},{1,4},{2,8},{3,12},{4,1},{5,5},{6,9},{7,13},{8,2},{9,6},{10,... | collective-permute-start | bytes 589832 | tf_op jit(solution)/shard_map/ppermute | solution.py:478
  233.6 5.3 %collective-permute-done.37 = bf16[128,768]{1,0:T(8,128)(2,1)S(1)} collective-permute-done((bf16[128,768]{1,0:T(8,128)(2,1)S(1)}, bf16[128,768]{1,0:T(8,128)(2,1)S(1)}, u32[]{:S(2)}, u32[]{:S(2)}) %collective-permute-start.37) | collective-permute-done | bytes 196640 | tf_op jit(solution)/shard_map/ppermute | solution.py:478
  238.9 3.9 %collective-permute-done.36 = bf16[128,768]{1,0:T(8,128)(2,1)S(1)} collective-permute-done((bf16[128,768]{1,0:T(8,128)(2,1)S(1)}, bf16[128,768]{1,0:T(8,128)(2,1)S(1)}, u32[]{:S(2)}, u32[]{:S(2)}) %collective-permute-start.36) | collective-permute-done | bytes 196640 | tf_op jit(solution)/shard_map/ppermute | solution.py:478
  242.7 0.7 add_convert_fusion
  (123 shorter events, 7.5 us)
Async XLA Ops:
  0.0 26.1 %copy-start = (bf16[1024,768]{1,0:T(8,128)(2,1)S(1)}, bf16[1024,768]{1,0:T(8,128)(2,1)}, u32[]{:S(2)}) copy-start(bf16[1024,768]{1,0:T(8,128)(2,1)} %param.19) | copy-start | bytes 4718596
  0.0 15.6 %copy-start.19 = (s32[4]{0:T(128)S(1)}, s32[4]{0:T(128)}, u32[]{:S(2)}) copy-start(s32[4]{0:T(128)} %param.27) | copy-start | bytes 52
  1.8 28.1 %collective-permute-start = (bf16[128,768]{1,0:T(8,128)(2,1)}, bf16[128,768]{1,0:T(8,128)(2,1)S(1)}, u32[]{:S(2)}, u32[]{:S(2)}) collective-permute-start(bf16[128,768]{1,0:T(8,128)(2,1)} %get-tuple-element.46), channel_id=1, source_target_pairs={{0,4},{4,0},{8,12},{12,8},{1,5},{5,1},{9,13},{13,9},{2,6},{6,2},{1... | collective-permute-start | bytes 589832 | tf_op jit(solution)/shard_map/ppermute | solution.py:390
  3.4 22.7 %collective-permute-start.1 = (bf16[128,768]{1,0:T(8,128)(2,1)}, bf16[128,768]{1,0:T(8,128)(2,1)S(1)}, u32[]{:S(2)}, u32[]{:S(2)}) collective-permute-start(bf16[128,768]{1,0:T(8,128)(2,1)} %get-tuple-element.46), channel_id=1, source_target_pairs={{0,8},{4,12},{8,0},{12,4},{1,9},{5,13},{9,1},{13,5},{2,10},{6,14},... | collective-permute-start | bytes 589832 | tf_op jit(solution)/shard_map/ppermute | solution.py:390
  9.9 13.0 %copy-start.21 = (s32[4,4]{1,0:T(4,128)S(1)}, s32[4,4]{1,0:T(4,128)}, u32[]{:S(2)}) copy-start(s32[4,4]{1,0:T(4,128)} %param.25) | copy-start | bytes 196
  9.9 14.4 %copy-start.18 = (s32[8]{0:T(128)S(1)}, s32[8]{0:T(128)}, u32[]{:S(2)}) copy-start(s32[8]{0:T(128)} %param.26) | copy-start | bytes 100
  9.9 45.8 %collective-permute-start.9 = (bf16[768,384]{1,0:T(8,128)(2,1)}, bf16[768,384]{1,0:T(8,128)(2,1)S(1)}, u32[]{:S(2)}, u32[]{:S(2)}) collective-permute-start(bf16[768,384]{1,0:T(8,128)(2,1)} %get-tuple-element.26), channel_id=1, source_target_pairs={{0,4},{4,0},{8,12},{12,8},{1,5},{5,1},{9,13},{13,9},{2,6},{6,2},{1... | collective-permute-start | bytes 1769480 | tf_op jit(solution)/shard_map/ppermute | solution.py:390
  10.4 45.8 %collective-permute-start.11 = (bf16[768,384]{1,0:T(8,128)(2,1)}, bf16[768,384]{1,0:T(8,128)(2,1)S(1)}, u32[]{:S(2)}, u32[]{:S(2)}) collective-permute-start(bf16[768,384]{1,0:T(8,128)(2,1)} %get-tuple-element.27), channel_id=1, source_target_pairs={{0,8},{4,12},{8,0},{12,4},{1,9},{5,13},{9,1},{13,5},{2,10},{6,14},... | collective-permute-start | bytes 1769480 | tf_op jit(solution)/shard_map/ppermute | solution.py:390
  10.7 45.6 %collective-permute-start.13 = (bf16[768,384]{1,0:T(8,128)(2,1)}, bf16[768,384]{1,0:T(8,128)(2,1)}, u32[]{:S(2)}, u32[]{:S(2)}) collective-permute-start(bf16[768,384]{1,0:T(8,128)(2,1)} %get-tuple-element.28), channel_id=1, source_target_pairs={{0,12},{4,8},{8,4},{12,0},{1,13},{5,9},{9,5},{13,1},{2,14},{6,10},... | collective-permute-start | bytes 1769480 | tf_op jit(solution)/shard_map/ppermute | solution.py:390
  16.8 6.0 %copy-start.23 = (s32[8,1]{0,1:T(1,128)S(1)}, s32[8,1]{0,1:T(1,128)}, u32[]{:S(2)}) copy-start(s32[8,1]{0,1:T(1,128)} %reshape.271) | copy-start | bytes 100
  16.8 6.0 %copy-start.22 = (s32[8]{0:T(128)S(1)}, s32[8]{0:T(128)}, u32[]{:S(2)}) copy-start(s32[8]{0:T(128)} %reshape.269) | copy-start | bytes 100
  19.2 3.7 %copy-start.24 = (s32[4]{0:T(128)S(1)}, s32[4]{0:T(128)}, u32[]{:S(2)}) copy-start(s32[4]{0:T(128)} %fusion.9) | copy-start | bytes 52
  21.2 0.8 copy-start.5
  22.0 0.8 copy-start.7
  26.1 28.9 %collective-permute-start.2 = (bf16[128,768]{1,0:T(8,128)(2,1)S(1)}, bf16[128,768]{1,0:T(8,128)(2,1)S(1)}, u32[]{:S(2)}, u32[]{:S(2)}) collective-permute-start(bf16[128,768]{1,0:T(8,128)(2,1)S(1)} %collective-permute-done.1), channel_id=1, source_target_pairs={{0,4},{4,0},{8,12},{12,8},{1,5},{5,1},{9,13},{13,9},{2,6},{6,2},{1... | collective-permute-start | bytes 589832 | tf_op jit(solution)/shard_map/ppermute | solution.py:390
  28.0 27.7 %copy-start.1 = (bf16[16,128,768]{2,1,0:T(8,128)(2,1)S(1)}, bf16[16,128,768]{2,1,0:T(8,128)(2,1)}, u32[]{:S(2)}) copy-start(bf16[16,128,768]{2,1,0:T(8,128)(2,1)} %get-tuple-element.45) | copy-start | bytes 9437188
  29.9 76.5 %copy-start.12 = (bf16[512,512]{1,0:T(8,128)(2,1)}, bf16[512,512]{1,0:T(8,128)(2,1)S(1)}, u32[]{:S(2)}) copy-start(bf16[512,512]{1,0:T(8,128)(2,1)S(1)} %get-tuple-element.32.refs_0_.refs_16_) | copy-start | bytes 1572868
  31.1 24.5 %collective-permute-start.5 = (bf16[2,128,768]{2,1,0:T(8,128)(2,1)S(1)}, bf16[2,128,768]{2,1,0:T(8,128)(2,1)S(1)}, u32[]{:S(2)}, u32[]{:S(2)}) collective-permute-start(bf16[2,128,768]{2,1,0:T(8,128)(2,1)S(1)} %pad_maximum_fusion), channel_id=1, source_target_pairs={{0,2},{2,0},{1,3},{3,1},{4,6},{6,4},{5,7},{7,5},{8,10},{10,8},{9,1... | collective-permute-start | bytes 1179656 | tf_op jit(solution)/shard_map/ppermute | solution.py:420
  55.1 43.5 %copy-start.6 = (bf16[768,384]{1,0:T(8,128)(2,1)S(1)}, bf16[768,384]{1,0:T(8,128)(2,1)}, u32[]{:S(2)}) copy-start(bf16[768,384]{1,0:T(8,128)(2,1)} %copy-done.5) | copy-start | bytes 1769476
  55.1 43.5 %copy-start.8 = (bf16[768,384]{1,0:T(8,128)(2,1)S(1)}, bf16[768,384]{1,0:T(8,128)(2,1)}, u32[]{:S(2)}) copy-start(bf16[768,384]{1,0:T(8,128)(2,1)} %copy-done.7) | copy-start | bytes 1769476
  55.1 43.5 %copy-start.16 = (f32[128]{0:T(128)S(1)}, f32[128]{0:T(128)}, u32[]{:S(2)}) copy-start(f32[128]{0:T(128)} %param.20) | copy-start | bytes 1540
  55.1 43.5 %copy-start.17 = (f32[128]{0:T(128)S(1)}, f32[128]{0:T(128)}, u32[]{:S(2)}) copy-start(f32[128]{0:T(128)} %param.21) | copy-start | bytes 1540
  55.1 10.1 %collective-permute-start.6 = (bf16[2,128,768]{2,1,0:T(8,128)(2,1)S(1)}, bf16[2,128,768]{2,1,0:T(8,128)(2,1)S(1)}, u32[]{:S(2)}, u32[]{:S(2)}) collective-permute-start(bf16[2,128,768]{2,1,0:T(8,128)(2,1)S(1)} %pad_maximum_fusion.1), channel_id=1, source_target_pairs={{0,2},{2,0},{1,3},{3,1},{4,6},{6,4},{5,7},{7,5},{8,10},{10,8},{9,1... | collective-permute-start | bytes 1179656 | tf_op jit(solution)/shard_map/ppermute | solution.py:422
  55.7 9.6 %collective-permute-start.3 = (bf16[2,128,768]{2,1,0:T(8,128)(2,1)S(1)}, bf16[2,128,768]{2,1,0:T(8,128)(2,1)S(1)}, u32[]{:S(2)}, u32[]{:S(2)}) collective-permute-start(bf16[2,128,768]{2,1,0:T(8,128)(2,1)S(1)} %pad_maximum_fusion), channel_id=1, source_target_pairs={{0,1},{1,0},{2,3},{3,2},{4,5},{5,4},{6,7},{7,6},{8,9},{9,8},{10,11... | collective-permute-start | bytes 1179656 | tf_op jit(solution)/shard_map/ppermute | solution.py:424
  55.7 47.9 %copy-start.3 = (bf16[768,384]{1,0:T(8,128)(2,1)}, bf16[768,384]{1,0:T(8,128)(2,1)S(1)}, u32[]{:S(2)}) copy-start(bf16[768,384]{1,0:T(8,128)(2,1)S(1)} %collective-permute-done.9.refs_2_.refs_10_) | copy-start | bytes 1769476
  55.8 12.4 %collective-permute-start.4 = (bf16[2,128,768]{2,1,0:T(8,128)(2,1)S(1)}, bf16[2,128,768]{2,1,0:T(8,128)(2,1)S(1)}, u32[]{:S(2)}, u32[]{:S(2)}) collective-permute-start(bf16[2,128,768]{2,1,0:T(8,128)(2,1)S(1)} %pad_maximum_fusion.1), channel_id=1, source_target_pairs={{0,1},{1,0},{2,3},{3,2},{4,5},{5,4},{6,7},{7,6},{8,9},{9,8},{10,11... | collective-permute-start | bytes 1179656 | tf_op jit(solution)/shard_map/ppermute | solution.py:424
  56.2 47.5 %copy-start.4 = (bf16[768,384]{1,0:T(8,128)(2,1)}, bf16[768,384]{1,0:T(8,128)(2,1)S(1)}, u32[]{:S(2)}) copy-start(bf16[768,384]{1,0:T(8,128)(2,1)S(1)} %collective-permute-done.11.refs_4_.refs_12_) | copy-start | bytes 1769476
  56.2 13.3 %collective-permute-start.7 = (bf16[2,128,768]{2,1,0:T(8,128)(2,1)S(1)}, bf16[2,128,768]{2,1,0:T(8,128)(2,1)S(1)}, u32[]{:S(2)}, u32[]{:S(2)}) collective-permute-start(bf16[2,128,768]{2,1,0:T(8,128)(2,1)S(1)} %collective-permute-done.5), channel_id=1, source_target_pairs={{0,1},{1,0},{2,3},{3,2},{4,5},{5,4},{6,7},{7,6},{8,9},{9,8},{10,11... | collective-permute-start | bytes 1179656 | tf_op jit(solution)/shard_map/ppermute | solution.py:424
  56.3 15.7 %collective-permute-start.10 = (bf16[768,384]{1,0:T(8,128)(2,1)S(1)}, bf16[768,384]{1,0:T(8,128)(2,1)S(1)}, u32[]{:S(2)}, u32[]{:S(2)}) collective-permute-start(bf16[768,384]{1,0:T(8,128)(2,1)S(1)} %collective-permute-done.9.refs_2_.refs_10_), channel_id=1, source_target_pairs={{0,16},{16,0},{1,17},{17,1},{2,18},{18,2},{3,19},{19,3},{4,20},{20... | collective-permute-start | bytes 1769480 | tf_op jit(solution)/shard_map/ppermute | solution.py:439
  65.2 5.5 %collective-permute-start.8 = (bf16[2,128,768]{2,1,0:T(8,128)(2,1)S(1)}, bf16[2,128,768]{2,1,0:T(8,128)(2,1)S(1)}, u32[]{:S(2)}, u32[]{:S(2)}) collective-permute-start(bf16[2,128,768]{2,1,0:T(8,128)(2,1)S(1)} %collective-permute-done.6), channel_id=1, source_target_pairs={{0,1},{1,0},{2,3},{3,2},{4,5},{5,4},{6,7},{7,6},{8,9},{9,8},{10,11... | collective-permute-start | bytes 1179656 | tf_op jit(solution)/shard_map/ppermute | solution.py:424
  65.3 38.5 %collective-permute-start.15 = (bf16[512,512]{1,0:T(8,128)(2,1)S(1)}, bf16[512,512]{1,0:T(8,128)(2,1)S(1)}, u32[]{:S(2)}, u32[]{:S(2)}) collective-permute-start(bf16[512,512]{1,0:T(8,128)(2,1)S(1)} %get-tuple-element.34), channel_id=1, source_target_pairs={{0,4},{4,0},{8,12},{12,8},{1,5},{5,1},{9,13},{13,9},{2,6},{6,2},{1... | collective-permute-start | bytes 1572872 | tf_op jit(solution)/shard_map/ppermute | solution.py:390
  68.2 38.2 %collective-permute-start.16 = (bf16[512,512]{1,0:T(8,128)(2,1)S(1)}, bf16[512,512]{1,0:T(8,128)(2,1)S(1)}, u32[]{:S(2)}, u32[]{:S(2)}) collective-permute-start(bf16[512,512]{1,0:T(8,128)(2,1)S(1)} %get-tuple-element.36), channel_id=1, source_target_pairs={{0,8},{4,12},{8,0},{12,4},{1,9},{5,13},{9,1},{13,5},{2,10},{6,14},... | collective-permute-start | bytes 1572872 | tf_op jit(solution)/shard_map/ppermute | solution.py:390
  69.6 36.8 %collective-permute-start.17 = (bf16[512,512]{1,0:T(8,128)(2,1)S(1)}, bf16[512,512]{1,0:T(8,128)(2,1)S(1)}, u32[]{:S(2)}, u32[]{:S(2)}) collective-permute-start(bf16[512,512]{1,0:T(8,128)(2,1)S(1)} %get-tuple-element.38), channel_id=1, source_target_pairs={{0,12},{4,8},{8,4},{12,0},{1,13},{5,9},{9,5},{13,1},{2,14},{6,10},... | collective-permute-start | bytes 1572872 | tf_op jit(solution)/shard_map/ppermute | solution.py:390
  70.8 16.2 %collective-permute-start.12 = (bf16[768,384]{1,0:T(8,128)(2,1)S(1)}, bf16[768,384]{1,0:T(8,128)(2,1)S(1)}, u32[]{:S(2)}, u32[]{:S(2)}) collective-permute-start(bf16[768,384]{1,0:T(8,128)(2,1)S(1)} %collective-permute-done.11.refs_4_.refs_12_), channel_id=1, source_target_pairs={{0,16},{16,0},{1,17},{17,1},{2,18},{18,2},{3,19},{19,3},{4,20},{20... | collective-permute-start | bytes 1769480 | tf_op jit(solution)/shard_map/ppermute | solution.py:439
  72.0 31.7 %copy-start.9 = (bf16[768,384]{1,0:T(8,128)(2,1)}, bf16[768,384]{1,0:T(8,128)(2,1)S(1)}, u32[]{:S(2)}) copy-start(bf16[768,384]{1,0:T(8,128)(2,1)S(1)} %collective-permute-done.10.refs_3_.refs_11_) | copy-start | bytes 1769476
  72.0 26.6 %collective-permute-start.14 = (bf16[768,384]{1,0:T(8,128)(2,1)}, bf16[768,384]{1,0:T(8,128)(2,1)S(1)}, u32[]{:S(2)}, u32[]{:S(2)}) collective-permute-start(bf16[768,384]{1,0:T(8,128)(2,1)} %collective-permute-done.13.refs_6_.refs_14_), channel_id=1, source_target_pairs={{0,16},{16,0},{1,17},{17,1},{2,18},{18,2},{3,19},{19,3},{4,20},{20... | collective-permute-start | bytes 1769480 | tf_op jit(solution)/shard_map/ppermute | solution.py:439
  73.9 29.9 %copy-start.2 = (bf16[16,128,768]{2,1,0:T(8,128)(2,1)}, bf16[16,128,768]{2,1,0:T(8,128)(2,1)S(1)}, u32[]{:S(2)}) copy-start(bf16[16,128,768]{2,1,0:T(8,128)(2,1)S(1)} %constant_dynamic-update-slice_fusion.gathered_ref) | copy-start | bytes 9437188
  87.0 16.8 %copy-start.10 = (bf16[768,384]{1,0:T(8,128)(2,1)}, bf16[768,384]{1,0:T(8,128)(2,1)S(1)}, u32[]{:S(2)}) copy-start(bf16[768,384]{1,0:T(8,128)(2,1)S(1)} %collective-permute-done.12.refs_5_.refs_13_) | copy-start | bytes 1769476
  98.6 5.2 %copy-start.11 = (bf16[768,384]{1,0:T(8,128)(2,1)}, bf16[768,384]{1,0:T(8,128)(2,1)S(1)}, u32[]{:S(2)}) copy-start(bf16[768,384]{1,0:T(8,128)(2,1)S(1)} %collective-permute-done.14.refs_7_.refs_15_) | copy-start | bytes 1769476
  103.8 20.2 %copy-start.20 = (bf16[8,128,768]{2,1,0:T(8,128)(2,1)S(1)}, bf16[8,128,768]{2,1,0:T(8,128)(2,1)}, u32[]{:S(2)}) copy-start(bf16[8,128,768]{2,1,0:T(8,128)(2,1)} %gather_fusion) | copy-start | bytes 4718596
  103.8 18.7 %copy-start.13 = (bf16[512,512]{1,0:T(8,128)(2,1)}, bf16[512,512]{1,0:T(8,128)(2,1)S(1)}, u32[]{:S(2)}) copy-start(bf16[512,512]{1,0:T(8,128)(2,1)S(1)} %collective-permute-done.15.refs_1_.refs_17_) | copy-start | bytes 1572868
  106.4 16.1 %copy-start.14 = (bf16[512,512]{1,0:T(8,128)(2,1)}, bf16[512,512]{1,0:T(8,128)(2,1)S(1)}, u32[]{:S(2)}) copy-start(bf16[512,512]{1,0:T(8,128)(2,1)S(1)} %collective-permute-done.16.refs_2_.refs_18_) | copy-start | bytes 1572868
  106.4 16.1 %copy-start.15 = (bf16[512,512]{1,0:T(8,128)(2,1)}, bf16[512,512]{1,0:T(8,128)(2,1)S(1)}, u32[]{:S(2)}) copy-start(bf16[512,512]{1,0:T(8,128)(2,1)S(1)} %collective-permute-done.17.refs_3_.refs_19_) | copy-start | bytes 1572868
  110.3 21.6 %collective-permute-start.18 = (bf16[512,256]{1,0:T(8,128)(2,1)S(1)}, bf16[512,256]{1,0:T(8,128)(2,1)S(1)}, u32[]{:S(2)}, u32[]{:S(2)}) collective-permute-start(bf16[512,256]{1,0:T(8,128)(2,1)S(1)} %shard_map.140.refs_0_), channel_id=1, source_target_pairs={{0,4},{4,0},{8,12},{12,8},{1,5},{5,1},{9,13},{13,9},{2,6},{6,2},{1... | collective-permute-start | bytes 786440 | tf_op jit(solution)/shard_map/ppermute | solution.py:390
  121.4 21.4 %collective-permute-start.19 = (bf16[512,256]{1,0:T(8,128)(2,1)S(1)}, bf16[512,256]{1,0:T(8,128)(2,1)S(1)}, u32[]{:S(2)}, u32[]{:S(2)}) collective-permute-start(bf16[512,256]{1,0:T(8,128)(2,1)S(1)} %shard_map.140.refs_0_), channel_id=1, source_target_pairs={{0,8},{4,12},{8,0},{12,4},{1,9},{5,13},{9,1},{13,5},{2,10},{6,14},... | collective-permute-start | bytes 786440 | tf_op jit(solution)/shard_map/ppermute | solution.py:390
  122.5 20.3 %collective-permute-start.20 = (bf16[512,256]{1,0:T(8,128)(2,1)S(1)}, bf16[512,256]{1,0:T(8,128)(2,1)S(1)}, u32[]{:S(2)}, u32[]{:S(2)}) collective-permute-start(bf16[512,256]{1,0:T(8,128)(2,1)S(1)} %shard_map.140.refs_0_), channel_id=1, source_target_pairs={{0,12},{4,8},{8,4},{12,0},{1,13},{5,9},{9,5},{13,1},{2,14},{6,10},... | collective-permute-start | bytes 786440 | tf_op jit(solution)/shard_map/ppermute | solution.py:390
  143.8 1.8 collective-permute-start.21
  147.6 7.0 %collective-permute-start.22 = (bf16[128,768]{1,0:T(8,128)(2,1)S(1)}, bf16[128,768]{1,0:T(8,128)(2,1)S(1)}, u32[]{:S(2)}, u32[]{:S(2)}) collective-permute-start(bf16[128,768]{1,0:T(8,128)(2,1)S(1)} %slice.58), channel_id=1, source_target_pairs={{0,2},{2,0},{1,3},{3,1},{4,6},{6,4},{5,7},{7,5},{8,10},{10,8},{9,1... | collective-permute-start | bytes 589832 | tf_op jit(solution)/shard_map/ppermute | solution.py:470
  155.7 14.1 %collective-permute-start.24 = (bf16[128,768]{1,0:T(8,128)(2,1)S(1)}, bf16[128,768]{1,0:T(8,128)(2,1)S(1)}, u32[]{:S(2)}, u32[]{:S(2)}) collective-permute-start(bf16[128,768]{1,0:T(8,128)(2,1)S(1)} %fusion.5), channel_id=1, source_target_pairs={{0,8},{4,12},{8,0},{12,4},{1,9},{5,13},{9,1},{13,5},{2,10},{6,14},... | collective-permute-start | bytes 589832 | tf_op jit(solution)/shard_map/ppermute | solution.py:390
  161.1 8.9 %collective-permute-start.23 = (bf16[128,768]{1,0:T(8,128)(2,1)S(1)}, bf16[128,768]{1,0:T(8,128)(2,1)S(1)}, u32[]{:S(2)}, u32[]{:S(2)}) collective-permute-start(bf16[128,768]{1,0:T(8,128)(2,1)S(1)} %fusion.5), channel_id=1, source_target_pairs={{0,4},{4,0},{8,12},{12,8},{1,5},{5,1},{9,13},{13,9},{2,6},{6,2},{1... | collective-permute-start | bytes 589832 | tf_op jit(solution)/shard_map/ppermute | solution.py:390
  169.8 5.7 %collective-permute-start.25 = (bf16[128,768]{1,0:T(8,128)(2,1)S(1)}, bf16[128,768]{1,0:T(8,128)(2,1)S(1)}, u32[]{:S(2)}, u32[]{:S(2)}) collective-permute-start(bf16[128,768]{1,0:T(8,128)(2,1)S(1)} %collective-permute-done.24), channel_id=1, source_target_pairs={{0,4},{4,0},{8,12},{12,8},{1,5},{5,1},{9,13},{13,9},{2,6},{6,2},{1... | collective-permute-start | bytes 589832 | tf_op jit(solution)/shard_map/ppermute | solution.py:390
  170.0 12.1 %collective-permute-start.28 = (bf16[2,128,768]{2,1,0:T(8,128)(2,1)S(1)}, bf16[2,128,768]{2,1,0:T(8,128)(2,1)S(1)}, u32[]{:S(2)}, u32[]{:S(2)}) collective-permute-start(bf16[2,128,768]{2,1,0:T(8,128)(2,1)S(1)} %pad_maximum_fusion.2.refs_0_), channel_id=1, source_target_pairs={{0,2},{2,0},{1,3},{3,1},{4,6},{6,4},{5,7},{7,5},{8,10},{10,8},{9,1... | collective-permute-start | bytes 1179656 | tf_op jit(solution)/shard_map/ppermute | solution.py:420
  175.5 12.6 %collective-permute-start.29 = (bf16[2,128,768]{2,1,0:T(8,128)(2,1)S(1)}, bf16[2,128,768]{2,1,0:T(8,128)(2,1)S(1)}, u32[]{:S(2)}, u32[]{:S(2)}) collective-permute-start(bf16[2,128,768]{2,1,0:T(8,128)(2,1)S(1)} %pad_maximum_fusion.3.refs_1_), channel_id=1, source_target_pairs={{0,2},{2,0},{1,3},{3,1},{4,6},{6,4},{5,7},{7,5},{8,10},{10,8},{9,1... | collective-permute-start | bytes 1179656 | tf_op jit(solution)/shard_map/ppermute | solution.py:422
  176.1 12.0 %collective-permute-start.26 = (bf16[2,128,768]{2,1,0:T(8,128)(2,1)S(1)}, bf16[2,128,768]{2,1,0:T(8,128)(2,1)S(1)}, u32[]{:S(2)}, u32[]{:S(2)}) collective-permute-start(bf16[2,128,768]{2,1,0:T(8,128)(2,1)S(1)} %pad_maximum_fusion.2.refs_0_), channel_id=1, source_target_pairs={{0,1},{1,0},{2,3},{3,2},{4,5},{5,4},{6,7},{7,6},{8,9},{9,8},{10,11... | collective-permute-start | bytes 1179656 | tf_op jit(solution)/shard_map/ppermute | solution.py:424
  176.1 12.0 %collective-permute-start.27 = (bf16[2,128,768]{2,1,0:T(8,128)(2,1)S(1)}, bf16[2,128,768]{2,1,0:T(8,128)(2,1)S(1)}, u32[]{:S(2)}, u32[]{:S(2)}) collective-permute-start(bf16[2,128,768]{2,1,0:T(8,128)(2,1)S(1)} %pad_maximum_fusion.3.refs_1_), channel_id=1, source_target_pairs={{0,1},{1,0},{2,3},{3,2},{4,5},{5,4},{6,7},{7,6},{8,9},{9,8},{10,11... | collective-permute-start | bytes 1179656 | tf_op jit(solution)/shard_map/ppermute | solution.py:424
  182.1 6.0 %collective-permute-start.30 = (bf16[2,128,768]{2,1,0:T(8,128)(2,1)S(1)}, bf16[2,128,768]{2,1,0:T(8,128)(2,1)S(1)}, u32[]{:S(2)}, u32[]{:S(2)}) collective-permute-start(bf16[2,128,768]{2,1,0:T(8,128)(2,1)S(1)} %collective-permute-done.28.refs_4_), channel_id=1, source_target_pairs={{0,1},{1,0},{2,3},{3,2},{4,5},{5,4},{6,7},{7,6},{8,9},{9,8},{10,11... | collective-permute-start | bytes 1179656 | tf_op jit(solution)/shard_map/ppermute | solution.py:424
  188.1 1.7 collective-permute-start.31
  199.6 12.4 %collective-permute-start.32 = (bf16[512,256]{1,0:T(8,128)(2,1)S(1)}, bf16[512,256]{1,0:T(8,128)(2,1)S(1)}, u32[]{:S(2)}, u32[]{:S(2)}) collective-permute-start(bf16[512,256]{1,0:T(8,128)(2,1)S(1)} %shard_map.142.refs_0_), channel_id=1, source_target_pairs={{0,4},{4,0},{8,12},{12,8},{1,5},{5,1},{9,13},{13,9},{2,6},{6,2},{1... | collective-permute-start | bytes 786440 | tf_op jit(solution)/shard_map/ppermute | solution.py:390
  201.4 21.3 %collective-permute-start.33 = (bf16[512,256]{1,0:T(8,128)(2,1)S(1)}, bf16[512,256]{1,0:T(8,128)(2,1)S(1)}, u32[]{:S(2)}, u32[]{:S(2)}) collective-permute-start(bf16[512,256]{1,0:T(8,128)(2,1)S(1)} %shard_map.142.refs_0_), channel_id=1, source_target_pairs={{0,8},{4,12},{8,0},{12,4},{1,9},{5,13},{9,1},{13,5},{2,10},{6,14},... | collective-permute-start | bytes 786440 | tf_op jit(solution)/shard_map/ppermute | solution.py:390
  201.4 21.3 %collective-permute-start.34 = (bf16[512,256]{1,0:T(8,128)(2,1)S(1)}, bf16[512,256]{1,0:T(8,128)(2,1)S(1)}, u32[]{:S(2)}, u32[]{:S(2)}) collective-permute-start(bf16[512,256]{1,0:T(8,128)(2,1)S(1)} %shard_map.142.refs_0_), channel_id=1, source_target_pairs={{0,12},{4,8},{8,4},{12,0},{1,13},{5,9},{9,5},{13,1},{2,14},{6,10},... | collective-permute-start | bytes 786440 | tf_op jit(solution)/shard_map/ppermute | solution.py:390
  223.7 1.8 collective-permute-start.35
  225.6 13.3 %collective-permute-start.37 = (bf16[128,768]{1,0:T(8,128)(2,1)S(1)}, bf16[128,768]{1,0:T(8,128)(2,1)S(1)}, u32[]{:S(2)}, u32[]{:S(2)}) collective-permute-start(bf16[128,768]{1,0:T(8,128)(2,1)S(1)} %get-tuple-element.50), channel_id=1, source_target_pairs={{0,8},{1,12},{2,0},{3,4},{4,9},{5,13},{6,1},{7,5},{8,10},{9,14},{1... | collective-permute-start | bytes 589832 | tf_op jit(solution)/shard_map/ppermute | solution.py:478
  226.2 16.5 %collective-permute-start.36 = (bf16[128,768]{1,0:T(8,128)(2,1)S(1)}, bf16[128,768]{1,0:T(8,128)(2,1)S(1)}, u32[]{:S(2)}, u32[]{:S(2)}) collective-permute-start(bf16[128,768]{1,0:T(8,128)(2,1)S(1)} %get-tuple-element.49), channel_id=1, source_target_pairs={{0,0},{1,4},{2,8},{3,12},{4,1},{5,5},{6,9},{7,13},{8,2},{9,6},{10,... | collective-permute-start | bytes 589832 | tf_op jit(solution)/shard_map/ppermute | solution.py:478

commit v4 on v3

--- a/solution.py
+++ b/solution.py
@@ -214,20 +214,20 @@
     )(*map(in_hbm, (keys, values)))
 
 
-def project_rows(part, panel, query_gain_ref, key_gain_ref, outs):
+def project_rows(tiles, part, panel, query_gain_ref, key_gain_ref, outs):
     q_ref, k_ref, v_ref = outs
     head_dim = query_gain_ref.shape[1]
     totals = [None, None]
-    squares = [0.0] * WAYS
+    squares = [0.0] * tiles
     columns = 0
     for k in range(WAYS):
-        blocks = [part(r, k) for r in range(WAYS)]
+        blocks = [part(r, k) for r in range(tiles)]
         rows = jnp.concatenate(blocks, axis=0)
         columns += rows.shape[1]
         for h in range(2):
             product = jnp.dot(rows, panel(k, h), preferred_element_type=jnp.float32)
             totals[h] = product if k == 0 else totals[h] + product
-        for r in range(WAYS):
+        for r in range(tiles):
             wide = blocks[r].astype(jnp.float32)
             squares[r] += jnp.sum(wide * wide, axis=-1, keepdims=True)
     scale = lax.rsqrt(jnp.concatenate(squares, axis=0) / columns + epsilon)
@@ -241,13 +241,14 @@
         v_ref[:, lanes] = total[:, 2 * head_dim :].astype(jnp.bfloat16)
 
 
-def attend_rows(pos_ref, q_ref, k_ref, v_ref, held, mixed_ref):
+def attend_rows(pair, start, pos_ref, q_ref, k_ref, v_ref, held, mixed_ref):
     head_dim = q_ref.shape[1] // 2
-    tile = q_ref.shape[0] // WAYS
+    tile = mixed_ref.shape[0] // 2
     across = (((1,), (1,)), ((), ()))
     for h in range(2):
-        for r in range(WAYS):
-            rows = slice(r * tile, (r + 1) * tile)
+        for r in range(2 * pair, 2 * pair + 2):
+            at = (r - 2 * pair) * tile
+            rows = slice(start + at, start + at + tile)
             lanes = slice(h * head_dim, (h + 1) * head_dim)
             value_lanes = slice((2 + h) * head_dim, (3 + h) * head_dim)
             query = q_ref[rows, lanes]
@@ -266,7 +267,7 @@
                 summed += jnp.dot(
                     weights.astype(jnp.bfloat16), value, preferred_element_type=jnp.float32
                 )
-            mixed_ref[rows, lanes] = (summed / total).astype(jnp.bfloat16)
+            mixed_ref[at : at + tile, lanes] = (summed / total).astype(jnp.bfloat16)
 
 
 def project_kernel(source_ref, query_gain_ref, key_gain_ref, gathered_ref, *refs):
@@ -278,16 +279,17 @@
     def panel(k, h):
         return panels[2 * k + h][...]
 
-    project_rows(part, panel, query_gain_ref, key_gain_ref, outs)
-
-
-def attend_kernel(pos_ref, q_ref, k_ref, v_ref, *refs):
-    attend_rows(pos_ref, q_ref, k_ref, v_ref, refs[:WAYS], refs[WAYS])
-
-
-def both_kernel(pos_ref, query_gain_ref, key_gain_ref, *refs):
-    pairs, panels, caches = refs[: 2 * WAYS], refs[2 * WAYS : 4 * WAYS], refs[4 * WAYS : 5 * WAYS]
-    mixed_ref, panel_ref, held_ref, *outs, panel_sems, held_sems = refs[5 * WAYS :]
+    project_rows(WAYS, part, panel, query_gain_ref, key_gain_ref, outs)
+
+
+def attend_kernel(pair, pos_ref, q_ref, k_ref, v_ref, *refs):
+    start = pair * refs[WAYS].shape[0]
+    attend_rows(pair, start, pos_ref, q_ref, k_ref, v_ref, refs[:WAYS], refs[WAYS])
+
+
+def both_kernel(pair, pos_ref, query_gain_ref, key_gain_ref, *refs):
+    parts, panels, caches = refs[:WAYS], refs[WAYS : 3 * WAYS], refs[3 * WAYS : 4 * WAYS]
+    mixed_ref, panel_ref, held_ref, *outs, panel_sems, held_sems = refs[4 * WAYS :]
     copies = [
         pltpu.make_async_copy(source, panel_ref.at[i], panel_sems.at[i])
         for i, source in enumerate(panels)
@@ -300,42 +302,45 @@
         copy.start()
 
     def part(j, k):
-        return pairs[2 * j + k // 2][k % 2]
+        return parts[2 * j + k // 2][k % 2]
 
     def panel(k, h):
         copies[2 * k + h].wait()
         return panel_ref[2 * k + h]
 
-    project_rows(part, panel, query_gain_ref, key_gain_ref, outs)
+    project_rows(2, part, panel, query_gain_ref, key_gain_ref, outs)
     for copy in late:
         copy.wait()
-    attend_rows(pos_ref, *outs, [held_ref.at[k] for k in range(WAYS)], mixed_ref)
-
-
-def mix_first(source, pos, gains, gathered, panels, held):
+    attend_rows(pair, 0, pos_ref, *outs, [held_ref.at[k] for k in range(WAYS)], mixed_ref)
+
+
+def project(source, gains, gathered, panels):
     tile, head_dim = gathered.shape[1], gains[0].shape[1]
-    shape = jax.ShapeDtypeStruct((WAYS * tile, 2 * head_dim), jnp.bfloat16)
-    qkv = pl.pallas_call(
+    return pl.pallas_call(
         project_kernel,
-        out_shape=[shape] * 3,
+        out_shape=[jax.ShapeDtypeStruct((WAYS * tile, 2 * head_dim), jnp.bfloat16)] * 3,
         in_specs=[pl.BlockSpec(memory_space=pltpu.SMEM)] + whole_specs(3 + len(panels)),
         out_specs=whole_specs(3),
         compiler_params=pltpu.CompilerParams(vmem_limit_bytes=14 * MIB),
     )(source, *gains, gathered, *panels)
+
+
+def attend_pair(pair, pos, qkv, held):
+    rows, columns = qkv[0].shape
     return pl.pallas_call(
-        attend_kernel,
-        out_shape=shape,
+        functools.partial(attend_kernel, pair),
+        out_shape=jax.ShapeDtypeStruct((rows // 2, columns), jnp.bfloat16),
         in_specs=[pl.BlockSpec(memory_space=pltpu.SMEM)] + whole_specs(3 + len(held)),
         out_specs=whole_specs(1)[0],
         compiler_params=pltpu.CompilerParams(vmem_limit_bytes=10 * MIB),
     )(pos, *qkv, *held)
 
 
-def mix_again(pos, gains, parts, panels, held):
+def mix_pair(pair, pos, gains, parts, panels, held):
     tile, head_dim = parts[0].shape[1], gains[0].shape[1]
-    shape = (WAYS * tile, 2 * head_dim)
+    shape = (2 * tile, 2 * head_dim)
     return pl.pallas_call(
-        both_kernel,
+        functools.partial(both_kernel, pair),
         out_shape=jax.ShapeDtypeStruct(shape, jnp.bfloat16),
         in_specs=[pl.BlockSpec(memory_space=pltpu.SMEM)]
         + whole_specs(2 + len(parts))
@@ -348,38 +353,30 @@
             pltpu.SemaphoreType.DMA((len(panels),)),
             pltpu.SemaphoreType.DMA((len(held),)),
         ],
-        compiler_params=pltpu.CompilerParams(vmem_limit_bytes=20 * MIB),
+        compiler_params=pltpu.CompilerParams(vmem_limit_bytes=16 * MIB),
     )(pos, *gains, *parts, *map(in_hbm, panels), *map(in_hbm, held))
 
 
 def out_kernel(w_ref, *refs):
     mixed, (keep_ref, send_ref) = refs[:WAYS], refs[WAYS:]
-    depth = mixed[0].shape[1]
-    tile = mixed[0].shape[0] // WAYS
-    for r in range(WAYS):
-        row = jnp.concatenate(
-            [mixed[k][r * tile : (r + 1) * tile, :] for k in range(WAYS)], axis=1
-        )
-        update = jnp.dot(row, w_ref[...], preferred_element_type=jnp.float32)
-        rows = slice((r // 2) * tile, (r // 2 + 1) * tile)
-        if r % 2 == 0:
-            keep_ref[rows, :] = update
-        else:
-            send_ref[rows, :] = update.astype(jnp.bfloat16)
+    tile = keep_ref.shape[0]
+    rows = jnp.concatenate([part[...] for part in mixed], axis=1)
+    update = jnp.dot(rows, w_ref[...], preferred_element_type=jnp.float32)
+    keep_ref[...] = update[:tile]
+    send_ref[...] = update[tile:].astype(jnp.bfloat16)
 
 
 def project_out(w_rows, mixed):
-    tile = mixed[0].shape[0] // WAYS
-    width = w_rows.shape[1]
+    shape = (mixed[0].shape[0] // 2, w_rows.shape[1])
     return pl.pallas_call(
         out_kernel,
         out_shape=[
-            jax.ShapeDtypeStruct((2 * tile, width), jnp.float32),
-            jax.ShapeDtypeStruct((2 * tile, width), jnp.bfloat16),
+            jax.ShapeDtypeStruct(shape, jnp.float32),
+            jax.ShapeDtypeStruct(shape, jnp.bfloat16),
         ],
         in_specs=whole_specs(1 + WAYS),
         out_specs=whole_specs(2),
-        compiler_params=pltpu.CompilerParams(vmem_limit_bytes=10 * MIB),
+        compiler_params=pltpu.CompilerParams(vmem_limit_bytes=6 * MIB),
     )(w_rows, *mixed)
 
 
@@ -457,31 +454,31 @@
     from_k = slots[:, :, None] // held_blocks == (z ^ ways)[None, None, :]
     pos = jnp.sum(jnp.where(from_k, (slots % held_blocks)[:, :, None], 0), axis=1).reshape(-1)
 
-    for step in range(ITERS):
-        if step == 0:
-            own = mix_first(source, pos, gains, gathered, panels, held)
-        else:
-            own = mix_again(pos, gains, parts, panels, held)
-        mixed = [own] + [from_z(own, k) for k in range(1, WAYS)]
+    def gather_z(own):
+        near, far = lax.optimization_barrier((from_z(own, 1), from_z(own, 2)))
+        return [own, near, far, from_z(far, 1)]
+
+    def summed(own):
+        mixed = gather_z(own)
         keep, send = project_out(w_rows, mixed)
-        half = keep + lax.ppermute(send, "head", SWAP).astype(jnp.float32)
-        base, other = x_share.astype(jnp.float32), half[tile:]
-        if step + 1 < ITERS:
-            other = lax.ppermute(other.astype(jnp.bfloat16), "fsdp", SWAP)
-            update = half[:tile] + other.astype(jnp.float32)
-            x_share = (base + gates[step] * update).astype(jnp.bfloat16)
-            far = from_z(x_share, 2)
-            parts = gather_pairs([x_share, from_z(x_share, 1), far, from_z(far, 1)])
-    base = (base + gates[step] * half[:tile]).astype(jnp.bfloat16)
-    other = (gates[step] * other).astype(jnp.bfloat16)
-    ends = [
-        lax.ppermute(
-            value,
-            ("cache", "fsdp", "head"),
-            [(a * WAYS + b, (b ^ flip) * WAYS + a) for a in range(WAYS) for b in range(WAYS)],
-        )
-        for value, flip in ((base, 0), (other, 2))
-    ]
+        return keep + lax.ppermute(send, "head", SWAP).astype(jnp.float32)
+
+    qkv = project(source, gains, gathered, panels)
+    own = attend_pair(1, pos, qkv, held)
+    other = lax.ppermute(summed(own).astype(jnp.bfloat16), "fsdp", SWAP)
+    pos_late, _ = lax.optimization_barrier((pos, own))
+    update = summed(attend_pair(0, pos_late, qkv, held)) + other.astype(jnp.float32)
+    x_share = (x_share.astype(jnp.float32) + gates[0] * update).astype(jnp.bfloat16)
+
+    parts = gather_pairs(gather_z(x_share))
+    ends = []
+    for pair in range(2):
+        own = mix_pair(pair, pos, gains, parts[4 * pair : 4 * pair + 4], panels, held)
+        value = gates[1] * summed(own)
+        if pair == 0:
+            value += x_share.astype(jnp.float32)
+        moves = [(a * WAYS + b, (b ^ (2 * pair)) * WAYS + a) for a in range(WAYS) for b in range(WAYS)]
+        ends.append(lax.ppermute(value.astype(jnp.bfloat16), ("cache", "fsdp", "head"), moves))
     return (ends[0].astype(jnp.float32) + ends[1].astype(jnp.float32)).astype(jnp.bfloat16)
 
 
@@ -511,6 +508,7 @@
             sizes == {"groups": 2, "cache": WAYS, "fsdp": 2, "head": 2}
             and panel_width == 2 * WAYS * head_dim
             and args[11].shape[1] == WAYS
+            and ITERS == 2
         )
         plan = split_heads if fits else gathered_panels
         return jax.shard_map(

time: 244 us -> 232 us (0.951)
  waiting for transfers between devices: 141 us -> 124 us
  Pallas kernels: 27.5 us -> 32.1 us
  other arithmetic: 8.63 us -> 5.87 us
  starting transfers between devices: 53.7 us -> 56.4 us
    ppermute x18 -> x24, waiting for transfers between devices: 76.9 us -> 63.1 us  [from_z(): return lax.ppermute(value, 'cache', [(i, i ^ k) for i in range(WAYS)])]
    ppermute x18 -> x24, starting transfers between devices: 37.6 us -> 42.9 us  [from_z(): return lax.ppermute(value, 'cache', [(i, i ^ k) for i in range(WAYS)])]
    pallas_call x5 -> x9, Pallas kernels: 20.6 us -> 25.1 us  [the longest x2 13.2 us: mix_pair(): pl.pallas_call(functools.partial(both_kernel, pair), out_shape=jax.ShapeD...]
    ppermute x5 -> x7, starting transfers between devices: 8.74 us -> 5.36 us  [the longest x2 4.61 us: split_heads(): lax.ppermute(value.astype(jnp.bfloat16), ('cache', 'fsdp', 'head'), moves)]
    unnamed x59 -> x61, local copies, waits for them, and re-layouts: 3.75 us -> 6.59 us
    ppermute x5 -> x7, waiting for transfers between devices: 18 us -> 18.4 us  [the longest x2 10.9 us: split_heads(): lax.ppermute(value.astype(jnp.bfloat16), ('cache', 'fsdp', 'head'), moves)]
  transfers between devices with their start and end apart: 38 -> 46, of which waited for: 21 -> 21; matrix products, arithmetic and copies ran while one was open for 6% -> 5% of each run, Pallas kernels for 5% -> 13%
where the time goes in v4:
time: 232 us
  waiting for transfers between devices  124 us (53%)
  starting transfers between devices  56.4 us (24%)
  Pallas kernels  32.1 us (14%)
  local copies, waits for them, and re-layouts  13.2 us (6%)
  other arithmetic  5.87 us (3%)
    ppermute x24, waiting for transfers between devices, from_z(): return lax.ppermute(value, 'cache', [(i, i ^ k) for i in range(WAYS)])  63.1 us
    ppermute x24, starting transfers between devices, from_z(): return lax.ppermute(value, 'cache', [(i, i ^ k) for i in range(WAYS)])  42.9 us
    ppermute x3, waiting for transfers between devices, split_heads(): far = {k: lax.ppermute(near[k], 'groups', SWAP) for k in order}  24.5 us
    pallas_call x2, Pallas kernels, mix_pair(): pl.pallas_call(functools.partial(both_kernel, pair), out_shape=jax.ShapeD...  13.2 us
    ppermute x2, waiting for transfers between devices, gather_pairs(): high_x = lax.ppermute(high, 'fsdp', SWAP)  11.9 us
    ppermute x2, waiting for transfers between devices, split_heads(): lax.ppermute(value.astype(jnp.bfloat16), ('cache', 'fsdp', 'head'), moves)  10.9 us
    unnamed x61, local copies, waits for them, and re-layouts  6.59 us
    ppermute x1, waiting for transfers between devices, split_heads(): other = lax.ppermute(summed(own).astype(jnp.bfloat16), 'fsdp', SWAP)  6.11 us
  transfers between devices with their start and end apart: 46, of which 21 were waited for; matrix products, arithmetic and copies ran while one was open for 5% of the time, Pallas kernels for 13%

profile of v4, /device:TPU:2, one launch (start us, length us, event | category | flops | bytes accessed | tf_op | source)
XLA Modules:
  0.0 232.0 jit_solution(941796087567743047)
XLA Ops:
  0.0 1.8 constant_dynamic-update-slice_fusion.9
  1.8 1.6 collective-permute-start
  3.4 2.6 %collective-permute-start.1 = (bf16[128,768]{1,0:T(8,128)(2,1)}, bf16[128,768]{1,0:T(8,128)(2,1)}, u32[]{:S(2)}, u32[]{:S(2)}) collective-permute-start(bf16[128,768]{1,0:T(8,128)(2,1)} %get-tuple-element.76), channel_id=1, source_target_pairs={{0,8},{4,12},{8,0},{12,4},{1,9},{5,13},{9,1},{13,5},{2,10},{6,14},... | collective-permute-start | bytes 589832 | tf_op jit(solution)/shard_map/ppermute | solution.py:387
  6.0 0.8 dynamic_slice.16
  6.9 3.0 %shard_map.137 = (bf16[768,384]{1,0:T(8,128)(2,1)}, bf16[768,384]{1,0:T(8,128)(2,1)}, bf16[768,384]{1,0:T(8,128)(2,1)}, f32[8,128]{1,0:T(8,128)}) custom-call(f32[768,128]{1,0:T(8,128)S(1)} %broadcast_in_dim.65.gain_ref, bf16[768,1024]{1,0:T(8,128)(2,1)} %refs_0_.3, bf16[768,1024]{1,0:T(8,128)(2,1)} %refs_1_.3, bf16[768,1024]{1,0:T(8,128)(2,1)} %refs_2_.3), custom_call_target="tpu_custom_call" | custom-call | tf_op jit(solution)/shard_map/pallas_call | solution.py:173
  10.9 3.6 %collective-permute-start.13 = (bf16[768,384]{1,0:T(8,128)(2,1)}, bf16[768,384]{1,0:T(8,128)(2,1)S(1)}, u32[]{:S(2)}, u32[]{:S(2)}) collective-permute-start(bf16[768,384]{1,0:T(8,128)(2,1)} %get-tuple-element.43), channel_id=1, source_target_pairs={{0,12},{4,8},{8,4},{12,0},{1,13},{5,9},{9,5},{13,1},{2,14},{6,10},... | collective-permute-start | bytes 1769480 | tf_op jit(solution)/shard_map/ppermute | solution.py:387
  15.9 1.0 copy-done.18
  16.9 2.0 shard_map.136
  19.0 0.8 copy-done.8
  19.8 0.8 copy-done.10
  21.3 0.7 gather_fusion.3
  22.6 1.8 gather_fusion
  24.4 1.9 shard_map.139
  26.4 1.2 pad_maximum_fusion
  28.2 26.8 %collective-permute-done.2 = bf16[128,768]{1,0:T(8,128)(2,1)S(1)} collective-permute-done((bf16[128,768]{1,0:T(8,128)(2,1)}, bf16[128,768]{1,0:T(8,128)(2,1)S(1)}, u32[]{:S(2)}, u32[]{:S(2)}) %collective-permute-start.2) | collective-permute-done | bytes 196640 | tf_op jit(solution)/shard_map/ppermute | solution.py:387
  55.0 1.0 pad_maximum_fusion.1
  56.5 0.9 constant_dynamic-update-slice_fusion.8
  58.1 1.7 collective-permute-start.10
  59.8 6.0 %collective-permute-done.6 = bf16[2,128,768]{2,1,0:T(8,128)(2,1)S(1)} collective-permute-done((bf16[2,128,768]{2,1,0:T(8,128)(2,1)S(1)}, bf16[2,128,768]{2,1,0:T(8,128)(2,1)S(1)}, u32[]{:S(2)}, u32[]{:S(2)}) %collective-permute-start.6) | collective-permute-done | bytes 393248 | tf_op jit(solution)/shard_map/ppermute | solution.py:419
  65.9 0.9 constant_dynamic-update-slice_fusion.7
  66.8 2.1 collective-permute-start.15
  69.0 2.4 %collective-permute-start.16 = (bf16[512,512]{1,0:T(8,128)(2,1)S(1)}, bf16[512,512]{1,0:T(8,128)(2,1)S(1)}, u32[]{:S(2)}, u32[]{:S(2)}) collective-permute-start(bf16[512,512]{1,0:T(8,128)(2,1)S(1)} %get-tuple-element.51), channel_id=1, source_target_pairs={{0,8},{4,12},{8,0},{12,4},{1,9},{5,13},{9,1},{13,5},{2,10},{6,14},... | collective-permute-start | bytes 1572872 | tf_op jit(solution)/shard_map/ppermute | solution.py:387
  71.6 1.4 collective-permute-start.12
  73.0 0.8 collective-permute-done.10.refs_3_.refs_7_
  73.8 1.7 collective-permute-start.14
  75.7 12.1 %collective-permute-done.12.refs_5_.refs_9_ = bf16[768,384]{1,0:T(8,128)(2,1)S(1)} collective-permute-done((bf16[768,384]{1,0:T(8,128)(2,1)S(1)}, bf16[768,384]{1,0:T(8,128)(2,1)S(1)}, u32[]{:S(2)}, u32[]{:S(2)}) %collective-permute-start.12) | collective-permute-done | bytes 589856 | tf_op jit(solution)/shard_map/ppermute | solution.py:436
  87.8 11.6 %collective-permute-done.14.refs_7_.refs_11_ = bf16[768,384]{1,0:T(8,128)(2,1)S(1)} collective-permute-done((bf16[768,384]{1,0:T(8,128)(2,1)S(1)}, bf16[768,384]{1,0:T(8,128)(2,1)S(1)}, u32[]{:S(2)}, u32[]{:S(2)}) %collective-permute-start.14) | collective-permute-done | bytes 589856 | tf_op jit(solution)/shard_map/ppermute | solution.py:436
  99.4 4.3 %shard_map.138 = (bf16[512,256]{1,0:T(8,128)(2,1)S(1)}, bf16[512,256]{1,0:T(8,128)(2,1)S(1)}, bf16[512,256]{1,0:T(8,128)(2,1)S(1)}) custom-call(s32[16]{0:T(128)S(1)} %add.184.source_ref, f32[1,128]{1,0:T(1,128)S(1)} %bitcast.41, f32[1,128]{1,0:T(1,128)S(1)} %bitcast.44, bf16[16,128,768]{2,1,0:T(8,128)(2,1)S(1)} %constant_dynamic-update-slice_fusion.gathered_ref, ...), custom_call_target="tpu_custom_call" | custom-call | tf_op jit(solution)/shard_map/pallas_call | solution.py:319
  103.9 3.3 %collective-permute-done.16.refs_2_.refs_14_ = bf16[512,512]{1,0:T(8,128)(2,1)S(1)} collective-permute-done((bf16[512,512]{1,0:T(8,128)(2,1)S(1)}, bf16[512,512]{1,0:T(8,128)(2,1)S(1)}, u32[]{:S(2)}, u32[]{:S(2)}) %collective-permute-start.16) | collective-permute-done | bytes 524320 | tf_op jit(solution)/shard_map/ppermute | solution.py:387
  107.2 2.3 shard_map.140.refs_0_
  109.5 11.2 %collective-permute-start.22 = (bf16[256,256]{1,0:T(8,128)(2,1)S(1)}, bf16[256,256]{1,0:T(8,128)(2,1)S(1)}, u32[]{:S(2)}, u32[]{:S(2)}) collective-permute-start(bf16[256,256]{1,0:T(8,128)(2,1)S(1)} %shard_map.140.refs_0_), channel_id=1, source_target_pairs={{0,4},{4,0},{8,12},{12,8},{1,5},{5,1},{9,13},{13,9},{2,6},{6,2},{1... | collective-permute-start | bytes 393224 | tf_op jit(solution)/shard_map/ppermute | solution.py:387
  120.7 1.1 collective-permute-start.23
  121.8 2.3 shard_map.141.refs_0_
  124.1 2.0 collective-permute-start.18
  126.1 1.5 collective-permute-done.23.refs_2_
  127.6 3.4 %collective-permute-start.24 = (bf16[256,256]{1,0:T(8,128)(2,1)S(1)}, bf16[256,256]{1,0:T(8,128)(2,1)S(1)}, u32[]{:S(2)}, u32[]{:S(2)}) collective-permute-start(bf16[256,256]{1,0:T(8,128)(2,1)S(1)} %collective-permute-done.23.refs_2_), channel_id=1, source_target_pairs={{0,4},{4,0},{8,12},{12,8},{1,5},{5,1},{9,13},{13,9},{2,6},{6,2},{1... | collective-permute-start | bytes 393224 | tf_op jit(solution)/shard_map/ppermute | solution.py:387
  131.4 4.0 %collective-permute-done.24.refs_3_ = bf16[256,256]{1,0:T(8,128)(2,1)S(1)} collective-permute-done((bf16[256,256]{1,0:T(8,128)(2,1)S(1)}, bf16[256,256]{1,0:T(8,128)(2,1)S(1)}, u32[]{:S(2)}, u32[]{:S(2)}) %collective-permute-start.24) | collective-permute-done | bytes 131104 | tf_op jit(solution)/shard_map/ppermute | solution.py:387
  136.1 1.4 collective-permute-start.20
  137.5 4.5 %collective-permute-done.20.refs_3_ = bf16[256,256]{1,0:T(8,128)(2,1)S(1)} collective-permute-done((bf16[256,256]{1,0:T(8,128)(2,1)S(1)}, bf16[256,256]{1,0:T(8,128)(2,1)S(1)}, u32[]{:S(2)}, u32[]{:S(2)}) %collective-permute-start.20) | collective-permute-done | bytes 131104 | tf_op jit(solution)/shard_map/ppermute | solution.py:387
  142.0 1.3 shard_map.142
  143.2 0.7 add_convert_fusion.2
  144.6 0.9 dynamic-slice_reduce_fusion.1
  145.5 6.1 %collective-permute-done.26 = bf16[128,768]{1,0:T(8,128)(2,1)} collective-permute-done((bf16[128,768]{1,0:T(8,128)(2,1)}, bf16[128,768]{1,0:T(8,128)(2,1)}, u32[]{:S(2)}, u32[]{:S(2)}) %collective-permute-start.26) | collective-permute-done | bytes 196640 | tf_op jit(solution)/shard_map/ppermute | solution.py:468
  151.6 1.2 fusion
  152.8 1.4 collective-permute-start.27
  154.2 2.0 collective-permute-start.28
  156.2 7.3 %collective-permute-done.27 = bf16[128,768]{1,0:T(8,128)(2,1)S(1)} collective-permute-done((bf16[128,768]{1,0:T(8,128)(2,1)S(1)}, bf16[128,768]{1,0:T(8,128)(2,1)S(1)}, u32[]{:S(2)}, u32[]{:S(2)}) %collective-permute-start.27) | collective-permute-done | bytes 196640 | tf_op jit(solution)/shard_map/ppermute | solution.py:387
  163.5 2.1 collective-permute-done.28
  166.7 4.6 %collective-permute-done.29 = bf16[128,768]{1,0:T(8,128)(2,1)S(1)} collective-permute-done((bf16[128,768]{1,0:T(8,128)(2,1)S(1)}, bf16[128,768]{1,0:T(8,128)(2,1)S(1)}, u32[]{:S(2)}, u32[]{:S(2)}) %collective-permute-start.29) | collective-permute-done | bytes 196640 | tf_op jit(solution)/shard_map/ppermute | solution.py:387
  172.4 5.8 %collective-permute-done.37.refs_0_ = bf16[2,128,768]{2,1,0:T(8,128)(2,1)S(1)} collective-permute-done((bf16[2,128,768]{2,1,0:T(8,128)(2,1)S(1)}, bf16[2,128,768]{2,1,0:T(8,128)(2,1)S(1)}, u32[]{:S(2)}, u32[]{:S(2)}) %collective-permute-start.37) | collective-permute-done | bytes 393248 | tf_op jit(solution)/shard_map/ppermute | solution.py:417
  178.2 5.9 %collective-permute-done.38.refs_1_ = bf16[2,128,768]{2,1,0:T(8,128)(2,1)S(1)} collective-permute-done((bf16[2,128,768]{2,1,0:T(8,128)(2,1)S(1)}, bf16[2,128,768]{2,1,0:T(8,128)(2,1)S(1)}, u32[]{:S(2)}, u32[]{:S(2)}) %collective-permute-start.38) | collective-permute-done | bytes 393248 | tf_op jit(solution)/shard_map/ppermute | solution.py:419
  184.1 6.6 %shard_map.144.refs_0_ = bf16[256,256]{1,0:T(8,128)(2,1)S(1)} custom-call(s32[16]{0:T(128)S(1)} %reshape.272.pos_ref, f32[1,128]{1,0:T(1,128)S(1)} %bitcast.42, f32[1,128]{1,0:T(1,128)S(1)} %bitcast.45, bf16[2,128,768]{2,1,0:T(8,128)(2,1)S(1)} %pad_maximum_fusion.2.refs_0_, bf16[2,128,768]{2,1,0:T(8,128)(2,1)S(1)} %pad_maximum_fusion.3.refs_1_, ...), custom_call_target="tpu_custom_call" | custom-call | tf_op jit(solution)/shard_map/pallas_call | solution.py:342
  191.1 1.6 collective-permute-start.33
  192.7 6.6 %shard_map.146.refs_0_ = bf16[256,256]{1,0:T(8,128)(2,1)S(1)} custom-call(s32[16]{0:T(128)S(1)} %reshape.272.pos_ref, f32[1,128]{1,0:T(1,128)S(1)} %bitcast.43, f32[1,128]{1,0:T(1,128)S(1)} %bitcast.46, bf16[2,128,768]{2,1,0:T(8,128)(2,1)S(1)} %collective-permute-done.37.refs_0_, bf16[2,128,768]{2,1,0:T(8,128)(2,1)S(1)} %collective-permute-done.38.refs_1_, ...), custom_call_target="tpu_custom_call" | custom-call | tf_op jit(solution)/shard_map/pallas_call | solution.py:342
  200.0 2.4 %collective-permute-start.42 = (bf16[256,256]{1,0:T(8,128)(2,1)S(1)}, bf16[256,256]{1,0:T(8,128)(2,1)S(1)}, u32[]{:S(2)}, u32[]{:S(2)}) collective-permute-start(bf16[256,256]{1,0:T(8,128)(2,1)S(1)} %shard_map.146.refs_0_), channel_id=1, source_target_pairs={{0,8},{4,12},{8,0},{12,4},{1,9},{5,13},{9,1},{13,5},{2,10},{6,14},... | collective-permute-start | bytes 393224 | tf_op jit(solution)/shard_map/ppermute | solution.py:387
  202.7 5.9 %collective-permute-done.41.refs_1_ = bf16[256,256]{1,0:T(8,128)(2,1)S(1)} collective-permute-done((bf16[256,256]{1,0:T(8,128)(2,1)S(1)}, bf16[256,256]{1,0:T(8,128)(2,1)S(1)}, u32[]{:S(2)}, u32[]{:S(2)}) %collective-permute-start.41) | collective-permute-done | bytes 131104 | tf_op jit(solution)/shard_map/ppermute | solution.py:387
  208.6 1.3 collective-permute-start.43
  209.8 1.5 collective-permute-done.34.refs_3_
  212.0 1.5 collective-permute-done.43.refs_3_
  214.2 1.4 collective-permute-done.44
  216.4 4.0 %collective-permute-start.36 = (bf16[128,768]{1,0:T(8,128)(2,1)S(1)}, bf16[128,768]{1,0:T(8,128)(2,1)S(1)}, u32[]{:S(2)}, u32[]{:S(2)}) collective-permute-start(bf16[128,768]{1,0:T(8,128)(2,1)S(1)} %get-tuple-element.79), channel_id=1, source_target_pairs={{0,0},{1,4},{2,8},{3,12},{4,1},{5,5},{6,9},{7,13},{8,2},{9,6},{10,... | collective-permute-start | bytes 589832 | tf_op jit(solution)/shard_map/ppermute | solution.py:481
  220.4 7.5 %collective-permute-done.45 = bf16[128,768]{1,0:T(8,128)(2,1)S(1)} collective-permute-done((bf16[128,768]{1,0:T(8,128)(2,1)S(1)}, bf16[128,768]{1,0:T(8,128)(2,1)S(1)}, u32[]{:S(2)}, u32[]{:S(2)}) %collective-permute-start.45) | collective-permute-done | bytes 196640 | tf_op jit(solution)/shard_map/ppermute | solution.py:481
  227.9 3.3 %collective-permute-done.36 = bf16[128,768]{1,0:T(8,128)(2,1)S(1)} collective-permute-done((bf16[128,768]{1,0:T(8,128)(2,1)S(1)}, bf16[128,768]{1,0:T(8,128)(2,1)S(1)}, u32[]{:S(2)}, u32[]{:S(2)}) %collective-permute-start.36) | collective-permute-done | bytes 196640 | tf_op jit(solution)/shard_map/ppermute | solution.py:481
  231.2 0.7 add_convert_fusion
  (143 shorter events, 13.0 us)
Async XLA Ops:
  0.0 22.6 %copy-start = (bf16[1024,768]{1,0:T(8,128)(2,1)S(1)}, bf16[1024,768]{1,0:T(8,128)(2,1)}, u32[]{:S(2)}) copy-start(bf16[1024,768]{1,0:T(8,128)(2,1)} %param.19) | copy-start | bytes 4718596
  1.8 24.5 %collective-permute-start = (bf16[128,768]{1,0:T(8,128)(2,1)}, bf16[128,768]{1,0:T(8,128)(2,1)}, u32[]{:S(2)}, u32[]{:S(2)}) collective-permute-start(bf16[128,768]{1,0:T(8,128)(2,1)} %get-tuple-element.76), channel_id=1, source_target_pairs={{0,4},{4,0},{8,12},{12,8},{1,5},{5,1},{9,13},{13,9},{2,6},{6,2},{1... | collective-permute-start | bytes 589832 | tf_op jit(solution)/shard_map/ppermute | solution.py:387
  3.4 19.1 %collective-permute-start.1 = (bf16[128,768]{1,0:T(8,128)(2,1)}, bf16[128,768]{1,0:T(8,128)(2,1)}, u32[]{:S(2)}, u32[]{:S(2)}) collective-permute-start(bf16[128,768]{1,0:T(8,128)(2,1)} %get-tuple-element.76), channel_id=1, source_target_pairs={{0,8},{4,12},{8,0},{12,4},{1,9},{5,13},{9,1},{13,5},{2,10},{6,14},... | collective-permute-start | bytes 589832 | tf_op jit(solution)/shard_map/ppermute | solution.py:387
  10.0 47.5 %collective-permute-start.9 = (bf16[768,384]{1,0:T(8,128)(2,1)}, bf16[768,384]{1,0:T(8,128)(2,1)S(1)}, u32[]{:S(2)}, u32[]{:S(2)}) collective-permute-start(bf16[768,384]{1,0:T(8,128)(2,1)} %get-tuple-element.41), channel_id=1, source_target_pairs={{0,4},{4,0},{8,12},{12,8},{1,5},{5,1},{9,13},{13,9},{2,6},{6,2},{1... | collective-permute-start | bytes 1769480 | tf_op jit(solution)/shard_map/ppermute | solution.py:387
  10.5 47.5 %collective-permute-start.11 = (bf16[768,384]{1,0:T(8,128)(2,1)}, bf16[768,384]{1,0:T(8,128)(2,1)S(1)}, u32[]{:S(2)}, u32[]{:S(2)}) collective-permute-start(bf16[768,384]{1,0:T(8,128)(2,1)} %get-tuple-element.42), channel_id=1, source_target_pairs={{0,8},{4,12},{8,0},{12,4},{1,9},{5,13},{9,1},{13,5},{2,10},{6,14},... | collective-permute-start | bytes 1769480 | tf_op jit(solution)/shard_map/ppermute | solution.py:387
  10.9 47.3 %collective-permute-start.13 = (bf16[768,384]{1,0:T(8,128)(2,1)}, bf16[768,384]{1,0:T(8,128)(2,1)S(1)}, u32[]{:S(2)}, u32[]{:S(2)}) collective-permute-start(bf16[768,384]{1,0:T(8,128)(2,1)} %get-tuple-element.43), channel_id=1, source_target_pairs={{0,12},{4,8},{8,4},{12,0},{1,13},{5,9},{9,5},{13,1},{2,14},{6,10},... | collective-permute-start | bytes 1769480 | tf_op jit(solution)/shard_map/ppermute | solution.py:387
  22.6 32.5 %collective-permute-start.2 = (bf16[128,768]{1,0:T(8,128)(2,1)}, bf16[128,768]{1,0:T(8,128)(2,1)S(1)}, u32[]{:S(2)}, u32[]{:S(2)}) collective-permute-start(bf16[128,768]{1,0:T(8,128)(2,1)} %collective-permute-done.1), channel_id=1, source_target_pairs={{0,4},{4,0},{8,12},{12,8},{1,5},{5,1},{9,13},{13,9},{2,6},{6,2},{1... | collective-permute-start | bytes 589832 | tf_op jit(solution)/shard_map/ppermute | solution.py:387
  24.4 32.1 %copy-start.25 = (s32[8]{0:T(128)S(1)}, s32[8]{0:T(128)}, u32[]{:S(2)}) copy-start(s32[8]{0:T(128)} %reshape.269) | copy-start | bytes 100
  24.4 32.1 %copy-start.15 = (bf16[16,128,768]{2,1,0:T(8,128)(2,1)S(1)}, bf16[16,128,768]{2,1,0:T(8,128)(2,1)}, u32[]{:S(2)}) copy-start(bf16[16,128,768]{2,1,0:T(8,128)(2,1)} %get-tuple-element.75) | copy-start | bytes 9437188
  26.4 95.4 %copy-start.1 = (bf16[512,512]{1,0:T(8,128)(2,1)}, bf16[512,512]{1,0:T(8,128)(2,1)S(1)}, u32[]{:S(2)}) copy-start(bf16[512,512]{1,0:T(8,128)(2,1)S(1)} %get-tuple-element.47.refs_0_.refs_12_) | copy-start | bytes 1572868
  27.6 29.8 %collective-permute-start.5 = (bf16[2,128,768]{2,1,0:T(8,128)(2,1)S(1)}, bf16[2,128,768]{2,1,0:T(8,128)(2,1)S(1)}, u32[]{:S(2)}, u32[]{:S(2)}) collective-permute-start(bf16[2,128,768]{2,1,0:T(8,128)(2,1)S(1)} %pad_maximum_fusion), channel_id=1, source_target_pairs={{0,2},{2,0},{1,3},{3,1},{4,6},{6,4},{5,7},{7,5},{8,10},{10,8},{9,1... | collective-permute-start | bytes 1179656 | tf_op jit(solution)/shard_map/ppermute | solution.py:417
  56.0 43.4 %copy-start.9 = (bf16[768,384]{1,0:T(8,128)(2,1)S(1)}, bf16[768,384]{1,0:T(8,128)(2,1)}, u32[]{:S(2)}) copy-start(bf16[768,384]{1,0:T(8,128)(2,1)} %copy-done.8) | copy-start | bytes 1769476
  56.0 43.4 %copy-start.11 = (bf16[768,384]{1,0:T(8,128)(2,1)S(1)}, bf16[768,384]{1,0:T(8,128)(2,1)}, u32[]{:S(2)}) copy-start(bf16[768,384]{1,0:T(8,128)(2,1)} %copy-done.10) | copy-start | bytes 1769476
  56.0 43.4 %copy-start.19 = (f32[128]{0:T(128)S(1)}, f32[128]{0:T(128)}, u32[]{:S(2)}) copy-start(f32[128]{0:T(128)} %param.20) | copy-start | bytes 1540
  56.0 43.4 %copy-start.20 = (f32[128]{0:T(128)S(1)}, f32[128]{0:T(128)}, u32[]{:S(2)}) copy-start(f32[128]{0:T(128)} %param.21) | copy-start | bytes 1540
  56.0 9.8 %collective-permute-start.6 = (bf16[2,128,768]{2,1,0:T(8,128)(2,1)S(1)}, bf16[2,128,768]{2,1,0:T(8,128)(2,1)S(1)}, u32[]{:S(2)}, u32[]{:S(2)}) collective-permute-start(bf16[2,128,768]{2,1,0:T(8,128)(2,1)S(1)} %pad_maximum_fusion.1), channel_id=1, source_target_pairs={{0,2},{2,0},{1,3},{3,1},{4,6},{6,4},{5,7},{7,5},{8,10},{10,8},{9,1... | collective-permute-start | bytes 1179656 | tf_op jit(solution)/shard_map/ppermute | solution.py:419
  57.5 9.4 %collective-permute-start.3 = (bf16[2,128,768]{2,1,0:T(8,128)(2,1)S(1)}, bf16[2,128,768]{2,1,0:T(8,128)(2,1)S(1)}, u32[]{:S(2)}, u32[]{:S(2)}) collective-permute-start(bf16[2,128,768]{2,1,0:T(8,128)(2,1)S(1)} %pad_maximum_fusion), channel_id=1, source_target_pairs={{0,1},{1,0},{2,3},{3,2},{4,5},{5,4},{6,7},{7,6},{8,9},{9,8},{10,11... | collective-permute-start | bytes 1179656 | tf_op jit(solution)/shard_map/ppermute | solution.py:421
  57.5 46.2 %copy-start.5 = (bf16[768,384]{1,0:T(8,128)(2,1)}, bf16[768,384]{1,0:T(8,128)(2,1)S(1)}, u32[]{:S(2)}) copy-start(bf16[768,384]{1,0:T(8,128)(2,1)S(1)} %collective-permute-done.9.refs_2_.refs_6_) | copy-start | bytes 1769476
  57.6 11.4 %collective-permute-start.4 = (bf16[2,128,768]{2,1,0:T(8,128)(2,1)S(1)}, bf16[2,128,768]{2,1,0:T(8,128)(2,1)S(1)}, u32[]{:S(2)}, u32[]{:S(2)}) collective-permute-start(bf16[2,128,768]{2,1,0:T(8,128)(2,1)S(1)} %pad_maximum_fusion.1), channel_id=1, source_target_pairs={{0,1},{1,0},{2,3},{3,2},{4,5},{5,4},{6,7},{7,6},{8,9},{9,8},{10,11... | collective-permute-start | bytes 1179656 | tf_op jit(solution)/shard_map/ppermute | solution.py:421
  58.0 45.7 %copy-start.6 = (bf16[768,384]{1,0:T(8,128)(2,1)}, bf16[768,384]{1,0:T(8,128)(2,1)S(1)}, u32[]{:S(2)}) copy-start(bf16[768,384]{1,0:T(8,128)(2,1)S(1)} %collective-permute-done.11.refs_4_.refs_8_) | copy-start | bytes 1769476
  58.0 13.4 %collective-permute-start.7 = (bf16[2,128,768]{2,1,0:T(8,128)(2,1)S(1)}, bf16[2,128,768]{2,1,0:T(8,128)(2,1)S(1)}, u32[]{:S(2)}, u32[]{:S(2)}) collective-permute-start(bf16[2,128,768]{2,1,0:T(8,128)(2,1)S(1)} %collective-permute-done.5), channel_id=1, source_target_pairs={{0,1},{1,0},{2,3},{3,2},{4,5},{5,4},{6,7},{7,6},{8,9},{9,8},{10,11... | collective-permute-start | bytes 1179656 | tf_op jit(solution)/shard_map/ppermute | solution.py:421
  58.1 45.7 %copy-start.7 = (bf16[768,384]{1,0:T(8,128)(2,1)}, bf16[768,384]{1,0:T(8,128)(2,1)S(1)}, u32[]{:S(2)}) copy-start(bf16[768,384]{1,0:T(8,128)(2,1)S(1)} %collective-permute-done.13.refs_6_.refs_10_) | copy-start | bytes 1769476
  58.1 15.7 %collective-permute-start.10 = (bf16[768,384]{1,0:T(8,128)(2,1)S(1)}, bf16[768,384]{1,0:T(8,128)(2,1)S(1)}, u32[]{:S(2)}, u32[]{:S(2)}) collective-permute-start(bf16[768,384]{1,0:T(8,128)(2,1)S(1)} %collective-permute-done.9.refs_2_.refs_6_), channel_id=1, source_target_pairs={{0,16},{16,0},{1,17},{17,1},{2,18},{18,2},{3,19},{19,3},{4,20},{20... | collective-permute-start | bytes 1769480 | tf_op jit(solution)/shard_map/ppermute | solution.py:436
  65.9 5.7 %collective-permute-start.8 = (bf16[2,128,768]{2,1,0:T(8,128)(2,1)S(1)}, bf16[2,128,768]{2,1,0:T(8,128)(2,1)S(1)}, u32[]{:S(2)}, u32[]{:S(2)}) collective-permute-start(bf16[2,128,768]{2,1,0:T(8,128)(2,1)S(1)} %collective-permute-done.6), channel_id=1, source_target_pairs={{0,1},{1,0},{2,3},{3,2},{4,5},{5,4},{6,7},{7,6},{8,9},{9,8},{10,11... | collective-permute-start | bytes 1179656 | tf_op jit(solution)/shard_map/ppermute | solution.py:421
  66.8 37.0 %collective-permute-start.15 = (bf16[512,512]{1,0:T(8,128)(2,1)S(1)}, bf16[512,512]{1,0:T(8,128)(2,1)S(1)}, u32[]{:S(2)}, u32[]{:S(2)}) collective-permute-start(bf16[512,512]{1,0:T(8,128)(2,1)S(1)} %get-tuple-element.49), channel_id=1, source_target_pairs={{0,4},{4,0},{8,12},{12,8},{1,5},{5,1},{9,13},{13,9},{2,6},{6,2},{1... | collective-permute-start | bytes 1572872 | tf_op jit(solution)/shard_map/ppermute | solution.py:387
  69.0 38.2 %collective-permute-start.16 = (bf16[512,512]{1,0:T(8,128)(2,1)S(1)}, bf16[512,512]{1,0:T(8,128)(2,1)S(1)}, u32[]{:S(2)}, u32[]{:S(2)}) collective-permute-start(bf16[512,512]{1,0:T(8,128)(2,1)S(1)} %get-tuple-element.51), channel_id=1, source_target_pairs={{0,8},{4,12},{8,0},{12,4},{1,9},{5,13},{9,1},{13,5},{2,10},{6,14},... | collective-permute-start | bytes 1572872 | tf_op jit(solution)/shard_map/ppermute | solution.py:387
  71.4 35.8 %collective-permute-start.17 = (bf16[512,512]{1,0:T(8,128)(2,1)S(1)}, bf16[512,512]{1,0:T(8,128)(2,1)S(1)}, u32[]{:S(2)}, u32[]{:S(2)}) collective-permute-start(bf16[512,512]{1,0:T(8,128)(2,1)S(1)} %get-tuple-element.53), channel_id=1, source_target_pairs={{0,12},{4,8},{8,4},{12,0},{1,13},{5,9},{9,5},{13,1},{2,14},{6,10},... | collective-permute-start | bytes 1572872 | tf_op jit(solution)/shard_map/ppermute | solution.py:387
  71.6 16.2 %collective-permute-start.12 = (bf16[768,384]{1,0:T(8,128)(2,1)S(1)}, bf16[768,384]{1,0:T(8,128)(2,1)S(1)}, u32[]{:S(2)}, u32[]{:S(2)}) collective-permute-start(bf16[768,384]{1,0:T(8,128)(2,1)S(1)} %collective-permute-done.11.refs_4_.refs_8_), channel_id=1, source_target_pairs={{0,16},{16,0},{1,17},{17,1},{2,18},{18,2},{3,19},{19,3},{4,20},{20... | collective-permute-start | bytes 1769480 | tf_op jit(solution)/shard_map/ppermute | solution.py:436
  73.8 30.0 %copy-start.12 = (bf16[768,384]{1,0:T(8,128)(2,1)}, bf16[768,384]{1,0:T(8,128)(2,1)S(1)}, u32[]{:S(2)}) copy-start(bf16[768,384]{1,0:T(8,128)(2,1)S(1)} %collective-permute-done.10.refs_3_.refs_7_) | copy-start | bytes 1769476
  73.8 25.6 %collective-permute-start.14 = (bf16[768,384]{1,0:T(8,128)(2,1)S(1)}, bf16[768,384]{1,0:T(8,128)(2,1)S(1)}, u32[]{:S(2)}, u32[]{:S(2)}) collective-permute-start(bf16[768,384]{1,0:T(8,128)(2,1)S(1)} %collective-permute-done.13.refs_6_.refs_10_), channel_id=1, source_target_pairs={{0,16},{16,0},{1,17},{17,1},{2,18},{18,2},{3,19},{19,3},{4,20},{20... | collective-permute-start | bytes 1769480 | tf_op jit(solution)/shard_map/ppermute | solution.py:436
  75.7 28.1 %copy-start.16 = (bf16[16,128,768]{2,1,0:T(8,128)(2,1)}, bf16[16,128,768]{2,1,0:T(8,128)(2,1)S(1)}, u32[]{:S(2)}) copy-start(bf16[16,128,768]{2,1,0:T(8,128)(2,1)S(1)} %constant_dynamic-update-slice_fusion.gathered_ref) | copy-start | bytes 9437188
  87.8 16.0 %copy-start.13 = (bf16[768,384]{1,0:T(8,128)(2,1)}, bf16[768,384]{1,0:T(8,128)(2,1)S(1)}, u32[]{:S(2)}) copy-start(bf16[768,384]{1,0:T(8,128)(2,1)S(1)} %collective-permute-done.12.refs_5_.refs_9_) | copy-start | bytes 1769476
  103.8 27.2 %copy-start.23 = (bf16[8,128,768]{2,1,0:T(8,128)(2,1)S(1)}, bf16[8,128,768]{2,1,0:T(8,128)(2,1)}, u32[]{:S(2)}) copy-start(bf16[8,128,768]{2,1,0:T(8,128)(2,1)} %gather_fusion) | copy-start | bytes 4718596
  103.9 27.5 %copy-start.2 = (bf16[512,512]{1,0:T(8,128)(2,1)}, bf16[512,512]{1,0:T(8,128)(2,1)S(1)}, u32[]{:S(2)}) copy-start(bf16[512,512]{1,0:T(8,128)(2,1)S(1)} %collective-permute-done.15.refs_1_.refs_13_) | copy-start | bytes 1572868
  107.2 24.1 %copy-start.3 = (bf16[512,512]{1,0:T(8,128)(2,1)}, bf16[512,512]{1,0:T(8,128)(2,1)S(1)}, u32[]{:S(2)}) copy-start(bf16[512,512]{1,0:T(8,128)(2,1)S(1)} %collective-permute-done.16.refs_2_.refs_14_) | copy-start | bytes 1572868
  107.2 24.1 %copy-start.4 = (bf16[512,512]{1,0:T(8,128)(2,1)}, bf16[512,512]{1,0:T(8,128)(2,1)S(1)}, u32[]{:S(2)}) copy-start(bf16[512,512]{1,0:T(8,128)(2,1)S(1)} %collective-permute-done.17.refs_3_.refs_15_) | copy-start | bytes 1572868
  109.5 16.6 %collective-permute-start.22 = (bf16[256,256]{1,0:T(8,128)(2,1)S(1)}, bf16[256,256]{1,0:T(8,128)(2,1)S(1)}, u32[]{:S(2)}, u32[]{:S(2)}) collective-permute-start(bf16[256,256]{1,0:T(8,128)(2,1)S(1)} %shard_map.140.refs_0_), channel_id=1, source_target_pairs={{0,4},{4,0},{8,12},{12,8},{1,5},{5,1},{9,13},{13,9},{2,6},{6,2},{1... | collective-permute-start | bytes 393224 | tf_op jit(solution)/shard_map/ppermute | solution.py:387
  120.7 6.9 %collective-permute-start.23 = (bf16[256,256]{1,0:T(8,128)(2,1)S(1)}, bf16[256,256]{1,0:T(8,128)(2,1)S(1)}, u32[]{:S(2)}, u32[]{:S(2)}) collective-permute-start(bf16[256,256]{1,0:T(8,128)(2,1)S(1)} %shard_map.140.refs_0_), channel_id=1, source_target_pairs={{0,8},{4,12},{8,0},{12,4},{1,9},{5,13},{9,1},{13,5},{2,10},{6,14},... | collective-permute-start | bytes 393224 | tf_op jit(solution)/shard_map/ppermute | solution.py:387
  124.1 11.9 %collective-permute-start.18 = (bf16[256,256]{1,0:T(8,128)(2,1)S(1)}, bf16[256,256]{1,0:T(8,128)(2,1)S(1)}, u32[]{:S(2)}, u32[]{:S(2)}) collective-permute-start(bf16[256,256]{1,0:T(8,128)(2,1)S(1)} %shard_map.141.refs_0_), channel_id=1, source_target_pairs={{0,4},{4,0},{8,12},{12,8},{1,5},{5,1},{9,13},{13,9},{2,6},{6,2},{1... | collective-permute-start | bytes 393224 | tf_op jit(solution)/shard_map/ppermute | solution.py:387
  126.1 9.9 %collective-permute-start.19 = (bf16[256,256]{1,0:T(8,128)(2,1)S(1)}, bf16[256,256]{1,0:T(8,128)(2,1)S(1)}, u32[]{:S(2)}, u32[]{:S(2)}) collective-permute-start(bf16[256,256]{1,0:T(8,128)(2,1)S(1)} %shard_map.141.refs_0_), channel_id=1, source_target_pairs={{0,8},{4,12},{8,0},{12,4},{1,9},{5,13},{9,1},{13,5},{2,10},{6,14},... | collective-permute-start | bytes 393224 | tf_op jit(solution)/shard_map/ppermute | solution.py:387
  127.6 7.8 %collective-permute-start.24 = (bf16[256,256]{1,0:T(8,128)(2,1)S(1)}, bf16[256,256]{1,0:T(8,128)(2,1)S(1)}, u32[]{:S(2)}, u32[]{:S(2)}) collective-permute-start(bf16[256,256]{1,0:T(8,128)(2,1)S(1)} %collective-permute-done.23.refs_2_), channel_id=1, source_target_pairs={{0,4},{4,0},{8,12},{12,8},{1,5},{5,1},{9,13},{13,9},{2,6},{6,2},{1... | collective-permute-start | bytes 393224 | tf_op jit(solution)/shard_map/ppermute | solution.py:387
  136.0 7.3 %collective-permute-start.25 = (bf16[128,768]{1,0:T(8,128)(2,1)S(1)}, bf16[128,768]{1,0:T(8,128)(2,1)S(1)}, u32[]{:S(2)}, u32[]{:S(2)}) collective-permute-start(bf16[128,768]{1,0:T(8,128)(2,1)S(1)} %get-tuple-element.62), channel_id=1, source_target_pairs={{0,1},{1,0},{2,3},{3,2},{4,5},{5,4},{6,7},{7,6},{8,9},{9,8},{10,11... | collective-permute-start | bytes 589832 | tf_op jit(solution)/shard_map/ppermute | solution.py:464
  136.1 5.9 %collective-permute-start.20 = (bf16[256,256]{1,0:T(8,128)(2,1)S(1)}, bf16[256,256]{1,0:T(8,128)(2,1)S(1)}, u32[]{:S(2)}, u32[]{:S(2)}) collective-permute-start(bf16[256,256]{1,0:T(8,128)(2,1)S(1)} %collective-permute-done.19.refs_2_), channel_id=1, source_target_pairs={{0,4},{4,0},{8,12},{12,8},{1,5},{5,1},{9,13},{13,9},{2,6},{6,2},{1... | collective-permute-start | bytes 393224 | tf_op jit(solution)/shard_map/ppermute | solution.py:387
  143.2 2.2 collective-permute-start.21
  143.9 7.6 %collective-permute-start.26 = (bf16[128,768]{1,0:T(8,128)(2,1)}, bf16[128,768]{1,0:T(8,128)(2,1)}, u32[]{:S(2)}, u32[]{:S(2)}) collective-permute-start(bf16[128,768]{1,0:T(8,128)(2,1)} %add_convert_fusion.2), channel_id=1, source_target_pairs={{0,2},{2,0},{1,3},{3,1},{4,6},{6,4},{5,7},{7,5},{8,10},{10,8},{9,1... | collective-permute-start | bytes 589832 | tf_op jit(solution)/shard_map/ppermute | solution.py:468
  152.8 10.7 %collective-permute-start.27 = (bf16[128,768]{1,0:T(8,128)(2,1)S(1)}, bf16[128,768]{1,0:T(8,128)(2,1)S(1)}, u32[]{:S(2)}, u32[]{:S(2)}) collective-permute-start(bf16[128,768]{1,0:T(8,128)(2,1)S(1)} %fusion), channel_id=1, source_target_pairs={{0,4},{4,0},{8,12},{12,8},{1,5},{5,1},{9,13},{13,9},{2,6},{6,2},{1... | collective-permute-start | bytes 589832 | tf_op jit(solution)/shard_map/ppermute | solution.py:387
  154.2 11.4 %collective-permute-start.28 = (bf16[128,768]{1,0:T(8,128)(2,1)S(1)}, bf16[128,768]{1,0:T(8,128)(2,1)S(1)}, u32[]{:S(2)}, u32[]{:S(2)}) collective-permute-start(bf16[128,768]{1,0:T(8,128)(2,1)S(1)} %fusion), channel_id=1, source_target_pairs={{0,8},{4,12},{8,0},{12,4},{1,9},{5,13},{9,1},{13,5},{2,10},{6,14},... | collective-permute-start | bytes 589832 | tf_op jit(solution)/shard_map/ppermute | solution.py:387
  165.6 5.7 %collective-permute-start.29 = (bf16[128,768]{1,0:T(8,128)(2,1)S(1)}, bf16[128,768]{1,0:T(8,128)(2,1)S(1)}, u32[]{:S(2)}, u32[]{:S(2)}) collective-permute-start(bf16[128,768]{1,0:T(8,128)(2,1)S(1)} %collective-permute-done.28), channel_id=1, source_target_pairs={{0,4},{4,0},{8,12},{12,8},{1,5},{5,1},{9,13},{13,9},{2,6},{6,2},{1... | collective-permute-start | bytes 589832 | tf_op jit(solution)/shard_map/ppermute | solution.py:387
  166.1 12.1 %collective-permute-start.37 = (bf16[2,128,768]{2,1,0:T(8,128)(2,1)S(1)}, bf16[2,128,768]{2,1,0:T(8,128)(2,1)S(1)}, u32[]{:S(2)}, u32[]{:S(2)}) collective-permute-start(bf16[2,128,768]{2,1,0:T(8,128)(2,1)S(1)} %pad_maximum_fusion.2.refs_0_), channel_id=1, source_target_pairs={{0,2},{2,0},{1,3},{3,1},{4,6},{6,4},{5,7},{7,5},{8,10},{10,8},{9,1... | collective-permute-start | bytes 1179656 | tf_op jit(solution)/shard_map/ppermute | solution.py:417
  171.3 12.8 %collective-permute-start.38 = (bf16[2,128,768]{2,1,0:T(8,128)(2,1)S(1)}, bf16[2,128,768]{2,1,0:T(8,128)(2,1)S(1)}, u32[]{:S(2)}, u32[]{:S(2)}) collective-permute-start(bf16[2,128,768]{2,1,0:T(8,128)(2,1)S(1)} %pad_maximum_fusion.3.refs_1_), channel_id=1, source_target_pairs={{0,2},{2,0},{1,3},{3,1},{4,6},{6,4},{5,7},{7,5},{8,10},{10,8},{9,1... | collective-permute-start | bytes 1179656 | tf_op jit(solution)/shard_map/ppermute | solution.py:419
  171.9 12.2 %collective-permute-start.30 = (bf16[2,128,768]{2,1,0:T(8,128)(2,1)S(1)}, bf16[2,128,768]{2,1,0:T(8,128)(2,1)S(1)}, u32[]{:S(2)}, u32[]{:S(2)}) collective-permute-start(bf16[2,128,768]{2,1,0:T(8,128)(2,1)S(1)} %pad_maximum_fusion.2.refs_0_), channel_id=1, source_target_pairs={{0,1},{1,0},{2,3},{3,2},{4,5},{5,4},{6,7},{7,6},{8,9},{9,8},{10,11... | collective-permute-start | bytes 1179656 | tf_op jit(solution)/shard_map/ppermute | solution.py:421
  171.9 12.2 %collective-permute-start.31 = (bf16[2,128,768]{2,1,0:T(8,128)(2,1)S(1)}, bf16[2,128,768]{2,1,0:T(8,128)(2,1)S(1)}, u32[]{:S(2)}, u32[]{:S(2)}) collective-permute-start(bf16[2,128,768]{2,1,0:T(8,128)(2,1)S(1)} %pad_maximum_fusion.3.refs_1_), channel_id=1, source_target_pairs={{0,1},{1,0},{2,3},{3,2},{4,5},{5,4},{6,7},{7,6},{8,9},{9,8},{10,11... | collective-permute-start | bytes 1179656 | tf_op jit(solution)/shard_map/ppermute | solution.py:421
  178.2 14.5 %collective-permute-start.39 = (bf16[2,128,768]{2,1,0:T(8,128)(2,1)S(1)}, bf16[2,128,768]{2,1,0:T(8,128)(2,1)S(1)}, u32[]{:S(2)}, u32[]{:S(2)}) collective-permute-start(bf16[2,128,768]{2,1,0:T(8,128)(2,1)S(1)} %collective-permute-done.37.refs_0_), channel_id=1, source_target_pairs={{0,1},{1,0},{2,3},{3,2},{4,5},{5,4},{6,7},{7,6},{8,9},{9,8},{10,11... | collective-permute-start | bytes 1179656 | tf_op jit(solution)/shard_map/ppermute | solution.py:421
  184.1 8.6 %collective-permute-start.40 = (bf16[2,128,768]{2,1,0:T(8,128)(2,1)S(1)}, bf16[2,128,768]{2,1,0:T(8,128)(2,1)S(1)}, u32[]{:S(2)}, u32[]{:S(2)}) collective-permute-start(bf16[2,128,768]{2,1,0:T(8,128)(2,1)S(1)} %collective-permute-done.38.refs_1_), channel_id=1, source_target_pairs={{0,1},{1,0},{2,3},{3,2},{4,5},{5,4},{6,7},{7,6},{8,9},{9,8},{10,11... | collective-permute-start | bytes 1179656 | tf_op jit(solution)/shard_map/ppermute | solution.py:421
  190.7 11.7 %collective-permute-start.32 = (bf16[256,256]{1,0:T(8,128)(2,1)S(1)}, bf16[256,256]{1,0:T(8,128)(2,1)S(1)}, u32[]{:S(2)}, u32[]{:S(2)}) collective-permute-start(bf16[256,256]{1,0:T(8,128)(2,1)S(1)} %shard_map.144.refs_0_), channel_id=1, source_target_pairs={{0,4},{4,0},{8,12},{12,8},{1,5},{5,1},{9,13},{13,9},{2,6},{6,2},{1... | collective-permute-start | bytes 393224 | tf_op jit(solution)/shard_map/ppermute | solution.py:387
  191.1 11.4 %collective-permute-start.33 = (bf16[256,256]{1,0:T(8,128)(2,1)S(1)}, bf16[256,256]{1,0:T(8,128)(2,1)S(1)}, u32[]{:S(2)}, u32[]{:S(2)}) collective-permute-start(bf16[256,256]{1,0:T(8,128)(2,1)S(1)} %shard_map.144.refs_0_), channel_id=1, source_target_pairs={{0,8},{4,12},{8,0},{12,4},{1,9},{5,13},{9,1},{13,5},{2,10},{6,14},... | collective-permute-start | bytes 393224 | tf_op jit(solution)/shard_map/ppermute | solution.py:387
  199.3 9.2 %collective-permute-start.41 = (bf16[256,256]{1,0:T(8,128)(2,1)S(1)}, bf16[256,256]{1,0:T(8,128)(2,1)S(1)}, u32[]{:S(2)}, u32[]{:S(2)}) collective-permute-start(bf16[256,256]{1,0:T(8,128)(2,1)S(1)} %shard_map.146.refs_0_), channel_id=1, source_target_pairs={{0,4},{4,0},{8,12},{12,8},{1,5},{5,1},{9,13},{13,9},{2,6},{6,2},{1... | collective-permute-start | bytes 393224 | tf_op jit(solution)/shard_map/ppermute | solution.py:387
  200.0 8.6 %collective-permute-start.42 = (bf16[256,256]{1,0:T(8,128)(2,1)S(1)}, bf16[256,256]{1,0:T(8,128)(2,1)S(1)}, u32[]{:S(2)}, u32[]{:S(2)}) collective-permute-start(bf16[256,256]{1,0:T(8,128)(2,1)S(1)} %shard_map.146.refs_0_), channel_id=1, source_target_pairs={{0,8},{4,12},{8,0},{12,4},{1,9},{5,13},{9,1},{13,5},{2,10},{6,14},... | collective-permute-start | bytes 393224 | tf_op jit(solution)/shard_map/ppermute | solution.py:387
  202.4 9.0 %collective-permute-start.34 = (bf16[256,256]{1,0:T(8,128)(2,1)S(1)}, bf16[256,256]{1,0:T(8,128)(2,1)S(1)}, u32[]{:S(2)}, u32[]{:S(2)}) collective-permute-start(bf16[256,256]{1,0:T(8,128)(2,1)S(1)} %collective-permute-done.33.refs_2_), channel_id=1, source_target_pairs={{0,4},{4,0},{8,12},{12,8},{1,5},{5,1},{9,13},{13,9},{2,6},{6,2},{1... | collective-permute-start | bytes 393224 | tf_op jit(solution)/shard_map/ppermute | solution.py:387
  208.6 5.0 %collective-permute-start.43 = (bf16[256,256]{1,0:T(8,128)(2,1)S(1)}, bf16[256,256]{1,0:T(8,128)(2,1)S(1)}, u32[]{:S(2)}, u32[]{:S(2)}) collective-permute-start(bf16[256,256]{1,0:T(8,128)(2,1)S(1)} %collective-permute-done.42.refs_2_), channel_id=1, source_target_pairs={{0,4},{4,0},{8,12},{12,8},{1,5},{5,1},{9,13},{13,9},{2,6},{6,2},{1... | collective-permute-start | bytes 393224 | tf_op jit(solution)/shard_map/ppermute | solution.py:387
  212.0 2.2 collective-permute-start.35
  214.1 1.5 collective-permute-start.44
  215.8 12.2 %collective-permute-start.45 = (bf16[128,768]{1,0:T(8,128)(2,1)S(1)}, bf16[128,768]{1,0:T(8,128)(2,1)S(1)}, u32[]{:S(2)}, u32[]{:S(2)}) collective-permute-start(bf16[128,768]{1,0:T(8,128)(2,1)S(1)} %get-tuple-element.80), channel_id=1, source_target_pairs={{0,8},{1,12},{2,0},{3,4},{4,9},{5,13},{6,1},{7,5},{8,10},{9,14},{1... | collective-permute-start | bytes 589832 | tf_op jit(solution)/shard_map/ppermute | solution.py:481
  216.4 14.9 %collective-permute-start.36 = (bf16[128,768]{1,0:T(8,128)(2,1)S(1)}, bf16[128,768]{1,0:T(8,128)(2,1)S(1)}, u32[]{:S(2)}, u32[]{:S(2)}) collective-permute-start(bf16[128,768]{1,0:T(8,128)(2,1)S(1)} %get-tuple-element.79), channel_id=1, source_target_pairs={{0,0},{1,4},{2,8},{3,12},{4,1},{5,5},{6,9},{7,13},{8,2},{9,6},{10,... | collective-permute-start | bytes 589832 | tf_op jit(solution)/shard_map/ppermute | solution.py:481
  (8 other events, 48.2 us)

commit v5 on v4

--- a/solution.py
+++ b/solution.py
@@ -287,9 +287,11 @@
     attend_rows(pair, start, pos_ref, q_ref, k_ref, v_ref, refs[:WAYS], refs[WAYS])
 
 
-def both_kernel(pair, pos_ref, query_gain_ref, key_gain_ref, *refs):
-    parts, panels, caches = refs[:WAYS], refs[WAYS : 3 * WAYS], refs[3 * WAYS : 4 * WAYS]
-    mixed_ref, panel_ref, held_ref, *outs, panel_sems, held_sems = refs[4 * WAYS :]
+def both_kernel(pair, places, pos_ref, query_gain_ref, key_gain_ref, *refs):
+    count = 2 * (1 + places[-1][0])
+    parts, panels, caches = refs[:count], refs[count : count + 2 * WAYS], refs[count + 2 * WAYS :]
+    caches, rest = caches[:WAYS], caches[WAYS:]
+    mixed_ref, panel_ref, held_ref, *outs, panel_sems, held_sems = rest
     copies = [
         pltpu.make_async_copy(source, panel_ref.at[i], panel_sems.at[i])
         for i, source in enumerate(panels)
@@ -302,7 +304,8 @@
         copy.start()
 
     def part(j, k):
-        return parts[2 * j + k // 2][k % 2]
+        at, inner = places[k]
+        return parts[j * count // 2 + at][inner]
 
     def panel(k, h):
         copies[2 * k + h].wait()
@@ -336,11 +339,11 @@
     )(pos, *qkv, *held)
 
 
-def mix_pair(pair, pos, gains, parts, panels, held):
+def mix_pair(pair, places, pos, gains, parts, panels, held):
     tile, head_dim = parts[0].shape[1], gains[0].shape[1]
     shape = (2 * tile, 2 * head_dim)
     return pl.pallas_call(
-        functools.partial(both_kernel, pair),
+        functools.partial(both_kernel, pair, places),
         out_shape=jax.ShapeDtypeStruct(shape, jnp.bfloat16),
         in_specs=[pl.BlockSpec(memory_space=pltpu.SMEM)]
         + whole_specs(2 + len(parts))
@@ -458,28 +461,45 @@
         near, far = lax.optimization_barrier((from_z(own, 1), from_z(own, 2)))
         return [own, near, far, from_z(far, 1)]
 
-    def summed(own):
-        mixed = gather_z(own)
+    def summed(mixed):
         keep, send = project_out(w_rows, mixed)
         return keep + lax.ppermute(send, "head", SWAP).astype(jnp.float32)
 
     qkv = project(source, gains, gathered, panels)
-    own = attend_pair(1, pos, qkv, held)
-    other = lax.ppermute(summed(own).astype(jnp.bfloat16), "fsdp", SWAP)
-    pos_late, _ = lax.optimization_barrier((pos, own))
-    update = summed(attend_pair(0, pos_late, qkv, held)) + other.astype(jnp.float32)
+    mixed = gather_z(attend_pair(1, pos, qkv, held))
+    pos_late, _ = lax.optimization_barrier((pos, mixed[0]))
+    late = gather_z(attend_pair(0, pos_late, qkv, held))
+    mixed[3], late[1], late[2] = lax.optimization_barrier((mixed[3], late[1], late[2]))
+    other = summed(mixed).astype(jnp.bfloat16)
+    other, late[3] = lax.optimization_barrier((other, late[3]))
+    other = lax.ppermute(other, "fsdp", SWAP)
+    update = summed(late) + other.astype(jnp.float32)
     x_share = (x_share.astype(jnp.float32) + gates[0] * update).astype(jnp.bfloat16)
 
-    parts = gather_pairs(gather_z(x_share))
-    ends = []
-    for pair in range(2):
-        own = mix_pair(pair, pos, gains, parts[4 * pair : 4 * pair + 4], panels, held)
-        value = gates[1] * summed(own)
-        if pair == 0:
-            value += x_share.astype(jnp.float32)
-        moves = [(a * WAYS + b, (b ^ (2 * pair)) * WAYS + a) for a in range(WAYS) for b in range(WAYS)]
-        ends.append(lax.ppermute(value.astype(jnp.bfloat16), ("cache", "fsdp", "head"), moves))
-    return (ends[0].astype(jnp.float32) + ends[1].astype(jnp.float32)).astype(jnp.bfloat16)
+    near, far, own_x = lax.optimization_barrier(
+        (from_z(x_share, 1), from_z(x_share, 2), lax.ppermute(x_share[None], "fsdp", SWAP))
+    )
+    last = from_z(far, 1)
+    by_z = [jnp.stack([x_share, near]), jnp.stack([far, last])]
+    by_z += [lax.ppermute(part, "head", SWAP) for part in by_z]
+    by_x = [own_x, *[lax.ppermute(v, "fsdp", SWAP) for v in (jnp.stack([near, far]), last[None])]]
+    own = mix_pair(0, ((0, 0), (0, 1), (1, 0), (1, 1)), pos, gains, by_z, panels, held)
+    first = gather_z(own)
+    by_x[1], by_x[2], first[0] = lax.optimization_barrier((by_x[1], by_x[2], first[0]))
+    by_x += [lax.ppermute(part, "head", SWAP) for part in by_x]
+    second = gather_z(
+        mix_pair(1, ((0, 0), (1, 0), (1, 1), (2, 0)), pos, gains, by_x, panels, held)
+    )
+    values = [x_share.astype(jnp.float32) + gates[1] * summed(first), gates[1] * summed(second)]
+    ends = [
+        lax.ppermute(
+            value.astype(jnp.bfloat16),
+            ("cache", "fsdp", "head"),
+            [(a * WAYS + b, (b ^ flip) * WAYS + a) for a in range(WAYS) for b in range(WAYS)],
+        ).astype(jnp.float32)
+        for value, flip in zip(values, (0, 2))
+    ]
+    return (ends[0] + ends[1]).astype(jnp.bfloat16)
 
 
 def solution(mesh):

time: 232 us -> 227 us (0.978)
  waiting for transfers between devices: 124 us -> 118 us
    ppermute x2 -> x1, waiting for transfers between devices: 11.9 us -> 5.97 us  [gather_pairs(): high_x = lax.ppermute(high, 'fsdp', SWAP)]
    ppermute x2 -> x1, waiting for transfers between devices: 5.77 us -> 0.01 us  [gather_pairs(): low_x = lax.ppermute(low, 'fsdp', SWAP)]
    ppermute x3 -> x11, waiting for transfers between devices: 17 us -> 21.5 us  [the longest x2 10.9 us: split_heads(): lax.ppermute(value.astype(jnp.bfloat16), ('cache', 'fsdp', 'head'), [(a *...]
    ppermute x3 -> x11, starting transfers between devices: 5.14 us -> 8.39 us  [the longest x2 4.21 us: split_heads(): lax.ppermute(value.astype(jnp.bfloat16), ('cache', 'fsdp', 'head'), [(a *...]
  transfers between devices with their start and end apart: 46 -> 48, of which waited for: 21 -> 23; matrix products, arithmetic and copies ran while one was open for 5% -> 5% of each run, Pallas kernels for 13% -> 13%
where the time goes in v5:
time: 227 us; the launch traced here: 226 us
  waiting for transfers between devices  118 us (52%)
  starting transfers between devices  56.5 us (25%)
  Pallas kernels  32.1 us (14%)
  local copies, waits for them, and re-layouts  13.3 us (6%)
  other arithmetic  5.9 us (3%)
    ppermute x24, waiting for transfers between devices, from_z(): return lax.ppermute(value, 'cache', [(i, i ^ k) for i in range(WAYS)])  64.1 us
    ppermute x24, starting transfers between devices, from_z(): return lax.ppermute(value, 'cache', [(i, i ^ k) for i in range(WAYS)])  41.4 us
    ppermute x3, waiting for transfers between devices, split_heads(): far = {k: lax.ppermute(near[k], 'groups', SWAP) for k in order}  24.5 us
    pallas_call x2, Pallas kernels, mix_pair(): pl.pallas_call(functools.partial(both_kernel, pair, places), out_shape=ja...  13.2 us
    ppermute x2, waiting for transfers between devices, split_heads(): lax.ppermute(value.astype(jnp.bfloat16), ('cache', 'fsdp', 'head'), [(a *...  10.9 us
    ppermute x2, waiting for transfers between devices, split_heads(): lax.ppermute(v, 'fsdp', SWAP)  6.67 us
    unnamed x61, local copies, waits for them, and re-layouts  6.61 us
    ppermute x1, waiting for transfers between devices, gather_pairs(): high_x = lax.ppermute(high, 'fsdp', SWAP)  5.97 us
  transfers between devices with their start and end apart: 48, of which 23 were waited for; matrix products, arithmetic and copies ran while one was open for 5% of the time, Pallas kernels for 13%

profile of v5, /device:TPU:2, one launch (start us, length us, event | category | flops | bytes accessed | tf_op | source)
XLA Modules:
  0.0 226.1 jit_solution(2528764923500498623)
XLA Ops:
  0.0 1.8 constant_dynamic-update-slice_fusion.9
  1.8 1.6 collective-permute-start
  3.4 2.6 %collective-permute-start.1 = (bf16[128,768]{1,0:T(8,128)(2,1)}, bf16[128,768]{1,0:T(8,128)(2,1)}, u32[]{:S(2)}, u32[]{:S(2)}) collective-permute-start(bf16[128,768]{1,0:T(8,128)(2,1)} %get-tuple-element.94), channel_id=1, source_target_pairs={{0,8},{4,12},{8,0},{12,4},{1,9},{5,13},{9,1},{13,5},{2,10},{6,14},... | collective-permute-start | bytes 589832 | tf_op jit(solution)/shard_map/ppermute | solution.py:390
  6.0 0.8 dynamic_slice.16
  7.0 3.1 %shard_map.137 = (bf16[768,384]{1,0:T(8,128)(2,1)}, bf16[768,384]{1,0:T(8,128)(2,1)}, bf16[768,384]{1,0:T(8,128)(2,1)}, f32[8,128]{1,0:T(8,128)}) custom-call(f32[768,128]{1,0:T(8,128)S(1)} %broadcast_in_dim.71.gain_ref, bf16[768,1024]{1,0:T(8,128)(2,1)} %refs_0_.3, bf16[768,1024]{1,0:T(8,128)(2,1)} %refs_1_.3, bf16[768,1024]{1,0:T(8,128)(2,1)} %refs_2_.3), custom_call_target="tpu_custom_call" | custom-call | tf_op jit(solution)/shard_map/pallas_call | solution.py:173
  10.9 3.6 %collective-permute-start.13 = (bf16[768,384]{1,0:T(8,128)(2,1)}, bf16[768,384]{1,0:T(8,128)(2,1)S(1)}, u32[]{:S(2)}, u32[]{:S(2)}) collective-permute-start(bf16[768,384]{1,0:T(8,128)(2,1)} %get-tuple-element.52), channel_id=1, source_target_pairs={{0,12},{4,8},{8,4},{12,0},{1,13},{5,9},{9,5},{13,1},{2,14},{6,10},... | collective-permute-start | bytes 1769480 | tf_op jit(solution)/shard_map/ppermute | solution.py:390
  16.0 1.0 copy-done.18
  17.0 2.0 shard_map.136
  19.0 0.8 copy-done.8
  19.9 0.8 copy-done.10
  22.7 1.8 gather_fusion
  24.5 1.9 shard_map.139
  26.5 1.2 pad_maximum_fusion
  28.3 26.7 %collective-permute-done.2 = bf16[128,768]{1,0:T(8,128)(2,1)S(1)} collective-permute-done((bf16[128,768]{1,0:T(8,128)(2,1)}, bf16[128,768]{1,0:T(8,128)(2,1)S(1)}, u32[]{:S(2)}, u32[]{:S(2)}) %collective-permute-start.2) | collective-permute-done | bytes 196640 | tf_op jit(solution)/shard_map/ppermute | solution.py:390
  55.0 1.0 pad_maximum_fusion.1
  56.5 0.9 constant_dynamic-update-slice_fusion.8
  58.2 1.7 collective-permute-start.10
  59.8 6.0 %collective-permute-done.6 = bf16[2,128,768]{2,1,0:T(8,128)(2,1)S(1)} collective-permute-done((bf16[2,128,768]{2,1,0:T(8,128)(2,1)S(1)}, bf16[2,128,768]{2,1,0:T(8,128)(2,1)S(1)}, u32[]{:S(2)}, u32[]{:S(2)}) %collective-permute-start.6) | collective-permute-done | bytes 393248 | tf_op jit(solution)/shard_map/ppermute | solution.py:422
  65.8 0.9 constant_dynamic-update-slice_fusion.7
  66.8 2.2 collective-permute-start.15
  69.0 2.4 %collective-permute-start.16 = (bf16[512,512]{1,0:T(8,128)(2,1)S(1)}, bf16[512,512]{1,0:T(8,128)(2,1)S(1)}, u32[]{:S(2)}, u32[]{:S(2)}) collective-permute-start(bf16[512,512]{1,0:T(8,128)(2,1)S(1)} %get-tuple-element.60), channel_id=1, source_target_pairs={{0,8},{4,12},{8,0},{12,4},{1,9},{5,13},{9,1},{13,5},{2,10},{6,14},... | collective-permute-start | bytes 1572872 | tf_op jit(solution)/shard_map/ppermute | solution.py:390
  71.6 1.4 collective-permute-start.12
  73.1 0.8 collective-permute-done.10.refs_3_.refs_7_.refs_9_
  73.8 1.7 collective-permute-start.14
  75.7 12.1 %collective-permute-done.12.refs_5_.refs_9_.refs_11_ = bf16[768,384]{1,0:T(8,128)(2,1)S(1)} collective-permute-done((bf16[768,384]{1,0:T(8,128)(2,1)S(1)}, bf16[768,384]{1,0:T(8,128)(2,1)S(1)}, u32[]{:S(2)}, u32[]{:S(2)}) %collective-permute-start.12) | collective-permute-done | bytes 589856 | tf_op jit(solution)/shard_map/ppermute | solution.py:439
  87.8 11.6 %collective-permute-done.14.refs_7_.refs_11_.refs_13_ = bf16[768,384]{1,0:T(8,128)(2,1)S(1)} collective-permute-done((bf16[768,384]{1,0:T(8,128)(2,1)S(1)}, bf16[768,384]{1,0:T(8,128)(2,1)S(1)}, u32[]{:S(2)}, u32[]{:S(2)}) %collective-permute-start.14) | collective-permute-done | bytes 589856 | tf_op jit(solution)/shard_map/ppermute | solution.py:439
  99.5 4.3 %shard_map.138 = (bf16[512,256]{1,0:T(8,128)(2,1)S(1)}, bf16[512,256]{1,0:T(8,128)(2,1)S(1)}, bf16[512,256]{1,0:T(8,128)(2,1)S(1)}) custom-call(s32[16]{0:T(128)S(1)} %add.171.source_ref, f32[1,128]{1,0:T(1,128)S(1)} %bitcast.41, f32[1,128]{1,0:T(1,128)S(1)} %bitcast.44, bf16[16,128,768]{2,1,0:T(8,128)(2,1)S(1)} %constant_dynamic-update-slice_fusion.gathered_ref, ...), custom_call_target="tpu_custom_call" | custom-call | tf_op jit(solution)/shard_map/pallas_call | solution.py:322
  103.9 3.3 %collective-permute-done.16.refs_2_.refs_14_.refs_16_ = bf16[512,512]{1,0:T(8,128)(2,1)S(1)} collective-permute-done((bf16[512,512]{1,0:T(8,128)(2,1)S(1)}, bf16[512,512]{1,0:T(8,128)(2,1)S(1)}, u32[]{:S(2)}, u32[]{:S(2)}) %collective-permute-start.16) | collective-permute-done | bytes 524320 | tf_op jit(solution)/shard_map/ppermute | solution.py:390
  107.2 2.3 %shard_map.140.refs_0_ = bf16[256,256]{1,0:T(8,128)(2,1)S(1)} custom-call(s32[16]{0:T(128)S(1)} %reshape.272.pos_ref, bf16[512,256]{1,0:T(8,128)(2,1)S(1)} %get-tuple-element.53.q_ref, bf16[512,256]{1,0:T(8,128)(2,1)S(1)} %get-tuple-element.54.k_ref, bf16[512,256]{1,0:T(8,128)(2,1)S(1)} %get-tuple-element.55.v_ref, ...), custom_call_target="tpu_custom_call" | custom-call | tf_op jit(solution)/shard_map/pallas_call | solution.py:333
  109.5 11.2 %collective-permute-start.18 = (bf16[256,256]{1,0:T(8,128)(2,1)S(1)}, bf16[256,256]{1,0:T(8,128)(2,1)S(1)}, u32[]{:S(2)}, u32[]{:S(2)}) collective-permute-start(bf16[256,256]{1,0:T(8,128)(2,1)S(1)} %shard_map.140.refs_0_), channel_id=1, source_target_pairs={{0,4},{4,0},{8,12},{12,8},{1,5},{5,1},{9,13},{13,9},{2,6},{6,2},{1... | collective-permute-start | bytes 393224 | tf_op jit(solution)/shard_map/ppermute | solution.py:390
  120.7 1.1 collective-permute-start.19
  121.8 2.3 %shard_map.141.refs_0_ = bf16[256,256]{1,0:T(8,128)(2,1)S(1)} custom-call(s32[16]{0:T(128)S(1)} %reshape.272.pos_ref, bf16[512,256]{1,0:T(8,128)(2,1)S(1)} %get-tuple-element.53.q_ref, bf16[512,256]{1,0:T(8,128)(2,1)S(1)} %get-tuple-element.54.k_ref, bf16[512,256]{1,0:T(8,128)(2,1)S(1)} %get-tuple-element.55.v_ref, ...), custom_call_target="tpu_custom_call" | custom-call | tf_op jit(solution)/shard_map/pallas_call | solution.py:333
  124.1 2.0 collective-permute-start.21
  126.1 1.5 collective-permute-done.19.refs_2_
  127.6 3.4 %collective-permute-start.20 = (bf16[256,256]{1,0:T(8,128)(2,1)S(1)}, bf16[256,256]{1,0:T(8,128)(2,1)S(1)}, u32[]{:S(2)}, u32[]{:S(2)}) collective-permute-start(bf16[256,256]{1,0:T(8,128)(2,1)S(1)} %collective-permute-done.19.refs_2_), channel_id=1, source_target_pairs={{0,4},{4,0},{8,12},{12,8},{1,5},{5,1},{9,13},{13,9},{2,6},{6,2},{1... | collective-permute-start | bytes 393224 | tf_op jit(solution)/shard_map/ppermute | solution.py:390
  131.4 1.2 collective-permute-done.21.refs_1_
  132.6 1.2 collective-permute-done.22.refs_2_
  133.8 1.6 collective-permute-done.20.refs_3_
  136.1 1.4 collective-permute-start.24
  137.5 0.7 add_convert_fusion.2
  138.2 3.8 %collective-permute-done.24.refs_3_ = bf16[256,256]{1,0:T(8,128)(2,1)S(1)} collective-permute-done((bf16[256,256]{1,0:T(8,128)(2,1)S(1)}, bf16[256,256]{1,0:T(8,128)(2,1)S(1)}, u32[]{:S(2)}, u32[]{:S(2)}) %collective-permute-start.24) | collective-permute-done | bytes 131104 | tf_op jit(solution)/shard_map/ppermute | solution.py:390
  142.5 1.3 shard_map.143
  143.9 0.9 dynamic-slice_reduce_fusion
  144.8 4.0 %collective-permute-done.26 = bf16[128,768]{1,0:T(8,128)(2,1)} collective-permute-done((bf16[128,768]{1,0:T(8,128)(2,1)}, bf16[128,768]{1,0:T(8,128)(2,1)}, u32[]{:S(2)}, u32[]{:S(2)}) %collective-permute-start.26) | collective-permute-done | bytes 196640 | tf_op jit(solution)/shard_map/ppermute | solution.py:475
  148.8 1.2 fusion
  150.0 1.4 collective-permute-start.27
  151.4 2.0 collective-permute-start.28
  153.9 5.7 %collective-permute-done.27 = bf16[128,768]{1,0:T(8,128)(2,1)S(1)} collective-permute-done((bf16[128,768]{1,0:T(8,128)(2,1)S(1)}, bf16[128,768]{1,0:T(8,128)(2,1)S(1)}, u32[]{:S(2)}, u32[]{:S(2)}) %collective-permute-start.27) | collective-permute-done | bytes 196640 | tf_op jit(solution)/shard_map/ppermute | solution.py:390
  159.6 2.4 %collective-permute-done.28 = bf16[128,768]{1,0:T(8,128)(2,1)S(1)} collective-permute-done((bf16[128,768]{1,0:T(8,128)(2,1)S(1)}, bf16[128,768]{1,0:T(8,128)(2,1)S(1)}, u32[]{:S(2)}, u32[]{:S(2)}) %collective-permute-start.28) | collective-permute-done | bytes 196640 | tf_op jit(solution)/shard_map/ppermute | solution.py:390
  162.2 5.5 %collective-permute-done.31 = bf16[128,768]{1,0:T(8,128)(2,1)S(1)} collective-permute-done((bf16[128,768]{1,0:T(8,128)(2,1)S(1)}, bf16[128,768]{1,0:T(8,128)(2,1)S(1)}, u32[]{:S(2)}, u32[]{:S(2)}) %collective-permute-start.31) | collective-permute-done | bytes 196640 | tf_op jit(solution)/shard_map/ppermute | solution.py:390
  168.8 1.5 collective-permute-start.32
  170.3 6.6 %shard_map.144.refs_0_ = bf16[256,256]{1,0:T(8,128)(2,1)S(1)} custom-call(s32[16]{0:T(128)S(1)} %reshape.272.pos_ref, f32[1,128]{1,0:T(1,128)S(1)} %bitcast.42, f32[1,128]{1,0:T(1,128)S(1)} %bitcast.45, bf16[2,128,768]{2,1,0:T(8,128)(2,1)S(1)} %get-tuple-element.99.refs_0_, bf16[2,128,768]{2,1,0:T(8,128)(2,1)S(1)} %get-tuple-element.97.refs_1_, ...), custom_call_target="tpu_custom_call" | custom-call | tf_op jit(solution)/shard_map/pallas_call | solution.py:345
  176.9 6.7 %collective-permute-done.32.refs_2_ = bf16[1,128,768]{2,1,0:T(8,128)(2,1)S(1)} collective-permute-done((bf16[1,128,768]{2,1,0:T(8,128)(2,1)S(1)}, bf16[1,128,768]{2,1,0:T(8,128)(2,1)S(1)}, u32[]{:S(2)}, u32[]{:S(2)}) %collective-permute-start.32) | collective-permute-done | bytes 196640 | tf_op jit(solution)/shard_map/ppermute | solution.py:485
  184.3 2.7 %collective-permute-start.36 = (bf16[256,256]{1,0:T(8,128)(2,1)S(1)}, bf16[256,256]{1,0:T(8,128)(2,1)S(1)}, u32[]{:S(2)}, u32[]{:S(2)}) collective-permute-start(bf16[256,256]{1,0:T(8,128)(2,1)S(1)} %shard_map.144.refs_0_), channel_id=1, source_target_pairs={{0,8},{4,12},{8,0},{12,4},{1,9},{5,13},{9,1},{13,5},{2,10},{6,14},... | collective-permute-start | bytes 393224 | tf_op jit(solution)/shard_map/ppermute | solution.py:390
  187.1 6.6 %shard_map.146.refs_0_ = bf16[256,256]{1,0:T(8,128)(2,1)S(1)} custom-call(s32[16]{0:T(128)S(1)} %reshape.272.pos_ref, f32[1,128]{1,0:T(1,128)S(1)} %bitcast.43, f32[1,128]{1,0:T(1,128)S(1)} %bitcast.46, bf16[1,128,768]{2,1,0:T(8,128)(2,1)S(1)} %collective-permute-done.29.refs_0_, bf16[2,128,768]{2,1,0:T(8,128)(2,1)S(1)} %collective-permute-done.30.refs_1_, ...), custom_call_target="tpu_custom_call" | custom-call | tf_op jit(solution)/shard_map/pallas_call | solution.py:345
  193.8 2.0 collective-permute-start.44
  196.0 6.6 %collective-permute-done.43.refs_1_ = bf16[256,256]{1,0:T(8,128)(2,1)S(1)} collective-permute-done((bf16[256,256]{1,0:T(8,128)(2,1)S(1)}, bf16[256,256]{1,0:T(8,128)(2,1)S(1)}, u32[]{:S(2)}, u32[]{:S(2)}) %collective-permute-start.43) | collective-permute-done | bytes 131104 | tf_op jit(solution)/shard_map/ppermute | solution.py:390
  203.2 2.2 collective-permute-done.37.refs_3_
  206.0 2.0 collective-permute-done.45.refs_3_
  208.7 1.4 collective-permute-done.46
  210.9 3.6 %collective-permute-start.39 = (bf16[128,768]{1,0:T(8,128)(2,1)S(1)}, bf16[128,768]{1,0:T(8,128)(2,1)S(1)}, u32[]{:S(2)}, u32[]{:S(2)}) collective-permute-start(bf16[128,768]{1,0:T(8,128)(2,1)S(1)} %get-tuple-element.100), channel_id=1, source_target_pairs={{0,0},{1,4},{2,8},{3,12},{4,1},{5,5},{6,9},{7,13},{8,2},{9,6},{10,... | collective-permute-start | bytes 589832 | tf_op jit(solution)/shard_map/ppermute | solution.py:495
  214.5 6.8 %collective-permute-done.47 = bf16[128,768]{1,0:T(8,128)(2,1)S(1)} collective-permute-done((bf16[128,768]{1,0:T(8,128)(2,1)S(1)}, bf16[128,768]{1,0:T(8,128)(2,1)S(1)}, u32[]{:S(2)}, u32[]{:S(2)}) %collective-permute-start.47) | collective-permute-done | bytes 196640 | tf_op jit(solution)/shard_map/ppermute | solution.py:495
  221.3 4.1 %collective-permute-done.39 = bf16[128,768]{1,0:T(8,128)(2,1)S(1)} collective-permute-done((bf16[128,768]{1,0:T(8,128)(2,1)S(1)}, bf16[128,768]{1,0:T(8,128)(2,1)S(1)}, u32[]{:S(2)}, u32[]{:S(2)}) %collective-permute-start.39) | collective-permute-done | bytes 196640 | tf_op jit(solution)/shard_map/ppermute | solution.py:495
  225.3 0.7 add_convert_fusion
  (146 shorter events, 13.8 us)
Async XLA Ops:
  1.8 24.6 %collective-permute-start = (bf16[128,768]{1,0:T(8,128)(2,1)}, bf16[128,768]{1,0:T(8,128)(2,1)}, u32[]{:S(2)}, u32[]{:S(2)}) collective-permute-start(bf16[128,768]{1,0:T(8,128)(2,1)} %get-tuple-element.94), channel_id=1, source_target_pairs={{0,4},{4,0},{8,12},{12,8},{1,5},{5,1},{9,13},{13,9},{2,6},{6,2},{1... | collective-permute-start | bytes 589832 | tf_op jit(solution)/shard_map/ppermute | solution.py:390
  3.4 19.2 %collective-permute-start.1 = (bf16[128,768]{1,0:T(8,128)(2,1)}, bf16[128,768]{1,0:T(8,128)(2,1)}, u32[]{:S(2)}, u32[]{:S(2)}) collective-permute-start(bf16[128,768]{1,0:T(8,128)(2,1)} %get-tuple-element.94), channel_id=1, source_target_pairs={{0,8},{4,12},{8,0},{12,4},{1,9},{5,13},{9,1},{13,5},{2,10},{6,14},... | collective-permute-start | bytes 589832 | tf_op jit(solution)/shard_map/ppermute | solution.py:390
  10.0 47.5 %collective-permute-start.9 = (bf16[768,384]{1,0:T(8,128)(2,1)}, bf16[768,384]{1,0:T(8,128)(2,1)S(1)}, u32[]{:S(2)}, u32[]{:S(2)}) collective-permute-start(bf16[768,384]{1,0:T(8,128)(2,1)} %get-tuple-element.50), channel_id=1, source_target_pairs={{0,4},{4,0},{8,12},{12,8},{1,5},{5,1},{9,13},{13,9},{2,6},{6,2},{1... | collective-permute-start | bytes 1769480 | tf_op jit(solution)/shard_map/ppermute | solution.py:390
  10.6 47.5 %collective-permute-start.11 = (bf16[768,384]{1,0:T(8,128)(2,1)}, bf16[768,384]{1,0:T(8,128)(2,1)S(1)}, u32[]{:S(2)}, u32[]{:S(2)}) collective-permute-start(bf16[768,384]{1,0:T(8,128)(2,1)} %get-tuple-element.51), channel_id=1, source_target_pairs={{0,8},{4,12},{8,0},{12,4},{1,9},{5,13},{9,1},{13,5},{2,10},{6,14},... | collective-permute-start | bytes 1769480 | tf_op jit(solution)/shard_map/ppermute | solution.py:390
  10.9 47.3 %collective-permute-start.13 = (bf16[768,384]{1,0:T(8,128)(2,1)}, bf16[768,384]{1,0:T(8,128)(2,1)S(1)}, u32[]{:S(2)}, u32[]{:S(2)}) collective-permute-start(bf16[768,384]{1,0:T(8,128)(2,1)} %get-tuple-element.52), channel_id=1, source_target_pairs={{0,12},{4,8},{8,4},{12,0},{1,13},{5,9},{9,5},{13,1},{2,14},{6,10},... | collective-permute-start | bytes 1769480 | tf_op jit(solution)/shard_map/ppermute | solution.py:390
  22.6 32.4 %collective-permute-start.2 = (bf16[128,768]{1,0:T(8,128)(2,1)}, bf16[128,768]{1,0:T(8,128)(2,1)S(1)}, u32[]{:S(2)}, u32[]{:S(2)}) collective-permute-start(bf16[128,768]{1,0:T(8,128)(2,1)} %collective-permute-done.1), channel_id=1, source_target_pairs={{0,4},{4,0},{8,12},{12,8},{1,5},{5,1},{9,13},{13,9},{2,6},{6,2},{1... | collective-permute-start | bytes 589832 | tf_op jit(solution)/shard_map/ppermute | solution.py:390
  24.5 32.0 %copy-start.25 = (s32[8]{0:T(128)S(1)}, s32[8]{0:T(128)}, u32[]{:S(2)}) copy-start(s32[8]{0:T(128)} %reshape.269) | copy-start | bytes 100
  24.5 32.0 %copy-start.15 = (bf16[16,128,768]{2,1,0:T(8,128)(2,1)S(1)}, bf16[16,128,768]{2,1,0:T(8,128)(2,1)}, u32[]{:S(2)}) copy-start(bf16[16,128,768]{2,1,0:T(8,128)(2,1)} %get-tuple-element.93) | copy-start | bytes 9437188
  26.5 95.4 %copy-start.1 = (bf16[512,512]{1,0:T(8,128)(2,1)}, bf16[512,512]{1,0:T(8,128)(2,1)S(1)}, u32[]{:S(2)}) copy-start(bf16[512,512]{1,0:T(8,128)(2,1)S(1)} %get-tuple-element.56.refs_0_.refs_12_.refs_14_) | copy-start | bytes 1572868
  27.7 29.7 %collective-permute-start.5 = (bf16[2,128,768]{2,1,0:T(8,128)(2,1)S(1)}, bf16[2,128,768]{2,1,0:T(8,128)(2,1)S(1)}, u32[]{:S(2)}, u32[]{:S(2)}) collective-permute-start(bf16[2,128,768]{2,1,0:T(8,128)(2,1)S(1)} %pad_maximum_fusion), channel_id=1, source_target_pairs={{0,2},{2,0},{1,3},{3,1},{4,6},{6,4},{5,7},{7,5},{8,10},{10,8},{9,1... | collective-permute-start | bytes 1179656 | tf_op jit(solution)/shard_map/ppermute | solution.py:420
  56.0 43.4 %copy-start.9 = (bf16[768,384]{1,0:T(8,128)(2,1)S(1)}, bf16[768,384]{1,0:T(8,128)(2,1)}, u32[]{:S(2)}) copy-start(bf16[768,384]{1,0:T(8,128)(2,1)} %copy-done.8) | copy-start | bytes 1769476
  56.0 43.4 %copy-start.11 = (bf16[768,384]{1,0:T(8,128)(2,1)S(1)}, bf16[768,384]{1,0:T(8,128)(2,1)}, u32[]{:S(2)}) copy-start(bf16[768,384]{1,0:T(8,128)(2,1)} %copy-done.10) | copy-start | bytes 1769476
  56.0 43.4 %copy-start.19 = (f32[128]{0:T(128)S(1)}, f32[128]{0:T(128)}, u32[]{:S(2)}) copy-start(f32[128]{0:T(128)} %param.20) | copy-start | bytes 1540
  56.0 43.4 %copy-start.20 = (f32[128]{0:T(128)S(1)}, f32[128]{0:T(128)}, u32[]{:S(2)}) copy-start(f32[128]{0:T(128)} %param.21) | copy-start | bytes 1540
  56.1 9.8 %collective-permute-start.6 = (bf16[2,128,768]{2,1,0:T(8,128)(2,1)S(1)}, bf16[2,128,768]{2,1,0:T(8,128)(2,1)S(1)}, u32[]{:S(2)}, u32[]{:S(2)}) collective-permute-start(bf16[2,128,768]{2,1,0:T(8,128)(2,1)S(1)} %pad_maximum_fusion.1), channel_id=1, source_target_pairs={{0,2},{2,0},{1,3},{3,1},{4,6},{6,4},{5,7},{7,5},{8,10},{10,8},{9,1... | collective-permute-start | bytes 1179656 | tf_op jit(solution)/shard_map/ppermute | solution.py:422
  57.5 9.3 %collective-permute-start.3 = (bf16[2,128,768]{2,1,0:T(8,128)(2,1)S(1)}, bf16[2,128,768]{2,1,0:T(8,128)(2,1)S(1)}, u32[]{:S(2)}, u32[]{:S(2)}) collective-permute-start(bf16[2,128,768]{2,1,0:T(8,128)(2,1)S(1)} %pad_maximum_fusion), channel_id=1, source_target_pairs={{0,1},{1,0},{2,3},{3,2},{4,5},{5,4},{6,7},{7,6},{8,9},{9,8},{10,11... | collective-permute-start | bytes 1179656 | tf_op jit(solution)/shard_map/ppermute | solution.py:424
  57.6 46.2 %copy-start.5 = (bf16[768,384]{1,0:T(8,128)(2,1)}, bf16[768,384]{1,0:T(8,128)(2,1)S(1)}, u32[]{:S(2)}) copy-start(bf16[768,384]{1,0:T(8,128)(2,1)S(1)} %collective-permute-done.9.refs_2_.refs_6_.refs_8_) | copy-start | bytes 1769476
  57.6 11.4 %collective-permute-start.4 = (bf16[2,128,768]{2,1,0:T(8,128)(2,1)S(1)}, bf16[2,128,768]{2,1,0:T(8,128)(2,1)S(1)}, u32[]{:S(2)}, u32[]{:S(2)}) collective-permute-start(bf16[2,128,768]{2,1,0:T(8,128)(2,1)S(1)} %pad_maximum_fusion.1), channel_id=1, source_target_pairs={{0,1},{1,0},{2,3},{3,2},{4,5},{5,4},{6,7},{7,6},{8,9},{9,8},{10,11... | collective-permute-start | bytes 1179656 | tf_op jit(solution)/shard_map/ppermute | solution.py:424
  58.1 45.7 %copy-start.6 = (bf16[768,384]{1,0:T(8,128)(2,1)}, bf16[768,384]{1,0:T(8,128)(2,1)S(1)}, u32[]{:S(2)}) copy-start(bf16[768,384]{1,0:T(8,128)(2,1)S(1)} %collective-permute-done.11.refs_4_.refs_8_.refs_10_) | copy-start | bytes 1769476
  58.1 13.4 %collective-permute-start.7 = (bf16[2,128,768]{2,1,0:T(8,128)(2,1)S(1)}, bf16[2,128,768]{2,1,0:T(8,128)(2,1)S(1)}, u32[]{:S(2)}, u32[]{:S(2)}) collective-permute-start(bf16[2,128,768]{2,1,0:T(8,128)(2,1)S(1)} %collective-permute-done.5), channel_id=1, source_target_pairs={{0,1},{1,0},{2,3},{3,2},{4,5},{5,4},{6,7},{7,6},{8,9},{9,8},{10,11... | collective-permute-start | bytes 1179656 | tf_op jit(solution)/shard_map/ppermute | solution.py:424
  58.2 45.7 %copy-start.7 = (bf16[768,384]{1,0:T(8,128)(2,1)}, bf16[768,384]{1,0:T(8,128)(2,1)S(1)}, u32[]{:S(2)}) copy-start(bf16[768,384]{1,0:T(8,128)(2,1)S(1)} %collective-permute-done.13.refs_6_.refs_10_.refs_12_) | copy-start | bytes 1769476
  58.2 15.7 %collective-permute-start.10 = (bf16[768,384]{1,0:T(8,128)(2,1)S(1)}, bf16[768,384]{1,0:T(8,128)(2,1)S(1)}, u32[]{:S(2)}, u32[]{:S(2)}) collective-permute-start(bf16[768,384]{1,0:T(8,128)(2,1)S(1)} %collective-permute-done.9.refs_2_.refs_6_.refs_8_), channel_id=1, source_target_pairs={{0,16},{16,0},{1,17},{17,1},{2,18},{18,2},{3,19},{19,3},{4,20},{20... | collective-permute-start | bytes 1769480 | tf_op jit(solution)/shard_map/ppermute | solution.py:439
  65.8 5.8 %collective-permute-start.8 = (bf16[2,128,768]{2,1,0:T(8,128)(2,1)S(1)}, bf16[2,128,768]{2,1,0:T(8,128)(2,1)S(1)}, u32[]{:S(2)}, u32[]{:S(2)}) collective-permute-start(bf16[2,128,768]{2,1,0:T(8,128)(2,1)S(1)} %collective-permute-done.6), channel_id=1, source_target_pairs={{0,1},{1,0},{2,3},{3,2},{4,5},{5,4},{6,7},{7,6},{8,9},{9,8},{10,11... | collective-permute-start | bytes 1179656 | tf_op jit(solution)/shard_map/ppermute | solution.py:424
  66.8 37.1 %collective-permute-start.15 = (bf16[512,512]{1,0:T(8,128)(2,1)S(1)}, bf16[512,512]{1,0:T(8,128)(2,1)S(1)}, u32[]{:S(2)}, u32[]{:S(2)}) collective-permute-start(bf16[512,512]{1,0:T(8,128)(2,1)S(1)} %get-tuple-element.58), channel_id=1, source_target_pairs={{0,4},{4,0},{8,12},{12,8},{1,5},{5,1},{9,13},{13,9},{2,6},{6,2},{1... | collective-permute-start | bytes 1572872 | tf_op jit(solution)/shard_map/ppermute | solution.py:390
  69.0 38.2 %collective-permute-start.16 = (bf16[512,512]{1,0:T(8,128)(2,1)S(1)}, bf16[512,512]{1,0:T(8,128)(2,1)S(1)}, u32[]{:S(2)}, u32[]{:S(2)}) collective-permute-start(bf16[512,512]{1,0:T(8,128)(2,1)S(1)} %get-tuple-element.60), channel_id=1, source_target_pairs={{0,8},{4,12},{8,0},{12,4},{1,9},{5,13},{9,1},{13,5},{2,10},{6,14},... | collective-permute-start | bytes 1572872 | tf_op jit(solution)/shard_map/ppermute | solution.py:390
  71.4 35.8 %collective-permute-start.17 = (bf16[512,512]{1,0:T(8,128)(2,1)S(1)}, bf16[512,512]{1,0:T(8,128)(2,1)S(1)}, u32[]{:S(2)}, u32[]{:S(2)}) collective-permute-start(bf16[512,512]{1,0:T(8,128)(2,1)S(1)} %get-tuple-element.62), channel_id=1, source_target_pairs={{0,12},{4,8},{8,4},{12,0},{1,13},{5,9},{9,5},{13,1},{2,14},{6,10},... | collective-permute-start | bytes 1572872 | tf_op jit(solution)/shard_map/ppermute | solution.py:390
  71.6 16.2 %collective-permute-start.12 = (bf16[768,384]{1,0:T(8,128)(2,1)S(1)}, bf16[768,384]{1,0:T(8,128)(2,1)S(1)}, u32[]{:S(2)}, u32[]{:S(2)}) collective-permute-start(bf16[768,384]{1,0:T(8,128)(2,1)S(1)} %collective-permute-done.11.refs_4_.refs_8_.refs_10_), channel_id=1, source_target_pairs={{0,16},{16,0},{1,17},{17,1},{2,18},{18,2},{3,19},{19,3},{4,20},{20... | collective-permute-start | bytes 1769480 | tf_op jit(solution)/shard_map/ppermute | solution.py:439
  73.8 30.0 %copy-start.12 = (bf16[768,384]{1,0:T(8,128)(2,1)}, bf16[768,384]{1,0:T(8,128)(2,1)S(1)}, u32[]{:S(2)}) copy-start(bf16[768,384]{1,0:T(8,128)(2,1)S(1)} %collective-permute-done.10.refs_3_.refs_7_.refs_9_) | copy-start | bytes 1769476
  73.8 25.6 %collective-permute-start.14 = (bf16[768,384]{1,0:T(8,128)(2,1)S(1)}, bf16[768,384]{1,0:T(8,128)(2,1)S(1)}, u32[]{:S(2)}, u32[]{:S(2)}) collective-permute-start(bf16[768,384]{1,0:T(8,128)(2,1)S(1)} %collective-permute-done.13.refs_6_.refs_10_.refs_12_), channel_id=1, source_target_pairs={{0,16},{16,0},{1,17},{17,1},{2,18},{18,2},{3,19},{19,3},{4,20},{20... | collective-permute-start | bytes 1769480 | tf_op jit(solution)/shard_map/ppermute | solution.py:439
  75.7 28.1 %copy-start.16 = (bf16[16,128,768]{2,1,0:T(8,128)(2,1)}, bf16[16,128,768]{2,1,0:T(8,128)(2,1)S(1)}, u32[]{:S(2)}) copy-start(bf16[16,128,768]{2,1,0:T(8,128)(2,1)S(1)} %constant_dynamic-update-slice_fusion.gathered_ref) | copy-start | bytes 9437188
  103.9 27.2 %copy-start.23 = (bf16[8,128,768]{2,1,0:T(8,128)(2,1)S(1)}, bf16[8,128,768]{2,1,0:T(8,128)(2,1)}, u32[]{:S(2)}) copy-start(bf16[8,128,768]{2,1,0:T(8,128)(2,1)} %gather_fusion) | copy-start | bytes 4718596
  103.9 27.5 %copy-start.2 = (bf16[512,512]{1,0:T(8,128)(2,1)}, bf16[512,512]{1,0:T(8,128)(2,1)S(1)}, u32[]{:S(2)}) copy-start(bf16[512,512]{1,0:T(8,128)(2,1)S(1)} %collective-permute-done.15.refs_1_.refs_13_.refs_15_) | copy-start | bytes 1572868
  107.2 24.1 %copy-start.3 = (bf16[512,512]{1,0:T(8,128)(2,1)}, bf16[512,512]{1,0:T(8,128)(2,1)S(1)}, u32[]{:S(2)}) copy-start(bf16[512,512]{1,0:T(8,128)(2,1)S(1)} %collective-permute-done.16.refs_2_.refs_14_.refs_16_) | copy-start | bytes 1572868
  107.2 24.1 %copy-start.4 = (bf16[512,512]{1,0:T(8,128)(2,1)}, bf16[512,512]{1,0:T(8,128)(2,1)S(1)}, u32[]{:S(2)}) copy-start(bf16[512,512]{1,0:T(8,128)(2,1)S(1)} %collective-permute-done.17.refs_3_.refs_15_.refs_17_) | copy-start | bytes 1572868
  109.5 16.6 %collective-permute-start.18 = (bf16[256,256]{1,0:T(8,128)(2,1)S(1)}, bf16[256,256]{1,0:T(8,128)(2,1)S(1)}, u32[]{:S(2)}, u32[]{:S(2)}) collective-permute-start(bf16[256,256]{1,0:T(8,128)(2,1)S(1)} %shard_map.140.refs_0_), channel_id=1, source_target_pairs={{0,4},{4,0},{8,12},{12,8},{1,5},{5,1},{9,13},{13,9},{2,6},{6,2},{1... | collective-permute-start | bytes 393224 | tf_op jit(solution)/shard_map/ppermute | solution.py:390
  120.7 6.9 %collective-permute-start.19 = (bf16[256,256]{1,0:T(8,128)(2,1)S(1)}, bf16[256,256]{1,0:T(8,128)(2,1)S(1)}, u32[]{:S(2)}, u32[]{:S(2)}) collective-permute-start(bf16[256,256]{1,0:T(8,128)(2,1)S(1)} %shard_map.140.refs_0_), channel_id=1, source_target_pairs={{0,8},{4,12},{8,0},{12,4},{1,9},{5,13},{9,1},{13,5},{2,10},{6,14},... | collective-permute-start | bytes 393224 | tf_op jit(solution)/shard_map/ppermute | solution.py:390
  124.1 8.5 %collective-permute-start.21 = (bf16[256,256]{1,0:T(8,128)(2,1)S(1)}, bf16[256,256]{1,0:T(8,128)(2,1)S(1)}, u32[]{:S(2)}, u32[]{:S(2)}) collective-permute-start(bf16[256,256]{1,0:T(8,128)(2,1)S(1)} %shard_map.141.refs_0_), channel_id=1, source_target_pairs={{0,4},{4,0},{8,12},{12,8},{1,5},{5,1},{9,13},{13,9},{2,6},{6,2},{1... | collective-permute-start | bytes 393224 | tf_op jit(solution)/shard_map/ppermute | solution.py:390
  126.1 7.7 %collective-permute-start.22 = (bf16[256,256]{1,0:T(8,128)(2,1)S(1)}, bf16[256,256]{1,0:T(8,128)(2,1)S(1)}, u32[]{:S(2)}, u32[]{:S(2)}) collective-permute-start(bf16[256,256]{1,0:T(8,128)(2,1)S(1)} %shard_map.141.refs_0_), channel_id=1, source_target_pairs={{0,8},{4,12},{8,0},{12,4},{1,9},{5,13},{9,1},{13,5},{2,10},{6,14},... | collective-permute-start | bytes 393224 | tf_op jit(solution)/shard_map/ppermute | solution.py:390
  127.6 7.8 %collective-permute-start.20 = (bf16[256,256]{1,0:T(8,128)(2,1)S(1)}, bf16[256,256]{1,0:T(8,128)(2,1)S(1)}, u32[]{:S(2)}, u32[]{:S(2)}) collective-permute-start(bf16[256,256]{1,0:T(8,128)(2,1)S(1)} %collective-permute-done.19.refs_2_), channel_id=1, source_target_pairs={{0,4},{4,0},{8,12},{12,8},{1,5},{5,1},{9,13},{13,9},{2,6},{6,2},{1... | collective-permute-start | bytes 393224 | tf_op jit(solution)/shard_map/ppermute | solution.py:390
  136.0 1.5 collective-permute-start.23
  136.1 5.9 %collective-permute-start.24 = (bf16[256,256]{1,0:T(8,128)(2,1)S(1)}, bf16[256,256]{1,0:T(8,128)(2,1)S(1)}, u32[]{:S(2)}, u32[]{:S(2)}) collective-permute-start(bf16[256,256]{1,0:T(8,128)(2,1)S(1)} %collective-permute-done.22.refs_2_), channel_id=1, source_target_pairs={{0,4},{4,0},{8,12},{12,8},{1,5},{5,1},{9,13},{13,9},{2,6},{6,2},{1... | collective-permute-start | bytes 393224 | tf_op jit(solution)/shard_map/ppermute | solution.py:390
  142.0 6.8 %collective-permute-start.26 = (bf16[128,768]{1,0:T(8,128)(2,1)}, bf16[128,768]{1,0:T(8,128)(2,1)}, u32[]{:S(2)}, u32[]{:S(2)}) collective-permute-start(bf16[128,768]{1,0:T(8,128)(2,1)} %add_convert_fusion.2), channel_id=1, source_target_pairs={{0,2},{2,0},{1,3},{3,1},{4,6},{6,4},{5,7},{7,5},{8,10},{10,8},{9,1... | collective-permute-start | bytes 589832 | tf_op jit(solution)/shard_map/ppermute | solution.py:475
  143.8 5.0 %collective-permute-start.25 = (bf16[128,768]{1,0:T(8,128)(2,1)}, bf16[128,768]{1,0:T(8,128)(2,1)}, u32[]{:S(2)}, u32[]{:S(2)}) collective-permute-start(bf16[128,768]{1,0:T(8,128)(2,1)} %get-tuple-element.75), channel_id=1, source_target_pairs={{0,1},{1,0},{2,3},{3,2},{4,5},{5,4},{6,7},{7,6},{8,9},{9,8},{10,11... | collective-permute-start | bytes 589832 | tf_op jit(solution)/shard_map/ppermute | solution.py:466
  150.0 9.6 %collective-permute-start.27 = (bf16[128,768]{1,0:T(8,128)(2,1)S(1)}, bf16[128,768]{1,0:T(8,128)(2,1)S(1)}, u32[]{:S(2)}, u32[]{:S(2)}) collective-permute-start(bf16[128,768]{1,0:T(8,128)(2,1)S(1)} %fusion), channel_id=1, source_target_pairs={{0,4},{4,0},{8,12},{12,8},{1,5},{5,1},{9,13},{13,9},{2,6},{6,2},{1... | collective-permute-start | bytes 589832 | tf_op jit(solution)/shard_map/ppermute | solution.py:390
  151.4 10.6 %collective-permute-start.28 = (bf16[128,768]{1,0:T(8,128)(2,1)S(1)}, bf16[128,768]{1,0:T(8,128)(2,1)S(1)}, u32[]{:S(2)}, u32[]{:S(2)}) collective-permute-start(bf16[128,768]{1,0:T(8,128)(2,1)S(1)} %fusion), channel_id=1, source_target_pairs={{0,8},{4,12},{8,0},{12,4},{1,9},{5,13},{9,1},{13,5},{2,10},{6,14},... | collective-permute-start | bytes 589832 | tf_op jit(solution)/shard_map/ppermute | solution.py:390
  153.4 8.6 %collective-permute-start.29 = (bf16[1,128,768]{2,1,0:T(8,128)(2,1)S(1)}, bf16[1,128,768]{2,1,0:T(8,128)(2,1)S(1)}, u32[]{:S(2)}, u32[]{:S(2)}) collective-permute-start(bf16[1,128,768]{2,1,0:T(8,128)(2,1)S(1)} %bitcast.50), channel_id=1, source_target_pairs={{0,2},{2,0},{1,3},{3,1},{4,6},{6,4},{5,7},{7,5},{8,10},{10,8},{9,1... | collective-permute-start | bytes 589832 | tf_op jit(solution)/shard_map/ppermute | solution.py:480
  161.9 5.7 %collective-permute-start.31 = (bf16[128,768]{1,0:T(8,128)(2,1)S(1)}, bf16[128,768]{1,0:T(8,128)(2,1)S(1)}, u32[]{:S(2)}, u32[]{:S(2)}) collective-permute-start(bf16[128,768]{1,0:T(8,128)(2,1)S(1)} %collective-permute-done.28), channel_id=1, source_target_pairs={{0,4},{4,0},{8,12},{12,8},{1,5},{5,1},{9,13},{13,9},{2,6},{6,2},{1... | collective-permute-start | bytes 589832 | tf_op jit(solution)/shard_map/ppermute | solution.py:390
  167.7 2.6 %collective-permute-start.33 = (bf16[2,128,768]{2,1,0:T(8,128)(2,1)S(1)}, bf16[2,128,768]{2,1,0:T(8,128)(2,1)S(1)}, u32[]{:S(2)}, u32[]{:S(2)}) collective-permute-start(bf16[2,128,768]{2,1,0:T(8,128)(2,1)S(1)} %get-tuple-element.99.refs_0_), channel_id=1, source_target_pairs={{0,1},{1,0},{2,3},{3,2},{4,5},{5,4},{6,7},{7,6},{8,9},{9,8},{10,11... | collective-permute-start | bytes 1179656 | tf_op jit(solution)/shard_map/ppermute | solution.py:484
  167.8 2.5 %collective-permute-start.34 = (bf16[2,128,768]{2,1,0:T(8,128)(2,1)S(1)}, bf16[2,128,768]{2,1,0:T(8,128)(2,1)S(1)}, u32[]{:S(2)}, u32[]{:S(2)}) collective-permute-start(bf16[2,128,768]{2,1,0:T(8,128)(2,1)S(1)} %get-tuple-element.97.refs_1_), channel_id=1, source_target_pairs={{0,1},{1,0},{2,3},{3,2},{4,5},{5,4},{6,7},{7,6},{8,9},{9,8},{10,11... | collective-permute-start | bytes 1179656 | tf_op jit(solution)/shard_map/ppermute | solution.py:484
  168.3 15.3 %collective-permute-start.30 = (bf16[2,128,768]{2,1,0:T(8,128)(2,1)S(1)}, bf16[2,128,768]{2,1,0:T(8,128)(2,1)S(1)}, u32[]{:S(2)}, u32[]{:S(2)}) collective-permute-start(bf16[2,128,768]{2,1,0:T(8,128)(2,1)S(1)} %get-tuple-element.98), channel_id=1, source_target_pairs={{0,2},{2,0},{1,3},{3,1},{4,6},{6,4},{5,7},{7,5},{8,10},{10,8},{9,1... | collective-permute-start | bytes 1179656 | tf_op jit(solution)/shard_map/ppermute | solution.py:485
  168.8 14.8 %collective-permute-start.32 = (bf16[1,128,768]{2,1,0:T(8,128)(2,1)S(1)}, bf16[1,128,768]{2,1,0:T(8,128)(2,1)S(1)}, u32[]{:S(2)}, u32[]{:S(2)}) collective-permute-start(bf16[1,128,768]{2,1,0:T(8,128)(2,1)S(1)} %bitcast.54), channel_id=1, source_target_pairs={{0,2},{2,0},{1,3},{3,1},{4,6},{6,4},{5,7},{7,5},{8,10},{10,8},{9,1... | collective-permute-start | bytes 589832 | tf_op jit(solution)/shard_map/ppermute | solution.py:485
  183.6 3.5 %collective-permute-start.41 = (bf16[2,128,768]{2,1,0:T(8,128)(2,1)S(1)}, bf16[2,128,768]{2,1,0:T(8,128)(2,1)S(1)}, u32[]{:S(2)}, u32[]{:S(2)}) collective-permute-start(bf16[2,128,768]{2,1,0:T(8,128)(2,1)S(1)} %collective-permute-done.30.refs_1_), channel_id=1, source_target_pairs={{0,1},{1,0},{2,3},{3,2},{4,5},{5,4},{6,7},{7,6},{8,9},{9,8},{10,11... | collective-permute-start | bytes 1179656 | tf_op jit(solution)/shard_map/ppermute | solution.py:489
  183.6 3.5 %collective-permute-start.40 = (bf16[1,128,768]{2,1,0:T(8,128)(2,1)S(1)}, bf16[1,128,768]{2,1,0:T(8,128)(2,1)S(1)}, u32[]{:S(2)}, u32[]{:S(2)}) collective-permute-start(bf16[1,128,768]{2,1,0:T(8,128)(2,1)S(1)} %collective-permute-done.29.refs_0_), channel_id=1, source_target_pairs={{0,1},{1,0},{2,3},{3,2},{4,5},{5,4},{6,7},{7,6},{8,9},{9,8},{10,11... | collective-permute-start | bytes 589832 | tf_op jit(solution)/shard_map/ppermute | solution.py:489
  184.1 3.0 %collective-permute-start.42 = (bf16[1,128,768]{2,1,0:T(8,128)(2,1)S(1)}, bf16[1,128,768]{2,1,0:T(8,128)(2,1)S(1)}, u32[]{:S(2)}, u32[]{:S(2)}) collective-permute-start(bf16[1,128,768]{2,1,0:T(8,128)(2,1)S(1)} %collective-permute-done.32.refs_2_), channel_id=1, source_target_pairs={{0,1},{1,0},{2,3},{3,2},{4,5},{5,4},{6,7},{7,6},{8,9},{9,8},{10,11... | collective-permute-start | bytes 589832 | tf_op jit(solution)/shard_map/ppermute | solution.py:489
  184.1 11.7 %collective-permute-start.35 = (bf16[256,256]{1,0:T(8,128)(2,1)S(1)}, bf16[256,256]{1,0:T(8,128)(2,1)S(1)}, u32[]{:S(2)}, u32[]{:S(2)}) collective-permute-start(bf16[256,256]{1,0:T(8,128)(2,1)S(1)} %shard_map.144.refs_0_), channel_id=1, source_target_pairs={{0,4},{4,0},{8,12},{12,8},{1,5},{5,1},{9,13},{13,9},{2,6},{6,2},{1... | collective-permute-start | bytes 393224 | tf_op jit(solution)/shard_map/ppermute | solution.py:390
  184.3 11.4 %collective-permute-start.36 = (bf16[256,256]{1,0:T(8,128)(2,1)S(1)}, bf16[256,256]{1,0:T(8,128)(2,1)S(1)}, u32[]{:S(2)}, u32[]{:S(2)}) collective-permute-start(bf16[256,256]{1,0:T(8,128)(2,1)S(1)} %shard_map.144.refs_0_), channel_id=1, source_target_pairs={{0,8},{4,12},{8,0},{12,4},{1,9},{5,13},{9,1},{13,5},{2,10},{6,14},... | collective-permute-start | bytes 393224 | tf_op jit(solution)/shard_map/ppermute | solution.py:390
  193.7 8.8 %collective-permute-start.43 = (bf16[256,256]{1,0:T(8,128)(2,1)S(1)}, bf16[256,256]{1,0:T(8,128)(2,1)S(1)}, u32[]{:S(2)}, u32[]{:S(2)}) collective-permute-start(bf16[256,256]{1,0:T(8,128)(2,1)S(1)} %shard_map.146.refs_0_), channel_id=1, source_target_pairs={{0,4},{4,0},{8,12},{12,8},{1,5},{5,1},{9,13},{13,9},{2,6},{6,2},{1... | collective-permute-start | bytes 393224 | tf_op jit(solution)/shard_map/ppermute | solution.py:390
  193.8 9.3 %collective-permute-start.44 = (bf16[256,256]{1,0:T(8,128)(2,1)S(1)}, bf16[256,256]{1,0:T(8,128)(2,1)S(1)}, u32[]{:S(2)}, u32[]{:S(2)}) collective-permute-start(bf16[256,256]{1,0:T(8,128)(2,1)S(1)} %shard_map.146.refs_0_), channel_id=1, source_target_pairs={{0,8},{4,12},{8,0},{12,4},{1,9},{5,13},{9,1},{13,5},{2,10},{6,14},... | collective-permute-start | bytes 393224 | tf_op jit(solution)/shard_map/ppermute | solution.py:390
  195.8 9.6 %collective-permute-start.37 = (bf16[256,256]{1,0:T(8,128)(2,1)S(1)}, bf16[256,256]{1,0:T(8,128)(2,1)S(1)}, u32[]{:S(2)}, u32[]{:S(2)}) collective-permute-start(bf16[256,256]{1,0:T(8,128)(2,1)S(1)} %collective-permute-done.36.refs_2_), channel_id=1, source_target_pairs={{0,4},{4,0},{8,12},{12,8},{1,5},{5,1},{9,13},{13,9},{2,6},{6,2},{1... | collective-permute-start | bytes 393224 | tf_op jit(solution)/shard_map/ppermute | solution.py:390
  203.1 5.0 %collective-permute-start.45 = (bf16[256,256]{1,0:T(8,128)(2,1)S(1)}, bf16[256,256]{1,0:T(8,128)(2,1)S(1)}, u32[]{:S(2)}, u32[]{:S(2)}) collective-permute-start(bf16[256,256]{1,0:T(8,128)(2,1)S(1)} %collective-permute-done.44.refs_2_), channel_id=1, source_target_pairs={{0,4},{4,0},{8,12},{12,8},{1,5},{5,1},{9,13},{13,9},{2,6},{6,2},{1... | collective-permute-start | bytes 393224 | tf_op jit(solution)/shard_map/ppermute | solution.py:390
  205.9 2.8 %collective-permute-start.38 = (bf16[128,768]{1,0:T(8,128)(2,1)S(1)}, bf16[128,768]{1,0:T(8,128)(2,1)S(1)}, u32[]{:S(2)}, u32[]{:S(2)}) collective-permute-start(bf16[128,768]{1,0:T(8,128)(2,1)S(1)} %get-tuple-element.83), channel_id=1, source_target_pairs={{0,1},{1,0},{2,3},{3,2},{4,5},{5,4},{6,7},{7,6},{8,9},{9,8},{10,11... | collective-permute-start | bytes 589832 | tf_op jit(solution)/shard_map/ppermute | solution.py:466
  208.6 1.5 collective-permute-start.46
  210.3 11.0 %collective-permute-start.47 = (bf16[128,768]{1,0:T(8,128)(2,1)S(1)}, bf16[128,768]{1,0:T(8,128)(2,1)S(1)}, u32[]{:S(2)}, u32[]{:S(2)}) collective-permute-start(bf16[128,768]{1,0:T(8,128)(2,1)S(1)} %get-tuple-element.101), channel_id=1, source_target_pairs={{0,8},{1,12},{2,0},{3,4},{4,9},{5,13},{6,1},{7,5},{8,10},{9,14},{1... | collective-permute-start | bytes 589832 | tf_op jit(solution)/shard_map/ppermute | solution.py:495
  210.9 14.5 %collective-permute-start.39 = (bf16[128,768]{1,0:T(8,128)(2,1)S(1)}, bf16[128,768]{1,0:T(8,128)(2,1)S(1)}, u32[]{:S(2)}, u32[]{:S(2)}) collective-permute-start(bf16[128,768]{1,0:T(8,128)(2,1)S(1)} %get-tuple-element.100), channel_id=1, source_target_pairs={{0,0},{1,4},{2,8},{3,12},{4,1},{5,5},{6,9},{7,13},{8,2},{9,6},{10,... | collective-permute-start | bytes 589832 | tf_op jit(solution)/shard_map/ppermute | solution.py:495
  (10 other events, 87.1 us)

commit v6 on v5

--- a/solution.py
+++ b/solution.py
@@ -287,11 +287,20 @@
     attend_rows(pair, start, pos_ref, q_ref, k_ref, v_ref, refs[:WAYS], refs[WAYS])
 
 
-def both_kernel(pair, places, pos_ref, query_gain_ref, key_gain_ref, *refs):
-    count = 2 * (1 + places[-1][0])
-    parts, panels, caches = refs[:count], refs[count : count + 2 * WAYS], refs[count + 2 * WAYS :]
-    caches, rest = caches[:WAYS], caches[WAYS:]
-    mixed_ref, panel_ref, held_ref, *outs, panel_sems, held_sems = rest
+def mix_rows(pair, places, parts, panel, held, pos_ref, query_gain_ref, key_gain_ref, outs, mixed_ref):
+    count = len(parts) // 2
+
+    def part(j, k):
+        at, inner = places[k]
+        return parts[j * count + at][inner]
+
+    project_rows(2, part, panel, query_gain_ref, key_gain_ref, outs)
+    attend_rows(pair, 0, pos_ref, *outs, held(), mixed_ref)
+
+
+def mix_own_kernel(places, pos_ref, query_gain_ref, key_gain_ref, *refs):
+    parts, panels, caches = refs[:WAYS], refs[WAYS : 3 * WAYS], refs[3 * WAYS : 4 * WAYS]
+    mixed_ref, panel_ref, held_ref, *outs, panel_sems, held_sems = refs[4 * WAYS :]
     copies = [
         pltpu.make_async_copy(source, panel_ref.at[i], panel_sems.at[i])
         for i, source in enumerate(panels)
@@ -303,18 +312,29 @@
     for copy in copies + late:
         copy.start()
 
-    def part(j, k):
-        at, inner = places[k]
-        return parts[j * count // 2 + at][inner]
-
     def panel(k, h):
         copies[2 * k + h].wait()
         return panel_ref[2 * k + h]
 
-    project_rows(2, part, panel, query_gain_ref, key_gain_ref, outs)
-    for copy in late:
-        copy.wait()
-    attend_rows(pair, 0, pos_ref, *outs, [held_ref.at[k] for k in range(WAYS)], mixed_ref)
+    def held():
+        for copy in late:
+            copy.wait()
+        return [held_ref.at[k] for k in range(WAYS)]
+
+    mix_rows(0, places, parts, panel, held, pos_ref, query_gain_ref, key_gain_ref, outs, mixed_ref)
+
+
+def mix_other_kernel(places, pos_ref, query_gain_ref, key_gain_ref, *refs):
+    *parts, panel_ref, held_ref, mixed_ref, q_ref, k_ref, v_ref = refs
+
+    def panel(k, h):
+        return panel_ref[2 * k + h]
+
+    def held():
+        return [held_ref.at[k] for k in range(WAYS)]
+
+    outs = (q_ref, k_ref, v_ref)
+    mix_rows(1, places, parts, panel, held, pos_ref, query_gain_ref, key_gain_ref, outs, mixed_ref)
 
 
 def project(source, gains, gathered, panels):
@@ -339,25 +359,40 @@
     )(pos, *qkv, *held)
 
 
-def mix_pair(pair, places, pos, gains, parts, panels, held):
+def mix_own(places, pos, gains, parts, panels, held):
     tile, head_dim = parts[0].shape[1], gains[0].shape[1]
     shape = (2 * tile, 2 * head_dim)
     return pl.pallas_call(
-        functools.partial(both_kernel, pair, places),
-        out_shape=jax.ShapeDtypeStruct(shape, jnp.bfloat16),
+        functools.partial(mix_own_kernel, places),
+        out_shape=[
+            jax.ShapeDtypeStruct(shape, jnp.bfloat16),
+            jax.ShapeDtypeStruct((len(panels), *panels[0].shape), jnp.bfloat16),
+            jax.ShapeDtypeStruct((len(held), *held[0].shape), jnp.bfloat16),
+        ],
         in_specs=[pl.BlockSpec(memory_space=pltpu.SMEM)]
         + whole_specs(2 + len(parts))
         + [HBM_SPEC] * (len(panels) + len(held)),
-        out_specs=whole_specs(1)[0],
+        out_specs=whole_specs(3),
         scratch_shapes=[
-            pltpu.VMEM((len(panels), *panels[0].shape), jnp.bfloat16),
-            pltpu.VMEM((len(held), *held[0].shape), jnp.bfloat16),
             *[pltpu.VMEM(shape, jnp.bfloat16)] * 3,
             pltpu.SemaphoreType.DMA((len(panels),)),
             pltpu.SemaphoreType.DMA((len(held),)),
         ],
         compiler_params=pltpu.CompilerParams(vmem_limit_bytes=16 * MIB),
     )(pos, *gains, *parts, *map(in_hbm, panels), *map(in_hbm, held))
+
+
+def mix_other(places, pos, gains, parts, panels, held):
+    tile, head_dim = parts[0].shape[1], gains[0].shape[1]
+    shape = (2 * tile, 2 * head_dim)
+    return pl.pallas_call(
+        functools.partial(mix_other_kernel, places),
+        out_shape=jax.ShapeDtypeStruct(shape, jnp.bfloat16),
+        in_specs=[pl.BlockSpec(memory_space=pltpu.SMEM)] + whole_specs(4 + len(parts)),
+        out_specs=whole_specs(1)[0],
+        scratch_shapes=[pltpu.VMEM(shape, jnp.bfloat16)] * 3,
+        compiler_params=pltpu.CompilerParams(vmem_limit_bytes=16 * MIB),
+    )(pos, *gains, *parts, panels, held)
 
 
 def out_kernel(w_ref, *refs):
@@ -483,13 +518,13 @@
     by_z = [jnp.stack([x_share, near]), jnp.stack([far, last])]
     by_z += [lax.ppermute(part, "head", SWAP) for part in by_z]
     by_x = [own_x, *[lax.ppermute(v, "fsdp", SWAP) for v in (jnp.stack([near, far]), last[None])]]
-    own = mix_pair(0, ((0, 0), (0, 1), (1, 0), (1, 1)), pos, gains, by_z, panels, held)
+    places = ((0, 0), (0, 1), (1, 0), (1, 1))
+    own, panels, held = mix_own(places, pos, gains, by_z, panels, held)
     first = gather_z(own)
     by_x[1], by_x[2], first[0] = lax.optimization_barrier((by_x[1], by_x[2], first[0]))
     by_x += [lax.ppermute(part, "head", SWAP) for part in by_x]
-    second = gather_z(
-        mix_pair(1, ((0, 0), (1, 0), (1, 1), (2, 0)), pos, gains, by_x, panels, held)
-    )
+    places = ((0, 0), (1, 0), (1, 1), (2, 0))
+    second = gather_z(mix_other(places, pos, gains, by_x, panels, held))
     values = [x_share.astype(jnp.float32) + gates[1] * summed(first), gates[1] * summed(second)]
     ends = [
         lax.ppermute(

time: 227 us -> 223 us (0.982)
  local copies, waits for them, and re-layouts: 13.3 us -> 10.7 us
    pallas_call x2, Pallas kernels: 13.2 us -> 10.8 us  [the longest x1 6.66 us: mix_own(): pl.pallas_call(functools.partial(mix_own_kernel, places), out_shape=[jax....]
    unnamed x61 -> x53, local copies, waits for them, and re-layouts: 6.61 us -> 4.65 us
  transfers between devices with their start and end apart: 48 -> 48, of which waited for: 23 -> 24; matrix products, arithmetic and copies ran while one was open for 5% -> 4% of each run, Pallas kernels for 13% -> 12%
where the time goes in v6:
time: 223 us
  waiting for transfers between devices  119 us (53%)
  starting transfers between devices  56.9 us (26%)
  Pallas kernels  30.3 us (14%)
  local copies, waits for them, and re-layouts  10.7 us (5%)
  other arithmetic  4.99 us (2%)
    ppermute x24, waiting for transfers between devices, from_z(): return lax.ppermute(value, 'cache', [(i, i ^ k) for i in range(WAYS)])  64.9 us
    ppermute x24, starting transfers between devices, from_z(): return lax.ppermute(value, 'cache', [(i, i ^ k) for i in range(WAYS)])  42.2 us
    ppermute x3, waiting for transfers between devices, split_heads(): far = {k: lax.ppermute(near[k], 'groups', SWAP) for k in order}  24.9 us
    ppermute x2, waiting for transfers between devices, split_heads(): lax.ppermute(value.astype(jnp.bfloat16), ('cache', 'fsdp', 'head'), [(a *...  10.9 us
    pallas_call x1, Pallas kernels, mix_own(): pl.pallas_call(functools.partial(mix_own_kernel, places), out_shape=[jax....  6.66 us
    ppermute x2, waiting for transfers between devices, split_heads(): lax.ppermute(v, 'fsdp', SWAP)  6.61 us
    ppermute x1, waiting for transfers between devices, gather_pairs(): high_x = lax.ppermute(high, 'fsdp', SWAP)  6.32 us
    pallas_call x1, Pallas kernels, project(): pl.pallas_call(project_kernel, out_shape=[jax.ShapeDtypeStruct((WAYS * ti...  5.07 us
  transfers between devices with their start and end apart: 48, of which 24 were waited for; matrix products, arithmetic and copies ran while one was open for 4% of the time, Pallas kernels for 12%

profile of v6, /device:TPU:2, one launch (start us, length us, event | category | flops | bytes accessed | tf_op | source)
XLA Modules:
  0.0 222.8 jit_solution(9130942828829875839)
XLA Ops:
  0.0 1.8 constant_dynamic-update-slice_fusion.9
  1.8 1.6 collective-permute-start
  3.4 2.6 %collective-permute-start.1 = (bf16[128,768]{1,0:T(8,128)(2,1)}, bf16[128,768]{1,0:T(8,128)(2,1)S(1)}, u32[]{:S(2)}, u32[]{:S(2)}) collective-permute-start(bf16[128,768]{1,0:T(8,128)(2,1)} %get-tuple-element.100), channel_id=1, source_target_pairs={{0,8},{4,12},{8,0},{12,4},{1,9},{5,13},{9,1},{13,5},{2,10},{6,14},... | collective-permute-start | bytes 589832 | tf_op jit(solution)/shard_map/ppermute | solution.py:425
  6.0 0.8 dynamic_slice.16
  6.9 2.9 %shard_map.137 = (bf16[768,384]{1,0:T(8,128)(2,1)}, bf16[768,384]{1,0:T(8,128)(2,1)}, bf16[768,384]{1,0:T(8,128)(2,1)}, f32[8,128]{1,0:T(8,128)}) custom-call(f32[768,128]{1,0:T(8,128)S(1)} %broadcast_in_dim.71.gain_ref, bf16[768,1024]{1,0:T(8,128)(2,1)} %refs_0_.3, bf16[768,1024]{1,0:T(8,128)(2,1)} %refs_1_.3, bf16[768,1024]{1,0:T(8,128)(2,1)} %refs_2_.3), custom_call_target="tpu_custom_call" | custom-call | tf_op jit(solution)/shard_map/pallas_call | solution.py:173
  10.8 3.6 %collective-permute-start.13 = (bf16[768,384]{1,0:T(8,128)(2,1)}, bf16[768,384]{1,0:T(8,128)(2,1)}, u32[]{:S(2)}, u32[]{:S(2)}) collective-permute-start(bf16[768,384]{1,0:T(8,128)(2,1)} %get-tuple-element.55), channel_id=1, source_target_pairs={{0,12},{4,8},{8,4},{12,0},{1,13},{5,9},{9,5},{13,1},{2,14},{6,10},... | collective-permute-start | bytes 1769480 | tf_op jit(solution)/shard_map/ppermute | solution.py:425
  14.7 0.6 gather_fusion.1
  15.3 2.0 shard_map.136
  17.4 0.8 copy-done.9
  18.2 0.8 copy-done.11
  19.7 0.7 gather_fusion.3
  21.0 1.8 gather_fusion
  22.8 1.9 shard_map.139
  24.8 1.2 pad_maximum_fusion
  26.0 0.6 collective-permute-start.5
  26.6 28.4 %collective-permute-done.2 = bf16[128,768]{1,0:T(8,128)(2,1)S(1)} collective-permute-done((bf16[128,768]{1,0:T(8,128)(2,1)S(1)}, bf16[128,768]{1,0:T(8,128)(2,1)S(1)}, u32[]{:S(2)}, u32[]{:S(2)}) %collective-permute-start.2) | collective-permute-done | bytes 196640 | tf_op jit(solution)/shard_map/ppermute | solution.py:425
  55.6 0.9 constant_dynamic-update-slice_fusion.8
  57.2 1.7 collective-permute-start.10
  58.9 6.3 %collective-permute-done.6 = bf16[2,128,768]{2,1,0:T(8,128)(2,1)S(1)} collective-permute-done((bf16[2,128,768]{2,1,0:T(8,128)(2,1)S(1)}, bf16[2,128,768]{2,1,0:T(8,128)(2,1)S(1)}, u32[]{:S(2)}, u32[]{:S(2)}) %collective-permute-start.6) | collective-permute-done | bytes 393248 | tf_op jit(solution)/shard_map/ppermute | solution.py:457
  65.3 2.9 %collective-permute-start.15 = (bf16[512,512]{1,0:T(8,128)(2,1)S(1)}, bf16[512,512]{1,0:T(8,128)(2,1)S(1)}, u32[]{:S(2)}, u32[]{:S(2)}) collective-permute-start(bf16[512,512]{1,0:T(8,128)(2,1)S(1)} %get-tuple-element.61), channel_id=1, source_target_pairs={{0,4},{4,0},{8,12},{12,8},{1,5},{5,1},{9,13},{13,9},{2,6},{6,2},{1... | collective-permute-start | bytes 1572872 | tf_op jit(solution)/shard_map/ppermute | solution.py:425
  68.2 1.4 collective-permute-start.16
  69.6 1.2 collective-permute-start.17
  71.3 1.5 collective-permute-done.10.refs_3_.refs_7_
  72.9 2.2 collective-permute-start.14
  75.2 11.8 %collective-permute-done.12.refs_5_.refs_9_ = bf16[768,384]{1,0:T(8,128)(2,1)S(1)} collective-permute-done((bf16[768,384]{1,0:T(8,128)(2,1)S(1)}, bf16[768,384]{1,0:T(8,128)(2,1)S(1)}, u32[]{:S(2)}, u32[]{:S(2)}) %collective-permute-start.12) | collective-permute-done | bytes 589856 | tf_op jit(solution)/shard_map/ppermute | solution.py:474
  87.0 11.6 %collective-permute-done.14.refs_7_.refs_11_ = bf16[768,384]{1,0:T(8,128)(2,1)S(1)} collective-permute-done((bf16[768,384]{1,0:T(8,128)(2,1)}, bf16[768,384]{1,0:T(8,128)(2,1)S(1)}, u32[]{:S(2)}, u32[]{:S(2)}) %collective-permute-start.14) | collective-permute-done | bytes 589856 | tf_op jit(solution)/shard_map/ppermute | solution.py:474
  98.6 5.1 %shard_map.138 = (bf16[512,256]{1,0:T(8,128)(2,1)S(1)}, bf16[512,256]{1,0:T(8,128)(2,1)S(1)}, bf16[512,256]{1,0:T(8,128)(2,1)S(1)}) custom-call(s32[16]{0:T(128)S(1)} %add.171.source_ref, f32[1,128]{1,0:T(1,128)S(1)} %bitcast.41, f32[1,128]{1,0:T(1,128)S(1)} %bitcast.44, bf16[16,128,768]{2,1,0:T(8,128)(2,1)S(1)} %constant_dynamic-update-slice_fusion.gathered_ref, ...), custom_call_target="tpu_custom_call" | custom-call | tf_op jit(solution)/shard_map/pallas_call | solution.py:342
  103.8 2.6 %collective-permute-done.16.refs_2_.refs_14_ = bf16[512,512]{1,0:T(8,128)(2,1)S(1)} collective-permute-done((bf16[512,512]{1,0:T(8,128)(2,1)S(1)}, bf16[512,512]{1,0:T(8,128)(2,1)S(1)}, u32[]{:S(2)}, u32[]{:S(2)}) %collective-permute-start.16) | collective-permute-done | bytes 524320 | tf_op jit(solution)/shard_map/ppermute | solution.py:425
  106.4 2.3 %shard_map.140.refs_0_ = bf16[256,256]{1,0:T(8,128)(2,1)S(1)} custom-call(s32[16]{0:T(128)S(1)} %reshape.272.pos_ref, bf16[512,256]{1,0:T(8,128)(2,1)S(1)} %get-tuple-element.56.q_ref, bf16[512,256]{1,0:T(8,128)(2,1)S(1)} %get-tuple-element.57.k_ref, bf16[512,256]{1,0:T(8,128)(2,1)S(1)} %get-tuple-element.58.v_ref, ...), custom_call_target="tpu_custom_call" | custom-call | tf_op jit(solution)/shard_map/pallas_call | solution.py:353
  108.7 11.2 %collective-permute-start.18 = (bf16[256,256]{1,0:T(8,128)(2,1)S(1)}, bf16[256,256]{1,0:T(8,128)(2,1)S(1)}, u32[]{:S(2)}, u32[]{:S(2)}) collective-permute-start(bf16[256,256]{1,0:T(8,128)(2,1)S(1)} %shard_map.140.refs_0_), channel_id=1, source_target_pairs={{0,4},{4,0},{8,12},{12,8},{1,5},{5,1},{9,13},{13,9},{2,6},{6,2},{1... | collective-permute-start | bytes 393224 | tf_op jit(solution)/shard_map/ppermute | solution.py:425
  119.8 1.1 collective-permute-start.19
  121.0 2.3 %shard_map.141.refs_0_ = bf16[256,256]{1,0:T(8,128)(2,1)S(1)} custom-call(s32[16]{0:T(128)S(1)} %reshape.272.pos_ref, bf16[512,256]{1,0:T(8,128)(2,1)S(1)} %get-tuple-element.56.q_ref, bf16[512,256]{1,0:T(8,128)(2,1)S(1)} %get-tuple-element.57.k_ref, bf16[512,256]{1,0:T(8,128)(2,1)S(1)} %get-tuple-element.58.v_ref, ...), custom_call_target="tpu_custom_call" | custom-call | tf_op jit(solution)/shard_map/pallas_call | solution.py:353
  123.3 2.0 collective-permute-start.21
  125.3 1.5 collective-permute-done.19.refs_2_
  126.8 3.4 %collective-permute-start.20 = (bf16[256,256]{1,0:T(8,128)(2,1)S(1)}, bf16[256,256]{1,0:T(8,128)(2,1)S(1)}, u32[]{:S(2)}, u32[]{:S(2)}) collective-permute-start(bf16[256,256]{1,0:T(8,128)(2,1)S(1)} %collective-permute-done.19.refs_2_), channel_id=1, source_target_pairs={{0,4},{4,0},{8,12},{12,8},{1,5},{5,1},{9,13},{13,9},{2,6},{6,2},{1... | collective-permute-start | bytes 393224 | tf_op jit(solution)/shard_map/ppermute | solution.py:425
  130.5 1.2 collective-permute-done.21.refs_1_
  131.8 1.2 collective-permute-done.22.refs_2_
  133.0 1.6 collective-permute-done.20.refs_3_
  135.2 1.4 collective-permute-start.24
  136.6 0.7 add_convert_fusion.2
  137.4 3.8 %collective-permute-done.24.refs_3_ = bf16[256,256]{1,0:T(8,128)(2,1)S(1)} collective-permute-done((bf16[256,256]{1,0:T(8,128)(2,1)S(1)}, bf16[256,256]{1,0:T(8,128)(2,1)S(1)}, u32[]{:S(2)}, u32[]{:S(2)}) %collective-permute-start.24) | collective-permute-done | bytes 131104 | tf_op jit(solution)/shard_map/ppermute | solution.py:425
  141.7 1.3 shard_map.143
  143.0 0.9 dynamic-slice_reduce_fusion
  143.9 4.0 %collective-permute-done.26 = bf16[128,768]{1,0:T(8,128)(2,1)} collective-permute-done((bf16[128,768]{1,0:T(8,128)(2,1)}, bf16[128,768]{1,0:T(8,128)(2,1)}, u32[]{:S(2)}, u32[]{:S(2)}) %collective-permute-start.26) | collective-permute-done | bytes 196640 | tf_op jit(solution)/shard_map/ppermute | solution.py:510
  147.9 1.2 fusion
  149.1 1.4 collective-permute-start.27
  150.5 2.0 collective-permute-start.28
  153.1 5.7 %collective-permute-done.27 = bf16[128,768]{1,0:T(8,128)(2,1)S(1)} collective-permute-done((bf16[128,768]{1,0:T(8,128)(2,1)S(1)}, bf16[128,768]{1,0:T(8,128)(2,1)S(1)}, u32[]{:S(2)}, u32[]{:S(2)}) %collective-permute-start.27) | collective-permute-done | bytes 196640 | tf_op jit(solution)/shard_map/ppermute | solution.py:425
  158.8 2.3 %collective-permute-done.28 = bf16[128,768]{1,0:T(8,128)(2,1)S(1)} collective-permute-done((bf16[128,768]{1,0:T(8,128)(2,1)S(1)}, bf16[128,768]{1,0:T(8,128)(2,1)S(1)}, u32[]{:S(2)}, u32[]{:S(2)}) %collective-permute-start.28) | collective-permute-done | bytes 196640 | tf_op jit(solution)/shard_map/ppermute | solution.py:425
  161.3 5.4 %collective-permute-done.31 = bf16[128,768]{1,0:T(8,128)(2,1)S(1)} collective-permute-done((bf16[128,768]{1,0:T(8,128)(2,1)S(1)}, bf16[128,768]{1,0:T(8,128)(2,1)S(1)}, u32[]{:S(2)}, u32[]{:S(2)}) %collective-permute-start.31) | collective-permute-done | bytes 196640 | tf_op jit(solution)/shard_map/ppermute | solution.py:425
  168.0 1.5 collective-permute-start.32
  169.5 6.7 %shard_map.144 = (bf16[256,256]{1,0:T(8,128)(2,1)S(1)}, bf16[8,768,384]{2,1,0:T(8,128)(2,1)S(1)}, bf16[4,512,512]{2,1,0:T(8,128)(2,1)S(1)}) custom-call(s32[16]{0:T(128)S(1)} %reshape.272.pos_ref, f32[1,128]{1,0:T(1,128)S(1)} %bitcast.42, f32[1,128]{1,0:T(1,128)S(1)} %bitcast.45, bf16[2,128,768]{2,1,0:T(8,128)(2,1)S(1)} %get-tuple-element.105.refs_0_, ...), custom_call_target="tpu_custom_call" | custom-call | tf_op jit(solution)/shard_map/pallas_call | solution.py:365
  176.2 6.6 %collective-permute-done.32.refs_2_ = bf16[1,128,768]{2,1,0:T(8,128)(2,1)S(1)} collective-permute-done((bf16[1,128,768]{2,1,0:T(8,128)(2,1)S(1)}, bf16[1,128,768]{2,1,0:T(8,128)(2,1)S(1)}, u32[]{:S(2)}, u32[]{:S(2)}) %collective-permute-start.32) | collective-permute-done | bytes 196640 | tf_op jit(solution)/shard_map/ppermute | solution.py:520
  183.5 2.7 %collective-permute-start.36 = (bf16[256,256]{1,0:T(8,128)(2,1)S(1)}, bf16[256,256]{1,0:T(8,128)(2,1)S(1)}, u32[]{:S(2)}, u32[]{:S(2)}) collective-permute-start(bf16[256,256]{1,0:T(8,128)(2,1)S(1)} %get-tuple-element.83.refs_0_), channel_id=1, source_target_pairs={{0,8},{4,12},{8,0},{12,4},{1,9},{5,13},{9,1},{13,5},{2,10},{6,14},... | collective-permute-start | bytes 393224 | tf_op jit(solution)/shard_map/ppermute | solution.py:425
  186.3 4.1 %shard_map.146.refs_0_ = bf16[256,256]{1,0:T(8,128)(2,1)S(1)} custom-call(s32[16]{0:T(128)S(1)} %reshape.272.pos_ref, f32[1,128]{1,0:T(1,128)S(1)} %bitcast.43, f32[1,128]{1,0:T(1,128)S(1)} %bitcast.46, bf16[1,128,768]{2,1,0:T(8,128)(2,1)S(1)} %collective-permute-done.29.refs_0_, bf16[2,128,768]{2,1,0:T(8,128)(2,1)S(1)} %collective-permute-done.30.refs_1_, ...), custom_call_target="tpu_custom_call" | custom-call | tf_op jit(solution)/shard_map/pallas_call | solution.py:388
  190.4 2.0 collective-permute-start.44
  193.3 5.9 %collective-permute-done.43.refs_1_ = bf16[256,256]{1,0:T(8,128)(2,1)S(1)} collective-permute-done((bf16[256,256]{1,0:T(8,128)(2,1)S(1)}, bf16[256,256]{1,0:T(8,128)(2,1)S(1)}, u32[]{:S(2)}, u32[]{:S(2)}) %collective-permute-start.43) | collective-permute-done | bytes 131104 | tf_op jit(solution)/shard_map/ppermute | solution.py:425
  199.8 2.2 collective-permute-done.37.refs_3_
  202.7 2.0 collective-permute-done.45.refs_3_
  205.4 1.4 collective-permute-done.46
  207.5 3.6 %collective-permute-start.39 = (bf16[128,768]{1,0:T(8,128)(2,1)S(1)}, bf16[128,768]{1,0:T(8,128)(2,1)S(1)}, u32[]{:S(2)}, u32[]{:S(2)}) collective-permute-start(bf16[128,768]{1,0:T(8,128)(2,1)S(1)} %get-tuple-element.106), channel_id=1, source_target_pairs={{0,0},{1,4},{2,8},{3,12},{4,1},{5,5},{6,9},{7,13},{8,2},{9,6},{10,... | collective-permute-start | bytes 589832 | tf_op jit(solution)/shard_map/ppermute | solution.py:530
  211.1 6.8 %collective-permute-done.47 = bf16[128,768]{1,0:T(8,128)(2,1)S(1)} collective-permute-done((bf16[128,768]{1,0:T(8,128)(2,1)S(1)}, bf16[128,768]{1,0:T(8,128)(2,1)S(1)}, u32[]{:S(2)}, u32[]{:S(2)}) %collective-permute-start.47) | collective-permute-done | bytes 196640 | tf_op jit(solution)/shard_map/ppermute | solution.py:530
  217.9 4.1 %collective-permute-done.39 = bf16[128,768]{1,0:T(8,128)(2,1)S(1)} collective-permute-done((bf16[128,768]{1,0:T(8,128)(2,1)S(1)}, bf16[128,768]{1,0:T(8,128)(2,1)S(1)}, u32[]{:S(2)}, u32[]{:S(2)}) %collective-permute-start.39) | collective-permute-done | bytes 196640 | tf_op jit(solution)/shard_map/ppermute | solution.py:530
  222.0 0.7 add_convert_fusion
  (138 shorter events, 12.5 us)
Async XLA Ops:
  0.0 21.0 %copy-start = (bf16[1024,768]{1,0:T(8,128)(2,1)S(1)}, bf16[1024,768]{1,0:T(8,128)(2,1)}, u32[]{:S(2)}) copy-start(bf16[1024,768]{1,0:T(8,128)(2,1)} %param.19) | copy-start | bytes 4718596
  1.8 22.9 %collective-permute-start = (bf16[128,768]{1,0:T(8,128)(2,1)}, bf16[128,768]{1,0:T(8,128)(2,1)}, u32[]{:S(2)}, u32[]{:S(2)}) collective-permute-start(bf16[128,768]{1,0:T(8,128)(2,1)} %get-tuple-element.100), channel_id=1, source_target_pairs={{0,4},{4,0},{8,12},{12,8},{1,5},{5,1},{9,13},{13,9},{2,6},{6,2},{1... | collective-permute-start | bytes 589832 | tf_op jit(solution)/shard_map/ppermute | solution.py:425
  3.4 17.5 %collective-permute-start.1 = (bf16[128,768]{1,0:T(8,128)(2,1)}, bf16[128,768]{1,0:T(8,128)(2,1)S(1)}, u32[]{:S(2)}, u32[]{:S(2)}) collective-permute-start(bf16[128,768]{1,0:T(8,128)(2,1)} %get-tuple-element.100), channel_id=1, source_target_pairs={{0,8},{4,12},{8,0},{12,4},{1,9},{5,13},{9,1},{13,5},{2,10},{6,14},... | collective-permute-start | bytes 589832 | tf_op jit(solution)/shard_map/ppermute | solution.py:425
  9.9 46.7 %collective-permute-start.9 = (bf16[768,384]{1,0:T(8,128)(2,1)}, bf16[768,384]{1,0:T(8,128)(2,1)S(1)}, u32[]{:S(2)}, u32[]{:S(2)}) collective-permute-start(bf16[768,384]{1,0:T(8,128)(2,1)} %get-tuple-element.53), channel_id=1, source_target_pairs={{0,4},{4,0},{8,12},{12,8},{1,5},{5,1},{9,13},{13,9},{2,6},{6,2},{1... | collective-permute-start | bytes 1769480 | tf_op jit(solution)/shard_map/ppermute | solution.py:425
  10.4 46.7 %collective-permute-start.11 = (bf16[768,384]{1,0:T(8,128)(2,1)}, bf16[768,384]{1,0:T(8,128)(2,1)S(1)}, u32[]{:S(2)}, u32[]{:S(2)}) collective-permute-start(bf16[768,384]{1,0:T(8,128)(2,1)} %get-tuple-element.54), channel_id=1, source_target_pairs={{0,8},{4,12},{8,0},{12,4},{1,9},{5,13},{9,1},{13,5},{2,10},{6,14},... | collective-permute-start | bytes 1769480 | tf_op jit(solution)/shard_map/ppermute | solution.py:425
  10.8 46.4 %collective-permute-start.13 = (bf16[768,384]{1,0:T(8,128)(2,1)}, bf16[768,384]{1,0:T(8,128)(2,1)}, u32[]{:S(2)}, u32[]{:S(2)}) collective-permute-start(bf16[768,384]{1,0:T(8,128)(2,1)} %get-tuple-element.55), channel_id=1, source_target_pairs={{0,12},{4,8},{8,4},{12,0},{1,13},{5,9},{9,5},{13,1},{2,14},{6,10},... | collective-permute-start | bytes 1769480 | tf_op jit(solution)/shard_map/ppermute | solution.py:425
  21.0 34.1 %collective-permute-start.2 = (bf16[128,768]{1,0:T(8,128)(2,1)S(1)}, bf16[128,768]{1,0:T(8,128)(2,1)S(1)}, u32[]{:S(2)}, u32[]{:S(2)}) collective-permute-start(bf16[128,768]{1,0:T(8,128)(2,1)S(1)} %collective-permute-done.1), channel_id=1, source_target_pairs={{0,4},{4,0},{8,12},{12,8},{1,5},{5,1},{9,13},{13,9},{2,6},{6,2},{1... | collective-permute-start | bytes 589832 | tf_op jit(solution)/shard_map/ppermute | solution.py:425
  22.8 32.7 %copy-start.5 = (bf16[16,128,768]{2,1,0:T(8,128)(2,1)S(1)}, bf16[16,128,768]{2,1,0:T(8,128)(2,1)}, u32[]{:S(2)}) copy-start(bf16[16,128,768]{2,1,0:T(8,128)(2,1)} %get-tuple-element.99) | copy-start | bytes 9437188
  24.8 96.2 %copy-start.1 = (bf16[512,512]{1,0:T(8,128)(2,1)}, bf16[512,512]{1,0:T(8,128)(2,1)S(1)}, u32[]{:S(2)}) copy-start(bf16[512,512]{1,0:T(8,128)(2,1)S(1)} %get-tuple-element.59.refs_0_.refs_12_) | copy-start | bytes 1572868
  26.0 30.5 %collective-permute-start.5 = (bf16[2,128,768]{2,1,0:T(8,128)(2,1)S(1)}, bf16[2,128,768]{2,1,0:T(8,128)(2,1)S(1)}, u32[]{:S(2)}, u32[]{:S(2)}) collective-permute-start(bf16[2,128,768]{2,1,0:T(8,128)(2,1)S(1)} %pad_maximum_fusion), channel_id=1, source_target_pairs={{0,2},{2,0},{1,3},{3,1},{4,6},{6,4},{5,7},{7,5},{8,10},{10,8},{9,1... | collective-permute-start | bytes 1179656 | tf_op jit(solution)/shard_map/ppermute | solution.py:455
  55.1 43.5 %copy-start.10 = (bf16[768,384]{1,0:T(8,128)(2,1)S(1)}, bf16[768,384]{1,0:T(8,128)(2,1)}, u32[]{:S(2)}) copy-start(bf16[768,384]{1,0:T(8,128)(2,1)} %copy-done.9) | copy-start | bytes 1769476
  55.1 43.5 %copy-start.12 = (bf16[768,384]{1,0:T(8,128)(2,1)S(1)}, bf16[768,384]{1,0:T(8,128)(2,1)}, u32[]{:S(2)}) copy-start(bf16[768,384]{1,0:T(8,128)(2,1)} %copy-done.11) | copy-start | bytes 1769476
  55.1 43.5 %copy-start.16 = (f32[128]{0:T(128)S(1)}, f32[128]{0:T(128)}, u32[]{:S(2)}) copy-start(f32[128]{0:T(128)} %param.20) | copy-start | bytes 1540
  55.1 43.5 %copy-start.17 = (f32[128]{0:T(128)S(1)}, f32[128]{0:T(128)}, u32[]{:S(2)}) copy-start(f32[128]{0:T(128)} %param.21) | copy-start | bytes 1540
  55.1 10.1 %collective-permute-start.6 = (bf16[2,128,768]{2,1,0:T(8,128)(2,1)S(1)}, bf16[2,128,768]{2,1,0:T(8,128)(2,1)S(1)}, u32[]{:S(2)}, u32[]{:S(2)}) collective-permute-start(bf16[2,128,768]{2,1,0:T(8,128)(2,1)S(1)} %pad_maximum_fusion.1), channel_id=1, source_target_pairs={{0,2},{2,0},{1,3},{3,1},{4,6},{6,4},{5,7},{7,5},{8,10},{10,8},{9,1... | collective-permute-start | bytes 1179656 | tf_op jit(solution)/shard_map/ppermute | solution.py:457
  56.5 8.7 %collective-permute-start.3 = (bf16[2,128,768]{2,1,0:T(8,128)(2,1)S(1)}, bf16[2,128,768]{2,1,0:T(8,128)(2,1)S(1)}, u32[]{:S(2)}, u32[]{:S(2)}) collective-permute-start(bf16[2,128,768]{2,1,0:T(8,128)(2,1)S(1)} %pad_maximum_fusion), channel_id=1, source_target_pairs={{0,1},{1,0},{2,3},{3,2},{4,5},{5,4},{6,7},{7,6},{8,9},{9,8},{10,11... | collective-permute-start | bytes 1179656 | tf_op jit(solution)/shard_map/ppermute | solution.py:459
  56.6 47.1 %copy-start.7 = (bf16[768,384]{1,0:T(8,128)(2,1)}, bf16[768,384]{1,0:T(8,128)(2,1)S(1)}, u32[]{:S(2)}) copy-start(bf16[768,384]{1,0:T(8,128)(2,1)S(1)} %collective-permute-done.9.refs_2_.refs_6_) | copy-start | bytes 1769476
  56.6 11.5 %collective-permute-start.4 = (bf16[2,128,768]{2,1,0:T(8,128)(2,1)S(1)}, bf16[2,128,768]{2,1,0:T(8,128)(2,1)S(1)}, u32[]{:S(2)}, u32[]{:S(2)}) collective-permute-start(bf16[2,128,768]{2,1,0:T(8,128)(2,1)S(1)} %pad_maximum_fusion.1), channel_id=1, source_target_pairs={{0,1},{1,0},{2,3},{3,2},{4,5},{5,4},{6,7},{7,6},{8,9},{9,8},{10,11... | collective-permute-start | bytes 1179656 | tf_op jit(solution)/shard_map/ppermute | solution.py:459
  57.1 46.6 %copy-start.8 = (bf16[768,384]{1,0:T(8,128)(2,1)}, bf16[768,384]{1,0:T(8,128)(2,1)S(1)}, u32[]{:S(2)}) copy-start(bf16[768,384]{1,0:T(8,128)(2,1)S(1)} %collective-permute-done.11.refs_4_.refs_8_) | copy-start | bytes 1769476
  57.1 12.5 %collective-permute-start.7 = (bf16[2,128,768]{2,1,0:T(8,128)(2,1)S(1)}, bf16[2,128,768]{2,1,0:T(8,128)(2,1)S(1)}, u32[]{:S(2)}, u32[]{:S(2)}) collective-permute-start(bf16[2,128,768]{2,1,0:T(8,128)(2,1)S(1)} %collective-permute-done.5), channel_id=1, source_target_pairs={{0,1},{1,0},{2,3},{3,2},{4,5},{5,4},{6,7},{7,6},{8,9},{9,8},{10,11... | collective-permute-start | bytes 1179656 | tf_op jit(solution)/shard_map/ppermute | solution.py:459
  57.2 15.7 %collective-permute-start.10 = (bf16[768,384]{1,0:T(8,128)(2,1)S(1)}, bf16[768,384]{1,0:T(8,128)(2,1)S(1)}, u32[]{:S(2)}, u32[]{:S(2)}) collective-permute-start(bf16[768,384]{1,0:T(8,128)(2,1)S(1)} %collective-permute-done.9.refs_2_.refs_6_), channel_id=1, source_target_pairs={{0,16},{16,0},{1,17},{17,1},{2,18},{18,2},{3,19},{19,3},{4,20},{20... | collective-permute-start | bytes 1769480 | tf_op jit(solution)/shard_map/ppermute | solution.py:474
  65.2 5.6 %collective-permute-start.8 = (bf16[2,128,768]{2,1,0:T(8,128)(2,1)S(1)}, bf16[2,128,768]{2,1,0:T(8,128)(2,1)S(1)}, u32[]{:S(2)}, u32[]{:S(2)}) collective-permute-start(bf16[2,128,768]{2,1,0:T(8,128)(2,1)S(1)} %collective-permute-done.6), channel_id=1, source_target_pairs={{0,1},{1,0},{2,3},{3,2},{4,5},{5,4},{6,7},{7,6},{8,9},{9,8},{10,11... | collective-permute-start | bytes 1179656 | tf_op jit(solution)/shard_map/ppermute | solution.py:459
  65.3 38.5 %collective-permute-start.15 = (bf16[512,512]{1,0:T(8,128)(2,1)S(1)}, bf16[512,512]{1,0:T(8,128)(2,1)S(1)}, u32[]{:S(2)}, u32[]{:S(2)}) collective-permute-start(bf16[512,512]{1,0:T(8,128)(2,1)S(1)} %get-tuple-element.61), channel_id=1, source_target_pairs={{0,4},{4,0},{8,12},{12,8},{1,5},{5,1},{9,13},{13,9},{2,6},{6,2},{1... | collective-permute-start | bytes 1572872 | tf_op jit(solution)/shard_map/ppermute | solution.py:425
  68.2 38.2 %collective-permute-start.16 = (bf16[512,512]{1,0:T(8,128)(2,1)S(1)}, bf16[512,512]{1,0:T(8,128)(2,1)S(1)}, u32[]{:S(2)}, u32[]{:S(2)}) collective-permute-start(bf16[512,512]{1,0:T(8,128)(2,1)S(1)} %get-tuple-element.63), channel_id=1, source_target_pairs={{0,8},{4,12},{8,0},{12,4},{1,9},{5,13},{9,1},{13,5},{2,10},{6,14},... | collective-permute-start | bytes 1572872 | tf_op jit(solution)/shard_map/ppermute | solution.py:425
  69.6 36.8 %collective-permute-start.17 = (bf16[512,512]{1,0:T(8,128)(2,1)S(1)}, bf16[512,512]{1,0:T(8,128)(2,1)S(1)}, u32[]{:S(2)}, u32[]{:S(2)}) collective-permute-start(bf16[512,512]{1,0:T(8,128)(2,1)S(1)} %get-tuple-element.65), channel_id=1, source_target_pairs={{0,12},{4,8},{8,4},{12,0},{1,13},{5,9},{9,5},{13,1},{2,14},{6,10},... | collective-permute-start | bytes 1572872 | tf_op jit(solution)/shard_map/ppermute | solution.py:425
  70.8 16.2 %collective-permute-start.12 = (bf16[768,384]{1,0:T(8,128)(2,1)S(1)}, bf16[768,384]{1,0:T(8,128)(2,1)S(1)}, u32[]{:S(2)}, u32[]{:S(2)}) collective-permute-start(bf16[768,384]{1,0:T(8,128)(2,1)S(1)} %collective-permute-done.11.refs_4_.refs_8_), channel_id=1, source_target_pairs={{0,16},{16,0},{1,17},{17,1},{2,18},{18,2},{3,19},{19,3},{4,20},{20... | collective-permute-start | bytes 1769480 | tf_op jit(solution)/shard_map/ppermute | solution.py:474
  72.9 30.8 %copy-start.13 = (bf16[768,384]{1,0:T(8,128)(2,1)}, bf16[768,384]{1,0:T(8,128)(2,1)S(1)}, u32[]{:S(2)}) copy-start(bf16[768,384]{1,0:T(8,128)(2,1)S(1)} %collective-permute-done.10.refs_3_.refs_7_) | copy-start | bytes 1769476
  72.9 25.7 %collective-permute-start.14 = (bf16[768,384]{1,0:T(8,128)(2,1)}, bf16[768,384]{1,0:T(8,128)(2,1)S(1)}, u32[]{:S(2)}, u32[]{:S(2)}) collective-permute-start(bf16[768,384]{1,0:T(8,128)(2,1)} %collective-permute-done.13.refs_6_.refs_10_), channel_id=1, source_target_pairs={{0,16},{16,0},{1,17},{17,1},{2,18},{18,2},{3,19},{19,3},{4,20},{20... | collective-permute-start | bytes 1769480 | tf_op jit(solution)/shard_map/ppermute | solution.py:474
  75.2 28.5 %copy-start.6 = (bf16[16,128,768]{2,1,0:T(8,128)(2,1)}, bf16[16,128,768]{2,1,0:T(8,128)(2,1)S(1)}, u32[]{:S(2)}) copy-start(bf16[16,128,768]{2,1,0:T(8,128)(2,1)S(1)} %constant_dynamic-update-slice_fusion.gathered_ref) | copy-start | bytes 9437188
  87.0 16.8 %copy-start.14 = (bf16[768,384]{1,0:T(8,128)(2,1)}, bf16[768,384]{1,0:T(8,128)(2,1)S(1)}, u32[]{:S(2)}) copy-start(bf16[768,384]{1,0:T(8,128)(2,1)S(1)} %collective-permute-done.12.refs_5_.refs_9_) | copy-start | bytes 1769476
  103.8 26.4 %copy-start.20 = (bf16[8,128,768]{2,1,0:T(8,128)(2,1)S(1)}, bf16[8,128,768]{2,1,0:T(8,128)(2,1)}, u32[]{:S(2)}) copy-start(bf16[8,128,768]{2,1,0:T(8,128)(2,1)} %gather_fusion) | copy-start | bytes 4718596
  103.8 26.7 %copy-start.2 = (bf16[512,512]{1,0:T(8,128)(2,1)}, bf16[512,512]{1,0:T(8,128)(2,1)S(1)}, u32[]{:S(2)}) copy-start(bf16[512,512]{1,0:T(8,128)(2,1)S(1)} %collective-permute-done.15.refs_1_.refs_13_) | copy-start | bytes 1572868
  106.4 24.1 %copy-start.3 = (bf16[512,512]{1,0:T(8,128)(2,1)}, bf16[512,512]{1,0:T(8,128)(2,1)S(1)}, u32[]{:S(2)}) copy-start(bf16[512,512]{1,0:T(8,128)(2,1)S(1)} %collective-permute-done.16.refs_2_.refs_14_) | copy-start | bytes 1572868
  106.4 24.1 %copy-start.4 = (bf16[512,512]{1,0:T(8,128)(2,1)}, bf16[512,512]{1,0:T(8,128)(2,1)S(1)}, u32[]{:S(2)}) copy-start(bf16[512,512]{1,0:T(8,128)(2,1)S(1)} %collective-permute-done.17.refs_3_.refs_15_) | copy-start | bytes 1572868
  108.7 16.6 %collective-permute-start.18 = (bf16[256,256]{1,0:T(8,128)(2,1)S(1)}, bf16[256,256]{1,0:T(8,128)(2,1)S(1)}, u32[]{:S(2)}, u32[]{:S(2)}) collective-permute-start(bf16[256,256]{1,0:T(8,128)(2,1)S(1)} %shard_map.140.refs_0_), channel_id=1, source_target_pairs={{0,4},{4,0},{8,12},{12,8},{1,5},{5,1},{9,13},{13,9},{2,6},{6,2},{1... | collective-permute-start | bytes 393224 | tf_op jit(solution)/shard_map/ppermute | solution.py:425
  119.8 6.9 %collective-permute-start.19 = (bf16[256,256]{1,0:T(8,128)(2,1)S(1)}, bf16[256,256]{1,0:T(8,128)(2,1)S(1)}, u32[]{:S(2)}, u32[]{:S(2)}) collective-permute-start(bf16[256,256]{1,0:T(8,128)(2,1)S(1)} %shard_map.140.refs_0_), channel_id=1, source_target_pairs={{0,8},{4,12},{8,0},{12,4},{1,9},{5,13},{9,1},{13,5},{2,10},{6,14},... | collective-permute-start | bytes 393224 | tf_op jit(solution)/shard_map/ppermute | solution.py:425
  123.3 8.5 %collective-permute-start.21 = (bf16[256,256]{1,0:T(8,128)(2,1)S(1)}, bf16[256,256]{1,0:T(8,128)(2,1)S(1)}, u32[]{:S(2)}, u32[]{:S(2)}) collective-permute-start(bf16[256,256]{1,0:T(8,128)(2,1)S(1)} %shard_map.141.refs_0_), channel_id=1, source_target_pairs={{0,4},{4,0},{8,12},{12,8},{1,5},{5,1},{9,13},{13,9},{2,6},{6,2},{1... | collective-permute-start | bytes 393224 | tf_op jit(solution)/shard_map/ppermute | solution.py:425
  125.3 7.7 %collective-permute-start.22 = (bf16[256,256]{1,0:T(8,128)(2,1)S(1)}, bf16[256,256]{1,0:T(8,128)(2,1)S(1)}, u32[]{:S(2)}, u32[]{:S(2)}) collective-permute-start(bf16[256,256]{1,0:T(8,128)(2,1)S(1)} %shard_map.141.refs_0_), channel_id=1, source_target_pairs={{0,8},{4,12},{8,0},{12,4},{1,9},{5,13},{9,1},{13,5},{2,10},{6,14},... | collective-permute-start | bytes 393224 | tf_op jit(solution)/shard_map/ppermute | solution.py:425
  126.8 7.8 %collective-permute-start.20 = (bf16[256,256]{1,0:T(8,128)(2,1)S(1)}, bf16[256,256]{1,0:T(8,128)(2,1)S(1)}, u32[]{:S(2)}, u32[]{:S(2)}) collective-permute-start(bf16[256,256]{1,0:T(8,128)(2,1)S(1)} %collective-permute-done.19.refs_2_), channel_id=1, source_target_pairs={{0,4},{4,0},{8,12},{12,8},{1,5},{5,1},{9,13},{13,9},{2,6},{6,2},{1... | collective-permute-start | bytes 393224 | tf_op jit(solution)/shard_map/ppermute | solution.py:425
  135.1 1.5 collective-permute-start.23
  135.2 5.9 %collective-permute-start.24 = (bf16[256,256]{1,0:T(8,128)(2,1)S(1)}, bf16[256,256]{1,0:T(8,128)(2,1)S(1)}, u32[]{:S(2)}, u32[]{:S(2)}) collective-permute-start(bf16[256,256]{1,0:T(8,128)(2,1)S(1)} %collective-permute-done.22.refs_2_), channel_id=1, source_target_pairs={{0,4},{4,0},{8,12},{12,8},{1,5},{5,1},{9,13},{13,9},{2,6},{6,2},{1... | collective-permute-start | bytes 393224 | tf_op jit(solution)/shard_map/ppermute | solution.py:425
  141.1 6.8 %collective-permute-start.26 = (bf16[128,768]{1,0:T(8,128)(2,1)}, bf16[128,768]{1,0:T(8,128)(2,1)}, u32[]{:S(2)}, u32[]{:S(2)}) collective-permute-start(bf16[128,768]{1,0:T(8,128)(2,1)} %add_convert_fusion.2), channel_id=1, source_target_pairs={{0,2},{2,0},{1,3},{3,1},{4,6},{6,4},{5,7},{7,5},{8,10},{10,8},{9,1... | collective-permute-start | bytes 589832 | tf_op jit(solution)/shard_map/ppermute | solution.py:510
  142.9 5.0 %collective-permute-start.25 = (bf16[128,768]{1,0:T(8,128)(2,1)}, bf16[128,768]{1,0:T(8,128)(2,1)}, u32[]{:S(2)}, u32[]{:S(2)}) collective-permute-start(bf16[128,768]{1,0:T(8,128)(2,1)} %get-tuple-element.78), channel_id=1, source_target_pairs={{0,1},{1,0},{2,3},{3,2},{4,5},{5,4},{6,7},{7,6},{8,9},{9,8},{10,11... | collective-permute-start | bytes 589832 | tf_op jit(solution)/shard_map/ppermute | solution.py:501
  149.1 9.6 %collective-permute-start.27 = (bf16[128,768]{1,0:T(8,128)(2,1)S(1)}, bf16[128,768]{1,0:T(8,128)(2,1)S(1)}, u32[]{:S(2)}, u32[]{:S(2)}) collective-permute-start(bf16[128,768]{1,0:T(8,128)(2,1)S(1)} %fusion), channel_id=1, source_target_pairs={{0,4},{4,0},{8,12},{12,8},{1,5},{5,1},{9,13},{13,9},{2,6},{6,2},{1... | collective-permute-start | bytes 589832 | tf_op jit(solution)/shard_map/ppermute | solution.py:425
  150.5 10.6 %collective-permute-start.28 = (bf16[128,768]{1,0:T(8,128)(2,1)S(1)}, bf16[128,768]{1,0:T(8,128)(2,1)S(1)}, u32[]{:S(2)}, u32[]{:S(2)}) collective-permute-start(bf16[128,768]{1,0:T(8,128)(2,1)S(1)} %fusion), channel_id=1, source_target_pairs={{0,8},{4,12},{8,0},{12,4},{1,9},{5,13},{9,1},{13,5},{2,10},{6,14},... | collective-permute-start | bytes 589832 | tf_op jit(solution)/shard_map/ppermute | solution.py:425
  152.6 8.5 %collective-permute-start.29 = (bf16[1,128,768]{2,1,0:T(8,128)(2,1)S(1)}, bf16[1,128,768]{2,1,0:T(8,128)(2,1)S(1)}, u32[]{:S(2)}, u32[]{:S(2)}) collective-permute-start(bf16[1,128,768]{2,1,0:T(8,128)(2,1)S(1)} %bitcast.50), channel_id=1, source_target_pairs={{0,2},{2,0},{1,3},{3,1},{4,6},{6,4},{5,7},{7,5},{8,10},{10,8},{9,1... | collective-permute-start | bytes 589832 | tf_op jit(solution)/shard_map/ppermute | solution.py:515
  161.1 5.7 %collective-permute-start.31 = (bf16[128,768]{1,0:T(8,128)(2,1)S(1)}, bf16[128,768]{1,0:T(8,128)(2,1)S(1)}, u32[]{:S(2)}, u32[]{:S(2)}) collective-permute-start(bf16[128,768]{1,0:T(8,128)(2,1)S(1)} %collective-permute-done.28), channel_id=1, source_target_pairs={{0,4},{4,0},{8,12},{12,8},{1,5},{5,1},{9,13},{13,9},{2,6},{6,2},{1... | collective-permute-start | bytes 589832 | tf_op jit(solution)/shard_map/ppermute | solution.py:425
  166.9 2.6 %collective-permute-start.33 = (bf16[2,128,768]{2,1,0:T(8,128)(2,1)S(1)}, bf16[2,128,768]{2,1,0:T(8,128)(2,1)S(1)}, u32[]{:S(2)}, u32[]{:S(2)}) collective-permute-start(bf16[2,128,768]{2,1,0:T(8,128)(2,1)S(1)} %get-tuple-element.105.refs_0_), channel_id=1, source_target_pairs={{0,1},{1,0},{2,3},{3,2},{4,5},{5,4},{6,7},{7,6},{8,9},{9,8},{10,11... | collective-permute-start | bytes 1179656 | tf_op jit(solution)/shard_map/ppermute | solution.py:519
  167.0 2.5 %collective-permute-start.34 = (bf16[2,128,768]{2,1,0:T(8,128)(2,1)S(1)}, bf16[2,128,768]{2,1,0:T(8,128)(2,1)S(1)}, u32[]{:S(2)}, u32[]{:S(2)}) collective-permute-start(bf16[2,128,768]{2,1,0:T(8,128)(2,1)S(1)} %get-tuple-element.103.refs_1_), channel_id=1, source_target_pairs={{0,1},{1,0},{2,3},{3,2},{4,5},{5,4},{6,7},{7,6},{8,9},{9,8},{10,11... | collective-permute-start | bytes 1179656 | tf_op jit(solution)/shard_map/ppermute | solution.py:519
  167.5 15.3 %collective-permute-start.30 = (bf16[2,128,768]{2,1,0:T(8,128)(2,1)S(1)}, bf16[2,128,768]{2,1,0:T(8,128)(2,1)S(1)}, u32[]{:S(2)}, u32[]{:S(2)}) collective-permute-start(bf16[2,128,768]{2,1,0:T(8,128)(2,1)S(1)} %get-tuple-element.104), channel_id=1, source_target_pairs={{0,2},{2,0},{1,3},{3,1},{4,6},{6,4},{5,7},{7,5},{8,10},{10,8},{9,1... | collective-permute-start | bytes 1179656 | tf_op jit(solution)/shard_map/ppermute | solution.py:520
  168.0 14.8 %collective-permute-start.32 = (bf16[1,128,768]{2,1,0:T(8,128)(2,1)S(1)}, bf16[1,128,768]{2,1,0:T(8,128)(2,1)S(1)}, u32[]{:S(2)}, u32[]{:S(2)}) collective-permute-start(bf16[1,128,768]{2,1,0:T(8,128)(2,1)S(1)} %bitcast.55), channel_id=1, source_target_pairs={{0,2},{2,0},{1,3},{3,1},{4,6},{6,4},{5,7},{7,5},{8,10},{10,8},{9,1... | collective-permute-start | bytes 589832 | tf_op jit(solution)/shard_map/ppermute | solution.py:520
  182.8 3.5 %collective-permute-start.41 = (bf16[2,128,768]{2,1,0:T(8,128)(2,1)S(1)}, bf16[2,128,768]{2,1,0:T(8,128)(2,1)S(1)}, u32[]{:S(2)}, u32[]{:S(2)}) collective-permute-start(bf16[2,128,768]{2,1,0:T(8,128)(2,1)S(1)} %collective-permute-done.30.refs_1_), channel_id=1, source_target_pairs={{0,1},{1,0},{2,3},{3,2},{4,5},{5,4},{6,7},{7,6},{8,9},{9,8},{10,11... | collective-permute-start | bytes 1179656 | tf_op jit(solution)/shard_map/ppermute | solution.py:525
  182.8 3.5 %collective-permute-start.40 = (bf16[1,128,768]{2,1,0:T(8,128)(2,1)S(1)}, bf16[1,128,768]{2,1,0:T(8,128)(2,1)S(1)}, u32[]{:S(2)}, u32[]{:S(2)}) collective-permute-start(bf16[1,128,768]{2,1,0:T(8,128)(2,1)S(1)} %collective-permute-done.29.refs_0_), channel_id=1, source_target_pairs={{0,1},{1,0},{2,3},{3,2},{4,5},{5,4},{6,7},{7,6},{8,9},{9,8},{10,11... | collective-permute-start | bytes 589832 | tf_op jit(solution)/shard_map/ppermute | solution.py:525
  183.3 3.0 %collective-permute-start.42 = (bf16[1,128,768]{2,1,0:T(8,128)(2,1)S(1)}, bf16[1,128,768]{2,1,0:T(8,128)(2,1)S(1)}, u32[]{:S(2)}, u32[]{:S(2)}) collective-permute-start(bf16[1,128,768]{2,1,0:T(8,128)(2,1)S(1)} %collective-permute-done.32.refs_2_), channel_id=1, source_target_pairs={{0,1},{1,0},{2,3},{3,2},{4,5},{5,4},{6,7},{7,6},{8,9},{9,8},{10,11... | collective-permute-start | bytes 589832 | tf_op jit(solution)/shard_map/ppermute | solution.py:525
  183.3 9.1 %collective-permute-start.35 = (bf16[256,256]{1,0:T(8,128)(2,1)S(1)}, bf16[256,256]{1,0:T(8,128)(2,1)S(1)}, u32[]{:S(2)}, u32[]{:S(2)}) collective-permute-start(bf16[256,256]{1,0:T(8,128)(2,1)S(1)} %get-tuple-element.83.refs_0_), channel_id=1, source_target_pairs={{0,4},{4,0},{8,12},{12,8},{1,5},{5,1},{9,13},{13,9},{2,6},{6,2},{1... | collective-permute-start | bytes 393224 | tf_op jit(solution)/shard_map/ppermute | solution.py:425
  183.5 9.5 %collective-permute-start.36 = (bf16[256,256]{1,0:T(8,128)(2,1)S(1)}, bf16[256,256]{1,0:T(8,128)(2,1)S(1)}, u32[]{:S(2)}, u32[]{:S(2)}) collective-permute-start(bf16[256,256]{1,0:T(8,128)(2,1)S(1)} %get-tuple-element.83.refs_0_), channel_id=1, source_target_pairs={{0,8},{4,12},{8,0},{12,4},{1,9},{5,13},{9,1},{13,5},{2,10},{6,14},... | collective-permute-start | bytes 393224 | tf_op jit(solution)/shard_map/ppermute | solution.py:425
  190.4 8.8 %collective-permute-start.43 = (bf16[256,256]{1,0:T(8,128)(2,1)S(1)}, bf16[256,256]{1,0:T(8,128)(2,1)S(1)}, u32[]{:S(2)}, u32[]{:S(2)}) collective-permute-start(bf16[256,256]{1,0:T(8,128)(2,1)S(1)} %shard_map.146.refs_0_), channel_id=1, source_target_pairs={{0,4},{4,0},{8,12},{12,8},{1,5},{5,1},{9,13},{13,9},{2,6},{6,2},{1... | collective-permute-start | bytes 393224 | tf_op jit(solution)/shard_map/ppermute | solution.py:425
  190.4 9.3 %collective-permute-start.44 = (bf16[256,256]{1,0:T(8,128)(2,1)S(1)}, bf16[256,256]{1,0:T(8,128)(2,1)S(1)}, u32[]{:S(2)}, u32[]{:S(2)}) collective-permute-start(bf16[256,256]{1,0:T(8,128)(2,1)S(1)} %shard_map.146.refs_0_), channel_id=1, source_target_pairs={{0,8},{4,12},{8,0},{12,4},{1,9},{5,13},{9,1},{13,5},{2,10},{6,14},... | collective-permute-start | bytes 393224 | tf_op jit(solution)/shard_map/ppermute | solution.py:425
  193.0 9.0 %collective-permute-start.37 = (bf16[256,256]{1,0:T(8,128)(2,1)S(1)}, bf16[256,256]{1,0:T(8,128)(2,1)S(1)}, u32[]{:S(2)}, u32[]{:S(2)}) collective-permute-start(bf16[256,256]{1,0:T(8,128)(2,1)S(1)} %collective-permute-done.36.refs_2_), channel_id=1, source_target_pairs={{0,4},{4,0},{8,12},{12,8},{1,5},{5,1},{9,13},{13,9},{2,6},{6,2},{1... | collective-permute-start | bytes 393224 | tf_op jit(solution)/shard_map/ppermute | solution.py:425
  199.7 5.0 %collective-permute-start.45 = (bf16[256,256]{1,0:T(8,128)(2,1)S(1)}, bf16[256,256]{1,0:T(8,128)(2,1)S(1)}, u32[]{:S(2)}, u32[]{:S(2)}) collective-permute-start(bf16[256,256]{1,0:T(8,128)(2,1)S(1)} %collective-permute-done.44.refs_2_), channel_id=1, source_target_pairs={{0,4},{4,0},{8,12},{12,8},{1,5},{5,1},{9,13},{13,9},{2,6},{6,2},{1... | collective-permute-start | bytes 393224 | tf_op jit(solution)/shard_map/ppermute | solution.py:425
  202.6 2.8 %collective-permute-start.38 = (bf16[128,768]{1,0:T(8,128)(2,1)S(1)}, bf16[128,768]{1,0:T(8,128)(2,1)S(1)}, u32[]{:S(2)}, u32[]{:S(2)}) collective-permute-start(bf16[128,768]{1,0:T(8,128)(2,1)S(1)} %get-tuple-element.87), channel_id=1, source_target_pairs={{0,1},{1,0},{2,3},{3,2},{4,5},{5,4},{6,7},{7,6},{8,9},{9,8},{10,11... | collective-permute-start | bytes 589832 | tf_op jit(solution)/shard_map/ppermute | solution.py:501
  205.3 1.5 collective-permute-start.46
  206.9 11.0 %collective-permute-start.47 = (bf16[128,768]{1,0:T(8,128)(2,1)S(1)}, bf16[128,768]{1,0:T(8,128)(2,1)S(1)}, u32[]{:S(2)}, u32[]{:S(2)}) collective-permute-start(bf16[128,768]{1,0:T(8,128)(2,1)S(1)} %get-tuple-element.107), channel_id=1, source_target_pairs={{0,8},{1,12},{2,0},{3,4},{4,9},{5,13},{6,1},{7,5},{8,10},{9,14},{1... | collective-permute-start | bytes 589832 | tf_op jit(solution)/shard_map/ppermute | solution.py:530
  207.5 14.5 %collective-permute-start.39 = (bf16[128,768]{1,0:T(8,128)(2,1)S(1)}, bf16[128,768]{1,0:T(8,128)(2,1)S(1)}, u32[]{:S(2)}, u32[]{:S(2)}) collective-permute-start(bf16[128,768]{1,0:T(8,128)(2,1)S(1)} %get-tuple-element.106), channel_id=1, source_target_pairs={{0,0},{1,4},{2,8},{3,12},{4,1},{5,5},{6,9},{7,13},{8,2},{9,6},{10,... | collective-permute-start | bytes 589832 | tf_op jit(solution)/shard_map/ppermute | solution.py:530
  (6 other events, 40.4 us)

commit v7 on v6

--- a/solution.py
+++ b/solution.py
@@ -258,15 +258,13 @@
                 block = pl.ds(pl.multiple_of(pos_ref[r * WAYS + k] * BLOCK, BLOCK), BLOCK)
                 keys.append(held[k][block, lanes])
                 values.append(held[k][block, value_lanes])
-            total = jnp.zeros((tile, 1), jnp.float32)
-            summed = jnp.zeros((tile, head_dim), jnp.float32)
-            for key, value in zip(keys, values):
-                scores = lax.dot_general(query, key, across, preferred_element_type=jnp.float32)
-                weights = jnp.exp(scores * head_dim ** (-0.5))
-                total += jnp.sum(weights, axis=-1, keepdims=True)
-                summed += jnp.dot(
-                    weights.astype(jnp.bfloat16), value, preferred_element_type=jnp.float32
-                )
+            key, value = jnp.concatenate(keys, axis=0), jnp.concatenate(values, axis=0)
+            scores = lax.dot_general(query, key, across, preferred_element_type=jnp.float32)
+            weights = jnp.exp(scores * head_dim ** (-0.5))
+            total = jnp.sum(weights, axis=-1, keepdims=True)
+            summed = jnp.dot(
+                weights.astype(jnp.bfloat16), value, preferred_element_type=jnp.float32
+            )
             mixed_ref[at : at + tile, lanes] = (summed / total).astype(jnp.bfloat16)
 
 

time: 223 us -> 222 us (level)
  Pallas kernels: 30.3 us -> 27.9 us
  transfers between devices with their start and end apart: 48 -> 48, of which waited for: 24 -> 24; matrix products, arithmetic and copies ran while one was open for 4% -> 5% of each run, Pallas kernels for 12% -> 12%
where the time goes in v7:
time: 222 us; the launch traced here: 221 us
  waiting for transfers between devices  119 us (54%)
  starting transfers between devices  57.8 us (26%)
  Pallas kernels  27.9 us (13%)
  local copies, waits for them, and re-layouts  10.7 us (5%)
  other arithmetic  4.99 us (2%)
    ppermute x24, waiting for transfers between devices, from_z(): return lax.ppermute(value, 'cache', [(i, i ^ k) for i in range(WAYS)])  64.7 us
    ppermute x24, starting transfers between devices, from_z(): return lax.ppermute(value, 'cache', [(i, i ^ k) for i in range(WAYS)])  43 us
    ppermute x3, waiting for transfers between devices, split_heads(): far = {k: lax.ppermute(near[k], 'groups', SWAP) for k in order}  24.9 us
    ppermute x2, waiting for transfers between devices, split_heads(): lax.ppermute(value.astype(jnp.bfloat16), ('cache', 'fsdp', 'head'), [(a *...  10.9 us
    ppermute x2, waiting for transfers between devices, split_heads(): lax.ppermute(v, 'fsdp', SWAP)  7.1 us
    ppermute x1, waiting for transfers between devices, gather_pairs(): high_x = lax.ppermute(high, 'fsdp', SWAP)  6.32 us
    pallas_call x1, Pallas kernels, mix_own(): pl.pallas_call(functools.partial(mix_own_kernel, places), out_shape=[jax....  6.17 us
    pallas_call x1, Pallas kernels, project(): pl.pallas_call(project_kernel, out_shape=[jax.ShapeDtypeStruct((WAYS * ti...  5.07 us
  transfers between devices with their start and end apart: 48, of which 24 were waited for; matrix products, arithmetic and copies ran while one was open for 5% of the time, Pallas kernels for 12%

profile of v7, /device:TPU:2, one launch (start us, length us, event | category | flops | bytes accessed | tf_op | source)
XLA Modules:
  0.0 221.5 jit_solution(11781416973729739373)
XLA Ops:
  0.0 1.8 constant_dynamic-update-slice_fusion.9
  1.8 1.6 collective-permute-start
  3.4 2.6 %collective-permute-start.1 = (bf16[128,768]{1,0:T(8,128)(2,1)}, bf16[128,768]{1,0:T(8,128)(2,1)S(1)}, u32[]{:S(2)}, u32[]{:S(2)}) collective-permute-start(bf16[128,768]{1,0:T(8,128)(2,1)} %get-tuple-element.100), channel_id=1, source_target_pairs={{0,8},{4,12},{8,0},{12,4},{1,9},{5,13},{9,1},{13,5},{2,10},{6,14},... | collective-permute-start | bytes 589832 | tf_op jit(solution)/shard_map/ppermute | solution.py:423
  6.0 0.8 dynamic_slice.16
  6.9 2.9 %shard_map.137 = (bf16[768,384]{1,0:T(8,128)(2,1)}, bf16[768,384]{1,0:T(8,128)(2,1)}, bf16[768,384]{1,0:T(8,128)(2,1)}, f32[8,128]{1,0:T(8,128)}) custom-call(f32[768,128]{1,0:T(8,128)S(1)} %broadcast_in_dim.71.gain_ref, bf16[768,1024]{1,0:T(8,128)(2,1)} %refs_0_.3, bf16[768,1024]{1,0:T(8,128)(2,1)} %refs_1_.3, bf16[768,1024]{1,0:T(8,128)(2,1)} %refs_2_.3), custom_call_target="tpu_custom_call" | custom-call | tf_op jit(solution)/shard_map/pallas_call | solution.py:173
  10.8 3.6 %collective-permute-start.13 = (bf16[768,384]{1,0:T(8,128)(2,1)}, bf16[768,384]{1,0:T(8,128)(2,1)}, u32[]{:S(2)}, u32[]{:S(2)}) collective-permute-start(bf16[768,384]{1,0:T(8,128)(2,1)} %get-tuple-element.55), channel_id=1, source_target_pairs={{0,12},{4,8},{8,4},{12,0},{1,13},{5,9},{9,5},{13,1},{2,14},{6,10},... | collective-permute-start | bytes 1769480 | tf_op jit(solution)/shard_map/ppermute | solution.py:423
  14.7 0.6 gather_fusion.1
  15.3 2.0 shard_map.136
  17.4 0.8 copy-done.9
  18.2 0.8 copy-done.11
  19.7 0.7 gather_fusion.3
  21.0 1.8 gather_fusion
  22.8 1.9 shard_map.139
  24.8 1.2 pad_maximum_fusion
  26.0 0.6 collective-permute-start.5
  26.6 28.4 %collective-permute-done.2 = bf16[128,768]{1,0:T(8,128)(2,1)S(1)} collective-permute-done((bf16[128,768]{1,0:T(8,128)(2,1)S(1)}, bf16[128,768]{1,0:T(8,128)(2,1)S(1)}, u32[]{:S(2)}, u32[]{:S(2)}) %collective-permute-start.2) | collective-permute-done | bytes 196640 | tf_op jit(solution)/shard_map/ppermute | solution.py:423
  55.6 0.9 constant_dynamic-update-slice_fusion.8
  57.2 1.7 collective-permute-start.10
  58.9 6.3 %collective-permute-done.6 = bf16[2,128,768]{2,1,0:T(8,128)(2,1)S(1)} collective-permute-done((bf16[2,128,768]{2,1,0:T(8,128)(2,1)S(1)}, bf16[2,128,768]{2,1,0:T(8,128)(2,1)S(1)}, u32[]{:S(2)}, u32[]{:S(2)}) %collective-permute-start.6) | collective-permute-done | bytes 393248 | tf_op jit(solution)/shard_map/ppermute | solution.py:455
  65.3 2.9 %collective-permute-start.15 = (bf16[512,512]{1,0:T(8,128)(2,1)S(1)}, bf16[512,512]{1,0:T(8,128)(2,1)S(1)}, u32[]{:S(2)}, u32[]{:S(2)}) collective-permute-start(bf16[512,512]{1,0:T(8,128)(2,1)S(1)} %get-tuple-element.61), channel_id=1, source_target_pairs={{0,4},{4,0},{8,12},{12,8},{1,5},{5,1},{9,13},{13,9},{2,6},{6,2},{1... | collective-permute-start | bytes 1572872 | tf_op jit(solution)/shard_map/ppermute | solution.py:423
  68.2 1.4 collective-permute-start.16
  69.6 1.2 collective-permute-start.17
  71.3 1.5 collective-permute-done.10.refs_3_.refs_7_
  72.9 2.2 collective-permute-start.14
  75.2 11.8 %collective-permute-done.12.refs_5_.refs_9_ = bf16[768,384]{1,0:T(8,128)(2,1)S(1)} collective-permute-done((bf16[768,384]{1,0:T(8,128)(2,1)S(1)}, bf16[768,384]{1,0:T(8,128)(2,1)S(1)}, u32[]{:S(2)}, u32[]{:S(2)}) %collective-permute-start.12) | collective-permute-done | bytes 589856 | tf_op jit(solution)/shard_map/ppermute | solution.py:472
  87.0 11.6 %collective-permute-done.14.refs_7_.refs_11_ = bf16[768,384]{1,0:T(8,128)(2,1)S(1)} collective-permute-done((bf16[768,384]{1,0:T(8,128)(2,1)}, bf16[768,384]{1,0:T(8,128)(2,1)S(1)}, u32[]{:S(2)}, u32[]{:S(2)}) %collective-permute-start.14) | collective-permute-done | bytes 589856 | tf_op jit(solution)/shard_map/ppermute | solution.py:472
  98.6 5.1 %shard_map.138 = (bf16[512,256]{1,0:T(8,128)(2,1)S(1)}, bf16[512,256]{1,0:T(8,128)(2,1)S(1)}, bf16[512,256]{1,0:T(8,128)(2,1)S(1)}) custom-call(s32[16]{0:T(128)S(1)} %add.171.source_ref, f32[1,128]{1,0:T(1,128)S(1)} %bitcast.41, f32[1,128]{1,0:T(1,128)S(1)} %bitcast.44, bf16[16,128,768]{2,1,0:T(8,128)(2,1)S(1)} %constant_dynamic-update-slice_fusion.gathered_ref, ...), custom_call_target="tpu_custom_call" | custom-call | tf_op jit(solution)/shard_map/pallas_call | solution.py:340
  103.8 2.6 %collective-permute-done.16.refs_2_.refs_14_ = bf16[512,512]{1,0:T(8,128)(2,1)S(1)} collective-permute-done((bf16[512,512]{1,0:T(8,128)(2,1)S(1)}, bf16[512,512]{1,0:T(8,128)(2,1)S(1)}, u32[]{:S(2)}, u32[]{:S(2)}) %collective-permute-start.16) | collective-permute-done | bytes 524320 | tf_op jit(solution)/shard_map/ppermute | solution.py:423
  106.4 1.6 shard_map.140.refs_0_
  108.1 11.2 %collective-permute-start.18 = (bf16[256,256]{1,0:T(8,128)(2,1)S(1)}, bf16[256,256]{1,0:T(8,128)(2,1)S(1)}, u32[]{:S(2)}, u32[]{:S(2)}) collective-permute-start(bf16[256,256]{1,0:T(8,128)(2,1)S(1)} %shard_map.140.refs_0_), channel_id=1, source_target_pairs={{0,4},{4,0},{8,12},{12,8},{1,5},{5,1},{9,13},{13,9},{2,6},{6,2},{1... | collective-permute-start | bytes 393224 | tf_op jit(solution)/shard_map/ppermute | solution.py:423
  119.2 1.1 collective-permute-start.19
  120.4 1.6 shard_map.141.refs_0_
  122.0 2.0 collective-permute-start.21
  124.0 2.1 collective-permute-done.19.refs_2_
  126.1 3.4 %collective-permute-start.20 = (bf16[256,256]{1,0:T(8,128)(2,1)S(1)}, bf16[256,256]{1,0:T(8,128)(2,1)S(1)}, u32[]{:S(2)}, u32[]{:S(2)}) collective-permute-start(bf16[256,256]{1,0:T(8,128)(2,1)S(1)} %collective-permute-done.19.refs_2_), channel_id=1, source_target_pairs={{0,4},{4,0},{8,12},{12,8},{1,5},{5,1},{9,13},{13,9},{2,6},{6,2},{1... | collective-permute-start | bytes 393224 | tf_op jit(solution)/shard_map/ppermute | solution.py:423
  129.9 1.4 collective-permute-done.21.refs_1_
  131.8 1.8 collective-permute-done.20.refs_3_
  134.3 1.7 collective-permute-start.24
  136.0 0.7 add_convert_fusion.2
  136.7 3.5 %collective-permute-done.24.refs_3_ = bf16[256,256]{1,0:T(8,128)(2,1)S(1)} collective-permute-done((bf16[256,256]{1,0:T(8,128)(2,1)S(1)}, bf16[256,256]{1,0:T(8,128)(2,1)S(1)}, u32[]{:S(2)}, u32[]{:S(2)}) %collective-permute-start.24) | collective-permute-done | bytes 131104 | tf_op jit(solution)/shard_map/ppermute | solution.py:423
  140.7 1.3 shard_map.143
  142.1 0.9 dynamic-slice_reduce_fusion
  143.0 4.0 %collective-permute-done.26 = bf16[128,768]{1,0:T(8,128)(2,1)} collective-permute-done((bf16[128,768]{1,0:T(8,128)(2,1)}, bf16[128,768]{1,0:T(8,128)(2,1)}, u32[]{:S(2)}, u32[]{:S(2)}) %collective-permute-start.26) | collective-permute-done | bytes 196640 | tf_op jit(solution)/shard_map/ppermute | solution.py:508
  147.0 1.2 fusion
  148.2 1.7 collective-permute-start.27
  149.9 2.0 collective-permute-start.28
  152.5 5.2 %collective-permute-done.27 = bf16[128,768]{1,0:T(8,128)(2,1)S(1)} collective-permute-done((bf16[128,768]{1,0:T(8,128)(2,1)S(1)}, bf16[128,768]{1,0:T(8,128)(2,1)S(1)}, u32[]{:S(2)}, u32[]{:S(2)}) %collective-permute-start.27) | collective-permute-done | bytes 196640 | tf_op jit(solution)/shard_map/ppermute | solution.py:423
  157.6 2.8 %collective-permute-done.28 = bf16[128,768]{1,0:T(8,128)(2,1)S(1)} collective-permute-done((bf16[128,768]{1,0:T(8,128)(2,1)S(1)}, bf16[128,768]{1,0:T(8,128)(2,1)S(1)}, u32[]{:S(2)}, u32[]{:S(2)}) %collective-permute-start.28) | collective-permute-done | bytes 196640 | tf_op jit(solution)/shard_map/ppermute | solution.py:423
  160.7 5.4 %collective-permute-done.31 = bf16[128,768]{1,0:T(8,128)(2,1)S(1)} collective-permute-done((bf16[128,768]{1,0:T(8,128)(2,1)S(1)}, bf16[128,768]{1,0:T(8,128)(2,1)S(1)}, u32[]{:S(2)}, u32[]{:S(2)}) %collective-permute-start.31) | collective-permute-done | bytes 196640 | tf_op jit(solution)/shard_map/ppermute | solution.py:423
  167.4 1.5 collective-permute-start.32
  168.9 6.2 %shard_map.144 = (bf16[256,256]{1,0:T(8,128)(2,1)S(1)}, bf16[8,768,384]{2,1,0:T(8,128)(2,1)S(1)}, bf16[4,512,512]{2,1,0:T(8,128)(2,1)S(1)}) custom-call(s32[16]{0:T(128)S(1)} %reshape.272.pos_ref, f32[1,128]{1,0:T(1,128)S(1)} %bitcast.42, f32[1,128]{1,0:T(1,128)S(1)} %bitcast.45, bf16[2,128,768]{2,1,0:T(8,128)(2,1)S(1)} %get-tuple-element.105.refs_0_, ...), custom_call_target="tpu_custom_call" | custom-call | tf_op jit(solution)/shard_map/pallas_call | solution.py:363
  175.0 7.1 %collective-permute-done.32.refs_2_ = bf16[1,128,768]{2,1,0:T(8,128)(2,1)S(1)} collective-permute-done((bf16[1,128,768]{2,1,0:T(8,128)(2,1)S(1)}, bf16[1,128,768]{2,1,0:T(8,128)(2,1)S(1)}, u32[]{:S(2)}, u32[]{:S(2)}) %collective-permute-start.32) | collective-permute-done | bytes 196640 | tf_op jit(solution)/shard_map/ppermute | solution.py:518
  182.9 2.7 %collective-permute-start.36 = (bf16[256,256]{1,0:T(8,128)(2,1)S(1)}, bf16[256,256]{1,0:T(8,128)(2,1)S(1)}, u32[]{:S(2)}, u32[]{:S(2)}) collective-permute-start(bf16[256,256]{1,0:T(8,128)(2,1)S(1)} %get-tuple-element.83.refs_0_), channel_id=1, source_target_pairs={{0,8},{4,12},{8,0},{12,4},{1,9},{5,13},{9,1},{13,5},{2,10},{6,14},... | collective-permute-start | bytes 393224 | tf_op jit(solution)/shard_map/ppermute | solution.py:423
  185.6 3.5 %shard_map.146.refs_0_ = bf16[256,256]{1,0:T(8,128)(2,1)S(1)} custom-call(s32[16]{0:T(128)S(1)} %reshape.272.pos_ref, f32[1,128]{1,0:T(1,128)S(1)} %bitcast.43, f32[1,128]{1,0:T(1,128)S(1)} %bitcast.46, bf16[1,128,768]{2,1,0:T(8,128)(2,1)S(1)} %collective-permute-done.29.refs_0_, bf16[2,128,768]{2,1,0:T(8,128)(2,1)S(1)} %collective-permute-done.30.refs_1_, ...), custom_call_target="tpu_custom_call" | custom-call | tf_op jit(solution)/shard_map/pallas_call | solution.py:386
  189.2 2.0 collective-permute-start.44
  191.2 1.3 collective-permute-done.36.refs_2_
  192.8 5.3 %collective-permute-done.43.refs_1_ = bf16[256,256]{1,0:T(8,128)(2,1)S(1)} collective-permute-done((bf16[256,256]{1,0:T(8,128)(2,1)S(1)}, bf16[256,256]{1,0:T(8,128)(2,1)S(1)}, u32[]{:S(2)}, u32[]{:S(2)}) %collective-permute-start.43) | collective-permute-done | bytes 131104 | tf_op jit(solution)/shard_map/ppermute | solution.py:423
  198.7 2.5 %collective-permute-done.37.refs_3_ = bf16[256,256]{1,0:T(8,128)(2,1)S(1)} collective-permute-done((bf16[256,256]{1,0:T(8,128)(2,1)S(1)}, bf16[256,256]{1,0:T(8,128)(2,1)S(1)}, u32[]{:S(2)}, u32[]{:S(2)}) %collective-permute-start.37) | collective-permute-done | bytes 131104 | tf_op jit(solution)/shard_map/ppermute | solution.py:423
  201.8 1.6 collective-permute-done.45.refs_3_
  204.1 1.4 collective-permute-done.46
  206.2 3.7 %collective-permute-start.39 = (bf16[128,768]{1,0:T(8,128)(2,1)S(1)}, bf16[128,768]{1,0:T(8,128)(2,1)S(1)}, u32[]{:S(2)}, u32[]{:S(2)}) collective-permute-start(bf16[128,768]{1,0:T(8,128)(2,1)S(1)} %get-tuple-element.106), channel_id=1, source_target_pairs={{0,0},{1,4},{2,8},{3,12},{4,1},{5,5},{6,9},{7,13},{8,2},{9,6},{10,... | collective-permute-start | bytes 589832 | tf_op jit(solution)/shard_map/ppermute | solution.py:528
  209.9 6.9 %collective-permute-done.47 = bf16[128,768]{1,0:T(8,128)(2,1)S(1)} collective-permute-done((bf16[128,768]{1,0:T(8,128)(2,1)S(1)}, bf16[128,768]{1,0:T(8,128)(2,1)S(1)}, u32[]{:S(2)}, u32[]{:S(2)}) %collective-permute-start.47) | collective-permute-done | bytes 196640 | tf_op jit(solution)/shard_map/ppermute | solution.py:528
  216.7 4.0 %collective-permute-done.39 = bf16[128,768]{1,0:T(8,128)(2,1)S(1)} collective-permute-done((bf16[128,768]{1,0:T(8,128)(2,1)S(1)}, bf16[128,768]{1,0:T(8,128)(2,1)S(1)}, u32[]{:S(2)}, u32[]{:S(2)}) %collective-permute-start.39) | collective-permute-done | bytes 196640 | tf_op jit(solution)/shard_map/ppermute | solution.py:528
  220.8 0.7 add_convert_fusion
  (138 shorter events, 12.4 us)
Async XLA Ops:
  0.0 21.0 %copy-start = (bf16[1024,768]{1,0:T(8,128)(2,1)S(1)}, bf16[1024,768]{1,0:T(8,128)(2,1)}, u32[]{:S(2)}) copy-start(bf16[1024,768]{1,0:T(8,128)(2,1)} %param.19) | copy-start | bytes 4718596
  1.8 22.9 %collective-permute-start = (bf16[128,768]{1,0:T(8,128)(2,1)}, bf16[128,768]{1,0:T(8,128)(2,1)}, u32[]{:S(2)}, u32[]{:S(2)}) collective-permute-start(bf16[128,768]{1,0:T(8,128)(2,1)} %get-tuple-element.100), channel_id=1, source_target_pairs={{0,4},{4,0},{8,12},{12,8},{1,5},{5,1},{9,13},{13,9},{2,6},{6,2},{1... | collective-permute-start | bytes 589832 | tf_op jit(solution)/shard_map/ppermute | solution.py:423
  3.4 17.5 %collective-permute-start.1 = (bf16[128,768]{1,0:T(8,128)(2,1)}, bf16[128,768]{1,0:T(8,128)(2,1)S(1)}, u32[]{:S(2)}, u32[]{:S(2)}) collective-permute-start(bf16[128,768]{1,0:T(8,128)(2,1)} %get-tuple-element.100), channel_id=1, source_target_pairs={{0,8},{4,12},{8,0},{12,4},{1,9},{5,13},{9,1},{13,5},{2,10},{6,14},... | collective-permute-start | bytes 589832 | tf_op jit(solution)/shard_map/ppermute | solution.py:423
  9.9 46.7 %collective-permute-start.9 = (bf16[768,384]{1,0:T(8,128)(2,1)}, bf16[768,384]{1,0:T(8,128)(2,1)S(1)}, u32[]{:S(2)}, u32[]{:S(2)}) collective-permute-start(bf16[768,384]{1,0:T(8,128)(2,1)} %get-tuple-element.53), channel_id=1, source_target_pairs={{0,4},{4,0},{8,12},{12,8},{1,5},{5,1},{9,13},{13,9},{2,6},{6,2},{1... | collective-permute-start | bytes 1769480 | tf_op jit(solution)/shard_map/ppermute | solution.py:423
  10.4 46.7 %collective-permute-start.11 = (bf16[768,384]{1,0:T(8,128)(2,1)}, bf16[768,384]{1,0:T(8,128)(2,1)S(1)}, u32[]{:S(2)}, u32[]{:S(2)}) collective-permute-start(bf16[768,384]{1,0:T(8,128)(2,1)} %get-tuple-element.54), channel_id=1, source_target_pairs={{0,8},{4,12},{8,0},{12,4},{1,9},{5,13},{9,1},{13,5},{2,10},{6,14},... | collective-permute-start | bytes 1769480 | tf_op jit(solution)/shard_map/ppermute | solution.py:423
  10.8 46.4 %collective-permute-start.13 = (bf16[768,384]{1,0:T(8,128)(2,1)}, bf16[768,384]{1,0:T(8,128)(2,1)}, u32[]{:S(2)}, u32[]{:S(2)}) collective-permute-start(bf16[768,384]{1,0:T(8,128)(2,1)} %get-tuple-element.55), channel_id=1, source_target_pairs={{0,12},{4,8},{8,4},{12,0},{1,13},{5,9},{9,5},{13,1},{2,14},{6,10},... | collective-permute-start | bytes 1769480 | tf_op jit(solution)/shard_map/ppermute | solution.py:423
  21.0 34.1 %collective-permute-start.2 = (bf16[128,768]{1,0:T(8,128)(2,1)S(1)}, bf16[128,768]{1,0:T(8,128)(2,1)S(1)}, u32[]{:S(2)}, u32[]{:S(2)}) collective-permute-start(bf16[128,768]{1,0:T(8,128)(2,1)S(1)} %collective-permute-done.1), channel_id=1, source_target_pairs={{0,4},{4,0},{8,12},{12,8},{1,5},{5,1},{9,13},{13,9},{2,6},{6,2},{1... | collective-permute-start | bytes 589832 | tf_op jit(solution)/shard_map/ppermute | solution.py:423
  22.8 32.7 %copy-start.5 = (bf16[16,128,768]{2,1,0:T(8,128)(2,1)S(1)}, bf16[16,128,768]{2,1,0:T(8,128)(2,1)}, u32[]{:S(2)}) copy-start(bf16[16,128,768]{2,1,0:T(8,128)(2,1)} %get-tuple-element.99) | copy-start | bytes 9437188
  24.8 95.6 %copy-start.1 = (bf16[512,512]{1,0:T(8,128)(2,1)}, bf16[512,512]{1,0:T(8,128)(2,1)S(1)}, u32[]{:S(2)}) copy-start(bf16[512,512]{1,0:T(8,128)(2,1)S(1)} %get-tuple-element.59.refs_0_.refs_12_) | copy-start | bytes 1572868
  26.0 30.5 %collective-permute-start.5 = (bf16[2,128,768]{2,1,0:T(8,128)(2,1)S(1)}, bf16[2,128,768]{2,1,0:T(8,128)(2,1)S(1)}, u32[]{:S(2)}, u32[]{:S(2)}) collective-permute-start(bf16[2,128,768]{2,1,0:T(8,128)(2,1)S(1)} %pad_maximum_fusion), channel_id=1, source_target_pairs={{0,2},{2,0},{1,3},{3,1},{4,6},{6,4},{5,7},{7,5},{8,10},{10,8},{9,1... | collective-permute-start | bytes 1179656 | tf_op jit(solution)/shard_map/ppermute | solution.py:453
  55.1 43.5 %copy-start.10 = (bf16[768,384]{1,0:T(8,128)(2,1)S(1)}, bf16[768,384]{1,0:T(8,128)(2,1)}, u32[]{:S(2)}) copy-start(bf16[768,384]{1,0:T(8,128)(2,1)} %copy-done.9) | copy-start | bytes 1769476
  55.1 43.5 %copy-start.12 = (bf16[768,384]{1,0:T(8,128)(2,1)S(1)}, bf16[768,384]{1,0:T(8,128)(2,1)}, u32[]{:S(2)}) copy-start(bf16[768,384]{1,0:T(8,128)(2,1)} %copy-done.11) | copy-start | bytes 1769476
  55.1 43.5 %copy-start.16 = (f32[128]{0:T(128)S(1)}, f32[128]{0:T(128)}, u32[]{:S(2)}) copy-start(f32[128]{0:T(128)} %param.20) | copy-start | bytes 1540
  55.1 43.5 %copy-start.17 = (f32[128]{0:T(128)S(1)}, f32[128]{0:T(128)}, u32[]{:S(2)}) copy-start(f32[128]{0:T(128)} %param.21) | copy-start | bytes 1540
  55.1 10.1 %collective-permute-start.6 = (bf16[2,128,768]{2,1,0:T(8,128)(2,1)S(1)}, bf16[2,128,768]{2,1,0:T(8,128)(2,1)S(1)}, u32[]{:S(2)}, u32[]{:S(2)}) collective-permute-start(bf16[2,128,768]{2,1,0:T(8,128)(2,1)S(1)} %pad_maximum_fusion.1), channel_id=1, source_target_pairs={{0,2},{2,0},{1,3},{3,1},{4,6},{6,4},{5,7},{7,5},{8,10},{10,8},{9,1... | collective-permute-start | bytes 1179656 | tf_op jit(solution)/shard_map/ppermute | solution.py:455
  56.5 8.7 %collective-permute-start.3 = (bf16[2,128,768]{2,1,0:T(8,128)(2,1)S(1)}, bf16[2,128,768]{2,1,0:T(8,128)(2,1)S(1)}, u32[]{:S(2)}, u32[]{:S(2)}) collective-permute-start(bf16[2,128,768]{2,1,0:T(8,128)(2,1)S(1)} %pad_maximum_fusion), channel_id=1, source_target_pairs={{0,1},{1,0},{2,3},{3,2},{4,5},{5,4},{6,7},{7,6},{8,9},{9,8},{10,11... | collective-permute-start | bytes 1179656 | tf_op jit(solution)/shard_map/ppermute | solution.py:457
  56.6 47.1 %copy-start.7 = (bf16[768,384]{1,0:T(8,128)(2,1)}, bf16[768,384]{1,0:T(8,128)(2,1)S(1)}, u32[]{:S(2)}) copy-start(bf16[768,384]{1,0:T(8,128)(2,1)S(1)} %collective-permute-done.9.refs_2_.refs_6_) | copy-start | bytes 1769476
  56.6 11.5 %collective-permute-start.4 = (bf16[2,128,768]{2,1,0:T(8,128)(2,1)S(1)}, bf16[2,128,768]{2,1,0:T(8,128)(2,1)S(1)}, u32[]{:S(2)}, u32[]{:S(2)}) collective-permute-start(bf16[2,128,768]{2,1,0:T(8,128)(2,1)S(1)} %pad_maximum_fusion.1), channel_id=1, source_target_pairs={{0,1},{1,0},{2,3},{3,2},{4,5},{5,4},{6,7},{7,6},{8,9},{9,8},{10,11... | collective-permute-start | bytes 1179656 | tf_op jit(solution)/shard_map/ppermute | solution.py:457
  57.1 46.6 %copy-start.8 = (bf16[768,384]{1,0:T(8,128)(2,1)}, bf16[768,384]{1,0:T(8,128)(2,1)S(1)}, u32[]{:S(2)}) copy-start(bf16[768,384]{1,0:T(8,128)(2,1)S(1)} %collective-permute-done.11.refs_4_.refs_8_) | copy-start | bytes 1769476
  57.1 12.5 %collective-permute-start.7 = (bf16[2,128,768]{2,1,0:T(8,128)(2,1)S(1)}, bf16[2,128,768]{2,1,0:T(8,128)(2,1)S(1)}, u32[]{:S(2)}, u32[]{:S(2)}) collective-permute-start(bf16[2,128,768]{2,1,0:T(8,128)(2,1)S(1)} %collective-permute-done.5), channel_id=1, source_target_pairs={{0,1},{1,0},{2,3},{3,2},{4,5},{5,4},{6,7},{7,6},{8,9},{9,8},{10,11... | collective-permute-start | bytes 1179656 | tf_op jit(solution)/shard_map/ppermute | solution.py:457
  57.2 15.7 %collective-permute-start.10 = (bf16[768,384]{1,0:T(8,128)(2,1)S(1)}, bf16[768,384]{1,0:T(8,128)(2,1)S(1)}, u32[]{:S(2)}, u32[]{:S(2)}) collective-permute-start(bf16[768,384]{1,0:T(8,128)(2,1)S(1)} %collective-permute-done.9.refs_2_.refs_6_), channel_id=1, source_target_pairs={{0,16},{16,0},{1,17},{17,1},{2,18},{18,2},{3,19},{19,3},{4,20},{20... | collective-permute-start | bytes 1769480 | tf_op jit(solution)/shard_map/ppermute | solution.py:472
  65.2 5.6 %collective-permute-start.8 = (bf16[2,128,768]{2,1,0:T(8,128)(2,1)S(1)}, bf16[2,128,768]{2,1,0:T(8,128)(2,1)S(1)}, u32[]{:S(2)}, u32[]{:S(2)}) collective-permute-start(bf16[2,128,768]{2,1,0:T(8,128)(2,1)S(1)} %collective-permute-done.6), channel_id=1, source_target_pairs={{0,1},{1,0},{2,3},{3,2},{4,5},{5,4},{6,7},{7,6},{8,9},{9,8},{10,11... | collective-permute-start | bytes 1179656 | tf_op jit(solution)/shard_map/ppermute | solution.py:457
  65.3 38.5 %collective-permute-start.15 = (bf16[512,512]{1,0:T(8,128)(2,1)S(1)}, bf16[512,512]{1,0:T(8,128)(2,1)S(1)}, u32[]{:S(2)}, u32[]{:S(2)}) collective-permute-start(bf16[512,512]{1,0:T(8,128)(2,1)S(1)} %get-tuple-element.61), channel_id=1, source_target_pairs={{0,4},{4,0},{8,12},{12,8},{1,5},{5,1},{9,13},{13,9},{2,6},{6,2},{1... | collective-permute-start | bytes 1572872 | tf_op jit(solution)/shard_map/ppermute | solution.py:423
  68.2 38.2 %collective-permute-start.16 = (bf16[512,512]{1,0:T(8,128)(2,1)S(1)}, bf16[512,512]{1,0:T(8,128)(2,1)S(1)}, u32[]{:S(2)}, u32[]{:S(2)}) collective-permute-start(bf16[512,512]{1,0:T(8,128)(2,1)S(1)} %get-tuple-element.63), channel_id=1, source_target_pairs={{0,8},{4,12},{8,0},{12,4},{1,9},{5,13},{9,1},{13,5},{2,10},{6,14},... | collective-permute-start | bytes 1572872 | tf_op jit(solution)/shard_map/ppermute | solution.py:423
  69.6 36.8 %collective-permute-start.17 = (bf16[512,512]{1,0:T(8,128)(2,1)S(1)}, bf16[512,512]{1,0:T(8,128)(2,1)S(1)}, u32[]{:S(2)}, u32[]{:S(2)}) collective-permute-start(bf16[512,512]{1,0:T(8,128)(2,1)S(1)} %get-tuple-element.65), channel_id=1, source_target_pairs={{0,12},{4,8},{8,4},{12,0},{1,13},{5,9},{9,5},{13,1},{2,14},{6,10},... | collective-permute-start | bytes 1572872 | tf_op jit(solution)/shard_map/ppermute | solution.py:423
  70.8 16.2 %collective-permute-start.12 = (bf16[768,384]{1,0:T(8,128)(2,1)S(1)}, bf16[768,384]{1,0:T(8,128)(2,1)S(1)}, u32[]{:S(2)}, u32[]{:S(2)}) collective-permute-start(bf16[768,384]{1,0:T(8,128)(2,1)S(1)} %collective-permute-done.11.refs_4_.refs_8_), channel_id=1, source_target_pairs={{0,16},{16,0},{1,17},{17,1},{2,18},{18,2},{3,19},{19,3},{4,20},{20... | collective-permute-start | bytes 1769480 | tf_op jit(solution)/shard_map/ppermute | solution.py:472
  72.9 30.8 %copy-start.13 = (bf16[768,384]{1,0:T(8,128)(2,1)}, bf16[768,384]{1,0:T(8,128)(2,1)S(1)}, u32[]{:S(2)}) copy-start(bf16[768,384]{1,0:T(8,128)(2,1)S(1)} %collective-permute-done.10.refs_3_.refs_7_) | copy-start | bytes 1769476
  72.9 25.7 %collective-permute-start.14 = (bf16[768,384]{1,0:T(8,128)(2,1)}, bf16[768,384]{1,0:T(8,128)(2,1)S(1)}, u32[]{:S(2)}, u32[]{:S(2)}) collective-permute-start(bf16[768,384]{1,0:T(8,128)(2,1)} %collective-permute-done.13.refs_6_.refs_10_), channel_id=1, source_target_pairs={{0,16},{16,0},{1,17},{17,1},{2,18},{18,2},{3,19},{19,3},{4,20},{20... | collective-permute-start | bytes 1769480 | tf_op jit(solution)/shard_map/ppermute | solution.py:472
  75.2 28.5 %copy-start.6 = (bf16[16,128,768]{2,1,0:T(8,128)(2,1)}, bf16[16,128,768]{2,1,0:T(8,128)(2,1)S(1)}, u32[]{:S(2)}) copy-start(bf16[16,128,768]{2,1,0:T(8,128)(2,1)S(1)} %constant_dynamic-update-slice_fusion.gathered_ref) | copy-start | bytes 9437188
  87.0 16.8 %copy-start.14 = (bf16[768,384]{1,0:T(8,128)(2,1)}, bf16[768,384]{1,0:T(8,128)(2,1)S(1)}, u32[]{:S(2)}) copy-start(bf16[768,384]{1,0:T(8,128)(2,1)S(1)} %collective-permute-done.12.refs_5_.refs_9_) | copy-start | bytes 1769476
  103.8 25.8 %copy-start.20 = (bf16[8,128,768]{2,1,0:T(8,128)(2,1)S(1)}, bf16[8,128,768]{2,1,0:T(8,128)(2,1)}, u32[]{:S(2)}) copy-start(bf16[8,128,768]{2,1,0:T(8,128)(2,1)} %gather_fusion) | copy-start | bytes 4718596
  103.8 26.1 %copy-start.2 = (bf16[512,512]{1,0:T(8,128)(2,1)}, bf16[512,512]{1,0:T(8,128)(2,1)S(1)}, u32[]{:S(2)}) copy-start(bf16[512,512]{1,0:T(8,128)(2,1)S(1)} %collective-permute-done.15.refs_1_.refs_13_) | copy-start | bytes 1572868
  106.4 23.5 %copy-start.3 = (bf16[512,512]{1,0:T(8,128)(2,1)}, bf16[512,512]{1,0:T(8,128)(2,1)S(1)}, u32[]{:S(2)}) copy-start(bf16[512,512]{1,0:T(8,128)(2,1)S(1)} %collective-permute-done.16.refs_2_.refs_14_) | copy-start | bytes 1572868
  106.4 23.5 %copy-start.4 = (bf16[512,512]{1,0:T(8,128)(2,1)}, bf16[512,512]{1,0:T(8,128)(2,1)S(1)}, u32[]{:S(2)}) copy-start(bf16[512,512]{1,0:T(8,128)(2,1)S(1)} %collective-permute-done.17.refs_3_.refs_15_) | copy-start | bytes 1572868
  108.1 16.0 %collective-permute-start.18 = (bf16[256,256]{1,0:T(8,128)(2,1)S(1)}, bf16[256,256]{1,0:T(8,128)(2,1)S(1)}, u32[]{:S(2)}, u32[]{:S(2)}) collective-permute-start(bf16[256,256]{1,0:T(8,128)(2,1)S(1)} %shard_map.140.refs_0_), channel_id=1, source_target_pairs={{0,4},{4,0},{8,12},{12,8},{1,5},{5,1},{9,13},{13,9},{2,6},{6,2},{1... | collective-permute-start | bytes 393224 | tf_op jit(solution)/shard_map/ppermute | solution.py:423
  119.2 6.9 %collective-permute-start.19 = (bf16[256,256]{1,0:T(8,128)(2,1)S(1)}, bf16[256,256]{1,0:T(8,128)(2,1)S(1)}, u32[]{:S(2)}, u32[]{:S(2)}) collective-permute-start(bf16[256,256]{1,0:T(8,128)(2,1)S(1)} %shard_map.140.refs_0_), channel_id=1, source_target_pairs={{0,8},{4,12},{8,0},{12,4},{1,9},{5,13},{9,1},{13,5},{2,10},{6,14},... | collective-permute-start | bytes 393224 | tf_op jit(solution)/shard_map/ppermute | solution.py:423
  122.0 9.3 %collective-permute-start.21 = (bf16[256,256]{1,0:T(8,128)(2,1)S(1)}, bf16[256,256]{1,0:T(8,128)(2,1)S(1)}, u32[]{:S(2)}, u32[]{:S(2)}) collective-permute-start(bf16[256,256]{1,0:T(8,128)(2,1)S(1)} %shard_map.141.refs_0_), channel_id=1, source_target_pairs={{0,4},{4,0},{8,12},{12,8},{1,5},{5,1},{9,13},{13,9},{2,6},{6,2},{1... | collective-permute-start | bytes 393224 | tf_op jit(solution)/shard_map/ppermute | solution.py:423
  124.0 7.8 %collective-permute-start.22 = (bf16[256,256]{1,0:T(8,128)(2,1)S(1)}, bf16[256,256]{1,0:T(8,128)(2,1)S(1)}, u32[]{:S(2)}, u32[]{:S(2)}) collective-permute-start(bf16[256,256]{1,0:T(8,128)(2,1)S(1)} %shard_map.141.refs_0_), channel_id=1, source_target_pairs={{0,8},{4,12},{8,0},{12,4},{1,9},{5,13},{9,1},{13,5},{2,10},{6,14},... | collective-permute-start | bytes 393224 | tf_op jit(solution)/shard_map/ppermute | solution.py:423
  126.1 7.5 %collective-permute-start.20 = (bf16[256,256]{1,0:T(8,128)(2,1)S(1)}, bf16[256,256]{1,0:T(8,128)(2,1)S(1)}, u32[]{:S(2)}, u32[]{:S(2)}) collective-permute-start(bf16[256,256]{1,0:T(8,128)(2,1)S(1)} %collective-permute-done.19.refs_2_), channel_id=1, source_target_pairs={{0,4},{4,0},{8,12},{12,8},{1,5},{5,1},{9,13},{13,9},{2,6},{6,2},{1... | collective-permute-start | bytes 393224 | tf_op jit(solution)/shard_map/ppermute | solution.py:423
  134.2 1.8 collective-permute-start.23
  134.3 5.9 %collective-permute-start.24 = (bf16[256,256]{1,0:T(8,128)(2,1)S(1)}, bf16[256,256]{1,0:T(8,128)(2,1)S(1)}, u32[]{:S(2)}, u32[]{:S(2)}) collective-permute-start(bf16[256,256]{1,0:T(8,128)(2,1)S(1)} %collective-permute-done.22.refs_2_), channel_id=1, source_target_pairs={{0,4},{4,0},{8,12},{12,8},{1,5},{5,1},{9,13},{13,9},{2,6},{6,2},{1... | collective-permute-start | bytes 393224 | tf_op jit(solution)/shard_map/ppermute | solution.py:423
  140.2 6.8 %collective-permute-start.26 = (bf16[128,768]{1,0:T(8,128)(2,1)}, bf16[128,768]{1,0:T(8,128)(2,1)}, u32[]{:S(2)}, u32[]{:S(2)}) collective-permute-start(bf16[128,768]{1,0:T(8,128)(2,1)} %add_convert_fusion.2), channel_id=1, source_target_pairs={{0,2},{2,0},{1,3},{3,1},{4,6},{6,4},{5,7},{7,5},{8,10},{10,8},{9,1... | collective-permute-start | bytes 589832 | tf_op jit(solution)/shard_map/ppermute | solution.py:508
  142.0 5.0 %collective-permute-start.25 = (bf16[128,768]{1,0:T(8,128)(2,1)}, bf16[128,768]{1,0:T(8,128)(2,1)}, u32[]{:S(2)}, u32[]{:S(2)}) collective-permute-start(bf16[128,768]{1,0:T(8,128)(2,1)} %get-tuple-element.78), channel_id=1, source_target_pairs={{0,1},{1,0},{2,3},{3,2},{4,5},{5,4},{6,7},{7,6},{8,9},{9,8},{10,11... | collective-permute-start | bytes 589832 | tf_op jit(solution)/shard_map/ppermute | solution.py:499
  148.2 9.4 %collective-permute-start.27 = (bf16[128,768]{1,0:T(8,128)(2,1)S(1)}, bf16[128,768]{1,0:T(8,128)(2,1)S(1)}, u32[]{:S(2)}, u32[]{:S(2)}) collective-permute-start(bf16[128,768]{1,0:T(8,128)(2,1)S(1)} %fusion), channel_id=1, source_target_pairs={{0,4},{4,0},{8,12},{12,8},{1,5},{5,1},{9,13},{13,9},{2,6},{6,2},{1... | collective-permute-start | bytes 589832 | tf_op jit(solution)/shard_map/ppermute | solution.py:423
  149.9 10.6 %collective-permute-start.28 = (bf16[128,768]{1,0:T(8,128)(2,1)S(1)}, bf16[128,768]{1,0:T(8,128)(2,1)S(1)}, u32[]{:S(2)}, u32[]{:S(2)}) collective-permute-start(bf16[128,768]{1,0:T(8,128)(2,1)S(1)} %fusion), channel_id=1, source_target_pairs={{0,8},{4,12},{8,0},{12,4},{1,9},{5,13},{9,1},{13,5},{2,10},{6,14},... | collective-permute-start | bytes 589832 | tf_op jit(solution)/shard_map/ppermute | solution.py:423
  151.9 8.5 %collective-permute-start.29 = (bf16[1,128,768]{2,1,0:T(8,128)(2,1)S(1)}, bf16[1,128,768]{2,1,0:T(8,128)(2,1)S(1)}, u32[]{:S(2)}, u32[]{:S(2)}) collective-permute-start(bf16[1,128,768]{2,1,0:T(8,128)(2,1)S(1)} %bitcast.50), channel_id=1, source_target_pairs={{0,2},{2,0},{1,3},{3,1},{4,6},{6,4},{5,7},{7,5},{8,10},{10,8},{9,1... | collective-permute-start | bytes 589832 | tf_op jit(solution)/shard_map/ppermute | solution.py:513
  160.5 5.7 %collective-permute-start.31 = (bf16[128,768]{1,0:T(8,128)(2,1)S(1)}, bf16[128,768]{1,0:T(8,128)(2,1)S(1)}, u32[]{:S(2)}, u32[]{:S(2)}) collective-permute-start(bf16[128,768]{1,0:T(8,128)(2,1)S(1)} %collective-permute-done.28), channel_id=1, source_target_pairs={{0,4},{4,0},{8,12},{12,8},{1,5},{5,1},{9,13},{13,9},{2,6},{6,2},{1... | collective-permute-start | bytes 589832 | tf_op jit(solution)/shard_map/ppermute | solution.py:423
  166.2 2.6 %collective-permute-start.33 = (bf16[2,128,768]{2,1,0:T(8,128)(2,1)S(1)}, bf16[2,128,768]{2,1,0:T(8,128)(2,1)S(1)}, u32[]{:S(2)}, u32[]{:S(2)}) collective-permute-start(bf16[2,128,768]{2,1,0:T(8,128)(2,1)S(1)} %get-tuple-element.105.refs_0_), channel_id=1, source_target_pairs={{0,1},{1,0},{2,3},{3,2},{4,5},{5,4},{6,7},{7,6},{8,9},{9,8},{10,11... | collective-permute-start | bytes 1179656 | tf_op jit(solution)/shard_map/ppermute | solution.py:517
  166.3 2.5 %collective-permute-start.34 = (bf16[2,128,768]{2,1,0:T(8,128)(2,1)S(1)}, bf16[2,128,768]{2,1,0:T(8,128)(2,1)S(1)}, u32[]{:S(2)}, u32[]{:S(2)}) collective-permute-start(bf16[2,128,768]{2,1,0:T(8,128)(2,1)S(1)} %get-tuple-element.103.refs_1_), channel_id=1, source_target_pairs={{0,1},{1,0},{2,3},{3,2},{4,5},{5,4},{6,7},{7,6},{8,9},{9,8},{10,11... | collective-permute-start | bytes 1179656 | tf_op jit(solution)/shard_map/ppermute | solution.py:517
  166.8 15.3 %collective-permute-start.30 = (bf16[2,128,768]{2,1,0:T(8,128)(2,1)S(1)}, bf16[2,128,768]{2,1,0:T(8,128)(2,1)S(1)}, u32[]{:S(2)}, u32[]{:S(2)}) collective-permute-start(bf16[2,128,768]{2,1,0:T(8,128)(2,1)S(1)} %get-tuple-element.104), channel_id=1, source_target_pairs={{0,2},{2,0},{1,3},{3,1},{4,6},{6,4},{5,7},{7,5},{8,10},{10,8},{9,1... | collective-permute-start | bytes 1179656 | tf_op jit(solution)/shard_map/ppermute | solution.py:518
  167.4 14.8 %collective-permute-start.32 = (bf16[1,128,768]{2,1,0:T(8,128)(2,1)S(1)}, bf16[1,128,768]{2,1,0:T(8,128)(2,1)S(1)}, u32[]{:S(2)}, u32[]{:S(2)}) collective-permute-start(bf16[1,128,768]{2,1,0:T(8,128)(2,1)S(1)} %bitcast.55), channel_id=1, source_target_pairs={{0,2},{2,0},{1,3},{3,1},{4,6},{6,4},{5,7},{7,5},{8,10},{10,8},{9,1... | collective-permute-start | bytes 589832 | tf_op jit(solution)/shard_map/ppermute | solution.py:518
  182.1 3.5 %collective-permute-start.41 = (bf16[2,128,768]{2,1,0:T(8,128)(2,1)S(1)}, bf16[2,128,768]{2,1,0:T(8,128)(2,1)S(1)}, u32[]{:S(2)}, u32[]{:S(2)}) collective-permute-start(bf16[2,128,768]{2,1,0:T(8,128)(2,1)S(1)} %collective-permute-done.30.refs_1_), channel_id=1, source_target_pairs={{0,1},{1,0},{2,3},{3,2},{4,5},{5,4},{6,7},{7,6},{8,9},{9,8},{10,11... | collective-permute-start | bytes 1179656 | tf_op jit(solution)/shard_map/ppermute | solution.py:523
  182.1 3.5 %collective-permute-start.40 = (bf16[1,128,768]{2,1,0:T(8,128)(2,1)S(1)}, bf16[1,128,768]{2,1,0:T(8,128)(2,1)S(1)}, u32[]{:S(2)}, u32[]{:S(2)}) collective-permute-start(bf16[1,128,768]{2,1,0:T(8,128)(2,1)S(1)} %collective-permute-done.29.refs_0_), channel_id=1, source_target_pairs={{0,1},{1,0},{2,3},{3,2},{4,5},{5,4},{6,7},{7,6},{8,9},{9,8},{10,11... | collective-permute-start | bytes 589832 | tf_op jit(solution)/shard_map/ppermute | solution.py:523
  182.6 3.0 %collective-permute-start.42 = (bf16[1,128,768]{2,1,0:T(8,128)(2,1)S(1)}, bf16[1,128,768]{2,1,0:T(8,128)(2,1)S(1)}, u32[]{:S(2)}, u32[]{:S(2)}) collective-permute-start(bf16[1,128,768]{2,1,0:T(8,128)(2,1)S(1)} %collective-permute-done.32.refs_2_), channel_id=1, source_target_pairs={{0,1},{1,0},{2,3},{3,2},{4,5},{5,4},{6,7},{7,6},{8,9},{9,8},{10,11... | collective-permute-start | bytes 589832 | tf_op jit(solution)/shard_map/ppermute | solution.py:523
  182.7 8.5 %collective-permute-start.35 = (bf16[256,256]{1,0:T(8,128)(2,1)S(1)}, bf16[256,256]{1,0:T(8,128)(2,1)S(1)}, u32[]{:S(2)}, u32[]{:S(2)}) collective-permute-start(bf16[256,256]{1,0:T(8,128)(2,1)S(1)} %get-tuple-element.83.refs_0_), channel_id=1, source_target_pairs={{0,4},{4,0},{8,12},{12,8},{1,5},{5,1},{9,13},{13,9},{2,6},{6,2},{1... | collective-permute-start | bytes 393224 | tf_op jit(solution)/shard_map/ppermute | solution.py:423
  182.9 9.6 %collective-permute-start.36 = (bf16[256,256]{1,0:T(8,128)(2,1)S(1)}, bf16[256,256]{1,0:T(8,128)(2,1)S(1)}, u32[]{:S(2)}, u32[]{:S(2)}) collective-permute-start(bf16[256,256]{1,0:T(8,128)(2,1)S(1)} %get-tuple-element.83.refs_0_), channel_id=1, source_target_pairs={{0,8},{4,12},{8,0},{12,4},{1,9},{5,13},{9,1},{13,5},{2,10},{6,14},... | collective-permute-start | bytes 393224 | tf_op jit(solution)/shard_map/ppermute | solution.py:423
  189.1 9.0 %collective-permute-start.43 = (bf16[256,256]{1,0:T(8,128)(2,1)S(1)}, bf16[256,256]{1,0:T(8,128)(2,1)S(1)}, u32[]{:S(2)}, u32[]{:S(2)}) collective-permute-start(bf16[256,256]{1,0:T(8,128)(2,1)S(1)} %shard_map.146.refs_0_), channel_id=1, source_target_pairs={{0,4},{4,0},{8,12},{12,8},{1,5},{5,1},{9,13},{13,9},{2,6},{6,2},{1... | collective-permute-start | bytes 393224 | tf_op jit(solution)/shard_map/ppermute | solution.py:423
  189.2 9.2 %collective-permute-start.44 = (bf16[256,256]{1,0:T(8,128)(2,1)S(1)}, bf16[256,256]{1,0:T(8,128)(2,1)S(1)}, u32[]{:S(2)}, u32[]{:S(2)}) collective-permute-start(bf16[256,256]{1,0:T(8,128)(2,1)S(1)} %shard_map.146.refs_0_), channel_id=1, source_target_pairs={{0,8},{4,12},{8,0},{12,4},{1,9},{5,13},{9,1},{13,5},{2,10},{6,14},... | collective-permute-start | bytes 393224 | tf_op jit(solution)/shard_map/ppermute | solution.py:423
  192.5 8.7 %collective-permute-start.37 = (bf16[256,256]{1,0:T(8,128)(2,1)S(1)}, bf16[256,256]{1,0:T(8,128)(2,1)S(1)}, u32[]{:S(2)}, u32[]{:S(2)}) collective-permute-start(bf16[256,256]{1,0:T(8,128)(2,1)S(1)} %collective-permute-done.36.refs_2_), channel_id=1, source_target_pairs={{0,4},{4,0},{8,12},{12,8},{1,5},{5,1},{9,13},{13,9},{2,6},{6,2},{1... | collective-permute-start | bytes 393224 | tf_op jit(solution)/shard_map/ppermute | solution.py:423
  198.4 5.0 %collective-permute-start.45 = (bf16[256,256]{1,0:T(8,128)(2,1)S(1)}, bf16[256,256]{1,0:T(8,128)(2,1)S(1)}, u32[]{:S(2)}, u32[]{:S(2)}) collective-permute-start(bf16[256,256]{1,0:T(8,128)(2,1)S(1)} %collective-permute-done.44.refs_2_), channel_id=1, source_target_pairs={{0,4},{4,0},{8,12},{12,8},{1,5},{5,1},{9,13},{13,9},{2,6},{6,2},{1... | collective-permute-start | bytes 393224 | tf_op jit(solution)/shard_map/ppermute | solution.py:423
  201.7 2.4 %collective-permute-start.38 = (bf16[128,768]{1,0:T(8,128)(2,1)S(1)}, bf16[128,768]{1,0:T(8,128)(2,1)S(1)}, u32[]{:S(2)}, u32[]{:S(2)}) collective-permute-start(bf16[128,768]{1,0:T(8,128)(2,1)S(1)} %get-tuple-element.87), channel_id=1, source_target_pairs={{0,1},{1,0},{2,3},{3,2},{4,5},{5,4},{6,7},{7,6},{8,9},{9,8},{10,11... | collective-permute-start | bytes 589832 | tf_op jit(solution)/shard_map/ppermute | solution.py:499
  204.0 1.5 collective-permute-start.46
  205.6 11.1 %collective-permute-start.47 = (bf16[128,768]{1,0:T(8,128)(2,1)S(1)}, bf16[128,768]{1,0:T(8,128)(2,1)S(1)}, u32[]{:S(2)}, u32[]{:S(2)}) collective-permute-start(bf16[128,768]{1,0:T(8,128)(2,1)S(1)} %get-tuple-element.107), channel_id=1, source_target_pairs={{0,8},{1,12},{2,0},{3,4},{4,9},{5,13},{6,1},{7,5},{8,10},{9,14},{1... | collective-permute-start | bytes 589832 | tf_op jit(solution)/shard_map/ppermute | solution.py:528
  206.2 14.6 %collective-permute-start.39 = (bf16[128,768]{1,0:T(8,128)(2,1)S(1)}, bf16[128,768]{1,0:T(8,128)(2,1)S(1)}, u32[]{:S(2)}, u32[]{:S(2)}) collective-permute-start(bf16[128,768]{1,0:T(8,128)(2,1)S(1)} %get-tuple-element.106), channel_id=1, source_target_pairs={{0,0},{1,4},{2,8},{3,12},{4,1},{5,5},{6,9},{7,13},{8,2},{9,6},{10,... | collective-permute-start | bytes 589832 | tf_op jit(solution)/shard_map/ppermute | solution.py:528
  (6 other events, 40.4 us)

commit v8 on v7

--- a/solution.py
+++ b/solution.py
@@ -220,16 +220,23 @@
     totals = [None, None]
     squares = [0.0] * tiles
     columns = 0
+    wide_rows = []
     for k in range(WAYS):
         blocks = [part(r, k) for r in range(tiles)]
         rows = jnp.concatenate(blocks, axis=0)
         columns += rows.shape[1]
-        for h in range(2):
-            product = jnp.dot(rows, panel(k, h), preferred_element_type=jnp.float32)
-            totals[h] = product if k == 0 else totals[h] + product
+        wide_rows.append(rows)
+        if callable(panel):
+            for h in range(2):
+                product = jnp.dot(rows, panel(k, h), preferred_element_type=jnp.float32)
+                totals[h] = product if k == 0 else totals[h] + product
         for r in range(tiles):
             wide = blocks[r].astype(jnp.float32)
             squares[r] += jnp.sum(wide * wide, axis=-1, keepdims=True)
+    if not callable(panel):
+        rows = jnp.concatenate(wide_rows, axis=1)
+        product = jnp.dot(rows, panel[...], preferred_element_type=jnp.float32)
+        totals = [product[:, : 3 * head_dim], product[:, 3 * head_dim :]]
     scale = lax.rsqrt(jnp.concatenate(squares, axis=0) / columns + epsilon)
     for h in range(2):
         total = totals[h] * scale
@@ -299,8 +306,15 @@
 def mix_own_kernel(places, pos_ref, query_gain_ref, key_gain_ref, *refs):
     parts, panels, caches = refs[:WAYS], refs[WAYS : 3 * WAYS], refs[3 * WAYS : 4 * WAYS]
     mixed_ref, panel_ref, held_ref, *outs, panel_sems, held_sems = refs[4 * WAYS :]
+    depth, lanes = panels[0].shape
     copies = [
-        pltpu.make_async_copy(source, panel_ref.at[i], panel_sems.at[i])
+        pltpu.make_async_copy(
+            source,
+            panel_ref.at[
+                i // 2 * depth : (i // 2 + 1) * depth, i % 2 * lanes : (i % 2 + 1) * lanes
+            ],
+            panel_sems.at[i],
+        )
         for i, source in enumerate(panels)
     ]
     late = [
@@ -312,7 +326,7 @@
 
     def panel(k, h):
         copies[2 * k + h].wait()
-        return panel_ref[2 * k + h]
+        return panel_ref[k * depth : (k + 1) * depth, h * lanes : (h + 1) * lanes]
 
     def held():
         for copy in late:
@@ -325,8 +339,7 @@
 def mix_other_kernel(places, pos_ref, query_gain_ref, key_gain_ref, *refs):
     *parts, panel_ref, held_ref, mixed_ref, q_ref, k_ref, v_ref = refs
 
-    def panel(k, h):
-        return panel_ref[2 * k + h]
+    panel = panel_ref
 
     def held():
         return [held_ref.at[k] for k in range(WAYS)]
@@ -364,7 +377,7 @@
         functools.partial(mix_own_kernel, places),
         out_shape=[
             jax.ShapeDtypeStruct(shape, jnp.bfloat16),
-            jax.ShapeDtypeStruct((len(panels), *panels[0].shape), jnp.bfloat16),
+            jax.ShapeDtypeStruct((WAYS * panels[0].shape[0], 2 * panels[0].shape[1]), jnp.bfloat16),
             jax.ShapeDtypeStruct((len(held), *held[0].shape), jnp.bfloat16),
         ],
         in_specs=[pl.BlockSpec(memory_space=pltpu.SMEM)]

time: 222 us -> 222 us (level)
  transfers between devices with their start and end apart: 48 -> 48, of which waited for: 24 -> 25; matrix products, arithmetic and copies ran while one was open for 5% -> 5% of each run, Pallas kernels for 12% -> 11%
where the time goes in v8:
time: 222 us; the launch traced here: 221 us
  waiting for transfers between devices  119 us (54%)
  starting transfers between devices  58.3 us (26%)
  Pallas kernels  27.6 us (12%)
  local copies, waits for them, and re-layouts  10.7 us (5%)
  other arithmetic  4.99 us (2%)
    ppermute x24, waiting for transfers between devices, from_z(): return lax.ppermute(value, 'cache', [(i, i ^ k) for i in range(WAYS)])  64.6 us
    ppermute x24, starting transfers between devices, from_z(): return lax.ppermute(value, 'cache', [(i, i ^ k) for i in range(WAYS)])  43.1 us
    ppermute x3, waiting for transfers between devices, split_heads(): far = {k: lax.ppermute(near[k], 'groups', SWAP) for k in order}  24.9 us
    ppermute x2, waiting for transfers between devices, split_heads(): lax.ppermute(value.astype(jnp.bfloat16), ('cache', 'fsdp', 'head'), [(a *...  10.7 us
    ppermute x2, waiting for transfers between devices, split_heads(): lax.ppermute(v, 'fsdp', SWAP)  7.1 us
    ppermute x1, waiting for transfers between devices, gather_pairs(): high_x = lax.ppermute(high, 'fsdp', SWAP)  6.32 us
    pallas_call x1, Pallas kernels, mix_own(): pl.pallas_call(functools.partial(mix_own_kernel, places), out_shape=[jax....  6.17 us
    pallas_call x1, Pallas kernels, project(): pl.pallas_call(project_kernel, out_shape=[jax.ShapeDtypeStruct((WAYS * ti...  5.07 us
  transfers between devices with their start and end apart: 48, of which 25 were waited for; matrix products, arithmetic and copies ran while one was open for 5% of the time, Pallas kernels for 11%

profile of v8, /device:TPU:2, one launch (start us, length us, event | category | flops | bytes accessed | tf_op | source)
XLA Modules:
  0.0 221.4 jit_solution(973316421459564582)
XLA Ops:
  0.0 1.8 constant_dynamic-update-slice_fusion.9
  1.8 1.6 collective-permute-start
  3.4 2.6 %collective-permute-start.1 = (bf16[128,768]{1,0:T(8,128)(2,1)}, bf16[128,768]{1,0:T(8,128)(2,1)S(1)}, u32[]{:S(2)}, u32[]{:S(2)}) collective-permute-start(bf16[128,768]{1,0:T(8,128)(2,1)} %get-tuple-element.100), channel_id=1, source_target_pairs={{0,8},{4,12},{8,0},{12,4},{1,9},{5,13},{9,1},{13,5},{2,10},{6,14},... | collective-permute-start | bytes 589832 | tf_op jit(solution)/shard_map/ppermute | solution.py:436
  6.0 0.8 dynamic_slice.16
  6.9 2.9 %shard_map.137 = (bf16[768,384]{1,0:T(8,128)(2,1)}, bf16[768,384]{1,0:T(8,128)(2,1)}, bf16[768,384]{1,0:T(8,128)(2,1)}, f32[8,128]{1,0:T(8,128)}) custom-call(f32[768,128]{1,0:T(8,128)S(1)} %broadcast_in_dim.71.gain_ref, bf16[768,1024]{1,0:T(8,128)(2,1)} %refs_0_.3, bf16[768,1024]{1,0:T(8,128)(2,1)} %refs_1_.3, bf16[768,1024]{1,0:T(8,128)(2,1)} %refs_2_.3), custom_call_target="tpu_custom_call" | custom-call | tf_op jit(solution)/shard_map/pallas_call | solution.py:173
  10.8 3.6 %collective-permute-start.13 = (bf16[768,384]{1,0:T(8,128)(2,1)}, bf16[768,384]{1,0:T(8,128)(2,1)}, u32[]{:S(2)}, u32[]{:S(2)}) collective-permute-start(bf16[768,384]{1,0:T(8,128)(2,1)} %get-tuple-element.55), channel_id=1, source_target_pairs={{0,12},{4,8},{8,4},{12,0},{1,13},{5,9},{9,5},{13,1},{2,14},{6,10},... | collective-permute-start | bytes 1769480 | tf_op jit(solution)/shard_map/ppermute | solution.py:436
  14.7 0.6 gather_fusion.1
  15.3 2.0 shard_map.136
  17.4 0.8 copy-done.9
  18.2 0.8 copy-done.11
  19.7 0.7 gather_fusion.3
  21.0 1.8 gather_fusion
  22.8 1.9 shard_map.139
  24.8 1.2 pad_maximum_fusion
  26.0 0.6 collective-permute-start.5
  26.6 28.4 %collective-permute-done.2 = bf16[128,768]{1,0:T(8,128)(2,1)S(1)} collective-permute-done((bf16[128,768]{1,0:T(8,128)(2,1)S(1)}, bf16[128,768]{1,0:T(8,128)(2,1)S(1)}, u32[]{:S(2)}, u32[]{:S(2)}) %collective-permute-start.2) | collective-permute-done | bytes 196640 | tf_op jit(solution)/shard_map/ppermute | solution.py:436
  55.6 0.9 constant_dynamic-update-slice_fusion.8
  57.2 1.7 collective-permute-start.10
  58.9 6.3 %collective-permute-done.6 = bf16[2,128,768]{2,1,0:T(8,128)(2,1)S(1)} collective-permute-done((bf16[2,128,768]{2,1,0:T(8,128)(2,1)S(1)}, bf16[2,128,768]{2,1,0:T(8,128)(2,1)S(1)}, u32[]{:S(2)}, u32[]{:S(2)}) %collective-permute-start.6) | collective-permute-done | bytes 393248 | tf_op jit(solution)/shard_map/ppermute | solution.py:468
  65.3 2.9 %collective-permute-start.15 = (bf16[512,512]{1,0:T(8,128)(2,1)S(1)}, bf16[512,512]{1,0:T(8,128)(2,1)S(1)}, u32[]{:S(2)}, u32[]{:S(2)}) collective-permute-start(bf16[512,512]{1,0:T(8,128)(2,1)S(1)} %get-tuple-element.61), channel_id=1, source_target_pairs={{0,4},{4,0},{8,12},{12,8},{1,5},{5,1},{9,13},{13,9},{2,6},{6,2},{1... | collective-permute-start | bytes 1572872 | tf_op jit(solution)/shard_map/ppermute | solution.py:436
  68.2 1.4 collective-permute-start.16
  69.6 1.2 collective-permute-start.17
  71.3 1.5 collective-permute-done.10.refs_3_.refs_7_
  72.9 2.2 collective-permute-start.14
  75.2 11.8 %collective-permute-done.12.refs_5_.refs_9_ = bf16[768,384]{1,0:T(8,128)(2,1)S(1)} collective-permute-done((bf16[768,384]{1,0:T(8,128)(2,1)S(1)}, bf16[768,384]{1,0:T(8,128)(2,1)S(1)}, u32[]{:S(2)}, u32[]{:S(2)}) %collective-permute-start.12) | collective-permute-done | bytes 589856 | tf_op jit(solution)/shard_map/ppermute | solution.py:485
  87.0 11.6 %collective-permute-done.14.refs_7_.refs_11_ = bf16[768,384]{1,0:T(8,128)(2,1)S(1)} collective-permute-done((bf16[768,384]{1,0:T(8,128)(2,1)}, bf16[768,384]{1,0:T(8,128)(2,1)S(1)}, u32[]{:S(2)}, u32[]{:S(2)}) %collective-permute-start.14) | collective-permute-done | bytes 589856 | tf_op jit(solution)/shard_map/ppermute | solution.py:485
  98.6 5.1 %shard_map.138 = (bf16[512,256]{1,0:T(8,128)(2,1)S(1)}, bf16[512,256]{1,0:T(8,128)(2,1)S(1)}, bf16[512,256]{1,0:T(8,128)(2,1)S(1)}) custom-call(s32[16]{0:T(128)S(1)} %add.171.source_ref, f32[1,128]{1,0:T(1,128)S(1)} %bitcast.41, f32[1,128]{1,0:T(1,128)S(1)} %bitcast.44, bf16[16,128,768]{2,1,0:T(8,128)(2,1)S(1)} %constant_dynamic-update-slice_fusion.gathered_ref, ...), custom_call_target="tpu_custom_call" | custom-call | tf_op jit(solution)/shard_map/pallas_call | solution.py:353
  103.8 2.6 %collective-permute-done.16.refs_2_.refs_14_ = bf16[512,512]{1,0:T(8,128)(2,1)S(1)} collective-permute-done((bf16[512,512]{1,0:T(8,128)(2,1)S(1)}, bf16[512,512]{1,0:T(8,128)(2,1)S(1)}, u32[]{:S(2)}, u32[]{:S(2)}) %collective-permute-start.16) | collective-permute-done | bytes 524320 | tf_op jit(solution)/shard_map/ppermute | solution.py:436
  106.4 1.6 shard_map.140.refs_0_
  108.1 11.2 %collective-permute-start.18 = (bf16[256,256]{1,0:T(8,128)(2,1)S(1)}, bf16[256,256]{1,0:T(8,128)(2,1)S(1)}, u32[]{:S(2)}, u32[]{:S(2)}) collective-permute-start(bf16[256,256]{1,0:T(8,128)(2,1)S(1)} %shard_map.140.refs_0_), channel_id=1, source_target_pairs={{0,4},{4,0},{8,12},{12,8},{1,5},{5,1},{9,13},{13,9},{2,6},{6,2},{1... | collective-permute-start | bytes 393224 | tf_op jit(solution)/shard_map/ppermute | solution.py:436
  119.2 1.1 collective-permute-start.19
  120.4 1.6 shard_map.141.refs_0_
  122.0 2.0 collective-permute-start.21
  124.0 2.1 collective-permute-done.19.refs_2_
  126.1 3.4 %collective-permute-start.20 = (bf16[256,256]{1,0:T(8,128)(2,1)S(1)}, bf16[256,256]{1,0:T(8,128)(2,1)S(1)}, u32[]{:S(2)}, u32[]{:S(2)}) collective-permute-start(bf16[256,256]{1,0:T(8,128)(2,1)S(1)} %collective-permute-done.19.refs_2_), channel_id=1, source_target_pairs={{0,4},{4,0},{8,12},{12,8},{1,5},{5,1},{9,13},{13,9},{2,6},{6,2},{1... | collective-permute-start | bytes 393224 | tf_op jit(solution)/shard_map/ppermute | solution.py:436
  129.9 1.4 collective-permute-done.21.refs_1_
  131.8 1.8 collective-permute-done.20.refs_3_
  134.3 1.7 collective-permute-start.24
  136.0 0.7 add_convert_fusion.2
  136.7 3.5 %collective-permute-done.24.refs_3_ = bf16[256,256]{1,0:T(8,128)(2,1)S(1)} collective-permute-done((bf16[256,256]{1,0:T(8,128)(2,1)S(1)}, bf16[256,256]{1,0:T(8,128)(2,1)S(1)}, u32[]{:S(2)}, u32[]{:S(2)}) %collective-permute-start.24) | collective-permute-done | bytes 131104 | tf_op jit(solution)/shard_map/ppermute | solution.py:436
  140.7 1.3 shard_map.143
  142.1 0.9 dynamic-slice_reduce_fusion
  143.0 4.0 %collective-permute-done.26 = bf16[128,768]{1,0:T(8,128)(2,1)} collective-permute-done((bf16[128,768]{1,0:T(8,128)(2,1)}, bf16[128,768]{1,0:T(8,128)(2,1)}, u32[]{:S(2)}, u32[]{:S(2)}) %collective-permute-start.26) | collective-permute-done | bytes 196640 | tf_op jit(solution)/shard_map/ppermute | solution.py:521
  147.0 1.2 fusion
  148.2 1.7 collective-permute-start.27
  149.9 2.0 collective-permute-start.28
  152.5 5.2 %collective-permute-done.27 = bf16[128,768]{1,0:T(8,128)(2,1)S(1)} collective-permute-done((bf16[128,768]{1,0:T(8,128)(2,1)S(1)}, bf16[128,768]{1,0:T(8,128)(2,1)S(1)}, u32[]{:S(2)}, u32[]{:S(2)}) %collective-permute-start.27) | collective-permute-done | bytes 196640 | tf_op jit(solution)/shard_map/ppermute | solution.py:436
  157.6 2.8 %collective-permute-done.28 = bf16[128,768]{1,0:T(8,128)(2,1)S(1)} collective-permute-done((bf16[128,768]{1,0:T(8,128)(2,1)S(1)}, bf16[128,768]{1,0:T(8,128)(2,1)S(1)}, u32[]{:S(2)}, u32[]{:S(2)}) %collective-permute-start.28) | collective-permute-done | bytes 196640 | tf_op jit(solution)/shard_map/ppermute | solution.py:436
  160.7 5.4 %collective-permute-done.31 = bf16[128,768]{1,0:T(8,128)(2,1)S(1)} collective-permute-done((bf16[128,768]{1,0:T(8,128)(2,1)S(1)}, bf16[128,768]{1,0:T(8,128)(2,1)S(1)}, u32[]{:S(2)}, u32[]{:S(2)}) %collective-permute-start.31) | collective-permute-done | bytes 196640 | tf_op jit(solution)/shard_map/ppermute | solution.py:436
  167.4 1.5 collective-permute-start.32
  168.9 6.2 %shard_map.144 = (bf16[256,256]{1,0:T(8,128)(2,1)S(1)}, bf16[3072,768]{1,0:T(8,128)(2,1)S(1)}, bf16[4,512,512]{2,1,0:T(8,128)(2,1)S(1)}) custom-call(s32[16]{0:T(128)S(1)} %reshape.272.pos_ref, f32[1,128]{1,0:T(1,128)S(1)} %bitcast.42, f32[1,128]{1,0:T(1,128)S(1)} %bitcast.45, bf16[2,128,768]{2,1,0:T(8,128)(2,1)S(1)} %get-tuple-element.105.refs_0_, ...), custom_call_target="tpu_custom_call" | custom-call | tf_op jit(solution)/shard_map/pallas_call | solution.py:376
  175.0 7.1 %collective-permute-done.32.refs_2_ = bf16[1,128,768]{2,1,0:T(8,128)(2,1)S(1)} collective-permute-done((bf16[1,128,768]{2,1,0:T(8,128)(2,1)S(1)}, bf16[1,128,768]{2,1,0:T(8,128)(2,1)S(1)}, u32[]{:S(2)}, u32[]{:S(2)}) %collective-permute-start.32) | collective-permute-done | bytes 196640 | tf_op jit(solution)/shard_map/ppermute | solution.py:531
  182.9 2.7 %collective-permute-start.36 = (bf16[256,256]{1,0:T(8,128)(2,1)S(1)}, bf16[256,256]{1,0:T(8,128)(2,1)S(1)}, u32[]{:S(2)}, u32[]{:S(2)}) collective-permute-start(bf16[256,256]{1,0:T(8,128)(2,1)S(1)} %get-tuple-element.83.refs_0_), channel_id=1, source_target_pairs={{0,8},{4,12},{8,0},{12,4},{1,9},{5,13},{9,1},{13,5},{2,10},{6,14},... | collective-permute-start | bytes 393224 | tf_op jit(solution)/shard_map/ppermute | solution.py:436
  185.6 3.2 %shard_map.146.refs_0_ = bf16[256,256]{1,0:T(8,128)(2,1)S(1)} custom-call(s32[16]{0:T(128)S(1)} %reshape.272.pos_ref, f32[1,128]{1,0:T(1,128)S(1)} %bitcast.43, f32[1,128]{1,0:T(1,128)S(1)} %bitcast.46, bf16[1,128,768]{2,1,0:T(8,128)(2,1)S(1)} %collective-permute-done.29.refs_0_, bf16[2,128,768]{2,1,0:T(8,128)(2,1)S(1)} %collective-permute-done.30.refs_1_, ...), custom_call_target="tpu_custom_call" | custom-call | tf_op jit(solution)/shard_map/pallas_call | solution.py:399
  188.9 2.0 collective-permute-start.44
  191.1 1.3 collective-permute-done.36.refs_2_
  192.8 5.2 %collective-permute-done.43.refs_1_ = bf16[256,256]{1,0:T(8,128)(2,1)S(1)} collective-permute-done((bf16[256,256]{1,0:T(8,128)(2,1)S(1)}, bf16[256,256]{1,0:T(8,128)(2,1)S(1)}, u32[]{:S(2)}, u32[]{:S(2)}) %collective-permute-start.43) | collective-permute-done | bytes 131104 | tf_op jit(solution)/shard_map/ppermute | solution.py:436
  198.5 2.4 %collective-permute-done.37.refs_3_ = bf16[256,256]{1,0:T(8,128)(2,1)S(1)} collective-permute-done((bf16[256,256]{1,0:T(8,128)(2,1)S(1)}, bf16[256,256]{1,0:T(8,128)(2,1)S(1)}, u32[]{:S(2)}, u32[]{:S(2)}) %collective-permute-start.37) | collective-permute-done | bytes 131104 | tf_op jit(solution)/shard_map/ppermute | solution.py:436
  201.6 1.6 collective-permute-done.45.refs_3_
  203.8 1.4 collective-permute-done.46
  205.9 4.1 %collective-permute-start.39 = (bf16[128,768]{1,0:T(8,128)(2,1)S(1)}, bf16[128,768]{1,0:T(8,128)(2,1)S(1)}, u32[]{:S(2)}, u32[]{:S(2)}) collective-permute-start(bf16[128,768]{1,0:T(8,128)(2,1)S(1)} %get-tuple-element.106), channel_id=1, source_target_pairs={{0,0},{1,4},{2,8},{3,12},{4,1},{5,5},{6,9},{7,13},{8,2},{9,6},{10,... | collective-permute-start | bytes 589832 | tf_op jit(solution)/shard_map/ppermute | solution.py:541
  210.0 6.8 %collective-permute-done.47 = bf16[128,768]{1,0:T(8,128)(2,1)S(1)} collective-permute-done((bf16[128,768]{1,0:T(8,128)(2,1)S(1)}, bf16[128,768]{1,0:T(8,128)(2,1)S(1)}, u32[]{:S(2)}, u32[]{:S(2)}) %collective-permute-start.47) | collective-permute-done | bytes 196640 | tf_op jit(solution)/shard_map/ppermute | solution.py:541
  216.8 3.9 %collective-permute-done.39 = bf16[128,768]{1,0:T(8,128)(2,1)S(1)} collective-permute-done((bf16[128,768]{1,0:T(8,128)(2,1)S(1)}, bf16[128,768]{1,0:T(8,128)(2,1)S(1)}, u32[]{:S(2)}, u32[]{:S(2)}) %collective-permute-start.39) | collective-permute-done | bytes 196640 | tf_op jit(solution)/shard_map/ppermute | solution.py:541
  220.7 0.7 add_convert_fusion
  (138 shorter events, 12.6 us)
Async XLA Ops:
  0.0 21.0 %copy-start = (bf16[1024,768]{1,0:T(8,128)(2,1)S(1)}, bf16[1024,768]{1,0:T(8,128)(2,1)}, u32[]{:S(2)}) copy-start(bf16[1024,768]{1,0:T(8,128)(2,1)} %param.19) | copy-start | bytes 4718596
  1.8 22.9 %collective-permute-start = (bf16[128,768]{1,0:T(8,128)(2,1)}, bf16[128,768]{1,0:T(8,128)(2,1)}, u32[]{:S(2)}, u32[]{:S(2)}) collective-permute-start(bf16[128,768]{1,0:T(8,128)(2,1)} %get-tuple-element.100), channel_id=1, source_target_pairs={{0,4},{4,0},{8,12},{12,8},{1,5},{5,1},{9,13},{13,9},{2,6},{6,2},{1... | collective-permute-start | bytes 589832 | tf_op jit(solution)/shard_map/ppermute | solution.py:436
  3.4 17.5 %collective-permute-start.1 = (bf16[128,768]{1,0:T(8,128)(2,1)}, bf16[128,768]{1,0:T(8,128)(2,1)S(1)}, u32[]{:S(2)}, u32[]{:S(2)}) collective-permute-start(bf16[128,768]{1,0:T(8,128)(2,1)} %get-tuple-element.100), channel_id=1, source_target_pairs={{0,8},{4,12},{8,0},{12,4},{1,9},{5,13},{9,1},{13,5},{2,10},{6,14},... | collective-permute-start | bytes 589832 | tf_op jit(solution)/shard_map/ppermute | solution.py:436
  9.9 46.7 %collective-permute-start.9 = (bf16[768,384]{1,0:T(8,128)(2,1)}, bf16[768,384]{1,0:T(8,128)(2,1)S(1)}, u32[]{:S(2)}, u32[]{:S(2)}) collective-permute-start(bf16[768,384]{1,0:T(8,128)(2,1)} %get-tuple-element.53), channel_id=1, source_target_pairs={{0,4},{4,0},{8,12},{12,8},{1,5},{5,1},{9,13},{13,9},{2,6},{6,2},{1... | collective-permute-start | bytes 1769480 | tf_op jit(solution)/shard_map/ppermute | solution.py:436
  10.4 46.7 %collective-permute-start.11 = (bf16[768,384]{1,0:T(8,128)(2,1)}, bf16[768,384]{1,0:T(8,128)(2,1)S(1)}, u32[]{:S(2)}, u32[]{:S(2)}) collective-permute-start(bf16[768,384]{1,0:T(8,128)(2,1)} %get-tuple-element.54), channel_id=1, source_target_pairs={{0,8},{4,12},{8,0},{12,4},{1,9},{5,13},{9,1},{13,5},{2,10},{6,14},... | collective-permute-start | bytes 1769480 | tf_op jit(solution)/shard_map/ppermute | solution.py:436
  10.8 46.4 %collective-permute-start.13 = (bf16[768,384]{1,0:T(8,128)(2,1)}, bf16[768,384]{1,0:T(8,128)(2,1)}, u32[]{:S(2)}, u32[]{:S(2)}) collective-permute-start(bf16[768,384]{1,0:T(8,128)(2,1)} %get-tuple-element.55), channel_id=1, source_target_pairs={{0,12},{4,8},{8,4},{12,0},{1,13},{5,9},{9,5},{13,1},{2,14},{6,10},... | collective-permute-start | bytes 1769480 | tf_op jit(solution)/shard_map/ppermute | solution.py:436
  21.0 34.1 %collective-permute-start.2 = (bf16[128,768]{1,0:T(8,128)(2,1)S(1)}, bf16[128,768]{1,0:T(8,128)(2,1)S(1)}, u32[]{:S(2)}, u32[]{:S(2)}) collective-permute-start(bf16[128,768]{1,0:T(8,128)(2,1)S(1)} %collective-permute-done.1), channel_id=1, source_target_pairs={{0,4},{4,0},{8,12},{12,8},{1,5},{5,1},{9,13},{13,9},{2,6},{6,2},{1... | collective-permute-start | bytes 589832 | tf_op jit(solution)/shard_map/ppermute | solution.py:436
  22.8 32.7 %copy-start.5 = (bf16[16,128,768]{2,1,0:T(8,128)(2,1)S(1)}, bf16[16,128,768]{2,1,0:T(8,128)(2,1)}, u32[]{:S(2)}) copy-start(bf16[16,128,768]{2,1,0:T(8,128)(2,1)} %get-tuple-element.99) | copy-start | bytes 9437188
  24.8 95.6 %copy-start.1 = (bf16[512,512]{1,0:T(8,128)(2,1)}, bf16[512,512]{1,0:T(8,128)(2,1)S(1)}, u32[]{:S(2)}) copy-start(bf16[512,512]{1,0:T(8,128)(2,1)S(1)} %get-tuple-element.59.refs_0_.refs_12_) | copy-start | bytes 1572868
  26.0 30.5 %collective-permute-start.5 = (bf16[2,128,768]{2,1,0:T(8,128)(2,1)S(1)}, bf16[2,128,768]{2,1,0:T(8,128)(2,1)S(1)}, u32[]{:S(2)}, u32[]{:S(2)}) collective-permute-start(bf16[2,128,768]{2,1,0:T(8,128)(2,1)S(1)} %pad_maximum_fusion), channel_id=1, source_target_pairs={{0,2},{2,0},{1,3},{3,1},{4,6},{6,4},{5,7},{7,5},{8,10},{10,8},{9,1... | collective-permute-start | bytes 1179656 | tf_op jit(solution)/shard_map/ppermute | solution.py:466
  55.1 43.5 %copy-start.10 = (bf16[768,384]{1,0:T(8,128)(2,1)S(1)}, bf16[768,384]{1,0:T(8,128)(2,1)}, u32[]{:S(2)}) copy-start(bf16[768,384]{1,0:T(8,128)(2,1)} %copy-done.9) | copy-start | bytes 1769476
  55.1 43.5 %copy-start.12 = (bf16[768,384]{1,0:T(8,128)(2,1)S(1)}, bf16[768,384]{1,0:T(8,128)(2,1)}, u32[]{:S(2)}) copy-start(bf16[768,384]{1,0:T(8,128)(2,1)} %copy-done.11) | copy-start | bytes 1769476
  55.1 43.5 %copy-start.16 = (f32[128]{0:T(128)S(1)}, f32[128]{0:T(128)}, u32[]{:S(2)}) copy-start(f32[128]{0:T(128)} %param.20) | copy-start | bytes 1540
  55.1 43.5 %copy-start.17 = (f32[128]{0:T(128)S(1)}, f32[128]{0:T(128)}, u32[]{:S(2)}) copy-start(f32[128]{0:T(128)} %param.21) | copy-start | bytes 1540
  55.1 10.1 %collective-permute-start.6 = (bf16[2,128,768]{2,1,0:T(8,128)(2,1)S(1)}, bf16[2,128,768]{2,1,0:T(8,128)(2,1)S(1)}, u32[]{:S(2)}, u32[]{:S(2)}) collective-permute-start(bf16[2,128,768]{2,1,0:T(8,128)(2,1)S(1)} %pad_maximum_fusion.1), channel_id=1, source_target_pairs={{0,2},{2,0},{1,3},{3,1},{4,6},{6,4},{5,7},{7,5},{8,10},{10,8},{9,1... | collective-permute-start | bytes 1179656 | tf_op jit(solution)/shard_map/ppermute | solution.py:468
  56.5 8.7 %collective-permute-start.3 = (bf16[2,128,768]{2,1,0:T(8,128)(2,1)S(1)}, bf16[2,128,768]{2,1,0:T(8,128)(2,1)S(1)}, u32[]{:S(2)}, u32[]{:S(2)}) collective-permute-start(bf16[2,128,768]{2,1,0:T(8,128)(2,1)S(1)} %pad_maximum_fusion), channel_id=1, source_target_pairs={{0,1},{1,0},{2,3},{3,2},{4,5},{5,4},{6,7},{7,6},{8,9},{9,8},{10,11... | collective-permute-start | bytes 1179656 | tf_op jit(solution)/shard_map/ppermute | solution.py:470
  56.6 47.1 %copy-start.7 = (bf16[768,384]{1,0:T(8,128)(2,1)}, bf16[768,384]{1,0:T(8,128)(2,1)S(1)}, u32[]{:S(2)}) copy-start(bf16[768,384]{1,0:T(8,128)(2,1)S(1)} %collective-permute-done.9.refs_2_.refs_6_) | copy-start | bytes 1769476
  56.6 11.5 %collective-permute-start.4 = (bf16[2,128,768]{2,1,0:T(8,128)(2,1)S(1)}, bf16[2,128,768]{2,1,0:T(8,128)(2,1)S(1)}, u32[]{:S(2)}, u32[]{:S(2)}) collective-permute-start(bf16[2,128,768]{2,1,0:T(8,128)(2,1)S(1)} %pad_maximum_fusion.1), channel_id=1, source_target_pairs={{0,1},{1,0},{2,3},{3,2},{4,5},{5,4},{6,7},{7,6},{8,9},{9,8},{10,11... | collective-permute-start | bytes 1179656 | tf_op jit(solution)/shard_map/ppermute | solution.py:470
  57.1 46.6 %copy-start.8 = (bf16[768,384]{1,0:T(8,128)(2,1)}, bf16[768,384]{1,0:T(8,128)(2,1)S(1)}, u32[]{:S(2)}) copy-start(bf16[768,384]{1,0:T(8,128)(2,1)S(1)} %collective-permute-done.11.refs_4_.refs_8_) | copy-start | bytes 1769476
  57.1 12.5 %collective-permute-start.7 = (bf16[2,128,768]{2,1,0:T(8,128)(2,1)S(1)}, bf16[2,128,768]{2,1,0:T(8,128)(2,1)S(1)}, u32[]{:S(2)}, u32[]{:S(2)}) collective-permute-start(bf16[2,128,768]{2,1,0:T(8,128)(2,1)S(1)} %collective-permute-done.5), channel_id=1, source_target_pairs={{0,1},{1,0},{2,3},{3,2},{4,5},{5,4},{6,7},{7,6},{8,9},{9,8},{10,11... | collective-permute-start | bytes 1179656 | tf_op jit(solution)/shard_map/ppermute | solution.py:470
  57.2 15.7 %collective-permute-start.10 = (bf16[768,384]{1,0:T(8,128)(2,1)S(1)}, bf16[768,384]{1,0:T(8,128)(2,1)S(1)}, u32[]{:S(2)}, u32[]{:S(2)}) collective-permute-start(bf16[768,384]{1,0:T(8,128)(2,1)S(1)} %collective-permute-done.9.refs_2_.refs_6_), channel_id=1, source_target_pairs={{0,16},{16,0},{1,17},{17,1},{2,18},{18,2},{3,19},{19,3},{4,20},{20... | collective-permute-start | bytes 1769480 | tf_op jit(solution)/shard_map/ppermute | solution.py:485
  65.2 5.6 %collective-permute-start.8 = (bf16[2,128,768]{2,1,0:T(8,128)(2,1)S(1)}, bf16[2,128,768]{2,1,0:T(8,128)(2,1)S(1)}, u32[]{:S(2)}, u32[]{:S(2)}) collective-permute-start(bf16[2,128,768]{2,1,0:T(8,128)(2,1)S(1)} %collective-permute-done.6), channel_id=1, source_target_pairs={{0,1},{1,0},{2,3},{3,2},{4,5},{5,4},{6,7},{7,6},{8,9},{9,8},{10,11... | collective-permute-start | bytes 1179656 | tf_op jit(solution)/shard_map/ppermute | solution.py:470
  65.3 38.5 %collective-permute-start.15 = (bf16[512,512]{1,0:T(8,128)(2,1)S(1)}, bf16[512,512]{1,0:T(8,128)(2,1)S(1)}, u32[]{:S(2)}, u32[]{:S(2)}) collective-permute-start(bf16[512,512]{1,0:T(8,128)(2,1)S(1)} %get-tuple-element.61), channel_id=1, source_target_pairs={{0,4},{4,0},{8,12},{12,8},{1,5},{5,1},{9,13},{13,9},{2,6},{6,2},{1... | collective-permute-start | bytes 1572872 | tf_op jit(solution)/shard_map/ppermute | solution.py:436
  68.2 38.2 %collective-permute-start.16 = (bf16[512,512]{1,0:T(8,128)(2,1)S(1)}, bf16[512,512]{1,0:T(8,128)(2,1)S(1)}, u32[]{:S(2)}, u32[]{:S(2)}) collective-permute-start(bf16[512,512]{1,0:T(8,128)(2,1)S(1)} %get-tuple-element.63), channel_id=1, source_target_pairs={{0,8},{4,12},{8,0},{12,4},{1,9},{5,13},{9,1},{13,5},{2,10},{6,14},... | collective-permute-start | bytes 1572872 | tf_op jit(solution)/shard_map/ppermute | solution.py:436
  69.6 36.8 %collective-permute-start.17 = (bf16[512,512]{1,0:T(8,128)(2,1)S(1)}, bf16[512,512]{1,0:T(8,128)(2,1)S(1)}, u32[]{:S(2)}, u32[]{:S(2)}) collective-permute-start(bf16[512,512]{1,0:T(8,128)(2,1)S(1)} %get-tuple-element.65), channel_id=1, source_target_pairs={{0,12},{4,8},{8,4},{12,0},{1,13},{5,9},{9,5},{13,1},{2,14},{6,10},... | collective-permute-start | bytes 1572872 | tf_op jit(solution)/shard_map/ppermute | solution.py:436
  70.8 16.2 %collective-permute-start.12 = (bf16[768,384]{1,0:T(8,128)(2,1)S(1)}, bf16[768,384]{1,0:T(8,128)(2,1)S(1)}, u32[]{:S(2)}, u32[]{:S(2)}) collective-permute-start(bf16[768,384]{1,0:T(8,128)(2,1)S(1)} %collective-permute-done.11.refs_4_.refs_8_), channel_id=1, source_target_pairs={{0,16},{16,0},{1,17},{17,1},{2,18},{18,2},{3,19},{19,3},{4,20},{20... | collective-permute-start | bytes 1769480 | tf_op jit(solution)/shard_map/ppermute | solution.py:485
  72.9 30.8 %copy-start.13 = (bf16[768,384]{1,0:T(8,128)(2,1)}, bf16[768,384]{1,0:T(8,128)(2,1)S(1)}, u32[]{:S(2)}) copy-start(bf16[768,384]{1,0:T(8,128)(2,1)S(1)} %collective-permute-done.10.refs_3_.refs_7_) | copy-start | bytes 1769476
  72.9 25.7 %collective-permute-start.14 = (bf16[768,384]{1,0:T(8,128)(2,1)}, bf16[768,384]{1,0:T(8,128)(2,1)S(1)}, u32[]{:S(2)}, u32[]{:S(2)}) collective-permute-start(bf16[768,384]{1,0:T(8,128)(2,1)} %collective-permute-done.13.refs_6_.refs_10_), channel_id=1, source_target_pairs={{0,16},{16,0},{1,17},{17,1},{2,18},{18,2},{3,19},{19,3},{4,20},{20... | collective-permute-start | bytes 1769480 | tf_op jit(solution)/shard_map/ppermute | solution.py:485
  75.2 28.5 %copy-start.6 = (bf16[16,128,768]{2,1,0:T(8,128)(2,1)}, bf16[16,128,768]{2,1,0:T(8,128)(2,1)S(1)}, u32[]{:S(2)}) copy-start(bf16[16,128,768]{2,1,0:T(8,128)(2,1)S(1)} %constant_dynamic-update-slice_fusion.gathered_ref) | copy-start | bytes 9437188
  87.0 16.8 %copy-start.14 = (bf16[768,384]{1,0:T(8,128)(2,1)}, bf16[768,384]{1,0:T(8,128)(2,1)S(1)}, u32[]{:S(2)}) copy-start(bf16[768,384]{1,0:T(8,128)(2,1)S(1)} %collective-permute-done.12.refs_5_.refs_9_) | copy-start | bytes 1769476
  103.8 25.8 %copy-start.20 = (bf16[8,128,768]{2,1,0:T(8,128)(2,1)S(1)}, bf16[8,128,768]{2,1,0:T(8,128)(2,1)}, u32[]{:S(2)}) copy-start(bf16[8,128,768]{2,1,0:T(8,128)(2,1)} %gather_fusion) | copy-start | bytes 4718596
  103.8 26.1 %copy-start.2 = (bf16[512,512]{1,0:T(8,128)(2,1)}, bf16[512,512]{1,0:T(8,128)(2,1)S(1)}, u32[]{:S(2)}) copy-start(bf16[512,512]{1,0:T(8,128)(2,1)S(1)} %collective-permute-done.15.refs_1_.refs_13_) | copy-start | bytes 1572868
  106.4 23.5 %copy-start.3 = (bf16[512,512]{1,0:T(8,128)(2,1)}, bf16[512,512]{1,0:T(8,128)(2,1)S(1)}, u32[]{:S(2)}) copy-start(bf16[512,512]{1,0:T(8,128)(2,1)S(1)} %collective-permute-done.16.refs_2_.refs_14_) | copy-start | bytes 1572868
  106.4 23.5 %copy-start.4 = (bf16[512,512]{1,0:T(8,128)(2,1)}, bf16[512,512]{1,0:T(8,128)(2,1)S(1)}, u32[]{:S(2)}) copy-start(bf16[512,512]{1,0:T(8,128)(2,1)S(1)} %collective-permute-done.17.refs_3_.refs_15_) | copy-start | bytes 1572868
  108.1 16.0 %collective-permute-start.18 = (bf16[256,256]{1,0:T(8,128)(2,1)S(1)}, bf16[256,256]{1,0:T(8,128)(2,1)S(1)}, u32[]{:S(2)}, u32[]{:S(2)}) collective-permute-start(bf16[256,256]{1,0:T(8,128)(2,1)S(1)} %shard_map.140.refs_0_), channel_id=1, source_target_pairs={{0,4},{4,0},{8,12},{12,8},{1,5},{5,1},{9,13},{13,9},{2,6},{6,2},{1... | collective-permute-start | bytes 393224 | tf_op jit(solution)/shard_map/ppermute | solution.py:436
  119.2 6.9 %collective-permute-start.19 = (bf16[256,256]{1,0:T(8,128)(2,1)S(1)}, bf16[256,256]{1,0:T(8,128)(2,1)S(1)}, u32[]{:S(2)}, u32[]{:S(2)}) collective-permute-start(bf16[256,256]{1,0:T(8,128)(2,1)S(1)} %shard_map.140.refs_0_), channel_id=1, source_target_pairs={{0,8},{4,12},{8,0},{12,4},{1,9},{5,13},{9,1},{13,5},{2,10},{6,14},... | collective-permute-start | bytes 393224 | tf_op jit(solution)/shard_map/ppermute | solution.py:436
  122.0 9.3 %collective-permute-start.21 = (bf16[256,256]{1,0:T(8,128)(2,1)S(1)}, bf16[256,256]{1,0:T(8,128)(2,1)S(1)}, u32[]{:S(2)}, u32[]{:S(2)}) collective-permute-start(bf16[256,256]{1,0:T(8,128)(2,1)S(1)} %shard_map.141.refs_0_), channel_id=1, source_target_pairs={{0,4},{4,0},{8,12},{12,8},{1,5},{5,1},{9,13},{13,9},{2,6},{6,2},{1... | collective-permute-start | bytes 393224 | tf_op jit(solution)/shard_map/ppermute | solution.py:436
  124.0 7.8 %collective-permute-start.22 = (bf16[256,256]{1,0:T(8,128)(2,1)S(1)}, bf16[256,256]{1,0:T(8,128)(2,1)S(1)}, u32[]{:S(2)}, u32[]{:S(2)}) collective-permute-start(bf16[256,256]{1,0:T(8,128)(2,1)S(1)} %shard_map.141.refs_0_), channel_id=1, source_target_pairs={{0,8},{4,12},{8,0},{12,4},{1,9},{5,13},{9,1},{13,5},{2,10},{6,14},... | collective-permute-start | bytes 393224 | tf_op jit(solution)/shard_map/ppermute | solution.py:436
  126.1 7.5 %collective-permute-start.20 = (bf16[256,256]{1,0:T(8,128)(2,1)S(1)}, bf16[256,256]{1,0:T(8,128)(2,1)S(1)}, u32[]{:S(2)}, u32[]{:S(2)}) collective-permute-start(bf16[256,256]{1,0:T(8,128)(2,1)S(1)} %collective-permute-done.19.refs_2_), channel_id=1, source_target_pairs={{0,4},{4,0},{8,12},{12,8},{1,5},{5,1},{9,13},{13,9},{2,6},{6,2},{1... | collective-permute-start | bytes 393224 | tf_op jit(solution)/shard_map/ppermute | solution.py:436
  134.2 1.8 collective-permute-start.23
  134.3 5.9 %collective-permute-start.24 = (bf16[256,256]{1,0:T(8,128)(2,1)S(1)}, bf16[256,256]{1,0:T(8,128)(2,1)S(1)}, u32[]{:S(2)}, u32[]{:S(2)}) collective-permute-start(bf16[256,256]{1,0:T(8,128)(2,1)S(1)} %collective-permute-done.22.refs_2_), channel_id=1, source_target_pairs={{0,4},{4,0},{8,12},{12,8},{1,5},{5,1},{9,13},{13,9},{2,6},{6,2},{1... | collective-permute-start | bytes 393224 | tf_op jit(solution)/shard_map/ppermute | solution.py:436
  140.2 6.8 %collective-permute-start.26 = (bf16[128,768]{1,0:T(8,128)(2,1)}, bf16[128,768]{1,0:T(8,128)(2,1)}, u32[]{:S(2)}, u32[]{:S(2)}) collective-permute-start(bf16[128,768]{1,0:T(8,128)(2,1)} %add_convert_fusion.2), channel_id=1, source_target_pairs={{0,2},{2,0},{1,3},{3,1},{4,6},{6,4},{5,7},{7,5},{8,10},{10,8},{9,1... | collective-permute-start | bytes 589832 | tf_op jit(solution)/shard_map/ppermute | solution.py:521
  142.0 5.0 %collective-permute-start.25 = (bf16[128,768]{1,0:T(8,128)(2,1)}, bf16[128,768]{1,0:T(8,128)(2,1)}, u32[]{:S(2)}, u32[]{:S(2)}) collective-permute-start(bf16[128,768]{1,0:T(8,128)(2,1)} %get-tuple-element.78), channel_id=1, source_target_pairs={{0,1},{1,0},{2,3},{3,2},{4,5},{5,4},{6,7},{7,6},{8,9},{9,8},{10,11... | collective-permute-start | bytes 589832 | tf_op jit(solution)/shard_map/ppermute | solution.py:512
  148.2 9.4 %collective-permute-start.27 = (bf16[128,768]{1,0:T(8,128)(2,1)S(1)}, bf16[128,768]{1,0:T(8,128)(2,1)S(1)}, u32[]{:S(2)}, u32[]{:S(2)}) collective-permute-start(bf16[128,768]{1,0:T(8,128)(2,1)S(1)} %fusion), channel_id=1, source_target_pairs={{0,4},{4,0},{8,12},{12,8},{1,5},{5,1},{9,13},{13,9},{2,6},{6,2},{1... | collective-permute-start | bytes 589832 | tf_op jit(solution)/shard_map/ppermute | solution.py:436
  149.9 10.6 %collective-permute-start.28 = (bf16[128,768]{1,0:T(8,128)(2,1)S(1)}, bf16[128,768]{1,0:T(8,128)(2,1)S(1)}, u32[]{:S(2)}, u32[]{:S(2)}) collective-permute-start(bf16[128,768]{1,0:T(8,128)(2,1)S(1)} %fusion), channel_id=1, source_target_pairs={{0,8},{4,12},{8,0},{12,4},{1,9},{5,13},{9,1},{13,5},{2,10},{6,14},... | collective-permute-start | bytes 589832 | tf_op jit(solution)/shard_map/ppermute | solution.py:436
  151.9 8.5 %collective-permute-start.29 = (bf16[1,128,768]{2,1,0:T(8,128)(2,1)S(1)}, bf16[1,128,768]{2,1,0:T(8,128)(2,1)S(1)}, u32[]{:S(2)}, u32[]{:S(2)}) collective-permute-start(bf16[1,128,768]{2,1,0:T(8,128)(2,1)S(1)} %bitcast.50), channel_id=1, source_target_pairs={{0,2},{2,0},{1,3},{3,1},{4,6},{6,4},{5,7},{7,5},{8,10},{10,8},{9,1... | collective-permute-start | bytes 589832 | tf_op jit(solution)/shard_map/ppermute | solution.py:526
  160.5 5.7 %collective-permute-start.31 = (bf16[128,768]{1,0:T(8,128)(2,1)S(1)}, bf16[128,768]{1,0:T(8,128)(2,1)S(1)}, u32[]{:S(2)}, u32[]{:S(2)}) collective-permute-start(bf16[128,768]{1,0:T(8,128)(2,1)S(1)} %collective-permute-done.28), channel_id=1, source_target_pairs={{0,4},{4,0},{8,12},{12,8},{1,5},{5,1},{9,13},{13,9},{2,6},{6,2},{1... | collective-permute-start | bytes 589832 | tf_op jit(solution)/shard_map/ppermute | solution.py:436
  166.2 2.6 %collective-permute-start.33 = (bf16[2,128,768]{2,1,0:T(8,128)(2,1)S(1)}, bf16[2,128,768]{2,1,0:T(8,128)(2,1)S(1)}, u32[]{:S(2)}, u32[]{:S(2)}) collective-permute-start(bf16[2,128,768]{2,1,0:T(8,128)(2,1)S(1)} %get-tuple-element.105.refs_0_), channel_id=1, source_target_pairs={{0,1},{1,0},{2,3},{3,2},{4,5},{5,4},{6,7},{7,6},{8,9},{9,8},{10,11... | collective-permute-start | bytes 1179656 | tf_op jit(solution)/shard_map/ppermute | solution.py:530
  166.3 2.5 %collective-permute-start.34 = (bf16[2,128,768]{2,1,0:T(8,128)(2,1)S(1)}, bf16[2,128,768]{2,1,0:T(8,128)(2,1)S(1)}, u32[]{:S(2)}, u32[]{:S(2)}) collective-permute-start(bf16[2,128,768]{2,1,0:T(8,128)(2,1)S(1)} %get-tuple-element.103.refs_1_), channel_id=1, source_target_pairs={{0,1},{1,0},{2,3},{3,2},{4,5},{5,4},{6,7},{7,6},{8,9},{9,8},{10,11... | collective-permute-start | bytes 1179656 | tf_op jit(solution)/shard_map/ppermute | solution.py:530
  166.8 15.3 %collective-permute-start.30 = (bf16[2,128,768]{2,1,0:T(8,128)(2,1)S(1)}, bf16[2,128,768]{2,1,0:T(8,128)(2,1)S(1)}, u32[]{:S(2)}, u32[]{:S(2)}) collective-permute-start(bf16[2,128,768]{2,1,0:T(8,128)(2,1)S(1)} %get-tuple-element.104), channel_id=1, source_target_pairs={{0,2},{2,0},{1,3},{3,1},{4,6},{6,4},{5,7},{7,5},{8,10},{10,8},{9,1... | collective-permute-start | bytes 1179656 | tf_op jit(solution)/shard_map/ppermute | solution.py:531
  167.4 14.8 %collective-permute-start.32 = (bf16[1,128,768]{2,1,0:T(8,128)(2,1)S(1)}, bf16[1,128,768]{2,1,0:T(8,128)(2,1)S(1)}, u32[]{:S(2)}, u32[]{:S(2)}) collective-permute-start(bf16[1,128,768]{2,1,0:T(8,128)(2,1)S(1)} %bitcast.55), channel_id=1, source_target_pairs={{0,2},{2,0},{1,3},{3,1},{4,6},{6,4},{5,7},{7,5},{8,10},{10,8},{9,1... | collective-permute-start | bytes 589832 | tf_op jit(solution)/shard_map/ppermute | solution.py:531
  182.1 3.5 %collective-permute-start.41 = (bf16[2,128,768]{2,1,0:T(8,128)(2,1)S(1)}, bf16[2,128,768]{2,1,0:T(8,128)(2,1)S(1)}, u32[]{:S(2)}, u32[]{:S(2)}) collective-permute-start(bf16[2,128,768]{2,1,0:T(8,128)(2,1)S(1)} %collective-permute-done.30.refs_1_), channel_id=1, source_target_pairs={{0,1},{1,0},{2,3},{3,2},{4,5},{5,4},{6,7},{7,6},{8,9},{9,8},{10,11... | collective-permute-start | bytes 1179656 | tf_op jit(solution)/shard_map/ppermute | solution.py:536
  182.1 3.5 %collective-permute-start.40 = (bf16[1,128,768]{2,1,0:T(8,128)(2,1)S(1)}, bf16[1,128,768]{2,1,0:T(8,128)(2,1)S(1)}, u32[]{:S(2)}, u32[]{:S(2)}) collective-permute-start(bf16[1,128,768]{2,1,0:T(8,128)(2,1)S(1)} %collective-permute-done.29.refs_0_), channel_id=1, source_target_pairs={{0,1},{1,0},{2,3},{3,2},{4,5},{5,4},{6,7},{7,6},{8,9},{9,8},{10,11... | collective-permute-start | bytes 589832 | tf_op jit(solution)/shard_map/ppermute | solution.py:536
  182.6 3.0 %collective-permute-start.42 = (bf16[1,128,768]{2,1,0:T(8,128)(2,1)S(1)}, bf16[1,128,768]{2,1,0:T(8,128)(2,1)S(1)}, u32[]{:S(2)}, u32[]{:S(2)}) collective-permute-start(bf16[1,128,768]{2,1,0:T(8,128)(2,1)S(1)} %collective-permute-done.32.refs_2_), channel_id=1, source_target_pairs={{0,1},{1,0},{2,3},{3,2},{4,5},{5,4},{6,7},{7,6},{8,9},{9,8},{10,11... | collective-permute-start | bytes 589832 | tf_op jit(solution)/shard_map/ppermute | solution.py:536
  182.7 8.5 %collective-permute-start.35 = (bf16[256,256]{1,0:T(8,128)(2,1)S(1)}, bf16[256,256]{1,0:T(8,128)(2,1)S(1)}, u32[]{:S(2)}, u32[]{:S(2)}) collective-permute-start(bf16[256,256]{1,0:T(8,128)(2,1)S(1)} %get-tuple-element.83.refs_0_), channel_id=1, source_target_pairs={{0,4},{4,0},{8,12},{12,8},{1,5},{5,1},{9,13},{13,9},{2,6},{6,2},{1... | collective-permute-start | bytes 393224 | tf_op jit(solution)/shard_map/ppermute | solution.py:436
  182.9 9.6 %collective-permute-start.36 = (bf16[256,256]{1,0:T(8,128)(2,1)S(1)}, bf16[256,256]{1,0:T(8,128)(2,1)S(1)}, u32[]{:S(2)}, u32[]{:S(2)}) collective-permute-start(bf16[256,256]{1,0:T(8,128)(2,1)S(1)} %get-tuple-element.83.refs_0_), channel_id=1, source_target_pairs={{0,8},{4,12},{8,0},{12,4},{1,9},{5,13},{9,1},{13,5},{2,10},{6,14},... | collective-permute-start | bytes 393224 | tf_op jit(solution)/shard_map/ppermute | solution.py:436
  188.8 9.2 %collective-permute-start.43 = (bf16[256,256]{1,0:T(8,128)(2,1)S(1)}, bf16[256,256]{1,0:T(8,128)(2,1)S(1)}, u32[]{:S(2)}, u32[]{:S(2)}) collective-permute-start(bf16[256,256]{1,0:T(8,128)(2,1)S(1)} %shard_map.146.refs_0_), channel_id=1, source_target_pairs={{0,4},{4,0},{8,12},{12,8},{1,5},{5,1},{9,13},{13,9},{2,6},{6,2},{1... | collective-permute-start | bytes 393224 | tf_op jit(solution)/shard_map/ppermute | solution.py:436
  188.9 9.2 %collective-permute-start.44 = (bf16[256,256]{1,0:T(8,128)(2,1)S(1)}, bf16[256,256]{1,0:T(8,128)(2,1)S(1)}, u32[]{:S(2)}, u32[]{:S(2)}) collective-permute-start(bf16[256,256]{1,0:T(8,128)(2,1)S(1)} %shard_map.146.refs_0_), channel_id=1, source_target_pairs={{0,8},{4,12},{8,0},{12,4},{1,9},{5,13},{9,1},{13,5},{2,10},{6,14},... | collective-permute-start | bytes 393224 | tf_op jit(solution)/shard_map/ppermute | solution.py:436
  192.5 8.4 %collective-permute-start.37 = (bf16[256,256]{1,0:T(8,128)(2,1)S(1)}, bf16[256,256]{1,0:T(8,128)(2,1)S(1)}, u32[]{:S(2)}, u32[]{:S(2)}) collective-permute-start(bf16[256,256]{1,0:T(8,128)(2,1)S(1)} %collective-permute-done.36.refs_2_), channel_id=1, source_target_pairs={{0,4},{4,0},{8,12},{12,8},{1,5},{5,1},{9,13},{13,9},{2,6},{6,2},{1... | collective-permute-start | bytes 393224 | tf_op jit(solution)/shard_map/ppermute | solution.py:436
  198.1 5.0 %collective-permute-start.45 = (bf16[256,256]{1,0:T(8,128)(2,1)S(1)}, bf16[256,256]{1,0:T(8,128)(2,1)S(1)}, u32[]{:S(2)}, u32[]{:S(2)}) collective-permute-start(bf16[256,256]{1,0:T(8,128)(2,1)S(1)} %collective-permute-done.44.refs_2_), channel_id=1, source_target_pairs={{0,4},{4,0},{8,12},{12,8},{1,5},{5,1},{9,13},{13,9},{2,6},{6,2},{1... | collective-permute-start | bytes 393224 | tf_op jit(solution)/shard_map/ppermute | solution.py:436
  201.5 2.3 %collective-permute-start.38 = (bf16[128,768]{1,0:T(8,128)(2,1)S(1)}, bf16[128,768]{1,0:T(8,128)(2,1)S(1)}, u32[]{:S(2)}, u32[]{:S(2)}) collective-permute-start(bf16[128,768]{1,0:T(8,128)(2,1)S(1)} %get-tuple-element.87), channel_id=1, source_target_pairs={{0,1},{1,0},{2,3},{3,2},{4,5},{5,4},{6,7},{7,6},{8,9},{9,8},{10,11... | collective-permute-start | bytes 589832 | tf_op jit(solution)/shard_map/ppermute | solution.py:512
  203.7 1.5 collective-permute-start.46
  205.3 11.4 %collective-permute-start.47 = (bf16[128,768]{1,0:T(8,128)(2,1)S(1)}, bf16[128,768]{1,0:T(8,128)(2,1)S(1)}, u32[]{:S(2)}, u32[]{:S(2)}) collective-permute-start(bf16[128,768]{1,0:T(8,128)(2,1)S(1)} %get-tuple-element.107), channel_id=1, source_target_pairs={{0,8},{1,12},{2,0},{3,4},{4,9},{5,13},{6,1},{7,5},{8,10},{9,14},{1... | collective-permute-start | bytes 589832 | tf_op jit(solution)/shard_map/ppermute | solution.py:541
  205.9 14.8 %collective-permute-start.39 = (bf16[128,768]{1,0:T(8,128)(2,1)S(1)}, bf16[128,768]{1,0:T(8,128)(2,1)S(1)}, u32[]{:S(2)}, u32[]{:S(2)}) collective-permute-start(bf16[128,768]{1,0:T(8,128)(2,1)S(1)} %get-tuple-element.106), channel_id=1, source_target_pairs={{0,0},{1,4},{2,8},{3,12},{4,1},{5,5},{6,9},{7,13},{8,2},{9,6},{10,... | collective-permute-start | bytes 589832 | tf_op jit(solution)/shard_map/ppermute | solution.py:541
  (6 other events, 40.4 us)
